TPU v7x, 128 devices: a whole 4x4x4 slice. The times are simulated.
128 devices in a mesh: gx: 8 (over y, x_lo), gy: 8 (over z, core), sa: 2 (over x_hi).
Axes of the slice: x: 4 (x_hi: 2, x_lo: 2; x = x_hi * 2 + x_lo), y: 4, z: 4, core: 2. Of those that a mesh axis runs over, the one named last changes fastest.
Arguments:
- sweep_bricks: bfloat16 [8, 8, 256, 64, 128], P('gx', 'gy', 'sa'), may hold values from -24 to 24
- target_rank: int32 [8, 8, 256, 1], P('gx', 'gy', 'sa'), may hold values from 0 to 15; in each aligned block of 128 rows (0 to 127, 128 to 255, ..., all dimensions but the last counted through in order) at most 16 rows name the same one
- target_slot: int32 [8, 8, 256], P('gx', 'gy', 'sa'), may hold values from 0 to 15
- conv_first: bfloat16 [27, 128, 128], replicated, may hold values from -0.109375 to 0.109375
- conv_second: bfloat16 [27, 128, 128], replicated, may hold values from -0.109375 to 0.109375
- norm_gain: float32 [128], replicated, may hold values from 0.1 to 1.9
- out_grad: bfloat16 [64, 128, 16, 128], P('gx', 'gy', 'sa'), may hold values from -6 to 6
Outputs:
- block_out: bfloat16 [64, 128, 16, 128], P('gx', 'gy', 'sa')
- grid_grad: bfloat16 [64, 128, 16, 128], P('gx', 'gy', 'sa')
- conv_first_grad: float32 [27, 128, 128], replicated
- conv_second_grad: float32 [27, 128, 128], replicated
- gain_grad: float32 [128], replicated
Inputs may be any that keep to these rules, and one draw needn't show every extreme that they name: `target_rank`: A contribution stays at its gy index; at most 16 of the rows of one device name the same destination, and some destination receives exactly 16 of them. `target_slot`: brick position (bx * 4 + by) * 2 + bz of the destination's 2 x 4 x 2 bricks.
All inputs are finite; a program needn't handle non-finite values.
Results may differ from a plain program's by a relative error of at most 0.017.
Values may be sent and summed in bfloat16 or wider, within the bound.
No kernel may reach another device: no remote copies, remote signals or barrier semaphores. Data moves between devices by JAX's collectives and lax.ppermute only.
A program may use at most 64 MiB of HBM per device.

v0:
```python
import math

import jax
import jax.numpy as jnp
from jax import lax
from jax.sharding import PartitionSpec as P

BX = 2
BY = 4
BZ = 2


epsilon = 1e-06


def extended(block, sides, width):
    for axis, dim in sides:
        count = lax.axis_size(axis)
        forward = [(i, i + 1) for i in range(count - 1)]
        backward = [(target, source) for source, target in forward]
        low = lax.ppermute(
            lax.slice_in_dim(block, block.shape[dim] - width, None, axis=dim), axis, forward
        )
        high = lax.ppermute(lax.slice_in_dim(block, 0, width, axis=dim), axis, backward)
        block = jnp.concatenate([low, block, high], axis=dim)
    return block


def surround(volume):
    return extended(volume, (("gx", 0), ("gy", 1), ("sa", 2)), 1)


def apply_conv(padded, weights):
    extent_x = padded.shape[0] - 2
    extent_y = padded.shape[1] - 2
    extent_z = padded.shape[2] - 2
    channels = padded.shape[3]
    summed = jnp.zeros((extent_x * extent_y * extent_z, weights.shape[2]), jnp.float32)
    for offset in range(27):
        along_x, along_y, along_z = (offset // 9, offset // 3 % 3, offset % 3)
        window = padded[
            along_x : along_x + extent_x, along_y : along_y + extent_y, along_z : along_z + extent_z
        ]
        summed = summed + jnp.dot(
            window.reshape(-1, channels), weights[offset], preferred_element_type=jnp.float32
        )
    return summed.reshape(extent_x, extent_y, extent_z, weights.shape[2])


def transposed_conv(padded, weights):
    extent_x = padded.shape[0] - 2
    extent_y = padded.shape[1] - 2
    extent_z = padded.shape[2] - 2
    channels = padded.shape[3]
    summed = jnp.zeros((extent_x * extent_y * extent_z, weights.shape[1]), jnp.float32)
    for offset in range(27):
        along_x, along_y, along_z = (2 - offset // 9, 2 - offset // 3 % 3, 2 - offset % 3)
        window = padded[
            along_x : along_x + extent_x, along_y : along_y + extent_y, along_z : along_z + extent_z
        ]
        summed = summed + lax.dot_general(
            window.reshape(-1, channels),
            weights[offset],
            (((1,), (1,)), ((), ())),
            preferred_element_type=jnp.float32,
        )
    return summed.reshape(extent_x, extent_y, extent_z, weights.shape[1])


def weight_grads(padded, grads):
    extent_x, extent_y, extent_z, channels = grads.shape
    grad_rows = grads.reshape(-1, channels)
    pieces = []
    for offset in range(27):
        along_x, along_y, along_z = (offset // 9, offset // 3 % 3, offset % 3)
        window = padded[
            along_x : along_x + extent_x, along_y : along_y + extent_y, along_z : along_z + extent_z
        ]
        pieces.append(
            lax.dot_general(
                window.reshape(-1, padded.shape[3]),
                grad_rows,
                (((0,), (0,)), ((), ())),
                preferred_element_type=jnp.float32,
            )
        )
    return jnp.stack(pieces)


def to_voxels(values):
    moved = values.transpose(0, 3, 1, 4, 2, 5, 6)
    return moved.reshape(BX * 4, BY * 4, BZ * 4, values.shape[6])


def local(sweep_bricks, target_rank, target_slot, conv_first, conv_second, norm_gain, out_grad):
    groups = lax.axis_size("gx") * lax.axis_size("sa")
    sends = sweep_bricks.shape[2]
    channels = sweep_bricks.shape[4]
    capacity = 2 * sends // groups
    positions = BX * BY * BZ
    ranks = target_rank.reshape(sends)
    slot_ids = target_slot.reshape(sends)
    member = (ranks[:, None] == jnp.arange(groups, dtype=jnp.int32)[None, :]).astype(jnp.int32)
    earlier = jnp.sum((jnp.cumsum(member, axis=0) - member) * member, axis=1)
    places = ranks * capacity + earlier
    placing = places[None, :] == jnp.arange(groups * capacity, dtype=jnp.int32)[:, None]
    rows = sweep_bricks.reshape(sends, -1)
    outgoing = jnp.dot(
        placing.astype(jnp.bfloat16), rows, preferred_element_type=jnp.float32
    ).astype(jnp.bfloat16)
    labels = (
        (jnp.sum(jnp.where(placing, slot_ids[None, :] + 1, 0), axis=1) - 1)
        .astype(jnp.float32)
        .astype(jnp.bfloat16)
    )
    arrived, arrived_labels = (
        lax.all_to_all(outgoing, ("gx", "sa"), split_axis=0, concat_axis=0, tiled=True),
        lax.all_to_all(labels, ("gx", "sa"), split_axis=0, concat_axis=0, tiled=True),
    )
    choose = (
        arrived_labels.astype(jnp.float32)[None, :]
        == jnp.arange(positions, dtype=jnp.float32)[:, None]
    )
    brick_sums = jnp.dot(choose.astype(jnp.bfloat16), arrived, preferred_element_type=jnp.float32)
    grid = to_voxels(brick_sums.astype(jnp.bfloat16).reshape(BX, BY, BZ, 4, 4, 4, channels))
    filled = jnp.any(choose, axis=1).astype(jnp.float32).reshape(BX, BY, BZ, 1, 1, 1, 1)
    live = to_voxels(jnp.broadcast_to(filled, (BX, BY, BZ, 4, 4, 4, 1)))
    grid_f = grid.astype(jnp.float32)
    inverse = lax.rsqrt(jnp.mean(grid_f * grid_f, axis=-1, keepdims=True) + epsilon)
    normed = (grid_f * inverse * norm_gain).astype(jnp.bfloat16)
    normed_pad = surround(normed)
    before_act = live * apply_conv(normed_pad, conv_first)
    sigmoid_act = jax.nn.sigmoid(before_act)
    active = (before_act * sigmoid_act).astype(jnp.bfloat16)
    active_pad = surround(active)
    branch = live * apply_conv(active_pad, conv_second)
    block_out = (grid_f + branch).astype(jnp.bfloat16)
    out_grad_f = out_grad.astype(jnp.float32)
    out_masked = (live * out_grad_f).astype(jnp.bfloat16)
    masked_pad = surround(out_masked)
    second_grad = weight_grads(active_pad, out_masked)
    active_grad = transposed_conv(masked_pad, conv_second)
    pre_grad = (active_grad * sigmoid_act * (1.0 + before_act * (1.0 - sigmoid_act))).astype(
        jnp.bfloat16
    )
    pre_pad = surround(pre_grad)
    first_grad = weight_grads(normed_pad, pre_grad)
    normed_grad = live * transposed_conv(pre_pad, conv_first)
    gain_grad = jnp.sum((normed_grad * grid_f * inverse).reshape(-1, channels), axis=0)
    first_total, second_total, gain_total = lax.psum(
        (first_grad, second_grad, gain_grad), ("gx", "gy", "sa")
    )
    upstream = normed_grad * norm_gain
    centred = jnp.mean(grid_f * upstream, axis=-1, keepdims=True)
    grid_grad = (out_grad_f + live * (inverse * upstream - grid_f * inverse**3 * centred)).astype(
        jnp.bfloat16
    )
    cells = groups * lax.axis_size("gy") * grid.shape[0] * grid.shape[1] * grid.shape[2]
    factor = 1.0 / math.sqrt(float(cells))
    return (block_out, grid_grad, first_total * factor, second_total * factor, gain_total * factor)


def solution(mesh):
    in_specs = (
        P("gx", "gy", "sa", None, None),
        P("gx", "gy", "sa", None),
        P("gx", "gy", "sa"),
        P(),
        P(),
        P(),
        P("gx", "gy", "sa", None),
    )
    out_specs = (P("gx", "gy", "sa", None), P("gx", "gy", "sa", None), P(), P(), P())
    return jax.shard_map(local, mesh=mesh, in_specs=in_specs, out_specs=out_specs, check_vma=False)
```

profile of v0, /device:TPU:1, one launch (start us, length us, event | category | flops | bytes accessed | tf_op | source)
XLA Modules:
  0.0 428.6 jit_solution(9511236412537976716)
XLA Ops:
  10.5 13.8 %all_to_all.18 = bf16[16,16,1]{1,2,0:T(2,128)(2,1)S(1)} all-to-all(bf16[16,16,1]{1,2,0:T(2,128)(2,1)S(1)} %convert_element_type.163), channel_id=1, replica_groups=mesh['gx'=8,'gy'=8,'sa'=2] {'gx','sa'}, dimensions={0} | all-to-all | bytes 1024 | tf_op jit(solution)/shard_map/all_to_all | solution.py:118
  26.1 2.2 collective-permute-start.12
  29.6 5.4 %convolution_convert_fusion = bf16[256,8192]{1,0:T(8,128)(2,1)} fusion(bf16[16,8,64,128]{3,2,1,0:T(8,128)(2,1)} %bitcast.1016, s32[128]{0:T(128)S(1)} %multiply_add_fusion), kind=kOutput, calls=%fused_computation | convolution fusion | flops 539000832 | bytes 6291968 | tf_op jit(solution)/shard_map/dot_general | solution.py:108
  35.0 5.6 %all-to-all-start.1 = ((bf16[16,16,8192]{2,1,0:T(8,128)(2,1)}), bf16[16,16,8192]{2,1,0:T(8,128)(2,1)}, u32[]{:S(2)}, u32[]{:S(2)}) async-start(bf16[16,16,8192]{2,1,0:T(8,128)(2,1)} %bitcast.1011), calls=%async_computation.1 | async-start | bytes 8388608 | tf_op jit(solution)/shard_map/all_to_all | solution.py:117
  41.0 6.4 %collective-permute-start.14 = (bf16[10,1,8,128]{3,1,2,0:T(2,128)(2,1)S(1)}, bf16[10,1,8,128]{3,1,2,0:T(2,128)(2,1)S(1)}, u32[]{:S(2)}, u32[]{:S(2)}) collective-permute-start(bf16[10,1,8,128]{3,1,2,0:T(2,128)(2,1)S(1)} %get-tuple-element.154), channel_id=1, source_target_pairs={{0,2},{2,4},{4,6},{6,8},{8,10},{10,12},{12,14},{1,3},{3,5},{5,7},{... | collective-permute-start | bytes 61448 | tf_op jit(solution)/shard_map/ppermute | solution.py:21
  47.4 1.9 collective-permute-start.15
  49.6 3.6 collective-permute-done.15
  54.5 6.0 %collective-permute-start.17 = (bf16[10,18,1,128]{3,1,2,0:T(8,128)(2,1)S(1)}, bf16[10,18,1,128]{3,1,2,0:T(8,128)(2,1)S(1)}, u32[]{:S(2)}, u32[]{:S(2)}) collective-permute-start(bf16[10,18,1,128]{3,1,2,0:T(8,128)(2,1)S(1)} %get-tuple-element.138), channel_id=1, source_target_pairs={{0,1},{2,3},{4,5},{6,7},{8,9},{10,11},{12,13},{14,15},{16,17},{18,... | collective-permute-start | bytes 138248 | tf_op jit(solution)/shard_map/ppermute | solution.py:21
  61.7 32.9 %collective-permute-done.16 = bf16[10,18,1,128]{3,1,2,0:T(8,128)(2,1)S(1)} collective-permute-done((bf16[10,18,1,128]{3,1,2,0:T(8,128)(2,1)S(1)}, bf16[10,18,1,128]{3,1,2,0:T(8,128)(2,1)S(1)}, u32[]{:S(2)}, u32[]{:S(2)}) %collective-permute-start.16) | collective-permute-done | bytes 46112 | tf_op jit(solution)/shard_map/ppermute | solution.py:24
  105.7 2.8 fusion
  114.3 2.4 collective-permute-done.1
  116.8 8.0 %collective-permute-start.2 = (bf16[10,1,8,128]{3,1,2,0:T(2,128)(2,1)S(1)}, bf16[10,1,8,128]{3,1,2,0:T(2,128)(2,1)S(1)}, u32[]{:S(2)}, u32[]{:S(2)}) collective-permute-start(bf16[10,1,8,128]{3,1,2,0:T(2,128)(2,1)S(1)} %get-tuple-element.162), channel_id=1, source_target_pairs={{0,2},{2,4},{4,6},{6,8},{8,10},{10,12},{12,14},{1,3},{3,5},{5,7},{... | collective-permute-start | bytes 61448 | tf_op jit(solution)/shard_map/ppermute | solution.py:21
  127.0 3.2 collective-permute-done.3
  134.1 3.9 collective-permute-done.5
  148.8 3.7 collective-permute-start.6
  161.9 4.8 %collective-permute-start.18 = (bf16[1,16,8,128]{3,1,2,0:T(8,128)(2,1)S(1)}, bf16[1,16,8,128]{3,1,2,0:T(8,128)(2,1)S(1)}, u32[]{:S(2)}, u32[]{:S(2)}) collective-permute-start(bf16[1,16,8,128]{3,1,2,0:T(8,128)(2,1)S(1)} %get-tuple-element.166), channel_id=1, source_target_pairs={{0,16},{16,32},{32,48},{48,64},{64,80},{80,96},{96,112},{1,17},{17... | collective-permute-start | bytes 98312 | tf_op jit(solution)/shard_map/ppermute | solution.py:21
  168.1 3.8 collective-permute-start.8
  171.9 1.9 collective-permute-start.9
  175.6 3.6 collective-permute-start.20
  179.3 1.9 collective-permute-start.21
  191.6 7.0 %collective-permute-start.23 = (bf16[10,18,1,128]{3,1,2,0:T(8,128)(2,1)}, bf16[10,18,1,128]{3,1,2,0:T(8,128)(2,1)}, u32[]{:S(2)}, u32[]{:S(2)}) collective-permute-start(bf16[10,18,1,128]{3,1,2,0:T(8,128)(2,1)} %get-tuple-element.134), channel_id=1, source_target_pairs={{0,1},{2,3},{4,5},{6,7},{8,9},{10,11},{12,13},{14,15},{16,17},{18,... | collective-permute-start | bytes 138248 | tf_op jit(solution)/shard_map/ppermute | solution.py:21
  277.2 68.9 %psum.23 = f32[128]{0:T(128)S(1)} all-reduce(f32[128]{0:T(128)S(1)} %get-tuple-element.182), channel_id=1, replica_groups=mesh['gx'=8,'gy'=8,'sa'=2] {'gx','gy','sa'}, use_global_device_ids=true, to_apply=%region_9.10 | all-reduce | flops 128 | bytes 1024 | tf_op jit(solution)/shard_map/psum | solution.py:150
  346.6 70.2 %all-reduce.3.cloned.1.call-done = (f32[27,128,128]{2,1,0:T(8,128)}, f32[27,128,128]{2,1,0:T(8,128)}) async-done(((f32[27,128,128]{2,1,0:T(8,128)}, f32[27,128,128]{2,1,0:T(8,128)}), (f32[27,128,128]{2,1,0:T(8,128)}, f32[27,128,128]{2,1,0:T(8,128)})) %all-reduce.3.cloned.1.call-update) | async-done | bytes 3538960 | tf_op jit(solution)/shard_map/psum | solution.py:150
  416.8 3.1 broadcast_multiply_fusion
  (470 shorter events, 144.4 us)
Async XLA Ops:
  26.1 14.8 %collective-permute-start.12 = (bf16[1,16,8,128]{3,1,2,0:T(8,128)(2,1)S(1)}, bf16[1,16,8,128]{3,1,2,0:T(8,128)(2,1)S(1)}, u32[]{:S(2)}, u32[]{:S(2)}) collective-permute-start(bf16[1,16,8,128]{3,1,2,0:T(8,128)(2,1)S(1)} %get-tuple-element.170), channel_id=1, source_target_pairs={{0,16},{16,32},{32,48},{48,64},{64,80},{80,96},{96,112},{1,17},{17... | collective-permute-start | bytes 98312 | tf_op jit(solution)/shard_map/ppermute | solution.py:21
  28.3 12.7 %collective-permute-start.13 = (bf16[1,16,8,128]{3,1,2,0:T(8,128)(2,1)S(1)}, bf16[1,16,8,128]{3,1,2,0:T(8,128)(2,1)S(1)}, u32[]{:S(2)}, u32[]{:S(2)}) collective-permute-start(bf16[1,16,8,128]{3,1,2,0:T(8,128)(2,1)S(1)} %get-tuple-element.171), channel_id=1, source_target_pairs={{16,0},{32,16},{48,32},{64,48},{80,64},{96,80},{112,96},{17,1},{33... | collective-permute-start | bytes 98312 | tf_op jit(solution)/shard_map/ppermute | solution.py:24
  35.0 70.6 %all-to-all-start.1 = ((bf16[16,16,8192]{2,1,0:T(8,128)(2,1)}), bf16[16,16,8192]{2,1,0:T(8,128)(2,1)}, u32[]{:S(2)}, u32[]{:S(2)}) async-start(bf16[16,16,8192]{2,1,0:T(8,128)(2,1)} %bitcast.1011), calls=%async_computation.1 | async-start | bytes 8388608 | tf_op jit(solution)/shard_map/all_to_all | solution.py:117
  40.6 376.1 %all-reduce.3.cloned.1.call-start = ((), (), s32[]{:S(2)}) async-start(), calls=%async_computation.2 | async-start | bytes 7077888 | tf_op jit(solution)/shard_map/psum | solution.py:150
  41.0 8.5 %collective-permute-start.14 = (bf16[10,1,8,128]{3,1,2,0:T(2,128)(2,1)S(1)}, bf16[10,1,8,128]{3,1,2,0:T(2,128)(2,1)S(1)}, u32[]{:S(2)}, u32[]{:S(2)}) collective-permute-start(bf16[10,1,8,128]{3,1,2,0:T(2,128)(2,1)S(1)} %get-tuple-element.154), channel_id=1, source_target_pairs={{0,2},{2,4},{4,6},{6,8},{8,10},{10,12},{12,14},{1,3},{3,5},{5,7},{... | collective-permute-start | bytes 61448 | tf_op jit(solution)/shard_map/ppermute | solution.py:21
  47.4 5.7 %collective-permute-start.15 = (bf16[10,1,8,128]{3,1,2,0:T(2,128)(2,1)S(1)}, bf16[10,1,8,128]{3,1,2,0:T(2,128)(2,1)S(1)}, u32[]{:S(2)}, u32[]{:S(2)}) collective-permute-start(bf16[10,1,8,128]{3,1,2,0:T(2,128)(2,1)S(1)} %get-tuple-element.155), channel_id=1, source_target_pairs={{2,0},{4,2},{6,4},{8,6},{10,8},{12,10},{14,12},{3,1},{5,3},{7,5},{... | collective-permute-start | bytes 61448 | tf_op jit(solution)/shard_map/ppermute | solution.py:24
  53.2 41.4 %collective-permute-start.16 = (bf16[10,18,1,128]{3,1,2,0:T(8,128)(2,1)S(1)}, bf16[10,18,1,128]{3,1,2,0:T(8,128)(2,1)S(1)}, u32[]{:S(2)}, u32[]{:S(2)}) collective-permute-start(bf16[10,18,1,128]{3,1,2,0:T(8,128)(2,1)S(1)} %get-tuple-element.139), channel_id=1, source_target_pairs={{1,0},{3,2},{5,4},{7,6},{9,8},{11,10},{13,12},{15,14},{17,16},{19,... | collective-permute-start | bytes 138248 | tf_op jit(solution)/shard_map/ppermute | solution.py:24
  54.5 40.1 %collective-permute-start.17 = (bf16[10,18,1,128]{3,1,2,0:T(8,128)(2,1)S(1)}, bf16[10,18,1,128]{3,1,2,0:T(8,128)(2,1)S(1)}, u32[]{:S(2)}, u32[]{:S(2)}) collective-permute-start(bf16[10,18,1,128]{3,1,2,0:T(8,128)(2,1)S(1)} %get-tuple-element.138), channel_id=1, source_target_pairs={{0,1},{2,3},{4,5},{6,7},{8,9},{10,11},{12,13},{14,15},{16,17},{18,... | collective-permute-start | bytes 138248 | tf_op jit(solution)/shard_map/ppermute | solution.py:21
  112.1 4.7 %collective-permute-start.1 = (bf16[1,16,8,128]{3,1,2,0:T(8,128)(2,1)S(1)}, bf16[1,16,8,128]{3,1,2,0:T(8,128)(2,1)S(1)}, u32[]{:S(2)}, u32[]{:S(2)}) collective-permute-start(bf16[1,16,8,128]{3,1,2,0:T(8,128)(2,1)S(1)} %get-tuple-element.179), channel_id=1, source_target_pairs={{16,0},{32,16},{48,32},{64,48},{80,64},{96,80},{112,96},{17,1},{33... | collective-permute-start | bytes 98312 | tf_op jit(solution)/shard_map/ppermute | solution.py:24
  116.8 10.2 %collective-permute-start.2 = (bf16[10,1,8,128]{3,1,2,0:T(2,128)(2,1)S(1)}, bf16[10,1,8,128]{3,1,2,0:T(2,128)(2,1)S(1)}, u32[]{:S(2)}, u32[]{:S(2)}) collective-permute-start(bf16[10,1,8,128]{3,1,2,0:T(2,128)(2,1)S(1)} %get-tuple-element.162), channel_id=1, source_target_pairs={{0,2},{2,4},{4,6},{6,8},{8,10},{10,12},{12,14},{1,3},{3,5},{5,7},{... | collective-permute-start | bytes 61448 | tf_op jit(solution)/shard_map/ppermute | solution.py:21
  124.8 5.3 %collective-permute-start.3 = (bf16[10,1,8,128]{3,1,2,0:T(2,128)(2,1)S(1)}, bf16[10,1,8,128]{3,1,2,0:T(2,128)(2,1)S(1)}, u32[]{:S(2)}, u32[]{:S(2)}) collective-permute-start(bf16[10,1,8,128]{3,1,2,0:T(2,128)(2,1)S(1)} %get-tuple-element.163), channel_id=1, source_target_pairs={{2,0},{4,2},{6,4},{8,6},{10,8},{12,10},{14,12},{3,1},{5,3},{7,5},{... | collective-permute-start | bytes 61448 | tf_op jit(solution)/shard_map/ppermute | solution.py:24
  131.5 6.5 %collective-permute-start.5 = (bf16[10,18,1,128]{3,1,2,0:T(8,128)(2,1)S(1)}, bf16[10,18,1,128]{3,1,2,0:T(8,128)(2,1)S(1)}, u32[]{:S(2)}, u32[]{:S(2)}) collective-permute-start(bf16[10,18,1,128]{3,1,2,0:T(8,128)(2,1)S(1)} %get-tuple-element.146), channel_id=1, source_target_pairs={{1,0},{3,2},{5,4},{7,6},{9,8},{11,10},{13,12},{15,14},{17,16},{19,... | collective-permute-start | bytes 138248 | tf_op jit(solution)/shard_map/ppermute | solution.py:24
  148.8 19.1 %collective-permute-start.6 = (bf16[1,16,8,128]{3,1,2,0:T(8,128)(2,1)S(1)}, bf16[1,16,8,128]{3,1,2,0:T(8,128)(2,1)S(1)}, u32[]{:S(2)}, u32[]{:S(2)}) collective-permute-start(bf16[1,16,8,128]{3,1,2,0:T(8,128)(2,1)S(1)} %get-tuple-element.174), channel_id=1, source_target_pairs={{0,16},{16,32},{32,48},{48,64},{64,80},{80,96},{96,112},{1,17},{17... | collective-permute-start | bytes 98312 | tf_op jit(solution)/shard_map/ppermute | solution.py:21
  152.5 15.4 %collective-permute-start.7 = (bf16[1,16,8,128]{3,1,2,0:T(8,128)(2,1)S(1)}, bf16[1,16,8,128]{3,1,2,0:T(8,128)(2,1)S(1)}, u32[]{:S(2)}, u32[]{:S(2)}) collective-permute-start(bf16[1,16,8,128]{3,1,2,0:T(8,128)(2,1)S(1)} %get-tuple-element.175), channel_id=1, source_target_pairs={{16,0},{32,16},{48,32},{64,48},{80,64},{96,80},{112,96},{17,1},{33... | collective-permute-start | bytes 98312 | tf_op jit(solution)/shard_map/ppermute | solution.py:24
  161.9 12.0 %collective-permute-start.18 = (bf16[1,16,8,128]{3,1,2,0:T(8,128)(2,1)S(1)}, bf16[1,16,8,128]{3,1,2,0:T(8,128)(2,1)S(1)}, u32[]{:S(2)}, u32[]{:S(2)}) collective-permute-start(bf16[1,16,8,128]{3,1,2,0:T(8,128)(2,1)S(1)} %get-tuple-element.166), channel_id=1, source_target_pairs={{0,16},{16,32},{32,48},{48,64},{64,80},{80,96},{96,112},{1,17},{17... | collective-permute-start | bytes 98312 | tf_op jit(solution)/shard_map/ppermute | solution.py:21
  166.7 7.2 %collective-permute-start.19 = (bf16[1,16,8,128]{3,1,2,0:T(8,128)(2,1)S(1)}, bf16[1,16,8,128]{3,1,2,0:T(8,128)(2,1)S(1)}, u32[]{:S(2)}, u32[]{:S(2)}) collective-permute-start(bf16[1,16,8,128]{3,1,2,0:T(8,128)(2,1)S(1)} %get-tuple-element.167), channel_id=1, source_target_pairs={{16,0},{32,16},{48,32},{64,48},{80,64},{96,80},{112,96},{17,1},{33... | collective-permute-start | bytes 98312 | tf_op jit(solution)/shard_map/ppermute | solution.py:24
  168.1 13.9 %collective-permute-start.8 = (bf16[10,1,8,128]{3,1,2,0:T(2,128)(2,1)S(1)}, bf16[10,1,8,128]{3,1,2,0:T(2,128)(2,1)S(1)}, u32[]{:S(2)}, u32[]{:S(2)}) collective-permute-start(bf16[10,1,8,128]{3,1,2,0:T(2,128)(2,1)S(1)} %get-tuple-element.158), channel_id=1, source_target_pairs={{0,2},{2,4},{4,6},{6,8},{8,10},{10,12},{12,14},{1,3},{3,5},{5,7},{... | collective-permute-start | bytes 61448 | tf_op jit(solution)/shard_map/ppermute | solution.py:21
  171.9 10.1 %collective-permute-start.9 = (bf16[10,1,8,128]{3,1,2,0:T(2,128)(2,1)S(1)}, bf16[10,1,8,128]{3,1,2,0:T(2,128)(2,1)S(1)}, u32[]{:S(2)}, u32[]{:S(2)}) collective-permute-start(bf16[10,1,8,128]{3,1,2,0:T(2,128)(2,1)S(1)} %get-tuple-element.159), channel_id=1, source_target_pairs={{2,0},{4,2},{6,4},{8,6},{10,8},{12,10},{14,12},{3,1},{5,3},{7,5},{... | collective-permute-start | bytes 61448 | tf_op jit(solution)/shard_map/ppermute | solution.py:24
  175.6 12.6 %collective-permute-start.20 = (bf16[10,1,8,128]{3,1,2,0:T(2,128)(2,1)S(1)}, bf16[10,1,8,128]{3,1,2,0:T(2,128)(2,1)S(1)}, u32[]{:S(2)}, u32[]{:S(2)}) collective-permute-start(bf16[10,1,8,128]{3,1,2,0:T(2,128)(2,1)S(1)} %get-tuple-element.150), channel_id=1, source_target_pairs={{0,2},{2,4},{4,6},{6,8},{8,10},{10,12},{12,14},{1,3},{3,5},{5,7},{... | collective-permute-start | bytes 61448 | tf_op jit(solution)/shard_map/ppermute | solution.py:21
  179.3 8.9 %collective-permute-start.21 = (bf16[10,1,8,128]{3,1,2,0:T(2,128)(2,1)S(1)}, bf16[10,1,8,128]{3,1,2,0:T(2,128)(2,1)S(1)}, u32[]{:S(2)}, u32[]{:S(2)}) collective-permute-start(bf16[10,1,8,128]{3,1,2,0:T(2,128)(2,1)S(1)} %get-tuple-element.151), channel_id=1, source_target_pairs={{2,0},{4,2},{6,4},{8,6},{10,8},{12,10},{14,12},{3,1},{5,3},{7,5},{... | collective-permute-start | bytes 61448 | tf_op jit(solution)/shard_map/ppermute | solution.py:24
  182.0 20.6 %collective-permute-start.10 = (bf16[10,18,1,128]{3,1,2,0:T(8,128)(2,1)S(1)}, bf16[10,18,1,128]{3,1,2,0:T(8,128)(2,1)S(1)}, u32[]{:S(2)}, u32[]{:S(2)}) collective-permute-start(bf16[10,18,1,128]{3,1,2,0:T(8,128)(2,1)S(1)} %get-tuple-element.143), channel_id=1, source_target_pairs={{0,1},{2,3},{4,5},{6,7},{8,9},{10,11},{12,13},{14,15},{16,17},{18,... | collective-permute-start | bytes 138248 | tf_op jit(solution)/shard_map/ppermute | solution.py:21
  183.7 18.9 %collective-permute-start.11 = (bf16[10,18,1,128]{3,1,2,0:T(8,128)(2,1)S(1)}, bf16[10,18,1,128]{3,1,2,0:T(8,128)(2,1)S(1)}, u32[]{:S(2)}, u32[]{:S(2)}) collective-permute-start(bf16[10,18,1,128]{3,1,2,0:T(8,128)(2,1)S(1)} %get-tuple-element.142), channel_id=1, source_target_pairs={{1,0},{3,2},{5,4},{7,6},{9,8},{11,10},{13,12},{15,14},{17,16},{19,... | collective-permute-start | bytes 138248 | tf_op jit(solution)/shard_map/ppermute | solution.py:24
  190.3 56.5 %collective-permute-start.22 = (bf16[10,18,1,128]{3,1,2,0:T(8,128)(2,1)}, bf16[10,18,1,128]{3,1,2,0:T(8,128)(2,1)}, u32[]{:S(2)}, u32[]{:S(2)}) collective-permute-start(bf16[10,18,1,128]{3,1,2,0:T(8,128)(2,1)} %get-tuple-element.135), channel_id=1, source_target_pairs={{1,0},{3,2},{5,4},{7,6},{9,8},{11,10},{13,12},{15,14},{17,16},{19,... | collective-permute-start | bytes 138248 | tf_op jit(solution)/shard_map/ppermute | solution.py:24
  191.6 55.3 %collective-permute-start.23 = (bf16[10,18,1,128]{3,1,2,0:T(8,128)(2,1)}, bf16[10,18,1,128]{3,1,2,0:T(8,128)(2,1)}, u32[]{:S(2)}, u32[]{:S(2)}) collective-permute-start(bf16[10,18,1,128]{3,1,2,0:T(8,128)(2,1)} %get-tuple-element.134), channel_id=1, source_target_pairs={{0,1},{2,3},{4,5},{6,7},{8,9},{10,11},{12,13},{14,15},{16,17},{18,... | collective-permute-start | bytes 138248 | tf_op jit(solution)/shard_map/ppermute | solution.py:21
  (49 other events, 193.0 us)
Sparse Core Ops, SparseCore 0:
  260.5 156.2 all-reduce.2
where the time goes:
time: 434 us; the launch traced here: 429 us
  waiting for transfers between devices  116 us (27%)
  blocking collectives  82.7 us (19%)
  matrix products  76.1 us (18%)
  starting transfers between devices  74.1 us (17%)
  local copies, waits for them, and re-layouts  43.7 us (10%)
  other arithmetic  18.5 us (4%)
  between operations  17.2 us (4%)
    psum x1, waiting for transfers between devices, local(): lax.psum((first_grad, second_grad, gain_grad), ('gx', 'gy', 'sa'))  70.2 us
    psum x1, blocking collectives, local(): lax.psum((first_grad, second_grad, gain_grad), ('gx', 'gy', 'sa'))  68.9 us
    ppermute x12, starting transfers between devices, extended(): lax.ppermute(lax.slice_in_dim(block, block.shape[dim] - width, None, axis...  50.1 us
    ppermute x12, waiting for transfers between devices, extended(): lax.ppermute(lax.slice_in_dim(block, 0, width, axis=dim), axis, backward)  46 us
    dot_general x54, matrix products, weight_grads(): lax.dot_general(window.reshape(-1, padded.shape[3]), grad_rows, (((0,), (...  31.9 us
    dot_general x54, matrix products, apply_conv(): jnp.dot(window.reshape(-1, channels), weights[offset], preferred_element_...  22.5 us
    slice x58, local copies, waits for them, and re-layouts, apply_conv(): padded[along_x:along_x + extent_x, along_y:along_y + extent_y, along_z:al...  22 us
    ppermute x12, starting transfers between devices, extended(): lax.ppermute(lax.slice_in_dim(block, 0, width, axis=dim), axis, backward)  18.4 us
  transfers between devices with their start and end apart: 26, of which 6 were waited for; matrix products, arithmetic and copies ran while one was open for 23% of the time, Pallas kernels for 0%

commit v1 on v0

v1 whole, which is shorter than its diff:
```python
import math

import jax
import jax.numpy as jnp
from jax import lax
from jax.experimental import pallas as pl
from jax.experimental.pallas import tpu as pltpu
from jax.sharding import Mesh
from jax.sharding import PartitionSpec as P

epsilon = 1e-06
DEAD = 1.0e30
OUT = -1.0e30
LIMIT = 1.0e29
GX = ("y", "xl")
GY = ("z", "c")
SA = "xh"
PLANE = ("y", "xl", "xh")
PEERS = ("y", "xl", "z", "xh")
F32 = jnp.float32
BF16 = jnp.bfloat16
VM = pl.BlockSpec(memory_space=pltpu.VMEM)
SM = pl.BlockSpec(memory_space=pltpu.SMEM)


def sum_bricks_kernel(arrived_ref, grid_ref, cells):
    values = arrived_ref[...].astype(F32)[:, 0]
    held = values < LIMIT
    total = jnp.sum(jnp.where(held, values, 0.0), axis=0)
    lowest = jnp.min(values, axis=0)
    total = jnp.where(lowest < LIMIT, total, DEAD).reshape(2, 4, 4, 4, 128)
    cells[:, :, 0:4, :] = total[0]
    cells[:, :, 4:8, :] = total[1]
    grid_ref[...] = cells[...].astype(BF16)


def sum_bricks(arrived):
    return pl.pallas_call(
        sum_bricks_kernel,
        out_shape=jax.ShapeDtypeStruct((8, 16, 8, 128), BF16),
        grid=(2, 4),
        in_specs=[pl.BlockSpec((16, 1, 2, 64, 128), lambda i, j: (0, i * 4 + j, 0, 0, 0))],
        out_specs=pl.BlockSpec((4, 4, 8, 128), lambda i, j: (i, j, 0, 0)),
        scratch_shapes=[pltpu.VMEM((4, 4, 8, 128), F32)],
        cost_estimate=pl.CostEstimate(flops=8 << 20, bytes_accessed=5 << 20, transcendentals=0),
    )(arrived.reshape(16, 8, 2, 64, 128))


def window_rows(ref, x, y, slabs, rows):
    part = ref[pl.ds(x, slabs), pl.ds(y, rows), :, :]
    return part.reshape(slabs * rows * 16, part.shape[3])


def gather_windows(ref, x, slabs, rows, sign):
    parts = []
    for i in range(3):
        for j in range(3):
            a, b = (i, j) if sign > 0 else (2 - i, 2 - j)
            parts.append(window_rows(ref, x + a, b, slabs, rows))
    return jnp.concatenate(parts, axis=1)


def neighbours(value, sign):
    count = value.shape[0]
    below = pltpu.roll(value, 1, 0)
    above = pltpu.roll(value, count - 1, 0)
    order = (below, value, above) if sign > 0 else (above, value, below)
    return jnp.concatenate([part.astype(BF16) for part in order], axis=1)


def fill(volume, centre, x_low, x_high, y_low, y_high, z_side, side, outside):
    volume[...] = jnp.full(volume.shape, outside, F32)
    volume[2:10, 2:18, 2:10, :] = centre[...].astype(F32)
    volume[0:2, 2:18, 2:10, :] = x_low[...].astype(F32)
    volume[10:12, 2:18, 2:10, :] = x_high[...].astype(F32)
    volume[:, 0:2, 2:10, :] = y_low[...].astype(F32)
    volume[:, 18:20, 2:10, :] = y_high[...].astype(F32)

    @pl.when(side == 0)
    def _():
        volume[:, :, 10:12, :] = z_side[...].astype(F32)

    @pl.when(side == 1)
    def _():
        volume[:, :, 0:2, :] = z_side[...].astype(F32)


def grads_kernel(
    where_ref,
    gain,
    g0, g1, g2, g3, g4, g5,
    o0, o1, o2, o3, o4, o5,
    first,
    second_t,
    act_ref,
    pre3_ref,
    own_ref,
    send_ref,
    cells,
    cots,
    normed3,
    masked3,
    act_t,
    normed_t,
):
    side = where_ref[0]
    core = where_ref[1]
    fill(cells, g0, g1, g2, g3, g4, g5, side, OUT)
    fill(cots, o0, o1, o2, o3, o4, o5, side, 0.0)
    z_of = lax.broadcasted_iota(jnp.int32, (256, 128), 0) % 16
    inside = (z_of >= 2) & (z_of < 10)

    def prepare(x, carry):
        values = cells[x].reshape(320, 128)
        live = jnp.abs(values) < LIMIT
        held = jnp.where(live, values, 0.0)
        inverse = lax.rsqrt(jnp.mean(held * held, axis=-1, keepdims=True) + epsilon)
        normed = held * inverse * gain[...]
        normed3[x] = neighbours(normed, 1).reshape(20, 16, 384)
        masked = jnp.where(live, cots[x].reshape(320, 128), 0.0)
        masked3[x] = neighbours(masked, -1).reshape(20, 16, 384)
        return carry

    lax.fori_loop(0, 12, prepare, 0)

    def turn(x, carry):
        normed = normed3[x + 2, 2:18, :, 128:256].reshape(256, 128).astype(F32)
        columns = pl.ds(pl.multiple_of(x * 256, 256), 256)
        normed_t[:, columns] = jnp.where(inside, normed, 0.0).T.astype(BF16)
        return carry

    lax.fori_loop(0, 8, turn, 0)

    def convolve(step, carry):
        x = step * 2
        values = cells[pl.ds(x + 1, 2), 1:19, :, :].reshape(576, 128)
        before = jnp.dot(
            gather_windows(normed3, x, 2, 18, 1), first[...], preferred_element_type=F32
        )
        before = jnp.where(jnp.abs(values) < LIMIT, before, 0.0)
        sigmoid = jax.nn.sigmoid(before)
        active = before * sigmoid
        act_ref[pl.ds(x, 2)] = active.astype(BF16).reshape(2, 18, 16, 128)
        active_grad = jnp.dot(
            gather_windows(masked3, x, 2, 18, -1), second_t[...], preferred_element_type=F32
        )
        pre = active_grad * sigmoid * (1.0 + before * (1.0 - sigmoid))
        pre = jnp.where(values > -LIMIT, pre, 0.0)
        pre3_ref[pl.ds(x, 2)] = neighbours(pre, -1).reshape(2, 18, 16, 384)
        return carry

    lax.fori_loop(0, 5, convolve, 0)

    def turn_active(x, carry):
        active = act_ref[x + 1, 1:17].reshape(256, 128).astype(F32)
        columns = pl.ds(pl.multiple_of(x * 256, 256), 256)
        act_t[:, columns] = jnp.where(inside, active, 0.0).T.astype(BF16)
        return carry

    lax.fori_loop(0, 8, turn_active, 0)

    for which, left, right, start in ((1, act_t, masked3, 3), (0, normed_t, pre3_ref, 2)):
        for target, here in ((own_ref, which), (send_ref, 1 - which)):

            @pl.when(core == here)
            def _():
                def weights(at, carry):
                    i = at // 3
                    j = at - i * 3
                    cot = window_rows(right, start - i, start - j, 8, 16)
                    total = jnp.dot(left[...], cot, preferred_element_type=F32).astype(BF16)
                    for k in range(3):
                        target[at * 3 + k] = total[:, k * 128 : (k + 1) * 128]
                    return carry

                lax.fori_loop(0, 9, weights, 0)

    own_ref[27] = jnp.zeros((128, 128), BF16)
    send_ref[27] = jnp.zeros((128, 128), BF16)


def grads_call(where, gain, grid_parts, cot_parts, first, second_t):
    return pl.pallas_call(
        grads_kernel,
        out_shape=(
            jax.ShapeDtypeStruct((10, 18, 16, 128), BF16),
            jax.ShapeDtypeStruct((10, 18, 16, 384), BF16),
            jax.ShapeDtypeStruct((28, 128, 128), BF16),
            jax.ShapeDtypeStruct((28, 128, 128), BF16),
        ),
        in_specs=[SM] + [VM] * 15,
        out_specs=(VM,) * 4,
        scratch_shapes=[
            pltpu.VMEM((12, 20, 16, 128), F32),
            pltpu.VMEM((12, 20, 16, 128), F32),
            pltpu.VMEM((12, 20, 16, 384), BF16),
            pltpu.VMEM((12, 20, 16, 384), BF16),
            pltpu.VMEM((128, 2048), BF16),
            pltpu.VMEM((128, 2048), BF16),
        ],
        compiler_params=pltpu.CompilerParams(vmem_limit_bytes=40 << 20),
        cost_estimate=pl.CostEstimate(flops=10 << 30, bytes_accessed=8 << 20, transcendentals=1 << 20),
    )(where, gain, *grid_parts, *cot_parts, first, second_t)


def outputs_kernel(
    gain, grid, out_grad, act, pre3, second, first_t, block_ref, grad_ref, gain_ref, act3, spread
):
    def prepare(x, carry):
        act3[x] = neighbours(act[x].reshape(288, 128).astype(F32), 1).reshape(18, 16, 384)
        return carry

    lax.fori_loop(0, 10, prepare, 0)
    gains = gain[...]

    def convolve(step, total):
        x = step * 2
        branch = jnp.dot(
            gather_windows(act3, x, 2, 16, 1), second[...], preferred_element_type=F32
        )
        spread[...] = branch.reshape(2, 16, 16, 128)
        branch = spread[:, :, 2:10, :].reshape(256, 128)
        values = grid[pl.ds(x, 2)].astype(F32).reshape(256, 128)
        live = values < LIMIT
        held = jnp.where(live, values, 0.0)
        block = jnp.where(live, branch, 0.0) + held
        block_ref[pl.ds(x, 2)] = block.astype(BF16).reshape(2, 16, 8, 128)
        normed_grad = jnp.dot(
            gather_windows(pre3, x, 2, 16, -1), first_t[...], preferred_element_type=F32
        )
        spread[...] = normed_grad.reshape(2, 16, 16, 128)
        normed_grad = jnp.where(live, spread[:, :, 2:10, :].reshape(256, 128), 0.0)
        inverse = lax.rsqrt(jnp.mean(held * held, axis=-1, keepdims=True) + epsilon)
        total = total + jnp.sum((normed_grad * held * inverse).reshape(32, 8, 128), axis=0)
        upstream = normed_grad * gains
        centred = jnp.mean(held * upstream, axis=-1, keepdims=True)
        extra = inverse * upstream - held * (inverse * inverse * inverse * centred)
        cot = out_grad[pl.ds(x, 2)].astype(F32).reshape(256, 128)
        grad = cot + jnp.where(live, extra, 0.0)
        grad_ref[pl.ds(x, 2)] = grad.astype(BF16).reshape(2, 16, 8, 128)
        return total

    total = lax.fori_loop(0, 4, convolve, jnp.zeros((8, 128), F32))
    gain_ref[...] = total


def outputs_call(gain, grid, out_grad, act, pre3, second, first_t):
    return pl.pallas_call(
        outputs_kernel,
        out_shape=(
            jax.ShapeDtypeStruct((8, 16, 8, 128), BF16),
            jax.ShapeDtypeStruct((8, 16, 8, 128), BF16),
            jax.ShapeDtypeStruct((8, 128), F32),
        ),
        in_specs=[VM] * 7,
        out_specs=(VM,) * 3,
        scratch_shapes=[
            pltpu.VMEM((10, 18, 16, 384), BF16),
            pltpu.VMEM((2, 16, 16, 128), F32),
        ],
        compiler_params=pltpu.CompilerParams(vmem_limit_bytes=24 << 20),
        cost_estimate=pl.CostEstimate(flops=8 << 30, bytes_accessed=6 << 20, transcendentals=4096),
    )(gain, grid, out_grad, act, pre3, second, first_t)


def swap_edges(block, axis, dim, count, outside):
    forward = [(i, i + 1) for i in range(count - 1)]
    backward = [(b, a) for a, b in forward]
    at = lax.axis_index(axis)
    low = lax.ppermute(lax.slice_in_dim(block, block.shape[dim] - 2, None, axis=dim), axis, forward)
    high = lax.ppermute(lax.slice_in_dim(block, 0, 2, axis=dim), axis, backward)
    if outside is not None:
        low = jnp.where(at == 0, jnp.asarray(outside, BF16), low)
        high = jnp.where(at == count - 1, jnp.asarray(outside, BF16), high)
    return low, high


def edges(volume, outside):
    x_low, x_high = swap_edges(volume, GX, 0, 8, outside)
    sides = []
    wide_low = jnp.concatenate([x_low[:, 14:16], volume[:, 14:16], x_high[:, 14:16]], axis=0)
    wide_high = jnp.concatenate([x_low[:, 0:2], volume[:, 0:2], x_high[:, 0:2]], axis=0)
    forward = [(i, i + 1) for i in range(7)]
    backward = [(b, a) for a, b in forward]
    at = lax.axis_index(GY)
    y_low = lax.ppermute(wide_low, GY, forward)
    y_high = lax.ppermute(wide_high, GY, backward)
    if outside is not None:
        y_low = jnp.where(at == 0, jnp.asarray(outside, BF16), y_low)
        y_high = jnp.where(at == 7, jnp.asarray(outside, BF16), y_high)
    side = lax.axis_index(SA)

    def layer(part):
        return jnp.where(side == 0, part[:, :, 6:8], part[:, :, 0:2])

    middle = jnp.concatenate([layer(x_low), layer(volume), layer(x_high)], axis=0)
    sent = jnp.concatenate([layer(y_low), middle, layer(y_high)], axis=1)
    z_side = lax.ppermute(sent, SA, [(0, 1), (1, 0)])
    return volume, x_low, x_high, y_low, y_high, z_side


def local(sweep_bricks, target_rank, target_slot, conv_first, conv_second, norm_gain, out_grad):
    code = target_rank.reshape(128) * 16 + target_slot.reshape(128)
    placing = code[None, :] == jnp.arange(256, dtype=jnp.int32)[:, None]
    rows = sweep_bricks.reshape(128, 64, 128)
    outgoing = lax.dot_general(
        placing.astype(BF16), rows, (((1,), (0,)), ((), ())), preferred_element_type=F32
    )
    named = jnp.any(placing, axis=1)[:, None, None]
    outgoing = jnp.where(named, outgoing, DEAD).astype(BF16)
    arrived = lax.all_to_all(outgoing, PLANE, split_axis=0, concat_axis=0, tiled=True)
    cot_parts = edges(out_grad, None)
    gain = norm_gain.reshape(1, 128)
    first = conv_first.reshape(3456, 128)
    second = conv_second.reshape(3456, 128)
    first_t = conv_first.transpose(0, 2, 1).reshape(3456, 128)
    second_t = conv_second.transpose(0, 2, 1).reshape(3456, 128)
    grid = sum_bricks(arrived)
    grid_parts = edges(grid, OUT)
    core = lax.axis_index("c")
    where = jnp.stack([lax.axis_index(SA), core]).astype(jnp.int32)
    act, pre3, own, send = grads_call(where, gain, grid_parts, cot_parts, first, second_t)
    other = lax.ppermute(send, "c", [(0, 1), (1, 0)])
    pair = (own.astype(F32) + other.astype(F32)).astype(BF16).reshape(64, 56, 128)
    shares = lax.all_to_all(pair, PEERS, split_axis=0, concat_axis=0, tiled=True)
    block_out, grid_grad, gain_part = outputs_call(
        gain, grid, out_grad, act, pre3, second, first_t
    )
    total = jnp.sum(shares.astype(F32), axis=0).astype(BF16)
    gain_own = jnp.sum(gain_part, axis=0, keepdims=True)
    gain_high = gain_own.astype(BF16)
    gain_low = (gain_own - gain_high.astype(F32)).astype(BF16)
    sent = jnp.concatenate([total, gain_high, gain_low, jnp.zeros((6, 128), BF16)], axis=0)
    sent = jnp.broadcast_to(sent[None], (64, 64, 128))
    gathered = lax.all_to_all(sent, PEERS, split_axis=0, concat_axis=0, tiled=True)
    swapped = lax.ppermute(gathered, "c", [(0, 1), (1, 0)])
    factor = 1.0 / math.sqrt(131072.0)

    def weights(low, high):
        picked = jnp.where(core == 0, low, high)[:, :56].reshape(28, 128, 128)[:27]
        return picked.astype(F32) * factor

    gains = jnp.sum(gathered[:, 56:58].astype(F32), axis=(0, 1))
    gains = gains + jnp.sum(swapped[:, 56:58].astype(F32), axis=(0, 1))
    return (
        block_out,
        grid_grad,
        weights(gathered, swapped),
        weights(swapped, gathered),
        gains * factor,
    )


def solution(mesh):
    inner = Mesh(mesh.devices.reshape(4, 2, 4, 2, 2), ("y", "xl", "z", "c", "xh"))
    in_specs = (
        P(GX, GY, SA, None, None),
        P(GX, GY, SA, None),
        P(GX, GY, SA),
        P(),
        P(),
        P(),
        P(GX, GY, SA, None),
    )
    out_specs = (P(GX, GY, SA, None), P(GX, GY, SA, None), P(), P(), P())
    return jax.shard_map(local, mesh=inner, in_specs=in_specs, out_specs=out_specs, check_vma=False)
```

time: 434 us -> 229 us (0.53)
  matrix products: 76.1 us -> 2.43 us
  blocking collectives: 82.7 us -> 25 us
  waiting for transfers between devices: 116 us -> 62.4 us
  Pallas kernels: 0 us -> 42.2 us
  starting transfers between devices: 74.1 us -> 51.8 us
  between operations: 17.2 us -> 1.07 us
  local copies, waits for them, and re-layouts: 43.7 us -> 30 us
  other arithmetic: 18.5 us -> 12.1 us
    dot_general x164 -> x1, matrix products: 76.1 us -> 2.43 us  [local(): lax.dot_general(placing.astype(BF16), rows, (((1,), (0,)), ((), ())), pre...]
    psum x1 -> x0, waiting for transfers between devices: 70.2 us -> none  [local(): lax.psum((first_grad, second_grad, gain_grad), ('gx', 'gy', 'sa'))]
    psum x1 -> x0, blocking collectives: 68.9 us -> none  [local(): lax.psum((first_grad, second_grad, gain_grad), ('gx', 'gy', 'sa'))]
    pallas_call x0 -> x3, Pallas kernels: none -> 42.2 us  [the longest x1 25.9 us: grads_call(): pl.pallas_call(grads_kernel, out_shape=(jax.ShapeDtypeStruct((10, 18, 16,...]
    ppermute x24 -> x12, starting transfers between devices: 68.5 us -> 28.6 us  [the longest x2 8.78 us: edges(): y_low = lax.ppermute(wide_low, GY, forward)]
    slice x120 -> x8, local copies, waits for them, and re-layouts: 34.5 us -> 1.74 us  [the longest x2 0.93 us: swap_edges(): high = lax.ppermute(lax.slice_in_dim(block, 0, 2, axis=dim), axis, backward)]
    all_to_all x1 -> x2, starting transfers between devices: 5.62 us -> 23.2 us  [the longest x1 15.5 us: local(): lax.all_to_all(pair, PEERS, split_axis=0, concat_axis=0, tiled=True)]
    ppermute x24 -> x12, waiting for transfers between devices: 46 us -> 61.4 us  [the longest x2 50.6 us: swap_edges(): high = lax.ppermute(lax.slice_in_dim(block, 0, 2, axis=dim), axis, backward)]
  transfers between devices with their start and end apart: 26 -> 14, of which waited for: 6 -> 8; matrix products, arithmetic and copies ran while one was open for 23% -> 4% of each run, Pallas kernels for 0% -> 7%
where the time goes in v1:
time: 229 us; the launch traced here: 227 us
  waiting for transfers between devices  62.4 us (27%)
  starting transfers between devices  51.8 us (23%)
  Pallas kernels  42.2 us (18%)
  local copies, waits for them, and re-layouts  30 us (13%)
  blocking collectives  25 us (11%)
  other arithmetic  12.1 us (5%)
  matrix products  2.43 us (1%)
    ppermute x2, waiting for transfers between devices, swap_edges(): high = lax.ppermute(lax.slice_in_dim(block, 0, 2, axis=dim), axis, backward)  50.6 us
    pallas_call x1, Pallas kernels, grads_call(): pl.pallas_call(grads_kernel, out_shape=(jax.ShapeDtypeStruct((10, 18, 16,...  25.9 us
    all_to_all x1, blocking collectives, local(): lax.all_to_all(sent, PEERS, split_axis=0, concat_axis=0, tiled=True)  25 us
    unnamed x58, local copies, waits for them, and re-layouts  19.4 us
    all_to_all x1, starting transfers between devices, local(): lax.all_to_all(pair, PEERS, split_axis=0, concat_axis=0, tiled=True)  15.5 us
    pallas_call x1, Pallas kernels, outputs_call(): pl.pallas_call(outputs_kernel, out_shape=(jax.ShapeDtypeStruct((8, 16, 8,...  9.68 us
    ppermute x2, starting transfers between devices, edges(): y_low = lax.ppermute(wide_low, GY, forward)  8.78 us
    all_to_all x1, starting transfers between devices, local(): lax.all_to_all(outgoing, PLANE, split_axis=0, concat_axis=0, tiled=True)  7.77 us
  transfers between devices with their start and end apart: 14, of which 8 were waited for; matrix products, arithmetic and copies ran while one was open for 4% of the time, Pallas kernels for 7%

profile of v1, /device:TPU:1, one launch (start us, length us, event | category | flops | bytes accessed | tf_op | source)
XLA Modules:
  0.0 227.0 jit_solution(14154970900217405554)
XLA Ops:
  2.3 2.4 %select_convert_fusion = bf16[256,64,128]{2,0,1:T(8,128)(2,1)S(1)} fusion(pred[256]{0:T(512)(128)(4,1)S(1)} %fusion.2, bf16[128,64,128]{2,1,0:T(8,128)(2,1)S(1)} %bitcast.28, s32[128]{0:T(128)S(1)} %bitcast_add_fusion), kind=kOutput, calls=%fused_computation | convolution fusion | flops 541097984 | bytes 6292224 | tf_op jit(solution)/shard_map/dot_general | solution.py:306
  4.7 4.7 %copy.17 = bf16[256,64,128]{2,1,0:T(8,128)(2,1)} copy(bf16[256,64,128]{2,0,1:T(8,128)(2,1)S(1)} %select_convert_fusion) | data formatting | bytes 8388608 | tf_op jit(solution)/shard_map/convert_element_type | solution.py:310
  9.4 7.8 %all-to-all-start = ((bf16[256,64,128]{2,1,0:T(8,128)(2,1)}), bf16[256,64,128]{2,1,0:T(8,128)(2,1)}, u32[]{:S(2)}, u32[]{:S(2)}) async-start(bf16[256,64,128]{2,1,0:T(8,128)(2,1)} %copy.17), calls=%async_computation | async-start | bytes 8388608 | tf_op jit(solution)/shard_map/all_to_all | solution.py:311
  17.2 3.2 %collective-permute-start.5 = (bf16[2,16,8,128]{3,2,1,0:T(8,128)(2,1)S(1)}, bf16[2,16,8,128]{3,2,1,0:T(8,128)(2,1)S(1)}, u32[]{:S(2)}, u32[]{:S(2)}) collective-permute-start(bf16[2,16,8,128]{3,2,1,0:T(8,128)(2,1)S(1)} %get-tuple-element.24), channel_id=1, source_target_pairs={{0,16},{16,32},{32,48},{48,64},{64,80},{80,96},{96,112},{1,17},{17... | collective-permute-start | bytes 196616 | tf_op jit(solution)/shard_map/ppermute | solution.py:270
  21.9 50.6 %collective-permute-done.6.o2 = bf16[2,16,8,128]{3,2,1,0:T(8,128)(2,1)S(1)} collective-permute-done((bf16[2,16,8,128]{3,2,1,0:T(8,128)(2,1)S(1)}, bf16[2,16,8,128]{3,2,1,0:T(8,128)(2,1)S(1)}, u32[]{:S(2)}, u32[]{:S(2)}) %collective-permute-start.6) | collective-permute-done | bytes 65568 | tf_op jit(solution)/shard_map/ppermute | solution.py:271
  72.5 5.1 %collective-permute-start.7 = (bf16[12,2,8,128]{3,2,1,0:T(8,128)(2,1)S(1)}, bf16[12,2,8,128]{3,2,1,0:T(8,128)(2,1)S(1)}, u32[]{:S(2)}, u32[]{:S(2)}) collective-permute-start(bf16[12,2,8,128]{3,2,1,0:T(8,128)(2,1)S(1)} %pad_maximum_fusion.4), channel_id=1, source_target_pairs={{0,2},{2,4},{4,6},{6,8},{8,10},{10,12},{12,14},{1,3},{3,5},{5,7},{... | collective-permute-start | bytes 147464 | tf_op jit(solution)/shard_map/ppermute | solution.py:286
  77.7 1.9 collective-permute-start.8
  79.7 3.4 %collective-permute-done.8.o4 = bf16[12,2,8,128]{3,2,1,0:T(8,128)(2,1)S(1)} collective-permute-done((bf16[12,2,8,128]{3,2,1,0:T(8,128)(2,1)S(1)}, bf16[12,2,8,128]{3,2,1,0:T(8,128)(2,1)S(1)}, u32[]{:S(2)}, u32[]{:S(2)}) %collective-permute-start.8) | collective-permute-done | bytes 49184 | tf_op jit(solution)/shard_map/ppermute | solution.py:287
  84.0 2.5 %collective-permute-start.9 = (bf16[12,20,2,128]{3,2,1,0:T(2,128)(2,1)}, bf16[12,20,2,128]{3,2,1,0:T(2,128)(2,1)}, u32[]{:S(2)}, u32[]{:S(2)}) collective-permute-start(bf16[12,20,2,128]{3,2,1,0:T(2,128)(2,1)} %pad_maximum_fusion.1), channel_id=1, source_target_pairs={{0,1},{1,0},{2,3},{3,2},{4,5},{5,4},{6,7},{7,6},{8,9},{9,8},{10,11... | collective-permute-start | bytes 368648 | tf_op jit(solution)/shard_map/ppermute | solution.py:298
  86.6 6.6 %shard_map.110.g0.grid = bf16[8,16,8,128]{3,2,1,0:T(8,128)(2,1)} custom-call(bf16[16,8,2,64,128]{4,3,2,1,0:T(8,128)(2,1)} %bitcast.5.arrived_ref), custom_call_target="tpu_custom_call" | custom-call | flops 8388608 | bytes 5242880 | tf_op jit(solution)/shard_map/pallas_call | solution.py:38
  97.4 4.1 %collective-permute-start = (bf16[2,16,8,128]{3,2,1,0:T(8,128)(2,1)S(1)}, bf16[2,16,8,128]{3,2,1,0:T(8,128)(2,1)S(1)}, u32[]{:S(2)}, u32[]{:S(2)}) collective-permute-start(bf16[2,16,8,128]{3,2,1,0:T(8,128)(2,1)S(1)} %get-tuple-element.28), channel_id=1, source_target_pairs={{0,16},{16,32},{32,48},{48,64},{64,80},{80,96},{96,112},{1,17},{17... | collective-permute-start | bytes 196616 | tf_op jit(solution)/shard_map/ppermute | solution.py:270
  103.5 1.9 collective-permute-start.3
  105.5 3.6 %collective-permute-start.2 = (bf16[12,2,8,128]{3,2,1,0:T(8,128)(2,1)S(1)}, bf16[12,2,8,128]{3,2,1,0:T(8,128)(2,1)S(1)}, u32[]{:S(2)}, u32[]{:S(2)}) collective-permute-start(bf16[12,2,8,128]{3,2,1,0:T(8,128)(2,1)S(1)} %pad_maximum_fusion.2), channel_id=1, source_target_pairs={{0,2},{2,4},{4,6},{6,8},{8,10},{10,12},{12,14},{1,3},{3,5},{5,7},{... | collective-permute-start | bytes 147464 | tf_op jit(solution)/shard_map/ppermute | solution.py:286
  112.4 1.6 copy.18
  114.1 3.5 %collective-permute-done.4.g5 = bf16[12,20,2,128]{3,2,1,0:T(2,128)(2,1)} collective-permute-done((bf16[12,20,2,128]{3,2,1,0:T(2,128)(2,1)}, bf16[12,20,2,128]{3,2,1,0:T(2,128)(2,1)}, u32[]{:S(2)}, u32[]{:S(2)}) %collective-permute-start.4) | collective-permute-done | bytes 122912 | tf_op jit(solution)/shard_map/ppermute | solution.py:298
  126.5 25.9 %shard_map.111 = (bf16[10,18,16,128]{3,2,1,0:T(8,128)(2,1)S(1)}, bf16[10,18,16,384]{3,2,1,0:T(8,128)(2,1)S(1)}, bf16[28,128,128]{2,1,0:T(8,128)(2,1)S(1)}, bf16[28,128,128]{2,1,0:T(8,128)(2,1)}) custom-call(s32[2]{0:T(128)S(1)} %pad_add_fusion.where_ref, f32[1,128]{1,0:T(1,128)S(1)} %bitcast.35, bf16[8,16,8,128]{3,2,1,0:T(8,128)(2,1)S(1)} %copy-done.1, ...), custom_call_target="tpu_custom_call" | custom-call | flops 10737418240 | bytes 8388608 | tf_op jit(solution)/shard_map/pallas_call | solution.py:183
  154.6 2.2 copy.19
  157.4 2.4 %add_convert_fusion = bf16[28,128,128]{2,1,0:T(8,128)(2,1)} fusion(bf16[28,128,128]{2,1,0:T(8,128)(2,1)} %collective-permute-done.10, bf16[28,128,128]{2,1,0:T(8,128)(2,1)S(1)} %get-tuple-element.16), kind=kLoop, calls=%fused_computation.2 | loop fusion | flops 1835008 | bytes 2752512 | tf_op jit(solution)/shard_map/convert_element_type | solution.py:324
  159.9 15.5 %all-to-all-start.1 = ((bf16[64,56,128]{2,1,0:T(8,128)(2,1)}), bf16[64,56,128]{2,1,0:T(8,128)(2,1)S(1)}, u32[]{:S(2)}, u32[]{:S(2)}) async-start(bf16[64,56,128]{2,1,0:T(8,128)(2,1)} %bitcast.37), calls=%async_computation.1 | async-start | bytes 1835008 | tf_op jit(solution)/shard_map/all_to_all | solution.py:325
  180.4 9.7 %shard_map.112 = (bf16[8,16,8,128]{3,2,1,0:T(8,128)(2,1)}, bf16[8,16,8,128]{3,2,1,0:T(8,128)(2,1)}, f32[8,128]{1,0:T(8,128)S(1)}) custom-call(f32[1,128]{1,0:T(1,128)S(1)} %bitcast.36, bf16[8,16,8,128]{3,2,1,0:T(8,128)(2,1)S(1)} %copy-done.1, bf16[8,16,8,128]{3,2,1,0:T(8,128)(2,1)S(1)} %copy-done.7, bf16[10,18,16,128]{3,2,1,0:T(8,128)(2,1)S(1)} %copy-done.28, ...), custom_call_target="tpu_custom_call" | custom-call | flops 8589934592 | bytes 6291456 | tf_op jit(solution)/shard_map/pallas_call | solution.py:248
  191.6 25.0 %all_to_all.15 = bf16[64,64,128]{2,1,0:T(8,128)(2,1)S(1)} all-to-all(bf16[64,64,128]{2,1,0:T(8,128)(2,1)S(1)} %broadcast_in_dim.40), channel_id=1, replica_groups=mesh['y'=4,'xl'=2,'z'=4,'c'=2,'xh'=2] {'y','xl','z','xh'}, dimensions={0} | all-to-all | bytes 2097152 | tf_op jit(solution)/shard_map/all_to_all | solution.py:335
  216.6 3.0 %collective-permute-start.11 = (bf16[64,64,128]{2,1,0:T(8,128)(2,1)S(1)}, bf16[64,64,128]{2,1,0:T(8,128)(2,1)}, u32[]{:S(2)}, u32[]{:S(2)}) collective-permute-start(bf16[64,64,128]{2,1,0:T(8,128)(2,1)S(1)} %all_to_all.15), channel_id=1, source_target_pairs={{0,2},{2,0},{1,3},{3,1},{4,6},{6,4},{5,7},{7,5},{8,10},{10,8},{9,1... | collective-permute-start | bytes 3145736 | tf_op jit(solution)/shard_map/ppermute | solution.py:336
  219.6 2.3 %collective-permute-done.11 = bf16[64,64,128]{2,1,0:T(8,128)(2,1)} collective-permute-done((bf16[64,64,128]{2,1,0:T(8,128)(2,1)S(1)}, bf16[64,64,128]{2,1,0:T(8,128)(2,1)}, u32[]{:S(2)}, u32[]{:S(2)}) %collective-permute-start.11) | collective-permute-done | bytes 1048608 | tf_op jit(solution)/shard_map/ppermute | solution.py:336
  223.2 2.2 convert_multiply_fusion
  (115 shorter events, 34.7 us)
Async XLA Ops:
  0.6 1.6 copy-start
  9.4 7.8 %copy-start.7 = (bf16[8,16,8,128]{3,2,1,0:T(8,128)(2,1)S(1)}, bf16[8,16,8,128]{3,2,1,0:T(8,128)(2,1)}, u32[]{:S(2)}) copy-start(bf16[8,16,8,128]{3,2,1,0:T(8,128)(2,1)} %out_grad.1) | copy-start | bytes 786436
  9.4 77.1 %all-to-all-start = ((bf16[256,64,128]{2,1,0:T(8,128)(2,1)}), bf16[256,64,128]{2,1,0:T(8,128)(2,1)}, u32[]{:S(2)}, u32[]{:S(2)}) async-start(bf16[256,64,128]{2,1,0:T(8,128)(2,1)} %copy.17), calls=%async_computation | async-start | bytes 8388608 | tf_op jit(solution)/shard_map/all_to_all | solution.py:311
  17.2 55.2 %collective-permute-start.5 = (bf16[2,16,8,128]{3,2,1,0:T(8,128)(2,1)S(1)}, bf16[2,16,8,128]{3,2,1,0:T(8,128)(2,1)S(1)}, u32[]{:S(2)}, u32[]{:S(2)}) collective-permute-start(bf16[2,16,8,128]{3,2,1,0:T(8,128)(2,1)S(1)} %get-tuple-element.24), channel_id=1, source_target_pairs={{0,16},{16,32},{32,48},{48,64},{64,80},{80,96},{96,112},{1,17},{17... | collective-permute-start | bytes 196616 | tf_op jit(solution)/shard_map/ppermute | solution.py:270
  20.5 52.0 %collective-permute-start.6 = (bf16[2,16,8,128]{3,2,1,0:T(8,128)(2,1)S(1)}, bf16[2,16,8,128]{3,2,1,0:T(8,128)(2,1)S(1)}, u32[]{:S(2)}, u32[]{:S(2)}) collective-permute-start(bf16[2,16,8,128]{3,2,1,0:T(8,128)(2,1)S(1)} %get-tuple-element.23), channel_id=1, source_target_pairs={{16,0},{32,16},{48,32},{64,48},{80,64},{96,80},{112,96},{17,1},{33... | collective-permute-start | bytes 196616 | tf_op jit(solution)/shard_map/ppermute | solution.py:271
  72.5 14.0 %copy-start.18 = (bf16[2,16,8,128]{3,2,1,0:T(8,128)(2,1)}, bf16[2,16,8,128]{3,2,1,0:T(8,128)(2,1)S(1)}, u32[]{:S(2)}) copy-start(bf16[2,16,8,128]{3,2,1,0:T(8,128)(2,1)S(1)} %collective-permute-done.6.o2) | copy-start | bytes 196612
  72.5 14.0 %copy-start.16 = (bf16[2,16,8,128]{3,2,1,0:T(8,128)(2,1)}, bf16[2,16,8,128]{3,2,1,0:T(8,128)(2,1)S(1)}, u32[]{:S(2)}) copy-start(bf16[2,16,8,128]{3,2,1,0:T(8,128)(2,1)S(1)} %collective-permute-done.5.o1) | copy-start | bytes 196612
  72.5 10.6 %collective-permute-start.7 = (bf16[12,2,8,128]{3,2,1,0:T(8,128)(2,1)S(1)}, bf16[12,2,8,128]{3,2,1,0:T(8,128)(2,1)S(1)}, u32[]{:S(2)}, u32[]{:S(2)}) collective-permute-start(bf16[12,2,8,128]{3,2,1,0:T(8,128)(2,1)S(1)} %pad_maximum_fusion.4), channel_id=1, source_target_pairs={{0,2},{2,4},{4,6},{6,8},{8,10},{10,12},{12,14},{1,3},{3,5},{5,7},{... | collective-permute-start | bytes 147464 | tf_op jit(solution)/shard_map/ppermute | solution.py:286
  77.7 5.4 %collective-permute-start.8 = (bf16[12,2,8,128]{3,2,1,0:T(8,128)(2,1)S(1)}, bf16[12,2,8,128]{3,2,1,0:T(8,128)(2,1)S(1)}, u32[]{:S(2)}, u32[]{:S(2)}) collective-permute-start(bf16[12,2,8,128]{3,2,1,0:T(8,128)(2,1)S(1)} %pad_maximum_fusion.5), channel_id=1, source_target_pairs={{2,0},{4,2},{6,4},{8,6},{10,8},{12,10},{14,12},{3,1},{5,3},{7,5},{... | collective-permute-start | bytes 147464 | tf_op jit(solution)/shard_map/ppermute | solution.py:287
  83.1 3.4 %copy-start.22 = (bf16[12,2,8,128]{3,2,1,0:T(8,128)(2,1)}, bf16[12,2,8,128]{3,2,1,0:T(8,128)(2,1)S(1)}, u32[]{:S(2)}) copy-start(bf16[12,2,8,128]{3,2,1,0:T(8,128)(2,1)S(1)} %collective-permute-done.8.o4) | copy-start | bytes 147460
  83.1 3.4 %copy-start.20 = (bf16[12,2,8,128]{3,2,1,0:T(8,128)(2,1)}, bf16[12,2,8,128]{3,2,1,0:T(8,128)(2,1)S(1)}, u32[]{:S(2)}) copy-start(bf16[12,2,8,128]{3,2,1,0:T(8,128)(2,1)S(1)} %collective-permute-done.7.o3) | copy-start | bytes 147460
  84.0 30.1 %collective-permute-start.9 = (bf16[12,20,2,128]{3,2,1,0:T(2,128)(2,1)}, bf16[12,20,2,128]{3,2,1,0:T(2,128)(2,1)}, u32[]{:S(2)}, u32[]{:S(2)}) collective-permute-start(bf16[12,20,2,128]{3,2,1,0:T(2,128)(2,1)} %pad_maximum_fusion.1), channel_id=1, source_target_pairs={{0,1},{1,0},{2,3},{3,2},{4,5},{5,4},{6,7},{7,6},{8,9},{9,8},{10,11... | collective-permute-start | bytes 368648 | tf_op jit(solution)/shard_map/ppermute | solution.py:298
  86.5 25.9 %copy-start.3 = (bf16[27,128,128]{2,1,0:T(8,128)(2,1)S(1)}, bf16[27,128,128]{2,1,0:T(8,128)(2,1)}, u32[]{:S(2)}) copy-start(bf16[27,128,128]{2,1,0:T(8,128)(2,1)} %param.11) | copy-start | bytes 2654212
  93.2 24.4 %copy-start.1 = (bf16[8,16,8,128]{3,2,1,0:T(8,128)(2,1)S(1)}, bf16[8,16,8,128]{3,2,1,0:T(8,128)(2,1)}, u32[]{:S(2)}) copy-start(bf16[8,16,8,128]{3,2,1,0:T(8,128)(2,1)} %shard_map.110.g0.grid) | copy-start | bytes 786436
  93.2 24.4 %copy-start.24 = (f32[128]{0:T(128)S(1)}, f32[128]{0:T(128)}, u32[]{:S(2)}) copy-start(f32[128]{0:T(128)} %param.12) | copy-start | bytes 1540
  95.3 6.2 %collective-permute-start.1 = (bf16[2,16,8,128]{3,2,1,0:T(8,128)(2,1)S(1)}, bf16[2,16,8,128]{3,2,1,0:T(8,128)(2,1)S(1)}, u32[]{:S(2)}, u32[]{:S(2)}) collective-permute-start(bf16[2,16,8,128]{3,2,1,0:T(8,128)(2,1)S(1)} %get-tuple-element.27), channel_id=1, source_target_pairs={{16,0},{32,16},{48,32},{64,48},{80,64},{96,80},{112,96},{17,1},{33... | collective-permute-start | bytes 196616 | tf_op jit(solution)/shard_map/ppermute | solution.py:271
  97.4 5.4 %collective-permute-start = (bf16[2,16,8,128]{3,2,1,0:T(8,128)(2,1)S(1)}, bf16[2,16,8,128]{3,2,1,0:T(8,128)(2,1)S(1)}, u32[]{:S(2)}, u32[]{:S(2)}) collective-permute-start(bf16[2,16,8,128]{3,2,1,0:T(8,128)(2,1)S(1)} %get-tuple-element.28), channel_id=1, source_target_pairs={{0,16},{16,32},{32,48},{48,64},{64,80},{80,96},{96,112},{1,17},{17... | collective-permute-start | bytes 196616 | tf_op jit(solution)/shard_map/ppermute | solution.py:270
  103.5 5.6 %collective-permute-start.3 = (bf16[12,2,8,128]{3,2,1,0:T(8,128)(2,1)S(1)}, bf16[12,2,8,128]{3,2,1,0:T(8,128)(2,1)S(1)}, u32[]{:S(2)}, u32[]{:S(2)}) collective-permute-start(bf16[12,2,8,128]{3,2,1,0:T(8,128)(2,1)S(1)} %pad_maximum_fusion.3), channel_id=1, source_target_pairs={{2,0},{4,2},{6,4},{8,6},{10,8},{12,10},{14,12},{3,1},{5,3},{7,5},{... | collective-permute-start | bytes 147464 | tf_op jit(solution)/shard_map/ppermute | solution.py:287
  105.5 4.8 %collective-permute-start.2 = (bf16[12,2,8,128]{3,2,1,0:T(8,128)(2,1)S(1)}, bf16[12,2,8,128]{3,2,1,0:T(8,128)(2,1)S(1)}, u32[]{:S(2)}, u32[]{:S(2)}) collective-permute-start(bf16[12,2,8,128]{3,2,1,0:T(8,128)(2,1)S(1)} %pad_maximum_fusion.2), channel_id=1, source_target_pairs={{0,2},{2,4},{4,6},{6,8},{8,10},{10,12},{12,14},{1,3},{3,5},{5,7},{... | collective-permute-start | bytes 147464 | tf_op jit(solution)/shard_map/ppermute | solution.py:286
  111.8 5.8 %collective-permute-start.4 = (bf16[12,20,2,128]{3,2,1,0:T(2,128)(2,1)}, bf16[12,20,2,128]{3,2,1,0:T(2,128)(2,1)}, u32[]{:S(2)}, u32[]{:S(2)}) collective-permute-start(bf16[12,20,2,128]{3,2,1,0:T(2,128)(2,1)} %pad_maximum_fusion), channel_id=1, source_target_pairs={{0,1},{1,0},{2,3},{3,2},{4,5},{5,4},{6,7},{7,6},{8,9},{9,8},{10,11... | collective-permute-start | bytes 368648 | tf_op jit(solution)/shard_map/ppermute | solution.py:298
  154.6 2.8 %collective-permute-start.10 = (bf16[28,128,128]{2,1,0:T(8,128)(2,1)}, bf16[28,128,128]{2,1,0:T(8,128)(2,1)}, u32[]{:S(2)}, u32[]{:S(2)}) collective-permute-start(bf16[28,128,128]{2,1,0:T(8,128)(2,1)} %get-tuple-element.17), channel_id=1, source_target_pairs={{0,2},{2,0},{1,3},{3,1},{4,6},{6,4},{5,7},{7,5},{8,10},{10,8},{9,1... | collective-permute-start | bytes 2752520 | tf_op jit(solution)/shard_map/ppermute | solution.py:323
  159.9 31.2 %all-to-all-start.1 = ((bf16[64,56,128]{2,1,0:T(8,128)(2,1)}), bf16[64,56,128]{2,1,0:T(8,128)(2,1)S(1)}, u32[]{:S(2)}, u32[]{:S(2)}) async-start(bf16[64,56,128]{2,1,0:T(8,128)(2,1)} %bitcast.37), calls=%async_computation.1 | async-start | bytes 1835008 | tf_op jit(solution)/shard_map/all_to_all | solution.py:325
  177.7 1.6 copy-start.26
  216.6 5.4 %collective-permute-start.11 = (bf16[64,64,128]{2,1,0:T(8,128)(2,1)S(1)}, bf16[64,64,128]{2,1,0:T(8,128)(2,1)}, u32[]{:S(2)}, u32[]{:S(2)}) collective-permute-start(bf16[64,64,128]{2,1,0:T(8,128)(2,1)S(1)} %all_to_all.15), channel_id=1, source_target_pairs={{0,2},{2,0},{1,3},{3,1},{4,6},{6,4},{5,7},{7,5},{8,10},{10,8},{9,1... | collective-permute-start | bytes 3145736 | tf_op jit(solution)/shard_map/ppermute | solution.py:336
  (19 other events, 17.1 us)

commit v2 on v1

v2 whole, which is shorter than its diff:
```python
import math

import jax
import jax.numpy as jnp
from jax import lax
from jax.experimental import pallas as pl
from jax.experimental.pallas import tpu as pltpu
from jax.sharding import Mesh
from jax.sharding import PartitionSpec as P

epsilon = 1e-06
DEAD = 1.0e30
OUT = -1.0e30
LIMIT = 1.0e29
GX = ("y", "xl")
GY = ("z", "c")
SA = "xh"
PLANE = ("y", "xl", "xh")
F32 = jnp.float32
BF16 = jnp.bfloat16
VM = pl.BlockSpec(memory_space=pltpu.VMEM)
SM = pl.BlockSpec(memory_space=pltpu.SMEM)


def place_kernel(code_ref, rows_ref, out_ref, flat, place, lift):
    @pl.when(pl.program_id(0) == 0)
    def _():
        slots = lax.broadcasted_iota(jnp.int32, (256, 128), 0)
        chosen = jnp.where(slots == code_ref[...], 1.0, 0.0)
        place[...] = chosen.astype(BF16)
        named = jnp.max(chosen, axis=1, keepdims=True)
        lift[...] = jnp.broadcast_to(jnp.where(named > 0.0, 0.0, DEAD), (256, 128))

    flat[...] = rows_ref[...].astype(F32).reshape(1024, 128)
    for voxel in range(8):
        values = flat[pl.ds(voxel, 128, stride=8), :].astype(BF16)
        summed = jnp.dot(place[...], values, preferred_element_type=F32) + lift[...]
        out_ref[:, voxel] = summed.astype(BF16).reshape(16, 16, 128)


def place_bricks(code, rows):
    return pl.pallas_call(
        place_kernel,
        out_shape=jax.ShapeDtypeStruct((16, 64, 16, 128), BF16),
        grid=(8,),
        in_specs=[
            pl.BlockSpec((1, 128), lambda i: (0, 0)),
            pl.BlockSpec((128, 8, 128), lambda i: (0, i, 0)),
        ],
        out_specs=pl.BlockSpec((16, 8, 16, 128), lambda i: (0, i, 0, 0)),
        scratch_shapes=[
            pltpu.VMEM((1024, 128), F32),
            pltpu.VMEM((256, 128), BF16),
            pltpu.VMEM((256, 128), F32),
        ],
        compiler_params=pltpu.CompilerParams(vmem_limit_bytes=16 << 20),
        cost_estimate=pl.CostEstimate(flops=1 << 29, bytes_accessed=6 << 20, transcendentals=0),
    )(code, rows)


def sum_bricks_kernel(arrived_ref, cot_ref, both_ref, low_ref, high_ref, sums, cells):
    step = pl.program_id(0)
    shift_x = step // 2
    shift_y = (step % 2) * 2

    @pl.when(step == 0)
    def _():
        both_ref[1] = cot_ref[...]
        low_ref[1] = cot_ref[0:2]
        high_ref[1] = cot_ref[6:8]

    total = jnp.zeros((8, 16, 128), F32)
    filled = jnp.zeros((16, 128), jnp.bool_)
    for source in range(16):
        held = arrived_ref[source, 0].astype(F32) < LIMIT
        filled = filled | held
        total = total + jnp.where(held, arrived_ref[source].astype(F32), 0.0)
    sums[...] = jnp.where(filled, total, DEAD).reshape(128, 128)
    for voxel in range(2):
        for bx in range(2):
            for by in range(4):
                slot = (bx * 4 + by) * 2
                cells[0:4, :] = sums[pl.ds(voxel * 64 + slot, 4, stride=16), :]
                cells[4:8, :] = sums[pl.ds(voxel * 64 + slot + 1, 4, stride=16), :]
                both_ref[0, bx * 4 + shift_x, by * 4 + shift_y + voxel] = cells[...].astype(BF16)

    @pl.when(step == 7)
    def _():
        low_ref[0] = both_ref[0, 0:2]
        high_ref[0] = both_ref[0, 6:8]


def sum_bricks(arrived, out_grad):
    return pl.pallas_call(
        sum_bricks_kernel,
        out_shape=(
            jax.ShapeDtypeStruct((2, 8, 16, 8, 128), BF16),
            jax.ShapeDtypeStruct((2, 2, 16, 8, 128), BF16),
            jax.ShapeDtypeStruct((2, 2, 16, 8, 128), BF16),
        ),
        grid=(8,),
        in_specs=[
            pl.BlockSpec((16, 8, 16, 128), lambda i: (0, i, 0, 0)),
            pl.BlockSpec((8, 16, 8, 128), lambda i: (0, 0, 0, 0)),
        ],
        out_specs=(
            pl.BlockSpec((2, 8, 16, 8, 128), lambda i: (0, 0, 0, 0, 0)),
            pl.BlockSpec((2, 2, 16, 8, 128), lambda i: (0, 0, 0, 0, 0)),
            pl.BlockSpec((2, 2, 16, 8, 128), lambda i: (0, 0, 0, 0, 0)),
        ),
        scratch_shapes=[pltpu.VMEM((128, 128), F32), pltpu.VMEM((8, 128), F32)],
        compiler_params=pltpu.CompilerParams(vmem_limit_bytes=16 << 20),
        cost_estimate=pl.CostEstimate(flops=8 << 20, bytes_accessed=5 << 20, transcendentals=0),
    )(arrived, out_grad)


def window_rows(ref, x, y, slabs, rows):
    part = ref[pl.ds(x, slabs), pl.ds(y, rows), :, :]
    return part.reshape(slabs * rows * 16, part.shape[3])


def gather_windows(ref, x, slabs, rows, sign):
    parts = []
    for i in range(3):
        for j in range(3):
            a, b = (i, j) if sign > 0 else (2 - i, 2 - j)
            parts.append(window_rows(ref, x + a, b, slabs, rows))
    return jnp.concatenate(parts, axis=1)


def neighbours(value, sign):
    count = value.shape[0]
    below = pltpu.roll(value, 1, 0)
    above = pltpu.roll(value, count - 1, 0)
    order = (below, value, above) if sign > 0 else (above, value, below)
    return jnp.concatenate([part.astype(BF16) for part in order], axis=1)


PIECES = (
    (2, 8, 16, 8, 128),
    (2, 2, 16, 8, 128),
    (2, 2, 16, 8, 128),
    (2, 12, 2, 8, 128),
    (2, 12, 2, 8, 128),
    (2, 12, 20, 2, 128),
)


def fill(volume, which, pieces, where_ref, outside):
    centre, x_low, x_high, y_low, y_high, z_side = pieces
    volume[...] = jnp.full(volume.shape, outside, F32)
    volume[2:10, 2:18, 2:10, :] = centre[which].astype(F32)
    volume[0:2, 2:18, 2:10, :] = x_low[which].astype(F32)
    volume[10:12, 2:18, 2:10, :] = x_high[which].astype(F32)
    volume[:, 0:2, 2:10, :] = y_low[which].astype(F32)
    volume[:, 18:20, 2:10, :] = y_high[which].astype(F32)

    @pl.when(where_ref[0] == 0)
    def _():
        volume[:, :, 10:12, :] = z_side[which].astype(F32)

    @pl.when(where_ref[0] == 1)
    def _():
        volume[:, :, 0:2, :] = z_side[which].astype(F32)

    @pl.when(where_ref[2] == 0)
    def _():
        volume[0:2] = jnp.full((2, 20, 16, 128), outside, F32)

    @pl.when(where_ref[2] == 7)
    def _():
        volume[10:12] = jnp.full((2, 20, 16, 128), outside, F32)

    @pl.when(where_ref[3] == 0)
    def _():
        volume[:, 0:2] = jnp.full((12, 2, 16, 128), outside, F32)

    @pl.when(where_ref[3] == 7)
    def _():
        volume[:, 18:20] = jnp.full((12, 2, 16, 128), outside, F32)


def grads_kernel(
    where_ref,
    gain,
    p0, p1, p2, p3, p4, p5,
    first_hbm,
    second_hbm,
    act_ref,
    pre3_ref,
    own_ref,
    send_ref,
    cells,
    cots,
    normed3,
    masked3,
    act_t,
    normed_t,
    s0, s1, s2, s3, s4, s5,
    first,
    second_t,
    sems,
):
    core = where_ref[1]
    pieces = (s0, s1, s2, s3, s4, s5)
    copies = [
        pltpu.make_async_copy(source, target, sems.at[n])
        for n, (source, target) in enumerate(
            zip((p0, p1, p2, p3, p4, p5, first_hbm, second_hbm), (*pieces, first, second_t))
        )
    ]
    for copy in copies:
        copy.start()
    for copy in copies[:6]:
        copy.wait()
    fill(cells, 0, pieces, where_ref, OUT)
    fill(cots, 1, pieces, where_ref, 0.0)
    z_of = lax.broadcasted_iota(jnp.int32, (256, 128), 0) % 16
    inside = (z_of >= 2) & (z_of < 10)

    def prepare(x, carry):
        values = cells[x].reshape(320, 128)
        live = jnp.abs(values) < LIMIT
        held = jnp.where(live, values, 0.0)
        inverse = lax.rsqrt(jnp.mean(held * held, axis=-1, keepdims=True) + epsilon)
        normed = held * inverse * gain[...]
        normed3[x] = neighbours(normed, 1).reshape(20, 16, 384)
        masked = jnp.where(live, cots[x].reshape(320, 128), 0.0)
        masked3[x] = neighbours(masked, -1).reshape(20, 16, 384)
        return carry

    lax.fori_loop(0, 12, prepare, 0)

    def turn(x, carry):
        normed = normed3[x + 2, 2:18, :, 128:256].reshape(256, 128).astype(F32)
        columns = pl.ds(pl.multiple_of(x * 256, 256), 256)
        normed_t[:, columns] = jnp.where(inside, normed, 0.0).T.astype(BF16)
        return carry

    lax.fori_loop(0, 8, turn, 0)
    for copy in copies[6:]:
        copy.wait()

    def convolve(step, carry):
        x = step * 2
        values = cells[pl.ds(x + 1, 2), 1:19, :, :].reshape(576, 128)
        before = jnp.dot(
            gather_windows(normed3, x, 2, 18, 1), first[...], preferred_element_type=F32
        )
        before = jnp.where(jnp.abs(values) < LIMIT, before, 0.0)
        sigmoid = jax.nn.sigmoid(before)
        active = before * sigmoid
        act_ref[pl.ds(x, 2)] = active.astype(BF16).reshape(2, 18, 16, 128)
        active_grad = jnp.dot(
            gather_windows(masked3, x, 2, 18, -1), second_t[...], preferred_element_type=F32
        )
        pre = active_grad * sigmoid * (1.0 + before * (1.0 - sigmoid))
        pre = jnp.where(values > -LIMIT, pre, 0.0)
        pre3_ref[pl.ds(x, 2)] = neighbours(pre, -1).reshape(2, 18, 16, 384)
        return carry

    lax.fori_loop(0, 5, convolve, 0)

    def turn_active(x, carry):
        active = act_ref[x + 1, 1:17].reshape(256, 128).astype(F32)
        columns = pl.ds(pl.multiple_of(x * 256, 256), 256)
        act_t[:, columns] = jnp.where(inside, active, 0.0).T.astype(BF16)
        return carry

    lax.fori_loop(0, 8, turn_active, 0)

    for which, left, right, start in ((1, act_t, masked3, 3), (0, normed_t, pre3_ref, 2)):
        for target, here in ((own_ref, which), (send_ref, 1 - which)):

            @pl.when(core == here)
            def _():
                def weights(at, carry):
                    i = at // 3
                    j = at - i * 3
                    cot = window_rows(right, start - i, start - j, 8, 16)
                    total = jnp.dot(left[...], cot, preferred_element_type=F32).astype(BF16)
                    for k in range(3):
                        target[at * 3 + k] = total[:, k * 128 : (k + 1) * 128]
                    return carry

                lax.fori_loop(0, 9, weights, 0)


def grads_call(where, gain, pieces, first, second_t):
    return pl.pallas_call(
        grads_kernel,
        out_shape=(
            jax.ShapeDtypeStruct((10, 18, 16, 128), BF16),
            jax.ShapeDtypeStruct((10, 18, 16, 384), BF16),
            jax.ShapeDtypeStruct((27, 128, 128), BF16),
            jax.ShapeDtypeStruct((27, 128, 128), BF16),
        ),
        in_specs=[SM, VM] + [pl.BlockSpec(memory_space=pl.ANY)] * 8,
        out_specs=(VM,) * 4,
        scratch_shapes=[
            pltpu.VMEM((12, 20, 16, 128), F32),
            pltpu.VMEM((12, 20, 16, 128), F32),
            pltpu.VMEM((12, 20, 16, 384), BF16),
            pltpu.VMEM((12, 20, 16, 384), BF16),
            pltpu.VMEM((128, 2048), BF16),
            pltpu.VMEM((128, 2048), BF16),
            *[pltpu.VMEM(shape, BF16) for shape in PIECES],
            pltpu.VMEM((3456, 128), BF16),
            pltpu.VMEM((3456, 128), BF16),
            pltpu.SemaphoreType.DMA((8,)),
        ],
        compiler_params=pltpu.CompilerParams(vmem_limit_bytes=44 << 20),
        cost_estimate=pl.CostEstimate(flops=10 << 30, bytes_accessed=8 << 20, transcendentals=1 << 20),
    )(where, gain, *pieces, first, second_t)


def outputs_kernel(
    gain, both, act, pre3, second, first_t, block_ref, grad_ref, gain_ref, act3, spread
):
    def prepare(x, carry):
        act3[x] = neighbours(act[x].reshape(288, 128).astype(F32), 1).reshape(18, 16, 384)
        return carry

    lax.fori_loop(0, 10, prepare, 0)
    gains = gain[...]

    def convolve(step, total):
        x = step * 2
        branch = jnp.dot(
            gather_windows(act3, x, 2, 16, 1), second[...], preferred_element_type=F32
        )
        spread[...] = branch.reshape(2, 16, 16, 128)
        branch = spread[:, :, 2:10, :].reshape(256, 128)
        values = both[0, pl.ds(x, 2)].astype(F32).reshape(256, 128)
        live = values < LIMIT
        held = jnp.where(live, values, 0.0)
        block = jnp.where(live, branch, 0.0) + held
        block_ref[pl.ds(x, 2)] = block.astype(BF16).reshape(2, 16, 8, 128)
        normed_grad = jnp.dot(
            gather_windows(pre3, x, 2, 16, -1), first_t[...], preferred_element_type=F32
        )
        spread[...] = normed_grad.reshape(2, 16, 16, 128)
        normed_grad = jnp.where(live, spread[:, :, 2:10, :].reshape(256, 128), 0.0)
        inverse = lax.rsqrt(jnp.mean(held * held, axis=-1, keepdims=True) + epsilon)
        total = total + jnp.sum((normed_grad * held * inverse).reshape(32, 8, 128), axis=0)
        upstream = normed_grad * gains
        centred = jnp.mean(held * upstream, axis=-1, keepdims=True)
        extra = inverse * upstream - held * (inverse * inverse * inverse * centred)
        cot = both[1, pl.ds(x, 2)].astype(F32).reshape(256, 128)
        grad = cot + jnp.where(live, extra, 0.0)
        grad_ref[pl.ds(x, 2)] = grad.astype(BF16).reshape(2, 16, 8, 128)
        return total

    total = lax.fori_loop(0, 4, convolve, jnp.zeros((8, 128), F32))
    gain_ref[...] = total


def outputs_call(gain, both, act, pre3, second, first_t):
    return pl.pallas_call(
        outputs_kernel,
        out_shape=(
            jax.ShapeDtypeStruct((8, 16, 8, 128), BF16),
            jax.ShapeDtypeStruct((8, 16, 8, 128), BF16),
            jax.ShapeDtypeStruct((8, 128), F32),
        ),
        in_specs=[VM] * 6,
        out_specs=(VM,) * 3,
        scratch_shapes=[
            pltpu.VMEM((10, 18, 16, 384), BF16),
            pltpu.VMEM((2, 16, 16, 128), F32),
        ],
        compiler_params=pltpu.CompilerParams(vmem_limit_bytes=24 << 20),
        cost_estimate=pl.CostEstimate(flops=8 << 30, bytes_accessed=6 << 20, transcendentals=4096),
    )(gain, both, act, pre3, second, first_t)


FORWARD = [(i, i + 1) for i in range(7)]
BACKWARD = [(i + 1, i) for i in range(7)]


def edges(both, send_low, send_high):
    x_low = lax.ppermute(send_high, GX, FORWARD)
    x_high = lax.ppermute(send_low, GX, BACKWARD)
    parts = (x_low, both, x_high)
    wide_low = jnp.concatenate([part[:, :, 14:16] for part in parts], axis=1)
    wide_high = jnp.concatenate([part[:, :, 0:2] for part in parts], axis=1)
    y_low = lax.ppermute(wide_low, GY, FORWARD)
    y_high = lax.ppermute(wide_high, GY, BACKWARD)
    side = lax.axis_index(SA)

    def layer(part):
        return jnp.where(side == 0, part[:, :, :, 6:8], part[:, :, :, 0:2])

    middle = jnp.concatenate([layer(part) for part in parts], axis=1)
    sent = jnp.concatenate([layer(y_low), middle, layer(y_high)], axis=2)
    z_side = lax.ppermute(sent, SA, [(0, 1), (1, 0)])
    return both, x_low, x_high, y_low, y_high, z_side


def exchange(values, axes):
    return lax.all_to_all(values, axes, split_axis=0, concat_axis=0, tiled=True)


def local(sweep_bricks, target_rank, target_slot, conv_first, conv_second, norm_gain, out_grad):
    code = target_rank.reshape(1, 128) * 16 + target_slot.reshape(1, 128)
    arrived = exchange(place_bricks(code, sweep_bricks.reshape(128, 64, 128)), PLANE)
    gain = norm_gain.reshape(1, 128)
    first = conv_first.reshape(3456, 128)
    second = conv_second.reshape(3456, 128)
    first_t = conv_first.transpose(0, 2, 1).reshape(3456, 128)
    second_t = conv_second.transpose(0, 2, 1).reshape(3456, 128)
    pieces = edges(*sum_bricks(arrived, out_grad))
    core = lax.axis_index("c")
    where = jnp.stack([lax.axis_index(SA), core, lax.axis_index(GX), lax.axis_index(GY)])
    act, pre3, own, send = grads_call(where.astype(jnp.int32), gain, pieces, first, second_t)
    other = lax.ppermute(send, "c", [(0, 1), (1, 0)])
    pair = (own.astype(F32) + other.astype(F32)).astype(BF16).reshape(16, 216, 128)
    shares = exchange(pair, PLANE)
    block_out, grid_grad, gain_part = outputs_call(gain, pieces[0], act, pre3, second, first_t)

    def halves(row):
        high = row.astype(BF16)
        low = (row - high.astype(F32)).astype(BF16)
        return [high, low, jnp.zeros((6, 128), BF16)]

    def spread(total, row, count):
        sent = jnp.concatenate([total.astype(BF16)] + halves(row), axis=0)
        return jnp.broadcast_to(sent[None], (count, 224, 128))

    total = jnp.sum(shares.astype(F32), axis=0)
    row = jnp.sum(gain_part, axis=0, keepdims=True)
    layers = exchange(spread(total, row, 4), "z").astype(F32)
    total = jnp.sum(layers[:, :216], axis=0)
    row = jnp.sum(layers[:, 216:218], axis=(0, 1))[None]
    gathered = exchange(spread(total, row, 16), PLANE)
    swapped = lax.ppermute(gathered, "c", [(0, 1), (1, 0)])
    factor = 1.0 / math.sqrt(131072.0)

    def weights(low, high):
        picked = jnp.where(core == 0, low[:, :216], high[:, :216])
        return (picked.astype(F32) * factor).reshape(27, 128, 128)

    gains = jnp.sum(gathered[:, 216:218].astype(F32), axis=(0, 1))
    gains = gains + jnp.sum(swapped[:, 216:218].astype(F32), axis=(0, 1))
    return (
        block_out,
        grid_grad,
        weights(gathered, swapped),
        weights(swapped, gathered),
        gains * factor,
    )


def solution(mesh):
    inner = Mesh(mesh.devices.reshape(4, 2, 4, 2, 2), ("y", "xl", "z", "c", "xh"))
    in_specs = (
        P(GX, GY, SA, None, None),
        P(GX, GY, SA, None),
        P(GX, GY, SA),
        P(),
        P(),
        P(),
        P(GX, GY, SA, None),
    )
    out_specs = (P(GX, GY, SA, None), P(GX, GY, SA, None), P(), P(), P())
    return jax.shard_map(local, mesh=inner, in_specs=in_specs, out_specs=out_specs, check_vma=False)
```

time: 229 us -> 205 us (0.90)
  starting transfers between devices: 51.8 us -> 34.8 us
  local copies, waits for them, and re-layouts: 30 us -> 18.6 us
  waiting for transfers between devices: 62.4 us -> 69.2 us
  other arithmetic: 12.1 us -> 8.35 us
  Pallas kernels: 42.2 us -> 45.4 us
  matrix products: 2.43 us -> 0 us
    all_to_all x2, waiting for transfers between devices: 0.96 us -> 56.7 us  [exchange(): return lax.all_to_all(values, axes, split_axis=0, concat_axis=0, tiled=True)]
    ppermute x8 -> x4, waiting for transfers between devices: 55.1 us -> 5.84 us  [the longest x1 5.04 us: edges(): x_high = lax.ppermute(send_low, GX, BACKWARD)]
    ppermute x8 -> x4, starting transfers between devices: 22.5 us -> 9.85 us  [the longest x1 3.66 us: edges(): y_high = lax.ppermute(wide_high, GY, BACKWARD)]
    all_to_all x2, starting transfers between devices: 23.2 us -> 15.1 us  [exchange(): return lax.all_to_all(values, axes, split_axis=0, concat_axis=0, tiled=True)]
    convert_element_type x1 -> x0, local copies, waits for them, and re-layouts: 4.74 us -> none  [local(): outgoing = jnp.where(named, outgoing, DEAD).astype(BF16)]
    unnamed x58 -> x46, local copies, waits for them, and re-layouts: 19.4 us -> 15.8 us
    pallas_call x1 -> x2, Pallas kernels: 6.62 us -> 9.07 us  [the longest x1 5.43 us: sum_bricks(): pl.pallas_call(sum_bricks_kernel, out_shape=(jax.ShapeDtypeStruct((2, 8,...]
    select_n x15 -> x5, other arithmetic: 2.85 us -> 0.41 us  [layer(): return jnp.where(side == 0, part[:, :, :, 6:8], part[:, :, :, 0:2])]
  transfers between devices with their start and end apart: 14 -> 9, of which waited for: 8 -> 8; matrix products, arithmetic and copies ran while one was open for 4% -> 2% of each run, Pallas kernels for 7% -> 5%
where the time goes in v2:
time: 205 us; the launch traced here: 204 us
  waiting for transfers between devices  69.2 us (34%)
  Pallas kernels  45.4 us (22%)
  starting transfers between devices  34.8 us (17%)
  blocking collectives  26.7 us (13%)
  local copies, waits for them, and re-layouts  18.6 us (9%)
  other arithmetic  8.35 us (4%)
    all_to_all x2, waiting for transfers between devices, exchange(): return lax.all_to_all(values, axes, split_axis=0, concat_axis=0, tiled=True)  56.7 us
    all_to_all x2, blocking collectives, exchange(): return lax.all_to_all(values, axes, split_axis=0, concat_axis=0, tiled=True)  26.7 us
    pallas_call x1, Pallas kernels, grads_call(): pl.pallas_call(grads_kernel, out_shape=(jax.ShapeDtypeStruct((10, 18, 16,...  26.7 us
    unnamed x46, local copies, waits for them, and re-layouts  15.8 us
    all_to_all x2, starting transfers between devices, exchange(): return lax.all_to_all(values, axes, split_axis=0, concat_axis=0, tiled=True)  15.1 us
    pallas_call x1, Pallas kernels, outputs_call(): pl.pallas_call(outputs_kernel, out_shape=(jax.ShapeDtypeStruct((8, 16, 8,...  9.68 us
    pallas_call x1, Pallas kernels, sum_bricks(): pl.pallas_call(sum_bricks_kernel, out_shape=(jax.ShapeDtypeStruct((2, 8,...  5.43 us
    ppermute x1, starting transfers between devices, local(): swapped = lax.ppermute(gathered, 'c', [(0, 1), (1, 0)])  5.16 us
  transfers between devices with their start and end apart: 9, of which 8 were waited for; matrix products, arithmetic and copies ran while one was open for 2% of the time, Pallas kernels for 5%

profile of v2, /device:TPU:1, one launch (start us, length us, event | category | flops | bytes accessed | tf_op | source)
XLA Modules:
  0.0 204.0 jit_solution(2056434409516980730)
XLA Ops:
  1.3 1.6 copy-done.1
  2.9 3.6 %shard_map.110 = bf16[16,64,16,128]{3,2,1,0:T(8,128)(2,1)S(1)} custom-call(s32[1,128]{1,0:T(1,128)S(1)} %bitcast_add_fusion.code_ref, bf16[128,64,128]{2,1,0:T(8,128)(2,1)S(1)} %bitcast.33), custom_call_target="tpu_custom_call" | custom-call | flops 536870912 | bytes 6291456 | tf_op jit(solution)/shard_map/pallas_call | solution.py:42
  6.6 2.0 copy-done
  8.6 7.8 %all-to-all-start = ((bf16[16,64,16,128]{3,2,1,0:T(8,128)(2,1)}), bf16[16,64,16,128]{3,2,1,0:T(8,128)(2,1)}, u32[]{:S(2)}, u32[]{:S(2)}) async-start(bf16[16,64,16,128]{3,2,1,0:T(8,128)(2,1)} %copy-done), calls=%async_computation | async-start | bytes 8388608 | tf_op jit(solution)/shard_map/all_to_all | solution.py:401
  16.3 54.3 %all-to-all-done.arrived_ref = bf16[16,64,16,128]{3,2,1,0:T(8,128)(2,1)} async-done(((bf16[16,64,16,128]{3,2,1,0:T(8,128)(2,1)}), bf16[16,64,16,128]{3,2,1,0:T(8,128)(2,1)}, u32[]{:S(2)}, u32[]{:S(2)}) %all-to-all-start) | async-done | bytes 4194336 | tf_op jit(solution)/shard_map/all_to_all | solution.py:401
  70.7 5.4 %shard_map.111 = (bf16[2,8,16,8,128]{4,3,2,1,0:T(8,128)(2,1)S(1)}, bf16[2,2,16,8,128]{4,3,2,1,0:T(8,128)(2,1)S(1)}, bf16[2,2,16,8,128]{4,3,2,1,0:T(8,128)(2,1)S(1)}) custom-call(bf16[16,64,16,128]{3,2,1,0:T(8,128)(2,1)} %all-to-all-done.arrived_ref, bf16[8,16,8,128]{3,2,1,0:T(8,128)(2,1)S(1)} %copy-done.7), custom_call_target="tpu_custom_call" | custom-call | flops 8388608 | bytes 5242880 | tf_op jit(solution)/shard_map/pallas_call | solution.py:94
  76.1 1.4 collective-permute-start
  79.9 5.0 %collective-permute-done.1.p2 = bf16[2,2,16,8,128]{4,3,2,1,0:T(8,128)(2,1)S(1)} collective-permute-done((bf16[2,2,16,8,128]{4,3,2,1,0:T(8,128)(2,1)S(1)}, bf16[2,2,16,8,128]{4,3,2,1,0:T(8,128)(2,1)S(1)}, u32[]{:S(2)}, u32[]{:S(2)}) %collective-permute-start.1) | collective-permute-done | bytes 131104 | tf_op jit(solution)/shard_map/ppermute | solution.py:383
  85.0 3.7 %collective-permute-start.3 = (bf16[2,12,2,8,128]{4,3,2,1,0:T(8,128)(2,1)S(1)}, bf16[2,12,2,8,128]{4,3,2,1,0:T(8,128)(2,1)S(1)}, u32[]{:S(2)}, u32[]{:S(2)}) collective-permute-start(bf16[2,12,2,8,128]{4,3,2,1,0:T(8,128)(2,1)S(1)} %pad_maximum_fusion.2), channel_id=1, source_target_pairs={{2,0},{4,2},{6,4},{8,6},{10,8},{12,10},{14,12},{3,1},{5,3},{7,5},{... | collective-permute-start | bytes 294920 | tf_op jit(solution)/shard_map/ppermute | solution.py:388
  88.7 3.5 %collective-permute-start.2 = (bf16[2,12,2,8,128]{4,3,2,1,0:T(8,128)(2,1)S(1)}, bf16[2,12,2,8,128]{4,3,2,1,0:T(8,128)(2,1)S(1)}, u32[]{:S(2)}, u32[]{:S(2)}) collective-permute-start(bf16[2,12,2,8,128]{4,3,2,1,0:T(8,128)(2,1)S(1)} %pad_maximum_fusion.1), channel_id=1, source_target_pairs={{0,2},{2,4},{4,6},{6,8},{8,10},{10,12},{12,14},{1,3},{3,5},{5,7},{... | collective-permute-start | bytes 294920 | tf_op jit(solution)/shard_map/ppermute | solution.py:387
  94.9 4.7 %collective-permute-start.4 = (bf16[2,12,20,2,128]{4,3,2,1,0:T(2,128)(2,1)S(1)}, bf16[2,12,20,2,128]{4,3,2,1,0:T(2,128)(2,1)S(1)}, u32[]{:S(2)}, u32[]{:S(2)}) collective-permute-start(bf16[2,12,20,2,128]{4,3,2,1,0:T(2,128)(2,1)S(1)} %pad_maximum_fusion), channel_id=1, source_target_pairs={{0,1},{1,0},{2,3},{3,2},{4,5},{5,4},{6,7},{7,6},{8,9},{9,8},{10,11... | collective-permute-start | bytes 737288 | tf_op jit(solution)/shard_map/ppermute | solution.py:396
  101.0 3.2 %collective-permute-done.4.p5 = bf16[2,12,20,2,128]{4,3,2,1,0:T(2,128)(2,1)S(1)} collective-permute-done((bf16[2,12,20,2,128]{4,3,2,1,0:T(2,128)(2,1)S(1)}, bf16[2,12,20,2,128]{4,3,2,1,0:T(2,128)(2,1)S(1)}, u32[]{:S(2)}, u32[]{:S(2)}) %collective-permute-start.4) | collective-permute-done | bytes 245792 | tf_op jit(solution)/shard_map/ppermute | solution.py:396
  110.5 26.7 %shard_map.112 = (bf16[10,18,16,128]{3,2,1,0:T(8,128)(2,1)S(1)}, bf16[10,18,16,384]{3,2,1,0:T(8,128)(2,1)S(1)}, bf16[27,128,128]{2,1,0:T(8,128)(2,1)S(1)}, bf16[27,128,128]{2,1,0:T(8,128)(2,1)}) custom-call(s32[4]{0:T(128)S(1)} %pad_add_fusion.where_ref, f32[1,128]{1,0:T(1,128)S(1)} %bitcast.40, bf16[2,8,16,8,128]{4,3,2,1,0:T(8,128)(2,1)S(1)} %copy-done.5, ...), custom_call_target="tpu_custom_call" | custom-call | flops 10737418240 | bytes 8388608 | tf_op jit(solution)/shard_map/pallas_call | solution.py:290
  137.2 1.4 copy-done.19
  142.2 2.4 %add_convert_fusion = bf16[27,128,128]{2,1,0:T(8,128)(2,1)} fusion(bf16[27,128,128]{2,1,0:T(8,128)(2,1)} %collective-permute-done.5, bf16[27,128,128]{2,1,0:T(8,128)(2,1)S(1)} %get-tuple-element.22), kind=kLoop, calls=%fused_computation.2 | loop fusion | flops 1769472 | bytes 2654208 | tf_op jit(solution)/shard_map/convert_element_type | solution.py:417
  144.6 7.3 %all-to-all-start.1 = ((bf16[16,216,128]{2,1,0:T(8,128)(2,1)}), bf16[16,216,128]{2,1,0:T(8,128)(2,1)}, u32[]{:S(2)}, u32[]{:S(2)}) async-start(bf16[16,216,128]{2,1,0:T(8,128)(2,1)} %bitcast.42), calls=%async_computation.1 | async-start | bytes 1769472 | tf_op jit(solution)/shard_map/all_to_all | solution.py:401
  151.9 1.6 copy-done.20
  153.6 9.7 %shard_map.113 = (bf16[8,16,8,128]{3,2,1,0:T(8,128)(2,1)}, bf16[8,16,8,128]{3,2,1,0:T(8,128)(2,1)}, f32[8,128]{1,0:T(8,128)S(1)}) custom-call(f32[1,128]{1,0:T(1,128)S(1)} %bitcast.41, bf16[2,8,16,8,128]{4,3,2,1,0:T(8,128)(2,1)S(1)} %copy-done.6, bf16[10,18,16,128]{3,2,1,0:T(8,128)(2,1)S(1)} %copy-done.22, bf16[10,18,16,384]{3,2,1,0:T(8,128)(2,1)S(1)} %copy-done.20, ...), custom_call_target="tpu_custom_call" | custom-call | flops 8589934592 | bytes 6291456 | tf_op jit(solution)/shard_map/pallas_call | solution.py:359
  163.3 2.3 %all-to-all-done.1 = bf16[16,216,128]{2,1,0:T(8,128)(2,1)} async-done(((bf16[16,216,128]{2,1,0:T(8,128)(2,1)}), bf16[16,216,128]{2,1,0:T(8,128)(2,1)}, u32[]{:S(2)}, u32[]{:S(2)}) %all-to-all-start.1) | async-done | bytes 884768 | tf_op jit(solution)/shard_map/all_to_all | solution.py:401
  167.0 11.1 %all_to_all.20 = bf16[4,224,128]{2,1,0:T(8,128)(2,1)S(1)} all-to-all(bf16[4,224,128]{2,1,0:T(8,128)(2,1)S(1)} %broadcast_in_dim.4), channel_id=1, replica_groups=mesh['y'=4,'xl'=2,'z'=4,'c'=2,'xh'=2] {'z'}, dimensions={0} | all-to-all | bytes 458752 | tf_op jit(solution)/shard_map/all_to_all | solution.py:401
  178.5 15.6 %all_to_all.21 = bf16[16,224,128]{2,1,0:T(8,128)(2,1)S(1)} all-to-all(bf16[16,224,128]{2,1,0:T(8,128)(2,1)S(1)} %broadcast_in_dim.5), channel_id=1, replica_groups=mesh['y'=4,'xl'=2,'z'=4,'c'=2,'xh'=2] {'y','xl','xh'}, dimensions={0} | all-to-all | bytes 1835008 | tf_op jit(solution)/shard_map/all_to_all | solution.py:401
  194.1 5.2 %collective-permute-start.6 = (bf16[16,224,128]{2,1,0:T(8,128)(2,1)S(1)}, bf16[16,224,128]{2,1,0:T(8,128)(2,1)S(1)}, u32[]{:S(2)}, u32[]{:S(2)}) collective-permute-start(bf16[16,224,128]{2,1,0:T(8,128)(2,1)S(1)} %all_to_all.21), channel_id=1, source_target_pairs={{0,2},{2,0},{1,3},{3,1},{4,6},{6,4},{5,7},{7,5},{8,10},{10,8},{9,1... | collective-permute-start | bytes 2752520 | tf_op jit(solution)/shard_map/ppermute | solution.py:436
  199.3 2.1 %collective-permute-done.6 = bf16[16,224,128]{2,1,0:T(8,128)(2,1)S(1)} collective-permute-done((bf16[16,224,128]{2,1,0:T(8,128)(2,1)S(1)}, bf16[16,224,128]{2,1,0:T(8,128)(2,1)S(1)}, u32[]{:S(2)}, u32[]{:S(2)}) %collective-permute-start.6) | collective-permute-done | bytes 917536 | tf_op jit(solution)/shard_map/ppermute | solution.py:436
  201.9 2.1 %convert_multiply_fusion = (f32[16,216,128]{2,1,0:T(8,128)}, f32[16,216,128]{2,1,0:T(8,128)}) fusion(pred[]{:T(512)S(6)} %eq.5, bf16[16,224,128]{2,1,0:T(8,128)(2,1)S(1)} %collective-permute-done.6, bf16[16,224,128]{2,1,0:T(8,128)(2,1)S(1)} %all_to_all.21), kind=kLoop, calls=%fused_computation | loop fusion | flops 2654208 | bytes 5308417 | tf_op jit(solution)/shard_map/mul | solution.py:441
  (81 shorter events, 19.3 us)
Async XLA Ops:
  1.3 1.6 copy-start.1
  6.5 2.0 copy-start
  8.5 62.1 %copy-start.7 = (bf16[8,16,8,128]{3,2,1,0:T(8,128)(2,1)S(1)}, bf16[8,16,8,128]{3,2,1,0:T(8,128)(2,1)}, u32[]{:S(2)}) copy-start(bf16[8,16,8,128]{3,2,1,0:T(8,128)(2,1)} %cot_ref.1) | copy-start | bytes 786436
  8.6 62.1 %all-to-all-start = ((bf16[16,64,16,128]{3,2,1,0:T(8,128)(2,1)}), bf16[16,64,16,128]{3,2,1,0:T(8,128)(2,1)}, u32[]{:S(2)}, u32[]{:S(2)}) async-start(bf16[16,64,16,128]{3,2,1,0:T(8,128)(2,1)} %copy-done), calls=%async_computation | async-start | bytes 8388608 | tf_op jit(solution)/shard_map/all_to_all | solution.py:401
  76.1 23.4 %copy-start.3 = (bf16[27,128,128]{2,1,0:T(8,128)(2,1)S(1)}, bf16[27,128,128]{2,1,0:T(8,128)(2,1)}, u32[]{:S(2)}) copy-start(bf16[27,128,128]{2,1,0:T(8,128)(2,1)} %param.11) | copy-start | bytes 2654212
  76.1 3.8 %collective-permute-start = (bf16[2,2,16,8,128]{4,3,2,1,0:T(8,128)(2,1)S(1)}, bf16[2,2,16,8,128]{4,3,2,1,0:T(8,128)(2,1)S(1)}, u32[]{:S(2)}, u32[]{:S(2)}) collective-permute-start(bf16[2,2,16,8,128]{4,3,2,1,0:T(8,128)(2,1)S(1)} %get-tuple-element.16), channel_id=1, source_target_pairs={{0,16},{16,32},{32,48},{48,64},{64,80},{80,96},{96,112},{1,17},{17... | collective-permute-start | bytes 393224 | tf_op jit(solution)/shard_map/ppermute | solution.py:382
  77.6 7.4 %collective-permute-start.1 = (bf16[2,2,16,8,128]{4,3,2,1,0:T(8,128)(2,1)S(1)}, bf16[2,2,16,8,128]{4,3,2,1,0:T(8,128)(2,1)S(1)}, u32[]{:S(2)}, u32[]{:S(2)}) collective-permute-start(bf16[2,2,16,8,128]{4,3,2,1,0:T(8,128)(2,1)S(1)} %get-tuple-element.17), channel_id=1, source_target_pairs={{16,0},{32,16},{48,32},{64,48},{80,64},{96,80},{112,96},{17,1},{33... | collective-permute-start | bytes 393224 | tf_op jit(solution)/shard_map/ppermute | solution.py:383
  79.1 25.8 %copy-start.2 = (bf16[27,128,128]{2,1,0:T(8,128)(2,1)S(1)}, bf16[27,128,128]{2,1,0:T(8,128)(2,1)}, u32[]{:S(2)}) copy-start(bf16[27,128,128]{2,1,0:T(8,128)(2,1)} %param.10) | copy-start | bytes 2654212
  79.1 25.8 %copy-start.18 = (f32[128]{0:T(128)S(1)}, f32[128]{0:T(128)}, u32[]{:S(2)}) copy-start(f32[128]{0:T(128)} %param.12) | copy-start | bytes 1540
  79.9 12.3 %copy-start.8 = (bf16[2,2,16,8,128]{4,3,2,1,0:T(8,128)(2,1)}, bf16[2,2,16,8,128]{4,3,2,1,0:T(8,128)(2,1)S(1)}, u32[]{:S(2)}) copy-start(bf16[2,2,16,8,128]{4,3,2,1,0:T(8,128)(2,1)S(1)} %collective-permute-done.p1) | copy-start | bytes 393220
  85.0 7.3 %copy-start.10 = (bf16[2,2,16,8,128]{4,3,2,1,0:T(8,128)(2,1)}, bf16[2,2,16,8,128]{4,3,2,1,0:T(8,128)(2,1)S(1)}, u32[]{:S(2)}) copy-start(bf16[2,2,16,8,128]{4,3,2,1,0:T(8,128)(2,1)S(1)} %collective-permute-done.1.p2) | copy-start | bytes 393220
  85.0 7.5 %collective-permute-start.3 = (bf16[2,12,2,8,128]{4,3,2,1,0:T(8,128)(2,1)S(1)}, bf16[2,12,2,8,128]{4,3,2,1,0:T(8,128)(2,1)S(1)}, u32[]{:S(2)}, u32[]{:S(2)}) collective-permute-start(bf16[2,12,2,8,128]{4,3,2,1,0:T(8,128)(2,1)S(1)} %pad_maximum_fusion.2), channel_id=1, source_target_pairs={{2,0},{4,2},{6,4},{8,6},{10,8},{12,10},{14,12},{3,1},{5,3},{7,5},{... | collective-permute-start | bytes 294920 | tf_op jit(solution)/shard_map/ppermute | solution.py:388
  88.7 5.1 %collective-permute-start.2 = (bf16[2,12,2,8,128]{4,3,2,1,0:T(8,128)(2,1)S(1)}, bf16[2,12,2,8,128]{4,3,2,1,0:T(8,128)(2,1)S(1)}, u32[]{:S(2)}, u32[]{:S(2)}) collective-permute-start(bf16[2,12,2,8,128]{4,3,2,1,0:T(8,128)(2,1)S(1)} %pad_maximum_fusion.1), channel_id=1, source_target_pairs={{0,2},{2,4},{4,6},{6,8},{8,10},{10,12},{12,14},{1,3},{3,5},{5,7},{... | collective-permute-start | bytes 294920 | tf_op jit(solution)/shard_map/ppermute | solution.py:387
  94.9 9.3 %collective-permute-start.4 = (bf16[2,12,20,2,128]{4,3,2,1,0:T(2,128)(2,1)S(1)}, bf16[2,12,20,2,128]{4,3,2,1,0:T(2,128)(2,1)S(1)}, u32[]{:S(2)}, u32[]{:S(2)}) collective-permute-start(bf16[2,12,20,2,128]{4,3,2,1,0:T(2,128)(2,1)S(1)} %pad_maximum_fusion), channel_id=1, source_target_pairs={{0,1},{1,0},{2,3},{3,2},{4,5},{5,4},{6,7},{7,6},{8,9},{9,8},{10,11... | collective-permute-start | bytes 737288 | tf_op jit(solution)/shard_map/ppermute | solution.py:396
  104.9 1.0 copy-start.5
  105.9 0.9 copy-start.9
  109.5 0.9 copy-start.17
  137.1 1.4 copy-start.19
  139.4 2.8 %collective-permute-start.5 = (bf16[27,128,128]{2,1,0:T(8,128)(2,1)}, bf16[27,128,128]{2,1,0:T(8,128)(2,1)}, u32[]{:S(2)}, u32[]{:S(2)}) collective-permute-start(bf16[27,128,128]{2,1,0:T(8,128)(2,1)} %get-tuple-element.23), channel_id=1, source_target_pairs={{0,2},{2,0},{1,3},{3,1},{4,6},{6,4},{5,7},{7,5},{8,10},{10,8},{9,1... | collective-permute-start | bytes 2654216 | tf_op jit(solution)/shard_map/ppermute | solution.py:416
  142.2 9.8 %copy-start.6 = (bf16[2,8,16,8,128]{4,3,2,1,0:T(8,128)(2,1)S(1)}, bf16[2,8,16,8,128]{4,3,2,1,0:T(8,128)(2,1)}, u32[]{:S(2)}) copy-start(bf16[2,8,16,8,128]{4,3,2,1,0:T(8,128)(2,1)} %copy-done.4) | copy-start | bytes 1572868
  144.6 7.3 %copy-start.22 = (bf16[10,18,16,128]{3,2,1,0:T(8,128)(2,1)S(1)}, bf16[10,18,16,128]{3,2,1,0:T(8,128)(2,1)}, u32[]{:S(2)}) copy-start(bf16[10,18,16,128]{3,2,1,0:T(8,128)(2,1)} %copy-done.21) | copy-start | bytes 2211844
  144.6 21.0 %all-to-all-start.1 = ((bf16[16,216,128]{2,1,0:T(8,128)(2,1)}), bf16[16,216,128]{2,1,0:T(8,128)(2,1)}, u32[]{:S(2)}, u32[]{:S(2)}) async-start(bf16[16,216,128]{2,1,0:T(8,128)(2,1)} %bitcast.42), calls=%async_computation.1 | async-start | bytes 1769472 | tf_op jit(solution)/shard_map/all_to_all | solution.py:401
  151.9 1.6 copy-start.20
  194.1 7.3 %collective-permute-start.6 = (bf16[16,224,128]{2,1,0:T(8,128)(2,1)S(1)}, bf16[16,224,128]{2,1,0:T(8,128)(2,1)S(1)}, u32[]{:S(2)}, u32[]{:S(2)}) collective-permute-start(bf16[16,224,128]{2,1,0:T(8,128)(2,1)S(1)} %all_to_all.21), channel_id=1, source_target_pairs={{0,2},{2,0},{1,3},{3,1},{4,6},{6,4},{5,7},{7,5},{8,10},{10,8},{9,1... | collective-permute-start | bytes 2752520 | tf_op jit(solution)/shard_map/ppermute | solution.py:436
  (8 other events, 6.3 us)

commit v3 on v2

--- a/solution.py
+++ b/solution.py
@@ -22,7 +22,7 @@
 SM = pl.BlockSpec(memory_space=pltpu.SMEM)
 
 
-def place_kernel(code_ref, rows_ref, out_ref, flat, place, lift):
+def place_kernel(code_ref, rows_ref, o0, o1, o2, o3, flat, place, lift):
     @pl.when(pl.program_id(0) == 0)
     def _():
         slots = lax.broadcasted_iota(jnp.int32, (256, 128), 0)
@@ -35,62 +35,88 @@
     for voxel in range(8):
         values = flat[pl.ds(voxel, 128, stride=8), :].astype(BF16)
         summed = jnp.dot(place[...], values, preferred_element_type=F32) + lift[...]
-        out_ref[:, voxel] = summed.astype(BF16).reshape(16, 16, 128)
-
-
-def place_bricks(code, rows):
+        summed = summed.astype(BF16).reshape(4, 4, 16, 128)
+        for shift, out in enumerate((o0, o1, o2, o3)):
+            out[:, voxel] = summed[shift]
+
+
+def place_bricks(code, rows, half):
     return pl.pallas_call(
         place_kernel,
-        out_shape=jax.ShapeDtypeStruct((16, 64, 16, 128), BF16),
-        grid=(8,),
+        out_shape=(jax.ShapeDtypeStruct((4, 32, 16, 128), BF16),) * 4,
+        grid=(4,),
         in_specs=[
             pl.BlockSpec((1, 128), lambda i: (0, 0)),
-            pl.BlockSpec((128, 8, 128), lambda i: (0, i, 0)),
+            pl.BlockSpec((128, 8, 128), lambda i: (0, i + 4 * half, 0)),
         ],
-        out_specs=pl.BlockSpec((16, 8, 16, 128), lambda i: (0, i, 0, 0)),
+        out_specs=(pl.BlockSpec((4, 8, 16, 128), lambda i: (0, i, 0, 0)),) * 4,
         scratch_shapes=[
             pltpu.VMEM((1024, 128), F32),
             pltpu.VMEM((256, 128), BF16),
             pltpu.VMEM((256, 128), F32),
         ],
-        compiler_params=pltpu.CompilerParams(vmem_limit_bytes=16 << 20),
-        cost_estimate=pl.CostEstimate(flops=1 << 29, bytes_accessed=6 << 20, transcendentals=0),
+        compiler_params=pltpu.CompilerParams(vmem_limit_bytes=10 << 20),
+        cost_estimate=pl.CostEstimate(flops=1 << 28, bytes_accessed=3 << 20, transcendentals=0),
     )(code, rows)
 
 
-def sum_bricks_kernel(arrived_ref, cot_ref, both_ref, low_ref, high_ref, sums, cells):
-    step = pl.program_id(0)
-    shift_x = step // 2
-    shift_y = (step % 2) * 2
-
-    @pl.when(step == 0)
-    def _():
-        both_ref[1] = cot_ref[...]
-        low_ref[1] = cot_ref[0:2]
-        high_ref[1] = cot_ref[6:8]
-
-    total = jnp.zeros((8, 16, 128), F32)
-    filled = jnp.zeros((16, 128), jnp.bool_)
-    for source in range(16):
-        held = arrived_ref[source, 0].astype(F32) < LIMIT
+def added(parts):
+    total = jnp.zeros(parts[0].shape, F32)
+    filled = jnp.zeros(parts[0].shape[1:], jnp.bool_)
+    for part in parts:
+        held = part[0] < LIMIT
         filled = filled | held
-        total = total + jnp.where(held, arrived_ref[source].astype(F32), 0.0)
-    sums[...] = jnp.where(filled, total, DEAD).reshape(128, 128)
-    for voxel in range(2):
-        for bx in range(2):
-            for by in range(4):
-                slot = (bx * 4 + by) * 2
-                cells[0:4, :] = sums[pl.ds(voxel * 64 + slot, 4, stride=16), :]
-                cells[4:8, :] = sums[pl.ds(voxel * 64 + slot + 1, 4, stride=16), :]
-                both_ref[0, bx * 4 + shift_x, by * 4 + shift_y + voxel] = cells[...].astype(BF16)
-
-    @pl.when(step == 7)
-    def _():
-        low_ref[0] = both_ref[0, 0:2]
-        high_ref[0] = both_ref[0, 6:8]
-
-
-def sum_bricks(arrived, out_grad):
+        total = total + jnp.where(held, part, 0.0)
+    return jnp.where(filled, total, DEAD)
+
+
+def merge_kernel(p0, p1, p2, p3, o0, o1, o2, o3):
+    for shift, out in enumerate((o0, o1, o2, o3)):
+        parts = [part[shift].astype(F32) for part in (p0, p1, p2, p3)]
+        out[...] = added(parts).astype(BF16)
+
+
+def merge_bricks(parts):
+    return pl.pallas_call(
+        merge_kernel,
+        out_shape=(jax.ShapeDtypeStruct((32, 16, 128), BF16),) * 4,
+        grid=(4,),
+        in_specs=[pl.BlockSpec((4, 8, 16, 128), lambda i: (0, i, 0, 0))] * 4,
+        out_specs=(pl.BlockSpec((8, 16, 128), lambda i: (i, 0, 0)),) * 4,
+        compiler_params=pltpu.CompilerParams(vmem_limit_bytes=10 << 20),
+        cost_estimate=pl.CostEstimate(flops=4 << 20, bytes_accessed=3 << 20, transcendentals=0),
+    )(*parts)
+
+
+def sum_bricks_kernel(
+    a0, a1, a2, a3, b0, b1, b2, b3, cot_ref, both_ref, low_ref, high_ref, sums, cells
+):
+    both_ref[1] = cot_ref[...]
+    for half, parts in enumerate(((a0, a1, a2, a3), (b0, b1, b2, b3))):
+
+        def block(step, carry):
+            shift_x = half * 2 + step // 2
+            shift_y = (step % 2) * 2
+            at = pl.ds(pl.multiple_of(step * 8, 8), 8)
+            sums[...] = added([part[at].astype(F32) for part in parts]).reshape(128, 128)
+            for voxel in range(2):
+                for bx in range(2):
+                    for by in range(4):
+                        slot = voxel * 64 + (bx * 4 + by) * 2
+                        spot = (voxel * 2 + bx) * 4 + by
+                        cells[spot, 0:4, :] = sums[pl.ds(slot, 4, stride=16), :]
+                        cells[spot, 4:8, :] = sums[pl.ds(slot + 1, 4, stride=16), :]
+                        both_ref[0, bx * 4 + shift_x, by * 4 + shift_y + voxel] = cells[
+                            spot
+                        ].astype(BF16)
+            return carry
+
+        lax.fori_loop(0, 4, block, 0)
+    low_ref[...] = both_ref[:, 0:2]
+    high_ref[...] = both_ref[:, 6:8]
+
+
+def sum_bricks(parts, out_grad):
     return pl.pallas_call(
         sum_bricks_kernel,
         out_shape=(
@@ -98,20 +124,42 @@
             jax.ShapeDtypeStruct((2, 2, 16, 8, 128), BF16),
             jax.ShapeDtypeStruct((2, 2, 16, 8, 128), BF16),
         ),
-        grid=(8,),
-        in_specs=[
-            pl.BlockSpec((16, 8, 16, 128), lambda i: (0, i, 0, 0)),
-            pl.BlockSpec((8, 16, 8, 128), lambda i: (0, 0, 0, 0)),
-        ],
-        out_specs=(
-            pl.BlockSpec((2, 8, 16, 8, 128), lambda i: (0, 0, 0, 0, 0)),
-            pl.BlockSpec((2, 2, 16, 8, 128), lambda i: (0, 0, 0, 0, 0)),
-            pl.BlockSpec((2, 2, 16, 8, 128), lambda i: (0, 0, 0, 0, 0)),
-        ),
-        scratch_shapes=[pltpu.VMEM((128, 128), F32), pltpu.VMEM((8, 128), F32)],
-        compiler_params=pltpu.CompilerParams(vmem_limit_bytes=16 << 20),
-        cost_estimate=pl.CostEstimate(flops=8 << 20, bytes_accessed=5 << 20, transcendentals=0),
-    )(arrived, out_grad)
+        in_specs=[VM] * 9,
+        out_specs=(VM,) * 3,
+        scratch_shapes=[pltpu.VMEM((128, 128), F32), pltpu.VMEM((16, 8, 128), F32)],
+        compiler_params=pltpu.CompilerParams(vmem_limit_bytes=8 << 20),
+        cost_estimate=pl.CostEstimate(flops=8 << 20, bytes_accessed=2 << 20, transcendentals=0),
+    )(*parts, out_grad)
+
+
+def ring(axes, shift, place_of):
+    size = 4
+    return [(place_of(i), place_of((i + shift) % size)) for i in range(size)]
+
+
+def along_x(value, shift):
+    return lax.ppermute(value, ("xl", "xh"), ring(0, shift, lambda i: (i % 2) * 2 + i // 2))
+
+
+def along_y(value, shift):
+    return lax.ppermute(value, "y", ring(0, shift, lambda i: i))
+
+
+def regroup(rows, target_rank, target_slot, out_grad):
+    to_x = target_rank % 2 * 2 + target_rank // 2 % 2
+    shift_x = (to_x - (lax.axis_index("xh") * 2 + lax.axis_index("xl"))) & 3
+    shift_y = (target_rank // 4 - lax.axis_index("y")) & 3
+    code_a = (shift_x * 4 + shift_y) * 16 + target_slot
+    code_b = (shift_y * 4 + shift_x) * 16 + target_slot
+    placed_a = place_bricks(code_a, rows, 0)
+    placed_b = place_bricks(code_b, rows, 1)
+    came_a = [placed_a[0]] + [along_x(placed_a[n], n) for n in (1, 2, 3)]
+    came_b = [placed_b[0]] + [along_y(placed_b[n], n) for n in (1, 2, 3)]
+    merged_a = merge_bricks(came_a)
+    merged_b = merge_bricks(came_b)
+    came_a = [merged_a[0]] + [along_y(merged_a[n], n) for n in (1, 2, 3)]
+    came_b = [merged_b[0]] + [along_x(merged_b[n], n) for n in (1, 2, 3)]
+    return sum_bricks(came_a + came_b, out_grad)
 
 
 def window_rows(ref, x, y, slabs, rows):
@@ -119,20 +167,30 @@
     return part.reshape(slabs * rows * 16, part.shape[3])
 
 
-def gather_windows(ref, x, slabs, rows, sign):
-    parts = []
-    for i in range(3):
-        for j in range(3):
-            a, b = (i, j) if sign > 0 else (2 - i, 2 - j)
-            parts.append(window_rows(ref, x + a, b, slabs, rows))
+def gather_windows(ref, x, rows):
+    parts = [window_rows(ref, x + i, j, 1, rows) for i in range(4) for j in range(3)]
     return jnp.concatenate(parts, axis=1)
 
 
-def neighbours(value, sign):
+def convolve_pair(ref, x, rows, weights):
+    both = jnp.dot(gather_windows(ref, x, rows), weights[...], preferred_element_type=F32)
+    return jnp.concatenate([both[:, 0:128], both[:, 128:256]], axis=0)
+
+
+def pair_weights(weights):
+    blocks = weights.reshape(3, 3, 384, 128)
+    left = jnp.pad(blocks, ((0, 1), (0, 0), (0, 0), (0, 0)))
+    right = jnp.pad(blocks, ((1, 0), (0, 0), (0, 0), (0, 0)))
+    return jnp.concatenate([left, right], axis=3).reshape(4608, 256)
+
+
+def turned(weights):
+    return pair_weights(weights[::-1].transpose(0, 2, 1))
+
+
+def neighbours(value):
     count = value.shape[0]
-    below = pltpu.roll(value, 1, 0)
-    above = pltpu.roll(value, count - 1, 0)
-    order = (below, value, above) if sign > 0 else (above, value, below)
+    order = (pltpu.roll(value, 1, 0), value, pltpu.roll(value, count - 1, 0))
     return jnp.concatenate([part.astype(BF16) for part in order], axis=1)
 
 
@@ -224,16 +282,20 @@
         held = jnp.where(live, values, 0.0)
         inverse = lax.rsqrt(jnp.mean(held * held, axis=-1, keepdims=True) + epsilon)
         normed = held * inverse * gain[...]
-        normed3[x] = neighbours(normed, 1).reshape(20, 16, 384)
+        normed3[x] = neighbours(normed).reshape(20, 16, 384)
         masked = jnp.where(live, cots[x].reshape(320, 128), 0.0)
-        masked3[x] = neighbours(masked, -1).reshape(20, 16, 384)
+        masked3[x] = neighbours(masked).reshape(20, 16, 384)
         return carry
 
     lax.fori_loop(0, 12, prepare, 0)
+
+    for turned_ref in (normed_t, act_t):
+        turned_ref[:, 0:512] = jnp.zeros((128, 512), BF16)
+        turned_ref[:, 2560:3072] = jnp.zeros((128, 512), BF16)
 
     def turn(x, carry):
         normed = normed3[x + 2, 2:18, :, 128:256].reshape(256, 128).astype(F32)
-        columns = pl.ds(pl.multiple_of(x * 256, 256), 256)
+        columns = pl.ds(pl.multiple_of(x * 256 + 512, 256), 256)
         normed_t[:, columns] = jnp.where(inside, normed, 0.0).T.astype(BF16)
         return carry
 
@@ -244,46 +306,45 @@
     def convolve(step, carry):
         x = step * 2
         values = cells[pl.ds(x + 1, 2), 1:19, :, :].reshape(576, 128)
-        before = jnp.dot(
-            gather_windows(normed3, x, 2, 18, 1), first[...], preferred_element_type=F32
-        )
+        before = convolve_pair(normed3, x, 18, first)
         before = jnp.where(jnp.abs(values) < LIMIT, before, 0.0)
         sigmoid = jax.nn.sigmoid(before)
         active = before * sigmoid
         act_ref[pl.ds(x, 2)] = active.astype(BF16).reshape(2, 18, 16, 128)
-        active_grad = jnp.dot(
-            gather_windows(masked3, x, 2, 18, -1), second_t[...], preferred_element_type=F32
-        )
+        active_grad = convolve_pair(masked3, x, 18, second_t)
         pre = active_grad * sigmoid * (1.0 + before * (1.0 - sigmoid))
         pre = jnp.where(values > -LIMIT, pre, 0.0)
-        pre3_ref[pl.ds(x, 2)] = neighbours(pre, -1).reshape(2, 18, 16, 384)
+        pre3_ref[pl.ds(x, 2)] = neighbours(pre).reshape(2, 18, 16, 384)
         return carry
 
     lax.fori_loop(0, 5, convolve, 0)
 
     def turn_active(x, carry):
         active = act_ref[x + 1, 1:17].reshape(256, 128).astype(F32)
-        columns = pl.ds(pl.multiple_of(x * 256, 256), 256)
+        columns = pl.ds(pl.multiple_of(x * 256 + 512, 256), 256)
         act_t[:, columns] = jnp.where(inside, active, 0.0).T.astype(BF16)
         return carry
 
     lax.fori_loop(0, 8, turn_active, 0)
 
-    for which, left, right, start in ((1, act_t, masked3, 3), (0, normed_t, pre3_ref, 2)):
+    for which, left, right, start in ((1, act_t, masked3, 1), (0, normed_t, pre3_ref, 0)):
         for target, here in ((own_ref, which), (send_ref, 1 - which)):
 
             @pl.when(core == here)
             def _():
-                def weights(at, carry):
-                    i = at // 3
-                    j = at - i * 3
-                    cot = window_rows(right, start - i, start - j, 8, 16)
-                    total = jnp.dot(left[...], cot, preferred_element_type=F32).astype(BF16)
-                    for k in range(3):
-                        target[at * 3 + k] = total[:, k * 128 : (k + 1) * 128]
+                def weights(j, carry):
+                    cot = window_rows(right, start, start + 2 - j, 10, 16)
+                    own = [left[:, 256 * (i + 0) : 256 * (i + 10)] for i in range(3)]
+                    own = jnp.concatenate(own, axis=0)
+                    total = jnp.dot(own, cot, preferred_element_type=F32).astype(BF16)
+                    for i in range(3):
+                        for k in range(3):
+                            target[i * 9 + j * 3 + k] = total[
+                                i * 128 : (i + 1) * 128, (2 - k) * 128 : (3 - k) * 128
+                            ]
                     return carry
 
-                lax.fori_loop(0, 9, weights, 0)
+                lax.fori_loop(0, 3, weights, 0)
 
 
 def grads_call(where, gain, pieces, first, second_t):
@@ -302,14 +363,14 @@
             pltpu.VMEM((12, 20, 16, 128), F32),
             pltpu.VMEM((12, 20, 16, 384), BF16),
             pltpu.VMEM((12, 20, 16, 384), BF16),
-            pltpu.VMEM((128, 2048), BF16),
-            pltpu.VMEM((128, 2048), BF16),
+            pltpu.VMEM((128, 3072), BF16),
+            pltpu.VMEM((128, 3072), BF16),
             *[pltpu.VMEM(shape, BF16) for shape in PIECES],
-            pltpu.VMEM((3456, 128), BF16),
-            pltpu.VMEM((3456, 128), BF16),
+            pltpu.VMEM((4608, 256), BF16),
+            pltpu.VMEM((4608, 256), BF16),
             pltpu.SemaphoreType.DMA((8,)),
         ],
-        compiler_params=pltpu.CompilerParams(vmem_limit_bytes=44 << 20),
+        compiler_params=pltpu.CompilerParams(vmem_limit_bytes=34 << 20),
         cost_estimate=pl.CostEstimate(flops=10 << 30, bytes_accessed=8 << 20, transcendentals=1 << 20),
     )(where, gain, *pieces, first, second_t)
 
@@ -318,7 +379,7 @@
     gain, both, act, pre3, second, first_t, block_ref, grad_ref, gain_ref, act3, spread
 ):
     def prepare(x, carry):
-        act3[x] = neighbours(act[x].reshape(288, 128).astype(F32), 1).reshape(18, 16, 384)
+        act3[x] = neighbours(act[x].reshape(288, 128).astype(F32)).reshape(18, 16, 384)
         return carry
 
     lax.fori_loop(0, 10, prepare, 0)
@@ -326,9 +387,7 @@
 
     def convolve(step, total):
         x = step * 2
-        branch = jnp.dot(
-            gather_windows(act3, x, 2, 16, 1), second[...], preferred_element_type=F32
-        )
+        branch = convolve_pair(act3, x, 16, second)
         spread[...] = branch.reshape(2, 16, 16, 128)
         branch = spread[:, :, 2:10, :].reshape(256, 128)
         values = both[0, pl.ds(x, 2)].astype(F32).reshape(256, 128)
@@ -336,9 +395,7 @@
         held = jnp.where(live, values, 0.0)
         block = jnp.where(live, branch, 0.0) + held
         block_ref[pl.ds(x, 2)] = block.astype(BF16).reshape(2, 16, 8, 128)
-        normed_grad = jnp.dot(
-            gather_windows(pre3, x, 2, 16, -1), first_t[...], preferred_element_type=F32
-        )
+        normed_grad = convolve_pair(pre3, x, 16, first_t)
         spread[...] = normed_grad.reshape(2, 16, 16, 128)
         normed_grad = jnp.where(live, spread[:, :, 2:10, :].reshape(256, 128), 0.0)
         inverse = lax.rsqrt(jnp.mean(held * held, axis=-1, keepdims=True) + epsilon)
@@ -369,7 +426,7 @@
             pltpu.VMEM((10, 18, 16, 384), BF16),
             pltpu.VMEM((2, 16, 16, 128), F32),
         ],
-        compiler_params=pltpu.CompilerParams(vmem_limit_bytes=24 << 20),
+        compiler_params=pltpu.CompilerParams(vmem_limit_bytes=20 << 20),
         cost_estimate=pl.CostEstimate(flops=8 << 30, bytes_accessed=6 << 20, transcendentals=4096),
     )(gain, both, act, pre3, second, first_t)
 
@@ -402,14 +459,18 @@
 
 
 def local(sweep_bricks, target_rank, target_slot, conv_first, conv_second, norm_gain, out_grad):
-    code = target_rank.reshape(1, 128) * 16 + target_slot.reshape(1, 128)
-    arrived = exchange(place_bricks(code, sweep_bricks.reshape(128, 64, 128)), PLANE)
+    both = regroup(
+        sweep_bricks.reshape(128, 64, 128),
+        target_rank.reshape(1, 128),
+        target_slot.reshape(1, 128),
+        out_grad,
+    )
     gain = norm_gain.reshape(1, 128)
-    first = conv_first.reshape(3456, 128)
-    second = conv_second.reshape(3456, 128)
-    first_t = conv_first.transpose(0, 2, 1).reshape(3456, 128)
-    second_t = conv_second.transpose(0, 2, 1).reshape(3456, 128)
-    pieces = edges(*sum_bricks(arrived, out_grad))
+    first = pair_weights(conv_first)
+    second = pair_weights(conv_second)
+    first_t = turned(conv_first)
+    second_t = turned(conv_second)
+    pieces = edges(*both)
     core = lax.axis_index("c")
     where = jnp.stack([lax.axis_index(SA), core, lax.axis_index(GX), lax.axis_index(GY)])
     act, pre3, own, send = grads_call(where.astype(jnp.int32), gain, pieces, first, second_t)

time: 205 us -> 177 us (0.86)
  waiting for transfers between devices: 69.2 us -> 32.4 us
  starting transfers between devices: 34.8 us -> 43.4 us
  Pallas kernels: 45.4 us -> 39.5 us
  other arithmetic: 8.35 us -> 12.9 us
  blocking collectives: 26.7 us -> 30 us
    all_to_all x2 -> x1, waiting for transfers between devices: 56.7 us -> 0.33 us  [exchange(): return lax.all_to_all(values, axes, split_axis=0, concat_axis=0, tiled=True)]
    ppermute x0 -> x12, starting transfers between devices: none -> 21.4 us  [the longest x6 11.9 us: along_y(): return lax.ppermute(value, 'y', ring(0, shift, lambda i: i))]
    ppermute x0 -> x12, waiting for transfers between devices: none -> 17.8 us  [the longest x6 17.8 us: along_x(): lax.ppermute(value, ('xl', 'xh'), ring(0, shift, lambda i: i % 2 * 2 + i...]
    all_to_all x2 -> x1, starting transfers between devices: 15.1 us -> 4.31 us  [exchange(): return lax.all_to_all(values, axes, split_axis=0, concat_axis=0, tiled=True)]
    pallas_call x1 -> x4, Pallas kernels: 3.64 us -> 7.83 us  [the longest x2 4.6 us: place_bricks(): pl.pallas_call(place_kernel, out_shape=(jax.ShapeDtypeStruct((4, 32, 16,...]
    pallas_call x1, Pallas kernels: 26.7 us -> 22.7 us  [grads_call(): pl.pallas_call(grads_kernel, out_shape=(jax.ShapeDtypeStruct((10, 18, 16,...]
    concatenate x0 -> x4, other arithmetic: none -> 3.9 us  [pair_weights(): return jnp.concatenate([left, right], axis=3).reshape(4608, 256)]
    pallas_call x1, Pallas kernels: 5.43 us -> 1.55 us  [sum_bricks(): pl.pallas_call(sum_bricks_kernel, out_shape=(jax.ShapeDtypeStruct((2, 8,...]
  transfers between devices with their start and end apart: 9 -> 20, of which waited for: 8 -> 12; matrix products, arithmetic and copies ran while one was open for 2% -> 7% of each run, Pallas kernels for 5% -> 8%
where the time goes in v3:
time: 177 us
  starting transfers between devices  43.4 us (25%)
  Pallas kernels  39.5 us (22%)
  waiting for transfers between devices  32.4 us (18%)
  blocking collectives  30 us (17%)
  local copies, waits for them, and re-layouts  17.4 us (10%)
  other arithmetic  12.9 us (7%)
    all_to_all x2, blocking collectives, exchange(): return lax.all_to_all(values, axes, split_axis=0, concat_axis=0, tiled=True)  30 us
    pallas_call x1, Pallas kernels, grads_call(): pl.pallas_call(grads_kernel, out_shape=(jax.ShapeDtypeStruct((10, 18, 16,...  22.7 us
    ppermute x6, waiting for transfers between devices, along_x(): lax.ppermute(value, ('xl', 'xh'), ring(0, shift, lambda i: i % 2 * 2 + i...  17.8 us
    unnamed x34, local copies, waits for them, and re-layouts  14 us
    ppermute x6, starting transfers between devices, along_y(): return lax.ppermute(value, 'y', ring(0, shift, lambda i: i))  11.9 us
    ppermute x6, starting transfers between devices, along_x(): lax.ppermute(value, ('xl', 'xh'), ring(0, shift, lambda i: i % 2 * 2 + i...  9.48 us
    pallas_call x1, Pallas kernels, outputs_call(): pl.pallas_call(outputs_kernel, out_shape=(jax.ShapeDtypeStruct((8, 16, 8,...  7.47 us
    ppermute x1, waiting for transfers between devices, edges(): z_side = lax.ppermute(sent, SA, [(0, 1), (1, 0)])  5.75 us
  transfers between devices with their start and end apart: 20, of which 12 were waited for; matrix products, arithmetic and copies ran while one was open for 7% of the time, Pallas kernels for 8%

profile of v3, /device:TPU:1, one launch (start us, length us, event | category | flops | bytes accessed | tf_op | source)
XLA Modules:
  0.0 176.6 jit_solution(16169020410503538887)
XLA Ops:
  5.5 2.1 %collective-permute-start = (bf16[4,32,16,128]{3,2,1,0:T(8,128)(2,1)S(1)}, bf16[4,32,16,128]{3,2,1,0:T(8,128)(2,1)S(1)}, u32[]{:S(2)}, u32[]{:S(2)}) collective-permute-start(bf16[4,32,16,128]{3,2,1,0:T(8,128)(2,1)S(1)} %get-tuple-element.32), channel_id=1, source_target_pairs={{0,16},{16,1},{1,17},{17,0},{2,18},{18,3},{3,19},{19,2},{4,20},{20... | collective-permute-start | bytes 1572872 | tf_op jit(solution)/shard_map/ppermute | solution.py:141
  7.6 2.5 %collective-permute-start.1 = (bf16[4,32,16,128]{3,2,1,0:T(8,128)(2,1)S(1)}, bf16[4,32,16,128]{3,2,1,0:T(8,128)(2,1)S(1)}, u32[]{:S(2)}, u32[]{:S(2)}) collective-permute-start(bf16[4,32,16,128]{3,2,1,0:T(8,128)(2,1)S(1)} %get-tuple-element.33), channel_id=1, source_target_pairs={{0,1},{16,17},{1,0},{17,16},{2,3},{18,19},{3,2},{19,18},{4,5},{20,... | collective-permute-start | bytes 1572872 | tf_op jit(solution)/shard_map/ppermute | solution.py:141
  11.2 2.7 %shard_map.112 = (bf16[4,32,16,128]{3,2,1,0:T(8,128)(2,1)S(1)}, bf16[4,32,16,128]{3,2,1,0:T(8,128)(2,1)S(1)}, bf16[4,32,16,128]{3,2,1,0:T(8,128)(2,1)}, bf16[4,32,16,128]{3,2,1,0:T(8,128)(2,1)S(1)}) custom-call(s32[1,128]{1,0:T(1,128)S(1)} %get-tuple-element.57.code_ref, bf16[128,64,128]{2,1,0:T(8,128)(2,1)S(1)} %bitcast.63), custom_call_target="tpu_custom_call" | custom-call | flops 268435456 | bytes 3145728 | tf_op jit(solution)/shard_map/pallas_call | solution.py:44
  15.2 2.6 %collective-permute-start.7 = (bf16[4,32,16,128]{3,2,1,0:T(8,128)(2,1)}, bf16[4,32,16,128]{3,2,1,0:T(8,128)(2,1)S(1)}, u32[]{:S(2)}, u32[]{:S(2)}) collective-permute-start(bf16[4,32,16,128]{3,2,1,0:T(8,128)(2,1)} %get-tuple-element.41), channel_id=1, source_target_pairs={{0,64},{32,96},{64,0},{96,32},{1,65},{33,97},{65,1},{97,33},{2,66}... | collective-permute-start | bytes 1572872 | tf_op jit(solution)/shard_map/ppermute | solution.py:145
  17.8 2.2 %collective-permute-done.p1 = bf16[4,32,16,128]{3,2,1,0:T(8,128)(2,1)S(1)} collective-permute-done((bf16[4,32,16,128]{3,2,1,0:T(8,128)(2,1)S(1)}, bf16[4,32,16,128]{3,2,1,0:T(8,128)(2,1)S(1)}, u32[]{:S(2)}, u32[]{:S(2)}) %collective-permute-start) | collective-permute-done | bytes 524320 | tf_op jit(solution)/shard_map/ppermute | solution.py:141
  20.1 3.1 %collective-permute-start.8 = (bf16[4,32,16,128]{3,2,1,0:T(8,128)(2,1)S(1)}, bf16[4,32,16,128]{3,2,1,0:T(8,128)(2,1)S(1)}, u32[]{:S(2)}, u32[]{:S(2)}) collective-permute-start(bf16[4,32,16,128]{3,2,1,0:T(8,128)(2,1)S(1)} %get-tuple-element.42), channel_id=1, source_target_pairs={{0,96},{32,0},{64,32},{96,64},{1,97},{33,1},{65,33},{97,65},{2,98}... | collective-permute-start | bytes 1572872 | tf_op jit(solution)/shard_map/ppermute | solution.py:145
  23.1 9.5 %collective-permute-done.1.p2 = bf16[4,32,16,128]{3,2,1,0:T(8,128)(2,1)S(1)} collective-permute-done((bf16[4,32,16,128]{3,2,1,0:T(8,128)(2,1)S(1)}, bf16[4,32,16,128]{3,2,1,0:T(8,128)(2,1)S(1)}, u32[]{:S(2)}, u32[]{:S(2)}) %collective-permute-start.1) | collective-permute-done | bytes 524320 | tf_op jit(solution)/shard_map/ppermute | solution.py:141
  36.1 2.2 %copy.17 = bf16[27,128,128]{1,2,0:T(8,128)(2,1)} copy(bf16[27,128,128]{2,1,0:T(8,128)(2,1)} %param.11) | data formatting | bytes 1769472 | tf_op args[4]
  38.3 2.2 %rev.6 = bf16[27,128,128]{1,2,0:T(8,128)(2,1)} reverse(bf16[27,128,128]{1,2,0:T(8,128)(2,1)} %copy.17), dimensions={0} | reverse | bytes 1769472 | tf_op jit(solution)/shard_map/rev | solution.py:188
  40.5 2.6 %collective-permute-start.4 = (bf16[32,16,128]{2,1,0:T(8,128)(2,1)}, bf16[32,16,128]{2,1,0:T(8,128)(2,1)S(1)}, u32[]{:S(2)}, u32[]{:S(2)}) collective-permute-start(bf16[32,16,128]{2,1,0:T(8,128)(2,1)} %copy-done.7), channel_id=1, source_target_pairs={{0,64},{32,96},{64,0},{96,32},{1,65},{33,97},{65,1},{97,33},{2,66}... | collective-permute-start | bytes 393224 | tf_op jit(solution)/shard_map/ppermute | solution.py:145
  45.9 2.1 %collective-permute-start.10 = (bf16[32,16,128]{2,1,0:T(8,128)(2,1)}, bf16[32,16,128]{2,1,0:T(8,128)(2,1)S(1)}, u32[]{:S(2)}, u32[]{:S(2)}) collective-permute-start(bf16[32,16,128]{2,1,0:T(8,128)(2,1)} %get-tuple-element.45), channel_id=1, source_target_pairs={{0,1},{16,17},{1,0},{17,16},{2,3},{18,19},{3,2},{19,18},{4,5},{20,... | collective-permute-start | bytes 393224 | tf_op jit(solution)/shard_map/ppermute | solution.py:141
  51.4 3.3 %collective-permute-done.11.b3 = bf16[32,16,128]{2,1,0:T(8,128)(2,1)S(1)} collective-permute-done((bf16[32,16,128]{2,1,0:T(8,128)(2,1)}, bf16[32,16,128]{2,1,0:T(8,128)(2,1)S(1)}, u32[]{:S(2)}, u32[]{:S(2)}) %collective-permute-start.11) | collective-permute-done | bytes 131104 | tf_op jit(solution)/shard_map/ppermute | solution.py:141
  60.8 4.6 %collective-permute-done.13.p2 = bf16[2,2,16,8,128]{4,3,2,1,0:T(8,128)(2,1)S(1)} collective-permute-done((bf16[2,2,16,8,128]{4,3,2,1,0:T(8,128)(2,1)S(1)}, bf16[2,2,16,8,128]{4,3,2,1,0:T(8,128)(2,1)S(1)}, u32[]{:S(2)}, u32[]{:S(2)}) %collective-permute-start.13) | collective-permute-done | bytes 131104 | tf_op jit(solution)/shard_map/ppermute | solution.py:440
  65.5 5.7 %collective-permute-start.15 = (bf16[2,12,2,8,128]{4,3,2,1,0:T(8,128)(2,1)S(1)}, bf16[2,12,2,8,128]{4,3,2,1,0:T(8,128)(2,1)S(1)}, u32[]{:S(2)}, u32[]{:S(2)}) collective-permute-start(bf16[2,12,2,8,128]{4,3,2,1,0:T(8,128)(2,1)S(1)} %pad_maximum_fusion.2), channel_id=1, source_target_pairs={{2,0},{4,2},{6,4},{8,6},{10,8},{12,10},{14,12},{3,1},{5,3},{7,5},{... | collective-permute-start | bytes 294920 | tf_op jit(solution)/shard_map/ppermute | solution.py:445
  71.2 3.4 %collective-permute-start.14 = (bf16[2,12,2,8,128]{4,3,2,1,0:T(8,128)(2,1)S(1)}, bf16[2,12,2,8,128]{4,3,2,1,0:T(8,128)(2,1)S(1)}, u32[]{:S(2)}, u32[]{:S(2)}) collective-permute-start(bf16[2,12,2,8,128]{4,3,2,1,0:T(8,128)(2,1)S(1)} %pad_maximum_fusion.1), channel_id=1, source_target_pairs={{0,2},{2,4},{4,6},{6,8},{8,10},{10,12},{12,14},{1,3},{3,5},{5,7},{... | collective-permute-start | bytes 294920 | tf_op jit(solution)/shard_map/ppermute | solution.py:444
  79.0 5.8 %collective-permute-done.16.p5 = bf16[2,12,20,2,128]{4,3,2,1,0:T(2,128)(2,1)S(1)} collective-permute-done((bf16[2,12,20,2,128]{4,3,2,1,0:T(2,128)(2,1)S(1)}, bf16[2,12,20,2,128]{4,3,2,1,0:T(2,128)(2,1)S(1)}, u32[]{:S(2)}, u32[]{:S(2)}) %collective-permute-start.16) | collective-permute-done | bytes 245792 | tf_op jit(solution)/shard_map/ppermute | solution.py:453
  84.7 22.7 %shard_map.115 = (bf16[10,18,16,128]{3,2,1,0:T(8,128)(2,1)S(1)}, bf16[10,18,16,384]{3,2,1,0:T(8,128)(2,1)S(1)}, bf16[27,128,128]{2,1,0:T(8,128)(2,1)S(1)}, bf16[27,128,128]{2,1,0:T(8,128)(2,1)}) custom-call(s32[4]{0:T(128)S(1)} %pad_add_fusion.where_ref, f32[1,128]{1,0:T(1,128)S(1)} %bitcast.68, bf16[2,8,16,8,128]{4,3,2,1,0:T(8,128)(2,1)S(1)} %get-tuple-element.47.p0.both, ...), custom_call_target="tpu_custom_call" | custom-call | flops 10737418240 | bytes 8388608 | tf_op jit(solution)/shard_map/pallas_call | solution.py:351
  116.1 2.4 %add_convert_fusion = bf16[27,128,128]{2,1,0:T(8,128)(2,1)} fusion(bf16[27,128,128]{2,1,0:T(8,128)(2,1)} %collective-permute-done.17, bf16[27,128,128]{2,1,0:T(8,128)(2,1)S(1)} %get-tuple-element.54), kind=kLoop, calls=%fused_computation.16 | loop fusion | flops 1769472 | bytes 2654208 | tf_op jit(solution)/shard_map/convert_element_type | solution.py:478
  118.5 4.3 %all-to-all-start = ((bf16[16,216,128]{2,1,0:T(8,128)(2,1)}), bf16[16,216,128]{2,1,0:T(8,128)(2,1)}, u32[]{:S(2)}, u32[]{:S(2)}) async-start(bf16[16,216,128]{2,1,0:T(8,128)(2,1)} %bitcast.74), calls=%async_computation | async-start | bytes 1769472 | tf_op jit(solution)/shard_map/all_to_all | solution.py:458
  128.2 7.5 %shard_map.116 = (bf16[8,16,8,128]{3,2,1,0:T(8,128)(2,1)}, bf16[8,16,8,128]{3,2,1,0:T(8,128)(2,1)}, f32[8,128]{1,0:T(8,128)S(1)}) custom-call(f32[1,128]{1,0:T(1,128)S(1)} %bitcast.69, bf16[2,8,16,8,128]{4,3,2,1,0:T(8,128)(2,1)S(1)} %copy-done.4, bf16[10,18,16,128]{3,2,1,0:T(8,128)(2,1)S(1)} %copy-done.12, bf16[10,18,16,384]{3,2,1,0:T(8,128)(2,1)S(1)} %copy-done.10, ...), custom_call_target="tpu_custom_call" | custom-call | flops 8589934592 | bytes 6291456 | tf_op jit(solution)/shard_map/pallas_call | solution.py:416
  137.5 12.1 %all_to_all.15 = bf16[4,224,128]{2,1,0:T(8,128)(2,1)S(1)} all-to-all(bf16[4,224,128]{2,1,0:T(8,128)(2,1)S(1)} %broadcast_in_dim.4), channel_id=1, replica_groups=mesh['y'=4,'xl'=2,'z'=4,'c'=2,'xh'=2] {'z'}, dimensions={0} | all-to-all | bytes 458752 | tf_op jit(solution)/shard_map/all_to_all | solution.py:458
  150.0 17.9 %all_to_all.16 = bf16[16,224,128]{2,1,0:T(8,128)(2,1)S(1)} all-to-all(bf16[16,224,128]{2,1,0:T(8,128)(2,1)S(1)} %broadcast_in_dim.5), channel_id=1, replica_groups=mesh['y'=4,'xl'=2,'z'=4,'c'=2,'xh'=2] {'y','xl','xh'}, dimensions={0} | all-to-all | bytes 1835008 | tf_op jit(solution)/shard_map/all_to_all | solution.py:458
  167.9 3.9 %collective-permute-start.18 = (bf16[16,224,128]{2,1,0:T(8,128)(2,1)S(1)}, bf16[16,224,128]{2,1,0:T(8,128)(2,1)S(1)}, u32[]{:S(2)}, u32[]{:S(2)}) collective-permute-start(bf16[16,224,128]{2,1,0:T(8,128)(2,1)S(1)} %all_to_all.16), channel_id=1, source_target_pairs={{0,2},{2,0},{1,3},{3,1},{4,6},{6,4},{5,7},{7,5},{8,10},{10,8},{9,1... | collective-permute-start | bytes 2752520 | tf_op jit(solution)/shard_map/ppermute | solution.py:497
  174.5 2.1 %convert_multiply_fusion = (f32[16,216,128]{2,1,0:T(8,128)}, f32[16,216,128]{2,1,0:T(8,128)}) fusion(pred[]{:T(512)S(6)} %eq.8, bf16[16,224,128]{2,1,0:T(8,128)(2,1)S(1)} %collective-permute-done.18, bf16[16,224,128]{2,1,0:T(8,128)(2,1)S(1)} %all_to_all.16), kind=kLoop, calls=%fused_computation.14 | loop fusion | flops 2654208 | bytes 5308417 | tf_op jit(solution)/shard_map/mul | solution.py:502
  (99 shorter events, 46.1 us)
Async XLA Ops:
  5.5 14.6 %collective-permute-start = (bf16[4,32,16,128]{3,2,1,0:T(8,128)(2,1)S(1)}, bf16[4,32,16,128]{3,2,1,0:T(8,128)(2,1)S(1)}, u32[]{:S(2)}, u32[]{:S(2)}) collective-permute-start(bf16[4,32,16,128]{3,2,1,0:T(8,128)(2,1)S(1)} %get-tuple-element.32), channel_id=1, source_target_pairs={{0,16},{16,1},{1,17},{17,0},{2,18},{18,3},{3,19},{19,2},{4,20},{20... | collective-permute-start | bytes 1572872 | tf_op jit(solution)/shard_map/ppermute | solution.py:141
  7.6 25.0 %collective-permute-start.1 = (bf16[4,32,16,128]{3,2,1,0:T(8,128)(2,1)S(1)}, bf16[4,32,16,128]{3,2,1,0:T(8,128)(2,1)S(1)}, u32[]{:S(2)}, u32[]{:S(2)}) collective-permute-start(bf16[4,32,16,128]{3,2,1,0:T(8,128)(2,1)S(1)} %get-tuple-element.33), channel_id=1, source_target_pairs={{0,1},{16,17},{1,0},{17,16},{2,3},{18,19},{3,2},{19,18},{4,5},{20,... | collective-permute-start | bytes 1572872 | tf_op jit(solution)/shard_map/ppermute | solution.py:141
  10.1 22.6 %collective-permute-start.2 = (bf16[4,32,16,128]{3,2,1,0:T(8,128)(2,1)S(1)}, bf16[4,32,16,128]{3,2,1,0:T(8,128)(2,1)S(1)}, u32[]{:S(2)}, u32[]{:S(2)}) collective-permute-start(bf16[4,32,16,128]{3,2,1,0:T(8,128)(2,1)S(1)} %get-tuple-element.34), channel_id=1, source_target_pairs={{0,17},{16,0},{1,16},{17,1},{2,19},{18,2},{3,18},{19,3},{4,21},{20... | collective-permute-start | bytes 1572872 | tf_op jit(solution)/shard_map/ppermute | solution.py:141
  13.9 29.2 %collective-permute-start.6 = (bf16[4,32,16,128]{3,2,1,0:T(8,128)(2,1)S(1)}, bf16[4,32,16,128]{3,2,1,0:T(8,128)(2,1)S(1)}, u32[]{:S(2)}, u32[]{:S(2)}) collective-permute-start(bf16[4,32,16,128]{3,2,1,0:T(8,128)(2,1)S(1)} %get-tuple-element.40), channel_id=1, source_target_pairs={{0,32},{32,64},{64,96},{96,0},{1,33},{33,65},{65,97},{97,1},{2,34}... | collective-permute-start | bytes 1572872 | tf_op jit(solution)/shard_map/ppermute | solution.py:145
  15.2 29.0 %collective-permute-start.7 = (bf16[4,32,16,128]{3,2,1,0:T(8,128)(2,1)}, bf16[4,32,16,128]{3,2,1,0:T(8,128)(2,1)S(1)}, u32[]{:S(2)}, u32[]{:S(2)}) collective-permute-start(bf16[4,32,16,128]{3,2,1,0:T(8,128)(2,1)} %get-tuple-element.41), channel_id=1, source_target_pairs={{0,64},{32,96},{64,0},{96,32},{1,65},{33,97},{65,1},{97,33},{2,66}... | collective-permute-start | bytes 1572872 | tf_op jit(solution)/shard_map/ppermute | solution.py:145
  20.1 24.1 %collective-permute-start.8 = (bf16[4,32,16,128]{3,2,1,0:T(8,128)(2,1)S(1)}, bf16[4,32,16,128]{3,2,1,0:T(8,128)(2,1)S(1)}, u32[]{:S(2)}, u32[]{:S(2)}) collective-permute-start(bf16[4,32,16,128]{3,2,1,0:T(8,128)(2,1)S(1)} %get-tuple-element.42), channel_id=1, source_target_pairs={{0,96},{32,0},{64,32},{96,64},{1,97},{33,1},{65,33},{97,65},{2,98}... | collective-permute-start | bytes 1572872 | tf_op jit(solution)/shard_map/ppermute | solution.py:145
  34.8 14.8 %collective-permute-start.3 = (bf16[32,16,128]{2,1,0:T(8,128)(2,1)}, bf16[32,16,128]{2,1,0:T(8,128)(2,1)S(1)}, u32[]{:S(2)}, u32[]{:S(2)}) collective-permute-start(bf16[32,16,128]{2,1,0:T(8,128)(2,1)} %get-tuple-element.36), channel_id=1, source_target_pairs={{0,32},{32,64},{64,96},{96,0},{1,33},{33,65},{65,97},{97,1},{2,34}... | collective-permute-start | bytes 393224 | tf_op jit(solution)/shard_map/ppermute | solution.py:145
  40.5 9.5 %collective-permute-start.4 = (bf16[32,16,128]{2,1,0:T(8,128)(2,1)}, bf16[32,16,128]{2,1,0:T(8,128)(2,1)S(1)}, u32[]{:S(2)}, u32[]{:S(2)}) collective-permute-start(bf16[32,16,128]{2,1,0:T(8,128)(2,1)} %copy-done.7), channel_id=1, source_target_pairs={{0,64},{32,96},{64,0},{96,32},{1,65},{33,97},{65,1},{97,33},{2,66}... | collective-permute-start | bytes 393224 | tf_op jit(solution)/shard_map/ppermute | solution.py:145
  43.1 6.9 %collective-permute-start.5 = (bf16[32,16,128]{2,1,0:T(8,128)(2,1)}, bf16[32,16,128]{2,1,0:T(8,128)(2,1)S(1)}, u32[]{:S(2)}, u32[]{:S(2)}) collective-permute-start(bf16[32,16,128]{2,1,0:T(8,128)(2,1)} %copy-done.6), channel_id=1, source_target_pairs={{0,96},{32,0},{64,32},{96,64},{1,97},{33,1},{65,33},{97,65},{2,98}... | collective-permute-start | bytes 393224 | tf_op jit(solution)/shard_map/ppermute | solution.py:145
  44.2 11.8 %copy-start.5 = (bf16[8,16,8,128]{3,2,1,0:T(8,128)(2,1)S(1)}, bf16[8,16,8,128]{3,2,1,0:T(8,128)(2,1)}, u32[]{:S(2)}) copy-start(bf16[8,16,8,128]{3,2,1,0:T(8,128)(2,1)} %cot_ref.1) | copy-start | bytes 786436
  45.9 5.5 %collective-permute-start.10 = (bf16[32,16,128]{2,1,0:T(8,128)(2,1)}, bf16[32,16,128]{2,1,0:T(8,128)(2,1)S(1)}, u32[]{:S(2)}, u32[]{:S(2)}) collective-permute-start(bf16[32,16,128]{2,1,0:T(8,128)(2,1)} %get-tuple-element.45), channel_id=1, source_target_pairs={{0,1},{16,17},{1,0},{17,16},{2,3},{18,19},{3,2},{19,18},{4,5},{20,... | collective-permute-start | bytes 393224 | tf_op jit(solution)/shard_map/ppermute | solution.py:141
  48.0 6.7 %collective-permute-start.11 = (bf16[32,16,128]{2,1,0:T(8,128)(2,1)}, bf16[32,16,128]{2,1,0:T(8,128)(2,1)S(1)}, u32[]{:S(2)}, u32[]{:S(2)}) collective-permute-start(bf16[32,16,128]{2,1,0:T(8,128)(2,1)} %get-tuple-element.46), channel_id=1, source_target_pairs={{0,17},{16,0},{1,16},{17,1},{2,19},{18,2},{3,18},{19,3},{4,21},{20... | collective-permute-start | bytes 393224 | tf_op jit(solution)/shard_map/ppermute | solution.py:141
  49.7 6.4 %collective-permute-start.9 = (bf16[32,16,128]{2,1,0:T(8,128)(2,1)}, bf16[32,16,128]{2,1,0:T(8,128)(2,1)}, u32[]{:S(2)}, u32[]{:S(2)}) collective-permute-start(bf16[32,16,128]{2,1,0:T(8,128)(2,1)} %get-tuple-element.44), channel_id=1, source_target_pairs={{0,16},{16,1},{1,17},{17,0},{2,18},{18,3},{3,19},{19,2},{4,20},{20... | collective-permute-start | bytes 393224 | tf_op jit(solution)/shard_map/ppermute | solution.py:141
  49.9 28.8 %copy-start.13 = (bf16[27,128,128]{2,1,0:T(8,128)(2,1)S(1)}, bf16[27,128,128]{2,1,0:T(8,128)(2,1)}, u32[]{:S(2)}) copy-start(bf16[27,128,128]{2,1,0:T(8,128)(2,1)} %param.10) | copy-start | bytes 2654212
  57.6 27.1 %copy-start.3 = (bf16[2,8,16,8,128]{4,3,2,1,0:T(8,128)(2,1)}, bf16[2,8,16,8,128]{4,3,2,1,0:T(8,128)(2,1)S(1)}, u32[]{:S(2)}) copy-start(bf16[2,8,16,8,128]{4,3,2,1,0:T(8,128)(2,1)S(1)} %get-tuple-element.47.p0.both) | copy-start | bytes 1572868
  57.6 3.2 %collective-permute-start.12 = (bf16[2,2,16,8,128]{4,3,2,1,0:T(8,128)(2,1)S(1)}, bf16[2,2,16,8,128]{4,3,2,1,0:T(8,128)(2,1)S(1)}, u32[]{:S(2)}, u32[]{:S(2)}) collective-permute-start(bf16[2,2,16,8,128]{4,3,2,1,0:T(8,128)(2,1)S(1)} %get-tuple-element.48), channel_id=1, source_target_pairs={{0,16},{16,32},{32,48},{48,64},{64,80},{80,96},{96,112},{1,17},{17... | collective-permute-start | bytes 393224 | tf_op jit(solution)/shard_map/ppermute | solution.py:439
  58.9 6.6 %collective-permute-start.13 = (bf16[2,2,16,8,128]{4,3,2,1,0:T(8,128)(2,1)S(1)}, bf16[2,2,16,8,128]{4,3,2,1,0:T(8,128)(2,1)S(1)}, u32[]{:S(2)}, u32[]{:S(2)}) collective-permute-start(bf16[2,2,16,8,128]{4,3,2,1,0:T(8,128)(2,1)S(1)} %get-tuple-element.49), channel_id=1, source_target_pairs={{16,0},{32,16},{48,32},{64,48},{80,64},{96,80},{112,96},{17,1},{33... | collective-permute-start | bytes 393224 | tf_op jit(solution)/shard_map/ppermute | solution.py:440
  60.5 24.3 %copy-start.8 = (f32[128]{0:T(128)S(1)}, f32[128]{0:T(128)}, u32[]{:S(2)}) copy-start(f32[128]{0:T(128)} %param.12) | copy-start | bytes 1540
  65.5 9.5 %collective-permute-start.15 = (bf16[2,12,2,8,128]{4,3,2,1,0:T(8,128)(2,1)S(1)}, bf16[2,12,2,8,128]{4,3,2,1,0:T(8,128)(2,1)S(1)}, u32[]{:S(2)}, u32[]{:S(2)}) collective-permute-start(bf16[2,12,2,8,128]{4,3,2,1,0:T(8,128)(2,1)S(1)} %pad_maximum_fusion.2), channel_id=1, source_target_pairs={{2,0},{4,2},{6,4},{8,6},{10,8},{12,10},{14,12},{3,1},{5,3},{7,5},{... | collective-permute-start | bytes 294920 | tf_op jit(solution)/shard_map/ppermute | solution.py:445
  71.2 5.1 %collective-permute-start.14 = (bf16[2,12,2,8,128]{4,3,2,1,0:T(8,128)(2,1)S(1)}, bf16[2,12,2,8,128]{4,3,2,1,0:T(8,128)(2,1)S(1)}, u32[]{:S(2)}, u32[]{:S(2)}) collective-permute-start(bf16[2,12,2,8,128]{4,3,2,1,0:T(8,128)(2,1)S(1)} %pad_maximum_fusion.1), channel_id=1, source_target_pairs={{0,2},{2,4},{4,6},{6,8},{8,10},{10,12},{12,14},{1,3},{3,5},{5,7},{... | collective-permute-start | bytes 294920 | tf_op jit(solution)/shard_map/ppermute | solution.py:444
  76.7 8.0 %collective-permute-start.16 = (bf16[2,12,20,2,128]{4,3,2,1,0:T(2,128)(2,1)S(1)}, bf16[2,12,20,2,128]{4,3,2,1,0:T(2,128)(2,1)S(1)}, u32[]{:S(2)}, u32[]{:S(2)}) collective-permute-start(bf16[2,12,20,2,128]{4,3,2,1,0:T(2,128)(2,1)S(1)} %pad_maximum_fusion), channel_id=1, source_target_pairs={{0,1},{1,0},{2,3},{3,2},{4,5},{5,4},{6,7},{7,6},{8,9},{9,8},{10,11... | collective-permute-start | bytes 737288 | tf_op jit(solution)/shard_map/ppermute | solution.py:453
  109.7 6.4 %collective-permute-start.17 = (bf16[27,128,128]{2,1,0:T(8,128)(2,1)}, bf16[27,128,128]{2,1,0:T(8,128)(2,1)}, u32[]{:S(2)}, u32[]{:S(2)}) collective-permute-start(bf16[27,128,128]{2,1,0:T(8,128)(2,1)} %get-tuple-element.55), channel_id=1, source_target_pairs={{0,2},{2,0},{1,3},{3,1},{4,6},{6,4},{5,7},{7,5},{8,10},{10,8},{9,1... | collective-permute-start | bytes 2654216 | tf_op jit(solution)/shard_map/ppermute | solution.py:477
  118.5 17.6 %all-to-all-start = ((bf16[16,216,128]{2,1,0:T(8,128)(2,1)}), bf16[16,216,128]{2,1,0:T(8,128)(2,1)}, u32[]{:S(2)}, u32[]{:S(2)}) async-start(bf16[16,216,128]{2,1,0:T(8,128)(2,1)} %bitcast.74), calls=%async_computation | async-start | bytes 1769472 | tf_op jit(solution)/shard_map/all_to_all | solution.py:458
  167.9 6.0 %collective-permute-start.18 = (bf16[16,224,128]{2,1,0:T(8,128)(2,1)S(1)}, bf16[16,224,128]{2,1,0:T(8,128)(2,1)S(1)}, u32[]{:S(2)}, u32[]{:S(2)}) collective-permute-start(bf16[16,224,128]{2,1,0:T(8,128)(2,1)S(1)} %all_to_all.16), channel_id=1, source_target_pairs={{0,2},{2,0},{1,3},{3,1},{4,6},{6,4},{5,7},{7,5},{8,10},{10,8},{9,1... | collective-permute-start | bytes 2752520 | tf_op jit(solution)/shard_map/ppermute | solution.py:497
  (12 other events, 34.2 us)

commit v4 on v3

--- a/solution.py
+++ b/solution.py
@@ -1,3 +1,4 @@
+import functools
 import math
 
 import jax
@@ -20,18 +21,34 @@
 BF16 = jnp.bfloat16
 VM = pl.BlockSpec(memory_space=pltpu.VMEM)
 SM = pl.BlockSpec(memory_space=pltpu.SMEM)
-
-
-def place_kernel(code_ref, rows_ref, o0, o1, o2, o3, flat, place, lift):
-    @pl.when(pl.program_id(0) == 0)
+AN = pl.BlockSpec(memory_space=pl.ANY)
+HB = pl.BlockSpec(memory_space=pltpu.HBM)
+
+
+def place_kernel(half, code_ref, rows_hbm, o0, o1, o2, o3, fetched, flat, place, lift, sems):
+    step = pl.program_id(0)
+
+    def copy(n):
+        voxels = rows_hbm.at[:, pl.ds(half * 32 + n * 8, 8), :]
+        return pltpu.make_async_copy(voxels, fetched.at[n], sems.at[n])
+
+    @pl.when(step == 0)
     def _():
+        for n in range(4):
+            copy(n).start()
         slots = lax.broadcasted_iota(jnp.int32, (256, 128), 0)
-        chosen = jnp.where(slots == code_ref[...], 1.0, 0.0)
+        chosen = jnp.where(slots == code_ref[half : half + 1, :], 1.0, 0.0)
         place[...] = chosen.astype(BF16)
         named = jnp.max(chosen, axis=1, keepdims=True)
         lift[...] = jnp.broadcast_to(jnp.where(named > 0.0, 0.0, DEAD), (256, 128))
 
-    flat[...] = rows_ref[...].astype(F32).reshape(1024, 128)
+    for n in range(4):
+
+        @pl.when(step == n)
+        def _():
+            copy(n).wait()
+            flat[...] = fetched[n].astype(F32).reshape(1024, 128)
+
     for voxel in range(8):
         values = flat[pl.ds(voxel, 128, stride=8), :].astype(BF16)
         summed = jnp.dot(place[...], values, preferred_element_type=F32) + lift[...]
@@ -42,18 +59,20 @@
 
 def place_bricks(code, rows, half):
     return pl.pallas_call(
-        place_kernel,
+        functools.partial(place_kernel, half),
         out_shape=(jax.ShapeDtypeStruct((4, 32, 16, 128), BF16),) * 4,
         grid=(4,),
         in_specs=[
-            pl.BlockSpec((1, 128), lambda i: (0, 0)),
-            pl.BlockSpec((128, 8, 128), lambda i: (0, i + 4 * half, 0)),
+            pl.BlockSpec((2, 128), lambda i: (0, 0)),
+            HB,
         ],
         out_specs=(pl.BlockSpec((4, 8, 16, 128), lambda i: (0, i, 0, 0)),) * 4,
         scratch_shapes=[
+            pltpu.VMEM((4, 128, 8, 128), BF16),
             pltpu.VMEM((1024, 128), F32),
             pltpu.VMEM((256, 128), BF16),
             pltpu.VMEM((256, 128), F32),
+            pltpu.SemaphoreType.DMA((4,)),
         ],
         compiler_params=pltpu.CompilerParams(vmem_limit_bytes=10 << 20),
         cost_estimate=pl.CostEstimate(flops=1 << 28, bytes_accessed=3 << 20, transcendentals=0),
@@ -89,7 +108,17 @@
 
 
 def sum_bricks_kernel(
-    a0, a1, a2, a3, b0, b1, b2, b3, cot_ref, both_ref, low_ref, high_ref, sums, cells
+    where_ref,
+    a0, a1, a2, a3, b0, b1, b2, b3,
+    cot_ref,
+    both_ref,
+    low_ref,
+    high_ref,
+    layer_ref,
+    layer_low_ref,
+    layer_high_ref,
+    sums,
+    cells,
 ):
     both_ref[1] = cot_ref[...]
     for half, parts in enumerate(((a0, a1, a2, a3), (b0, b1, b2, b3))):
@@ -114,22 +143,34 @@
         lax.fori_loop(0, 4, block, 0)
     low_ref[...] = both_ref[:, 0:2]
     high_ref[...] = both_ref[:, 6:8]
-
-
-def sum_bricks(parts, out_grad):
+    for side, rows in ((0, slice(6, 8)), (1, slice(0, 2))):
+
+        @pl.when(where_ref[0] == side)
+        def _():
+            for n in range(2):
+                layer_ref[n] = both_ref[n].astype(F32)[:, :, rows, :].astype(BF16)
+
+    layer_low_ref[...] = layer_ref[:, 0:2]
+    layer_high_ref[...] = layer_ref[:, 6:8]
+
+
+def sum_bricks(where, parts, out_grad):
     return pl.pallas_call(
         sum_bricks_kernel,
         out_shape=(
             jax.ShapeDtypeStruct((2, 8, 16, 8, 128), BF16),
             jax.ShapeDtypeStruct((2, 2, 16, 8, 128), BF16),
             jax.ShapeDtypeStruct((2, 2, 16, 8, 128), BF16),
+            jax.ShapeDtypeStruct((2, 8, 16, 2, 128), BF16),
+            jax.ShapeDtypeStruct((2, 2, 16, 2, 128), BF16),
+            jax.ShapeDtypeStruct((2, 2, 16, 2, 128), BF16),
         ),
-        in_specs=[VM] * 9,
-        out_specs=(VM,) * 3,
+        in_specs=[SM] + [VM] * 9,
+        out_specs=(VM,) * 6,
         scratch_shapes=[pltpu.VMEM((128, 128), F32), pltpu.VMEM((16, 8, 128), F32)],
         compiler_params=pltpu.CompilerParams(vmem_limit_bytes=8 << 20),
         cost_estimate=pl.CostEstimate(flops=8 << 20, bytes_accessed=2 << 20, transcendentals=0),
-    )(*parts, out_grad)
+    )(where, *parts, out_grad)
 
 
 def ring(axes, shift, place_of):
@@ -145,21 +186,23 @@
     return lax.ppermute(value, "y", ring(0, shift, lambda i: i))
 
 
-def regroup(rows, target_rank, target_slot, out_grad):
+def regroup(rows, target_rank, target_slot, out_grad, where, weights):
     to_x = target_rank % 2 * 2 + target_rank // 2 % 2
     shift_x = (to_x - (lax.axis_index("xh") * 2 + lax.axis_index("xl"))) & 3
     shift_y = (target_rank // 4 - lax.axis_index("y")) & 3
-    code_a = (shift_x * 4 + shift_y) * 16 + target_slot
-    code_b = (shift_y * 4 + shift_x) * 16 + target_slot
-    placed_a = place_bricks(code_a, rows, 0)
-    placed_b = place_bricks(code_b, rows, 1)
+    major = jnp.concatenate([shift_x, shift_y], axis=0)
+    minor = jnp.concatenate([shift_y, shift_x], axis=0)
+    codes = (major * 4 + minor) * 16 + target_slot
+    placed_a = place_bricks(codes, rows, 0)
+    placed_b = place_bricks(codes, rows, 1)
     came_a = [placed_a[0]] + [along_x(placed_a[n], n) for n in (1, 2, 3)]
     came_b = [placed_b[0]] + [along_y(placed_b[n], n) for n in (1, 2, 3)]
+    came_a, weights = lax.optimization_barrier((came_a, weights))
     merged_a = merge_bricks(came_a)
     merged_b = merge_bricks(came_b)
     came_a = [merged_a[0]] + [along_y(merged_a[n], n) for n in (1, 2, 3)]
     came_b = [merged_b[0]] + [along_x(merged_b[n], n) for n in (1, 2, 3)]
-    return sum_bricks(came_a + came_b, out_grad)
+    return sum_bricks(where, came_a + came_b, out_grad), weights
 
 
 def window_rows(ref, x, y, slabs, rows):
@@ -198,28 +241,33 @@
     (2, 8, 16, 8, 128),
     (2, 2, 16, 8, 128),
     (2, 2, 16, 8, 128),
-    (2, 12, 2, 8, 128),
-    (2, 12, 2, 8, 128),
-    (2, 12, 20, 2, 128),
+    (2, 8, 16, 2, 128),
+    (2, 2, 16, 2, 128),
+    (2, 2, 16, 2, 128),
+    (2, 12, 2, 10, 128),
+    (2, 12, 2, 10, 128),
 )
 
 
 def fill(volume, which, pieces, where_ref, outside):
-    centre, x_low, x_high, y_low, y_high, z_side = pieces
+    centre, x_low, x_high, layer, layer_low, layer_high, y_low, y_high = pieces
     volume[...] = jnp.full(volume.shape, outside, F32)
     volume[2:10, 2:18, 2:10, :] = centre[which].astype(F32)
     volume[0:2, 2:18, 2:10, :] = x_low[which].astype(F32)
     volume[10:12, 2:18, 2:10, :] = x_high[which].astype(F32)
-    volume[:, 0:2, 2:10, :] = y_low[which].astype(F32)
-    volume[:, 18:20, 2:10, :] = y_high[which].astype(F32)
-
-    @pl.when(where_ref[0] == 0)
-    def _():
-        volume[:, :, 10:12, :] = z_side[which].astype(F32)
-
-    @pl.when(where_ref[0] == 1)
-    def _():
-        volume[:, :, 0:2, :] = z_side[which].astype(F32)
+    low = y_low[which].astype(F32)
+    high = y_high[which].astype(F32)
+    volume[:, 0:2, 2:10, :] = low[:, :, 0:8]
+    volume[:, 18:20, 2:10, :] = high[:, :, 0:8]
+    for side, rows in ((0, slice(10, 12)), (1, slice(0, 2))):
+
+        @pl.when(where_ref[0] == side)
+        def _():
+            volume[2:10, 2:18, rows, :] = layer[which].astype(F32)
+            volume[0:2, 2:18, rows, :] = layer_low[which].astype(F32)
+            volume[10:12, 2:18, rows, :] = layer_high[which].astype(F32)
+            volume[:, 0:2, rows, :] = low[:, :, 8:10]
+            volume[:, 18:20, rows, :] = high[:, :, 8:10]
 
     @pl.when(where_ref[2] == 0)
     def _():
@@ -241,11 +289,11 @@
 def grads_kernel(
     where_ref,
     gain,
-    p0, p1, p2, p3, p4, p5,
+    p0, p1, p2, p3, p4, p5, p6, p7,
     first_hbm,
     second_hbm,
-    act_ref,
-    pre3_ref,
+    act_hbm,
+    pre_hbm,
     own_ref,
     send_ref,
     cells,
@@ -254,22 +302,25 @@
     masked3,
     act_t,
     normed_t,
-    s0, s1, s2, s3, s4, s5,
+    s0, s1, s2, s3, s4, s5, s6, s7,
     first,
     second_t,
+    act_ref,
+    pre_ref,
+    pre3_ref,
     sems,
 ):
     core = where_ref[1]
-    pieces = (s0, s1, s2, s3, s4, s5)
+    pieces = (s0, s1, s2, s3, s4, s5, s6, s7)
     copies = [
         pltpu.make_async_copy(source, target, sems.at[n])
         for n, (source, target) in enumerate(
-            zip((p0, p1, p2, p3, p4, p5, first_hbm, second_hbm), (*pieces, first, second_t))
+            zip((p0, p1, p2, p3, p4, p5, p6, p7, first_hbm, second_hbm), (*pieces, first, second_t))
         )
     ]
     for copy in copies:
         copy.start()
-    for copy in copies[:6]:
+    for copy in copies[:8]:
         copy.wait()
     fill(cells, 0, pieces, where_ref, OUT)
     fill(cots, 1, pieces, where_ref, 0.0)
@@ -300,7 +351,7 @@
         return carry
 
     lax.fori_loop(0, 8, turn, 0)
-    for copy in copies[6:]:
+    for copy in copies[8:]:
         copy.wait()
 
     def convolve(step, carry):
@@ -314,10 +365,17 @@
         active_grad = convolve_pair(masked3, x, 18, second_t)
         pre = active_grad * sigmoid * (1.0 + before * (1.0 - sigmoid))
         pre = jnp.where(values > -LIMIT, pre, 0.0)
+        pre_ref[pl.ds(x, 2)] = pre.astype(BF16).reshape(2, 18, 16, 128)
         pre3_ref[pl.ds(x, 2)] = neighbours(pre).reshape(2, 18, 16, 384)
         return carry
 
     lax.fori_loop(0, 5, convolve, 0)
+    results = [
+        pltpu.make_async_copy(source, target, sems.at[n])
+        for n, (source, target) in enumerate(((act_ref, act_hbm), (pre_ref, pre_hbm)))
+    ]
+    for copy in results:
+        copy.start()
 
     def turn_active(x, carry):
         active = act_ref[x + 1, 1:17].reshape(256, 128).astype(F32)
@@ -346,18 +404,21 @@
 
                 lax.fori_loop(0, 3, weights, 0)
 
+    for copy in results:
+        copy.wait()
+
 
 def grads_call(where, gain, pieces, first, second_t):
     return pl.pallas_call(
         grads_kernel,
         out_shape=(
             jax.ShapeDtypeStruct((10, 18, 16, 128), BF16),
-            jax.ShapeDtypeStruct((10, 18, 16, 384), BF16),
+            jax.ShapeDtypeStruct((10, 18, 16, 128), BF16),
             jax.ShapeDtypeStruct((27, 128, 128), BF16),
             jax.ShapeDtypeStruct((27, 128, 128), BF16),
         ),
-        in_specs=[SM, VM] + [pl.BlockSpec(memory_space=pl.ANY)] * 8,
-        out_specs=(VM,) * 4,
+        in_specs=[SM, VM] + [AN] * 8 + [HB] * 2,
+        out_specs=(HB, HB, VM, VM),
         scratch_shapes=[
             pltpu.VMEM((12, 20, 16, 128), F32),
             pltpu.VMEM((12, 20, 16, 128), F32),
@@ -368,7 +429,10 @@
             *[pltpu.VMEM(shape, BF16) for shape in PIECES],
             pltpu.VMEM((4608, 256), BF16),
             pltpu.VMEM((4608, 256), BF16),
-            pltpu.SemaphoreType.DMA((8,)),
+            pltpu.VMEM((10, 18, 16, 128), BF16),
+            pltpu.VMEM((10, 18, 16, 128), BF16),
+            pltpu.VMEM((10, 18, 16, 384), BF16),
+            pltpu.SemaphoreType.DMA((10,)),
         ],
         compiler_params=pltpu.CompilerParams(vmem_limit_bytes=34 << 20),
         cost_estimate=pl.CostEstimate(flops=10 << 30, bytes_accessed=8 << 20, transcendentals=1 << 20),
@@ -376,13 +440,51 @@
 
 
 def outputs_kernel(
-    gain, both, act, pre3, second, first_t, block_ref, grad_ref, gain_ref, act3, spread
+    gain,
+    both_hbm,
+    act_hbm,
+    pre_hbm,
+    second_hbm,
+    first_hbm,
+    block_ref,
+    grad_ref,
+    gain_ref,
+    both,
+    act,
+    pre,
+    second,
+    first_t,
+    act3,
+    pre3,
+    spread,
+    sems,
 ):
-    def prepare(x, carry):
-        act3[x] = neighbours(act[x].reshape(288, 128).astype(F32)).reshape(18, 16, 384)
-        return carry
-
-    lax.fori_loop(0, 10, prepare, 0)
+    copies = [
+        pltpu.make_async_copy(source, target, sems.at[n])
+        for n, (source, target) in enumerate(
+            (
+                (act_hbm, act),
+                (pre_hbm, pre),
+                (both_hbm, both),
+                (second_hbm, second),
+                (first_hbm, first_t),
+            )
+        )
+    ]
+    for copy in copies:
+        copy.start()
+    for copy, source, target in ((copies[0], act, act3), (copies[1], pre, pre3)):
+        copy.wait()
+
+        def prepare(x, carry):
+            values = source[x].reshape(288, 128).astype(F32)
+            target[x] = neighbours(values).reshape(18, 16, 384)
+            return carry
+
+        lax.fori_loop(0, 10, prepare, 0)
+
+    for copy in copies[2:]:
+        copy.wait()
     gains = gain[...]
 
     def convolve(step, total):
@@ -412,7 +514,7 @@
     gain_ref[...] = total
 
 
-def outputs_call(gain, both, act, pre3, second, first_t):
+def outputs_call(gain, both, act, pre, second, first_t):
     return pl.pallas_call(
         outputs_kernel,
         out_shape=(
@@ -420,38 +522,62 @@
             jax.ShapeDtypeStruct((8, 16, 8, 128), BF16),
             jax.ShapeDtypeStruct((8, 128), F32),
         ),
-        in_specs=[VM] * 6,
+        in_specs=[VM, AN, HB, HB, HB, HB],
         out_specs=(VM,) * 3,
         scratch_shapes=[
+            pltpu.VMEM((2, 8, 16, 8, 128), BF16),
+            pltpu.VMEM((10, 18, 16, 128), BF16),
+            pltpu.VMEM((10, 18, 16, 128), BF16),
+            pltpu.VMEM((4608, 256), BF16),
+            pltpu.VMEM((4608, 256), BF16),
+            pltpu.VMEM((10, 18, 16, 384), BF16),
             pltpu.VMEM((10, 18, 16, 384), BF16),
             pltpu.VMEM((2, 16, 16, 128), F32),
+            pltpu.SemaphoreType.DMA((5,)),
         ],
         compiler_params=pltpu.CompilerParams(vmem_limit_bytes=20 << 20),
         cost_estimate=pl.CostEstimate(flops=8 << 30, bytes_accessed=6 << 20, transcendentals=4096),
-    )(gain, both, act, pre3, second, first_t)
+    )(gain, both, act, pre, second, first_t)
+
+
+def add_kernel(own_ref, other_ref, out_ref):
+    out_ref[...] = (own_ref[...].astype(F32) + other_ref[...].astype(F32)).astype(BF16)
+
+
+def add_pair(own, other):
+    spec = pl.BlockSpec((9, 128, 128), lambda i: (i, 0, 0))
+    return pl.pallas_call(
+        add_kernel,
+        out_shape=jax.ShapeDtypeStruct((27, 128, 128), BF16),
+        grid=(3,),
+        in_specs=[spec, spec],
+        out_specs=spec,
+        compiler_params=pltpu.CompilerParams(vmem_limit_bytes=6 << 20),
+        cost_estimate=pl.CostEstimate(flops=1 << 19, bytes_accessed=3 << 20, transcendentals=0),
+    )(own, other)
 
 
 FORWARD = [(i, i + 1) for i in range(7)]
 BACKWARD = [(i + 1, i) for i in range(7)]
 
 
-def edges(both, send_low, send_high):
+def edges(both, send_low, send_high, layer, layer_low, layer_high):
+    far = [(a * 2 + s, b * 2 + 1 - s) for a, b in FORWARD for s in range(2)]
+    near = [(a * 2 + s, b * 2 + 1 - s) for a, b in BACKWARD for s in range(2)]
     x_low = lax.ppermute(send_high, GX, FORWARD)
     x_high = lax.ppermute(send_low, GX, BACKWARD)
-    parts = (x_low, both, x_high)
-    wide_low = jnp.concatenate([part[:, :, 14:16] for part in parts], axis=1)
-    wide_high = jnp.concatenate([part[:, :, 0:2] for part in parts], axis=1)
-    y_low = lax.ppermute(wide_low, GY, FORWARD)
-    y_high = lax.ppermute(wide_high, GY, BACKWARD)
-    side = lax.axis_index(SA)
-
-    def layer(part):
-        return jnp.where(side == 0, part[:, :, :, 6:8], part[:, :, :, 0:2])
-
-    middle = jnp.concatenate([layer(part) for part in parts], axis=1)
-    sent = jnp.concatenate([layer(y_low), middle, layer(y_high)], axis=2)
-    z_side = lax.ppermute(sent, SA, [(0, 1), (1, 0)])
-    return both, x_low, x_high, y_low, y_high, z_side
+    came = lax.ppermute(layer, SA, [(0, 1), (1, 0)])
+    came_low = lax.ppermute(layer_high, PLANE, far)
+    came_high = lax.ppermute(layer_low, PLANE, near)
+
+    def wide(rows):
+        inner = jnp.concatenate([part[:, :, rows] for part in (x_low, both, x_high)], axis=1)
+        outer = jnp.concatenate([part[:, :, rows] for part in (came_low, came, came_high)], axis=1)
+        return jnp.concatenate([inner, outer], axis=3)
+
+    y_low = lax.ppermute(wide(slice(14, 16)), GY, FORWARD)
+    y_high = lax.ppermute(wide(slice(0, 2)), GY, BACKWARD)
+    return both, x_low, x_high, came, came_low, came_high, y_low, y_high
 
 
 def exchange(values, axes):
@@ -459,41 +585,46 @@
 
 
 def local(sweep_bricks, target_rank, target_slot, conv_first, conv_second, norm_gain, out_grad):
-    both = regroup(
+    gain = norm_gain.reshape(1, 128)
+    core = lax.axis_index("c")
+    where = jnp.stack([lax.axis_index(SA), core, lax.axis_index(GX), lax.axis_index(GY)])
+    where = where.astype(jnp.int32)
+    both, (first, second, first_t, second_t) = regroup(
         sweep_bricks.reshape(128, 64, 128),
         target_rank.reshape(1, 128),
         target_slot.reshape(1, 128),
         out_grad,
+        where,
+        (
+            pair_weights(conv_first),
+            pair_weights(conv_second),
+            turned(conv_first),
+            turned(conv_second),
+        ),
     )
-    gain = norm_gain.reshape(1, 128)
-    first = pair_weights(conv_first)
-    second = pair_weights(conv_second)
-    first_t = turned(conv_first)
-    second_t = turned(conv_second)
     pieces = edges(*both)
-    core = lax.axis_index("c")
-    where = jnp.stack([lax.axis_index(SA), core, lax.axis_index(GX), lax.axis_index(GY)])
-    act, pre3, own, send = grads_call(where.astype(jnp.int32), gain, pieces, first, second_t)
+    act, pre, own, send = grads_call(where, gain, pieces, first, second_t)
     other = lax.ppermute(send, "c", [(0, 1), (1, 0)])
-    pair = (own.astype(F32) + other.astype(F32)).astype(BF16).reshape(16, 216, 128)
-    shares = exchange(pair, PLANE)
-    block_out, grid_grad, gain_part = outputs_call(gain, pieces[0], act, pre3, second, first_t)
+    shares = exchange(add_pair(own, other).reshape(16, 216, 128), PLANE)
+    block_out, grid_grad, gain_part = outputs_call(gain, pieces[0], act, pre, second, first_t)
 
     def halves(row):
         high = row.astype(BF16)
         low = (row - high.astype(F32)).astype(BF16)
         return [high, low, jnp.zeros((6, 128), BF16)]
 
-    def spread(total, row, count):
-        sent = jnp.concatenate([total.astype(BF16)] + halves(row), axis=0)
-        return jnp.broadcast_to(sent[None], (count, 224, 128))
+    def joined(total, row):
+        return jnp.concatenate([total.astype(BF16)] + halves(row), axis=0)
 
     total = jnp.sum(shares.astype(F32), axis=0)
-    row = jnp.sum(gain_part, axis=0, keepdims=True)
-    layers = exchange(spread(total, row, 4), "z").astype(F32)
-    total = jnp.sum(layers[:, :216], axis=0)
-    row = jnp.sum(layers[:, 216:218], axis=(0, 1))[None]
-    gathered = exchange(spread(total, row, 16), PLANE)
+    sent = joined(total, jnp.sum(gain_part, axis=0, keepdims=True))
+    parts = [sent] + [
+        lax.ppermute(sent, "z", [(i, (i + shift) % 4) for i in range(4)]) for shift in (1, 2, 3)
+    ]
+    parts = [part.astype(F32) for part in parts]
+    layers = (parts[0] + parts[2]) + (parts[1] + parts[3])
+    sent = joined(layers[:216], layers[216:217] + layers[217:218])
+    gathered = exchange(jnp.broadcast_to(sent[None], (16, 224, 128)), PLANE)
     swapped = lax.ppermute(gathered, "c", [(0, 1), (1, 0)])
     factor = 1.0 / math.sqrt(131072.0)
 

time: 177 us -> 176 us (level)
  starting transfers between devices: 43.4 us -> 57.7 us
  blocking collectives: 30 us -> 17.4 us
  waiting for transfers between devices: 32.4 us -> 20.7 us
  Pallas kernels: 39.5 us -> 47.2 us
    ppermute x3 -> x8, starting transfers between devices: 11.1 us -> 27.1 us  [the longest x1 8.87 us: edges(): y_high = lax.ppermute(wide(slice(0, 2)), GY, BACKWARD)]
    all_to_all x2 -> x1, blocking collectives: 30 us -> 17.4 us  [exchange(): return lax.all_to_all(values, axes, split_axis=0, concat_axis=0, tiled=True)]
    ppermute x6, waiting for transfers between devices: 17.8 us -> 6.22 us  [along_x(): lax.ppermute(value, ('xl', 'xh'), ring(0, shift, lambda i: i % 2 * 2 + i...]
    ppermute x1, waiting for transfers between devices: 4.63 us -> 0.01 us  [edges(): x_high = lax.ppermute(send_low, GX, BACKWARD)]
    pallas_call x2, Pallas kernels: 3.23 us -> 6.73 us  [merge_bricks(): pl.pallas_call(merge_kernel, out_shape=(jax.ShapeDtypeStruct((32, 16, 128...]
    concatenate x4, other arithmetic: 3.9 us -> 6.78 us  [pair_weights(): return jnp.concatenate([left, right], axis=3).reshape(4608, 256)]
    pallas_call x2 -> x3, Pallas kernels: 4.6 us -> 7.44 us  [the longest x2 5.88 us: place_bricks(): pl.pallas_call(functools.partial(place_kernel, half), out_shape=(jax.Shap...]
    convert_element_type x2 -> x0, other arithmetic: 2.41 us -> none  [the longest x1 2.38 us: local(): (own.astype(F32) + other.astype(F32)).astype(BF16).reshape(16, 216, 128)]
  transfers between devices with their start and end apart: 20 -> 25, of which waited for: 12 -> 10; matrix products, arithmetic and copies ran while one was open for 7% -> 8% of each run, Pallas kernels for 8% -> 10%
where the time goes in v4:
time: 176 us; the launch traced here: 175 us
  starting transfers between devices  57.7 us (33%)
  Pallas kernels  47.2 us (27%)
  waiting for transfers between devices  20.7 us (12%)
  local copies, waits for them, and re-layouts  18.4 us (10%)
  blocking collectives  17.4 us (10%)
  other arithmetic  12.6 us (7%)
    pallas_call x1, Pallas kernels, grads_call(): pl.pallas_call(grads_kernel, out_shape=(jax.ShapeDtypeStruct((10, 18, 16,...  22.6 us
    all_to_all x1, blocking collectives, exchange(): return lax.all_to_all(values, axes, split_axis=0, concat_axis=0, tiled=True)  17.4 us
    unnamed x48, local copies, waits for them, and re-layouts  15 us
    ppermute x6, starting transfers between devices, along_y(): return lax.ppermute(value, 'y', ring(0, shift, lambda i: i))  10 us
    ppermute x6, starting transfers between devices, along_x(): lax.ppermute(value, ('xl', 'xh'), ring(0, shift, lambda i: i % 2 * 2 + i...  9.47 us
    ppermute x1, starting transfers between devices, edges(): y_high = lax.ppermute(wide(slice(0, 2)), GY, BACKWARD)  8.87 us
    pallas_call x1, Pallas kernels, outputs_call(): pl.pallas_call(outputs_kernel, out_shape=(jax.ShapeDtypeStruct((8, 16, 8,...  8.59 us
    concatenate x4, other arithmetic, pair_weights(): return jnp.concatenate([left, right], axis=3).reshape(4608, 256)  6.78 us
  transfers between devices with their start and end apart: 25, of which 10 were waited for; matrix products, arithmetic and copies ran while one was open for 8% of the time, Pallas kernels for 10%

profile of v4, /device:TPU:1, one launch (start us, length us, event | category | flops | bytes accessed | tf_op | source)
XLA Modules:
  0.0 175.0 jit_solution(10352459275696844081)
XLA Ops:
  3.6 3.0 %shard_map.110 = (bf16[4,32,16,128]{3,2,1,0:T(8,128)(2,1)S(1)}, bf16[4,32,16,128]{3,2,1,0:T(8,128)(2,1)}, bf16[4,32,16,128]{3,2,1,0:T(8,128)(2,1)}, bf16[4,32,16,128]{3,2,1,0:T(8,128)(2,1)}) custom-call(s32[2,128]{1,0:T(2,128)S(1)} %fusion.14.code_ref, bf16[128,64,128]{2,1,0:T(8,128)(2,1)S(1)} %bitcast.51), custom_call_target="tpu_custom_call" | custom-call | flops 268435456 | bytes 3145728 | tf_op jit(solution)/shard_map/pallas_call | solution.py:61
  6.6 2.1 %collective-permute-start = (bf16[4,32,16,128]{3,2,1,0:T(8,128)(2,1)}, bf16[4,32,16,128]{3,2,1,0:T(8,128)(2,1)}, u32[]{:S(2)}, u32[]{:S(2)}) collective-permute-start(bf16[4,32,16,128]{3,2,1,0:T(8,128)(2,1)} %get-tuple-element.43), channel_id=1, source_target_pairs={{0,16},{16,1},{1,17},{17,0},{2,18},{18,3},{3,19},{19,2},{4,20},{20... | collective-permute-start | bytes 1572872 | tf_op jit(solution)/shard_map/ppermute | solution.py:182
  8.7 2.4 %collective-permute-start.1 = (bf16[4,32,16,128]{3,2,1,0:T(8,128)(2,1)}, bf16[4,32,16,128]{3,2,1,0:T(8,128)(2,1)}, u32[]{:S(2)}, u32[]{:S(2)}) collective-permute-start(bf16[4,32,16,128]{3,2,1,0:T(8,128)(2,1)} %get-tuple-element.44), channel_id=1, source_target_pairs={{0,1},{16,17},{1,0},{17,16},{2,3},{18,19},{3,2},{19,18},{4,5},{20,... | collective-permute-start | bytes 1572872 | tf_op jit(solution)/shard_map/ppermute | solution.py:182
  12.3 2.9 %shard_map.112 = (bf16[4,32,16,128]{3,2,1,0:T(8,128)(2,1)S(1)}, bf16[4,32,16,128]{3,2,1,0:T(8,128)(2,1)}, bf16[4,32,16,128]{3,2,1,0:T(8,128)(2,1)}, bf16[4,32,16,128]{3,2,1,0:T(8,128)(2,1)S(1)}) custom-call(s32[2,128]{1,0:T(2,128)S(1)} %fusion.14.code_ref, bf16[128,64,128]{2,1,0:T(8,128)(2,1)S(1)} %bitcast.52), custom_call_target="tpu_custom_call" | custom-call | flops 268435456 | bytes 3145728 | tf_op jit(solution)/shard_map/pallas_call | solution.py:61
  17.3 2.6 %collective-permute-start.7 = (bf16[4,32,16,128]{3,2,1,0:T(8,128)(2,1)}, bf16[4,32,16,128]{3,2,1,0:T(8,128)(2,1)}, u32[]{:S(2)}, u32[]{:S(2)}) collective-permute-start(bf16[4,32,16,128]{3,2,1,0:T(8,128)(2,1)} %get-tuple-element.56), channel_id=1, source_target_pairs={{0,64},{32,96},{64,0},{96,32},{1,65},{33,97},{65,1},{97,33},{2,66}... | collective-permute-start | bytes 1572872 | tf_op jit(solution)/shard_map/ppermute | solution.py:186
  21.6 2.2 %rev.6 = bf16[27,128,128]{1,2,0:T(8,128)(2,1)} reverse(bf16[27,128,128]{1,2,0:T(8,128)(2,1)} %copy.12), dimensions={0} | reverse | bytes 1769472 | tf_op jit(solution)/shard_map/rev | solution.py:231
  34.0 3.5 %shard_map.111 = (bf16[32,16,128]{2,1,0:T(8,128)(2,1)S(1)}, bf16[32,16,128]{2,1,0:T(8,128)(2,1)S(1)}, bf16[32,16,128]{2,1,0:T(8,128)(2,1)}, bf16[32,16,128]{2,1,0:T(8,128)(2,1)}) custom-call(bf16[4,32,16,128]{3,2,1,0:T(8,128)(2,1)S(1)} %copy-done.5, bf16[4,32,16,128]{3,2,1,0:T(8,128)(2,1)} %collective-permute-done.p1, ...), custom_call_target="tpu_custom_call" | custom-call | flops 4194304 | bytes 3145728 | tf_op jit(solution)/shard_map/pallas_call | solution.py:99
  38.8 2.6 %collective-permute-start.4 = (bf16[32,16,128]{2,1,0:T(8,128)(2,1)}, bf16[32,16,128]{2,1,0:T(8,128)(2,1)}, u32[]{:S(2)}, u32[]{:S(2)}) collective-permute-start(bf16[32,16,128]{2,1,0:T(8,128)(2,1)} %get-tuple-element.52), channel_id=1, source_target_pairs={{0,64},{32,96},{64,0},{96,32},{1,65},{33,97},{65,1},{97,33},{2,66}... | collective-permute-start | bytes 393224 | tf_op jit(solution)/shard_map/ppermute | solution.py:186
  42.5 3.3 %shard_map.113 = (bf16[32,16,128]{2,1,0:T(8,128)(2,1)S(1)}, bf16[32,16,128]{2,1,0:T(8,128)(2,1)}, bf16[32,16,128]{2,1,0:T(8,128)(2,1)}, bf16[32,16,128]{2,1,0:T(8,128)(2,1)}) custom-call(bf16[4,32,16,128]{3,2,1,0:T(8,128)(2,1)S(1)} %get-tuple-element.54.p0, bf16[4,32,16,128]{3,2,1,0:T(8,128)(2,1)S(1)} %collective-permute-done.6.p1, ...), custom_call_target="tpu_custom_call" | custom-call | flops 4194304 | bytes 3145728 | tf_op jit(solution)/shard_map/pallas_call | solution.py:99
  46.4 2.1 %collective-permute-start.10 = (bf16[32,16,128]{2,1,0:T(8,128)(2,1)}, bf16[32,16,128]{2,1,0:T(8,128)(2,1)S(1)}, u32[]{:S(2)}, u32[]{:S(2)}) collective-permute-start(bf16[32,16,128]{2,1,0:T(8,128)(2,1)} %get-tuple-element.60), channel_id=1, source_target_pairs={{0,1},{16,17},{1,0},{17,16},{2,3},{18,19},{3,2},{19,18},{4,5},{20,... | collective-permute-start | bytes 393224 | tf_op jit(solution)/shard_map/ppermute | solution.py:182
  51.9 3.3 %collective-permute-done.11.b3 = bf16[32,16,128]{2,1,0:T(8,128)(2,1)S(1)} collective-permute-done((bf16[32,16,128]{2,1,0:T(8,128)(2,1)}, bf16[32,16,128]{2,1,0:T(8,128)(2,1)S(1)}, u32[]{:S(2)}, u32[]{:S(2)}) %collective-permute-start.11) | collective-permute-done | bytes 131104 | tf_op jit(solution)/shard_map/ppermute | solution.py:182
  64.2 3.0 %collective-permute-start.14 = (bf16[2,8,16,2,128]{4,3,2,1,0:T(2,128)(2,1)S(1)}, bf16[2,8,16,2,128]{4,3,2,1,0:T(2,128)(2,1)S(1)}, u32[]{:S(2)}, u32[]{:S(2)}) collective-permute-start(bf16[2,8,16,2,128]{4,3,2,1,0:T(2,128)(2,1)S(1)} %get-tuple-element.65), channel_id=1, source_target_pairs={{0,1},{1,0},{2,3},{3,2},{4,5},{5,4},{6,7},{7,6},{8,9},{9,8},{10,11... | collective-permute-start | bytes 393224 | tf_op jit(solution)/shard_map/ppermute | solution.py:569
  67.2 3.9 %collective-permute-start.15 = (bf16[2,2,16,2,128]{4,3,2,1,0:T(2,128)(2,1)S(1)}, bf16[2,2,16,2,128]{4,3,2,1,0:T(2,128)(2,1)S(1)}, u32[]{:S(2)}, u32[]{:S(2)}) collective-permute-start(bf16[2,2,16,2,128]{4,3,2,1,0:T(2,128)(2,1)S(1)} %get-tuple-element.66), channel_id=1, source_target_pairs={{0,17},{1,16},{16,33},{17,32},{32,49},{33,48},{48,65},{49,64},{64,... | collective-permute-start | bytes 98312 | tf_op jit(solution)/shard_map/ppermute | solution.py:570
  72.4 4.5 %collective-permute-done.16.p5 = bf16[2,2,16,2,128]{4,3,2,1,0:T(2,128)(2,1)S(1)} collective-permute-done((bf16[2,2,16,2,128]{4,3,2,1,0:T(2,128)(2,1)S(1)}, bf16[2,2,16,2,128]{4,3,2,1,0:T(2,128)(2,1)S(1)}, u32[]{:S(2)}, u32[]{:S(2)}) %collective-permute-start.16) | collective-permute-done | bytes 32800 | tf_op jit(solution)/shard_map/ppermute | solution.py:571
  77.1 8.9 %collective-permute-start.18 = (bf16[2,12,2,10,128]{4,3,2,1,0:T(8,128)(2,1)S(1)}, bf16[2,12,2,10,128]{4,3,2,1,0:T(8,128)(2,1)S(1)}, u32[]{:S(2)}, u32[]{:S(2)}) collective-permute-start(bf16[2,12,2,10,128]{4,3,2,1,0:T(8,128)(2,1)S(1)} %maximum_maximum_fusion.1), channel_id=1, source_target_pairs={{2,0},{4,2},{6,4},{8,6},{10,8},{12,10},{14,12},{3,1},{5,3},{7,5},{... | collective-permute-start | bytes 368648 | tf_op jit(solution)/shard_map/ppermute | solution.py:579
  86.0 3.4 %collective-permute-start.17 = (bf16[2,12,2,10,128]{4,3,2,1,0:T(8,128)(2,1)S(1)}, bf16[2,12,2,10,128]{4,3,2,1,0:T(8,128)(2,1)S(1)}, u32[]{:S(2)}, u32[]{:S(2)}) collective-permute-start(bf16[2,12,2,10,128]{4,3,2,1,0:T(8,128)(2,1)S(1)} %maximum_maximum_fusion), channel_id=1, source_target_pairs={{0,2},{2,4},{4,6},{6,8},{8,10},{10,12},{12,14},{1,3},{3,5},{5,7},{... | collective-permute-start | bytes 368648 | tf_op jit(solution)/shard_map/ppermute | solution.py:578
  93.8 22.6 %shard_map.115 = (bf16[10,18,16,128]{3,2,1,0:T(8,128)(2,1)S(1)}, bf16[10,18,16,128]{3,2,1,0:T(8,128)(2,1)S(1)}, bf16[27,128,128]{2,1,0:T(8,128)(2,1)S(1)}, bf16[27,128,128]{2,1,0:T(8,128)(2,1)S(1)}) custom-call(s32[4]{0:T(128)S(1)} %pad_add_fusion.where_ref, f32[1,128]{1,0:T(1,128)S(1)} %bitcast.57, ...), custom_call_target="tpu_custom_call" | custom-call | flops 10737418240 | bytes 8388608 | tf_op jit(solution)/shard_map/pallas_call | solution.py:412
  116.6 2.3 %collective-permute-done.19.other_ref = bf16[27,128,128]{2,1,0:T(8,128)(2,1)S(1)} collective-permute-done((bf16[27,128,128]{2,1,0:T(8,128)(2,1)S(1)}, bf16[27,128,128]{2,1,0:T(8,128)(2,1)S(1)}, u32[]{:S(2)}, u32[]{:S(2)}) %collective-permute-start.19) | collective-permute-done | bytes 884768 | tf_op jit(solution)/shard_map/ppermute | solution.py:607
  120.5 4.3 %all-to-all-start = ((bf16[16,216,128]{2,1,0:T(8,128)(2,1)}), bf16[16,216,128]{2,1,0:T(8,128)(2,1)}, u32[]{:S(2)}, u32[]{:S(2)}) async-start(bf16[16,216,128]{2,1,0:T(8,128)(2,1)} %bitcast.20), calls=%async_computation | async-start | bytes 1769472 | tf_op jit(solution)/shard_map/all_to_all | solution.py:584
  128.7 8.6 %shard_map.116 = (bf16[8,16,8,128]{3,2,1,0:T(8,128)(2,1)}, bf16[8,16,8,128]{3,2,1,0:T(8,128)(2,1)}, f32[8,128]{1,0:T(8,128)S(1)}) custom-call(f32[1,128]{1,0:T(1,128)S(1)} %bitcast.58, bf16[2,8,16,8,128]{4,3,2,1,0:T(8,128)(2,1)S(1)} %get-tuple-element.62.p0.both_hbm, bf16[10,18,16,128]{3,2,1,0:T(8,128)(2,1)S(1)} %copy-done.15, ...), custom_call_target="tpu_custom_call" | custom-call | flops 8589934592 | bytes 6291456 | tf_op jit(solution)/shard_map/pallas_call | solution.py:518
  140.2 4.0 %collective-permute-start.20 = (bf16[224,128]{1,0:T(8,128)(2,1)S(1)}, bf16[224,128]{1,0:T(8,128)(2,1)S(1)}, u32[]{:S(2)}, u32[]{:S(2)}) collective-permute-start(bf16[224,128]{1,0:T(8,128)(2,1)S(1)} %maximum_maximum_fusion.2), channel_id=1, source_target_pairs={{0,8},{4,12},{8,0},{12,4},{1,9},{5,13},{9,1},{13,5},{2,10},{6,14},... | collective-permute-start | bytes 172040 | tf_op jit(solution)/shard_map/ppermute | solution.py:622
  148.8 17.4 %all_to_all.10 = bf16[16,224,128]{2,1,0:T(8,128)(2,1)S(1)} all-to-all(bf16[16,224,128]{2,1,0:T(8,128)(2,1)S(1)} %broadcast_in_dim.2), channel_id=1, replica_groups=mesh['y'=4,'xl'=2,'z'=4,'c'=2,'xh'=2] {'y','xl','xh'}, dimensions={0} | all-to-all | bytes 1835008 | tf_op jit(solution)/shard_map/all_to_all | solution.py:584
  166.1 4.1 %collective-permute-start.23 = (bf16[16,224,128]{2,1,0:T(8,128)(2,1)S(1)}, bf16[16,224,128]{2,1,0:T(8,128)(2,1)S(1)}, u32[]{:S(2)}, u32[]{:S(2)}) collective-permute-start(bf16[16,224,128]{2,1,0:T(8,128)(2,1)S(1)} %all_to_all.10), channel_id=1, source_target_pairs={{0,2},{2,0},{1,3},{3,1},{4,6},{6,4},{5,7},{7,5},{8,10},{10,8},{9,1... | collective-permute-start | bytes 2752520 | tf_op jit(solution)/shard_map/ppermute | solution.py:628
  172.8 2.1 %convert_multiply_fusion = (f32[16,216,128]{2,1,0:T(8,128)}, f32[16,216,128]{2,1,0:T(8,128)}) fusion(pred[]{:T(512)S(6)} %eq.7, bf16[16,224,128]{2,1,0:T(8,128)(2,1)S(1)} %collective-permute-done.23, bf16[16,224,128]{2,1,0:T(8,128)(2,1)S(1)} %all_to_all.10), kind=kLoop, calls=%fused_computation.14 | loop fusion | flops 2654208 | bytes 5308417 | tf_op jit(solution)/shard_map/mul | solution.py:633
  (116 shorter events, 54.9 us)
Async XLA Ops:
  6.6 22.9 %collective-permute-start = (bf16[4,32,16,128]{3,2,1,0:T(8,128)(2,1)}, bf16[4,32,16,128]{3,2,1,0:T(8,128)(2,1)}, u32[]{:S(2)}, u32[]{:S(2)}) collective-permute-start(bf16[4,32,16,128]{3,2,1,0:T(8,128)(2,1)} %get-tuple-element.43), channel_id=1, source_target_pairs={{0,16},{16,1},{1,17},{17,0},{2,18},{18,3},{3,19},{19,2},{4,20},{20... | collective-permute-start | bytes 1572872 | tf_op jit(solution)/shard_map/ppermute | solution.py:182
  8.7 25.3 %collective-permute-start.1 = (bf16[4,32,16,128]{3,2,1,0:T(8,128)(2,1)}, bf16[4,32,16,128]{3,2,1,0:T(8,128)(2,1)}, u32[]{:S(2)}, u32[]{:S(2)}) collective-permute-start(bf16[4,32,16,128]{3,2,1,0:T(8,128)(2,1)} %get-tuple-element.44), channel_id=1, source_target_pairs={{0,1},{16,17},{1,0},{17,16},{2,3},{18,19},{3,2},{19,18},{4,5},{20,... | collective-permute-start | bytes 1572872 | tf_op jit(solution)/shard_map/ppermute | solution.py:182
  11.1 22.9 %collective-permute-start.2 = (bf16[4,32,16,128]{3,2,1,0:T(8,128)(2,1)}, bf16[4,32,16,128]{3,2,1,0:T(8,128)(2,1)}, u32[]{:S(2)}, u32[]{:S(2)}) collective-permute-start(bf16[4,32,16,128]{3,2,1,0:T(8,128)(2,1)} %get-tuple-element.45), channel_id=1, source_target_pairs={{0,17},{16,0},{1,16},{17,1},{2,19},{18,2},{3,18},{19,3},{4,21},{20... | collective-permute-start | bytes 1572872 | tf_op jit(solution)/shard_map/ppermute | solution.py:182
  16.0 25.4 %collective-permute-start.6 = (bf16[4,32,16,128]{3,2,1,0:T(8,128)(2,1)}, bf16[4,32,16,128]{3,2,1,0:T(8,128)(2,1)S(1)}, u32[]{:S(2)}, u32[]{:S(2)}) collective-permute-start(bf16[4,32,16,128]{3,2,1,0:T(8,128)(2,1)} %get-tuple-element.55), channel_id=1, source_target_pairs={{0,32},{32,64},{64,96},{96,0},{1,33},{33,65},{65,97},{97,1},{2,34}... | collective-permute-start | bytes 1572872 | tf_op jit(solution)/shard_map/ppermute | solution.py:186
  17.3 25.2 %collective-permute-start.7 = (bf16[4,32,16,128]{3,2,1,0:T(8,128)(2,1)}, bf16[4,32,16,128]{3,2,1,0:T(8,128)(2,1)}, u32[]{:S(2)}, u32[]{:S(2)}) collective-permute-start(bf16[4,32,16,128]{3,2,1,0:T(8,128)(2,1)} %get-tuple-element.56), channel_id=1, source_target_pairs={{0,64},{32,96},{64,0},{96,32},{1,65},{33,97},{65,1},{97,33},{2,66}... | collective-permute-start | bytes 1572872 | tf_op jit(solution)/shard_map/ppermute | solution.py:186
  29.5 13.0 %collective-permute-start.8 = (bf16[4,32,16,128]{3,2,1,0:T(8,128)(2,1)S(1)}, bf16[4,32,16,128]{3,2,1,0:T(8,128)(2,1)S(1)}, u32[]{:S(2)}, u32[]{:S(2)}) collective-permute-start(bf16[4,32,16,128]{3,2,1,0:T(8,128)(2,1)S(1)} %copy-done.12), channel_id=1, source_target_pairs={{0,96},{32,0},{64,32},{96,64},{1,97},{33,1},{65,33},{97,65},{2,98}... | collective-permute-start | bytes 1572872 | tf_op jit(solution)/shard_map/ppermute | solution.py:186
  37.5 12.7 %collective-permute-start.3 = (bf16[32,16,128]{2,1,0:T(8,128)(2,1)S(1)}, bf16[32,16,128]{2,1,0:T(8,128)(2,1)S(1)}, u32[]{:S(2)}, u32[]{:S(2)}) collective-permute-start(bf16[32,16,128]{2,1,0:T(8,128)(2,1)S(1)} %get-tuple-element.51), channel_id=1, source_target_pairs={{0,32},{32,64},{64,96},{96,0},{1,33},{33,65},{65,97},{97,1},{2,34}... | collective-permute-start | bytes 393224 | tf_op jit(solution)/shard_map/ppermute | solution.py:186
  38.8 12.1 %collective-permute-start.4 = (bf16[32,16,128]{2,1,0:T(8,128)(2,1)}, bf16[32,16,128]{2,1,0:T(8,128)(2,1)}, u32[]{:S(2)}, u32[]{:S(2)}) collective-permute-start(bf16[32,16,128]{2,1,0:T(8,128)(2,1)} %get-tuple-element.52), channel_id=1, source_target_pairs={{0,64},{32,96},{64,0},{96,32},{1,65},{33,97},{65,1},{97,33},{2,66}... | collective-permute-start | bytes 393224 | tf_op jit(solution)/shard_map/ppermute | solution.py:186
  41.4 9.5 %collective-permute-start.5 = (bf16[32,16,128]{2,1,0:T(8,128)(2,1)}, bf16[32,16,128]{2,1,0:T(8,128)(2,1)}, u32[]{:S(2)}, u32[]{:S(2)}) collective-permute-start(bf16[32,16,128]{2,1,0:T(8,128)(2,1)} %get-tuple-element.53), channel_id=1, source_target_pairs={{0,96},{32,0},{64,32},{96,64},{1,97},{33,1},{65,33},{97,65},{2,98}... | collective-permute-start | bytes 393224 | tf_op jit(solution)/shard_map/ppermute | solution.py:186
  46.4 5.5 %collective-permute-start.10 = (bf16[32,16,128]{2,1,0:T(8,128)(2,1)}, bf16[32,16,128]{2,1,0:T(8,128)(2,1)S(1)}, u32[]{:S(2)}, u32[]{:S(2)}) collective-permute-start(bf16[32,16,128]{2,1,0:T(8,128)(2,1)} %get-tuple-element.60), channel_id=1, source_target_pairs={{0,1},{16,17},{1,0},{17,16},{2,3},{18,19},{3,2},{19,18},{4,5},{20,... | collective-permute-start | bytes 393224 | tf_op jit(solution)/shard_map/ppermute | solution.py:182
  48.5 6.7 %collective-permute-start.11 = (bf16[32,16,128]{2,1,0:T(8,128)(2,1)}, bf16[32,16,128]{2,1,0:T(8,128)(2,1)S(1)}, u32[]{:S(2)}, u32[]{:S(2)}) collective-permute-start(bf16[32,16,128]{2,1,0:T(8,128)(2,1)} %get-tuple-element.61), channel_id=1, source_target_pairs={{0,17},{16,0},{1,16},{17,1},{2,19},{18,2},{3,18},{19,3},{4,21},{20... | collective-permute-start | bytes 393224 | tf_op jit(solution)/shard_map/ppermute | solution.py:182
  50.8 6.3 %collective-permute-start.9 = (bf16[32,16,128]{2,1,0:T(8,128)(2,1)}, bf16[32,16,128]{2,1,0:T(8,128)(2,1)S(1)}, u32[]{:S(2)}, u32[]{:S(2)}) collective-permute-start(bf16[32,16,128]{2,1,0:T(8,128)(2,1)} %get-tuple-element.59), channel_id=1, source_target_pairs={{0,16},{16,1},{1,17},{17,0},{2,18},{18,3},{3,19},{19,2},{4,20},{20... | collective-permute-start | bytes 393224 | tf_op jit(solution)/shard_map/ppermute | solution.py:182
  61.6 15.3 %collective-permute-start.12 = (bf16[2,2,16,8,128]{4,3,2,1,0:T(8,128)(2,1)S(1)}, bf16[2,2,16,8,128]{4,3,2,1,0:T(8,128)(2,1)S(1)}, u32[]{:S(2)}, u32[]{:S(2)}) collective-permute-start(bf16[2,2,16,8,128]{4,3,2,1,0:T(8,128)(2,1)S(1)} %get-tuple-element.63), channel_id=1, source_target_pairs={{0,16},{16,32},{32,48},{48,64},{64,80},{80,96},{96,112},{1,17},{17... | collective-permute-start | bytes 393224 | tf_op jit(solution)/shard_map/ppermute | solution.py:567
  62.9 14.1 %collective-permute-start.13 = (bf16[2,2,16,8,128]{4,3,2,1,0:T(8,128)(2,1)S(1)}, bf16[2,2,16,8,128]{4,3,2,1,0:T(8,128)(2,1)S(1)}, u32[]{:S(2)}, u32[]{:S(2)}) collective-permute-start(bf16[2,2,16,8,128]{4,3,2,1,0:T(8,128)(2,1)S(1)} %get-tuple-element.64), channel_id=1, source_target_pairs={{16,0},{32,16},{48,32},{64,48},{80,64},{96,80},{112,96},{17,1},{33... | collective-permute-start | bytes 393224 | tf_op jit(solution)/shard_map/ppermute | solution.py:568
  64.2 12.8 %collective-permute-start.14 = (bf16[2,8,16,2,128]{4,3,2,1,0:T(2,128)(2,1)S(1)}, bf16[2,8,16,2,128]{4,3,2,1,0:T(2,128)(2,1)S(1)}, u32[]{:S(2)}, u32[]{:S(2)}) collective-permute-start(bf16[2,8,16,2,128]{4,3,2,1,0:T(2,128)(2,1)S(1)} %get-tuple-element.65), channel_id=1, source_target_pairs={{0,1},{1,0},{2,3},{3,2},{4,5},{5,4},{6,7},{7,6},{8,9},{9,8},{10,11... | collective-permute-start | bytes 393224 | tf_op jit(solution)/shard_map/ppermute | solution.py:569
  67.2 5.2 %collective-permute-start.15 = (bf16[2,2,16,2,128]{4,3,2,1,0:T(2,128)(2,1)S(1)}, bf16[2,2,16,2,128]{4,3,2,1,0:T(2,128)(2,1)S(1)}, u32[]{:S(2)}, u32[]{:S(2)}) collective-permute-start(bf16[2,2,16,2,128]{4,3,2,1,0:T(2,128)(2,1)S(1)} %get-tuple-element.66), channel_id=1, source_target_pairs={{0,17},{1,16},{16,33},{17,32},{32,49},{33,48},{48,65},{49,64},{64,... | collective-permute-start | bytes 98312 | tf_op jit(solution)/shard_map/ppermute | solution.py:570
  71.1 5.9 %collective-permute-start.16 = (bf16[2,2,16,2,128]{4,3,2,1,0:T(2,128)(2,1)S(1)}, bf16[2,2,16,2,128]{4,3,2,1,0:T(2,128)(2,1)S(1)}, u32[]{:S(2)}, u32[]{:S(2)}) collective-permute-start(bf16[2,2,16,2,128]{4,3,2,1,0:T(2,128)(2,1)S(1)} %get-tuple-element.67), channel_id=1, source_target_pairs={{16,1},{17,0},{32,17},{33,16},{48,33},{49,32},{64,49},{65,48},{80,... | collective-permute-start | bytes 98312 | tf_op jit(solution)/shard_map/ppermute | solution.py:571
  77.1 13.7 %collective-permute-start.18 = (bf16[2,12,2,10,128]{4,3,2,1,0:T(8,128)(2,1)S(1)}, bf16[2,12,2,10,128]{4,3,2,1,0:T(8,128)(2,1)S(1)}, u32[]{:S(2)}, u32[]{:S(2)}) collective-permute-start(bf16[2,12,2,10,128]{4,3,2,1,0:T(8,128)(2,1)S(1)} %maximum_maximum_fusion.1), channel_id=1, source_target_pairs={{2,0},{4,2},{6,4},{8,6},{10,8},{12,10},{14,12},{3,1},{5,3},{7,5},{... | collective-permute-start | bytes 368648 | tf_op jit(solution)/shard_map/ppermute | solution.py:579
  86.0 6.0 %collective-permute-start.17 = (bf16[2,12,2,10,128]{4,3,2,1,0:T(8,128)(2,1)S(1)}, bf16[2,12,2,10,128]{4,3,2,1,0:T(8,128)(2,1)S(1)}, u32[]{:S(2)}, u32[]{:S(2)}) collective-permute-start(bf16[2,12,2,10,128]{4,3,2,1,0:T(8,128)(2,1)S(1)} %maximum_maximum_fusion), channel_id=1, source_target_pairs={{0,2},{2,4},{4,6},{6,8},{8,10},{10,12},{12,14},{1,3},{3,5},{5,7},{... | collective-permute-start | bytes 368648 | tf_op jit(solution)/shard_map/ppermute | solution.py:578
  120.5 18.3 %all-to-all-start = ((bf16[16,216,128]{2,1,0:T(8,128)(2,1)}), bf16[16,216,128]{2,1,0:T(8,128)(2,1)}, u32[]{:S(2)}, u32[]{:S(2)}) async-start(bf16[16,216,128]{2,1,0:T(8,128)(2,1)} %bitcast.20), calls=%async_computation | async-start | bytes 1769472 | tf_op jit(solution)/shard_map/all_to_all | solution.py:584
  140.2 6.7 %collective-permute-start.20 = (bf16[224,128]{1,0:T(8,128)(2,1)S(1)}, bf16[224,128]{1,0:T(8,128)(2,1)S(1)}, u32[]{:S(2)}, u32[]{:S(2)}) collective-permute-start(bf16[224,128]{1,0:T(8,128)(2,1)S(1)} %maximum_maximum_fusion.2), channel_id=1, source_target_pairs={{0,8},{4,12},{8,0},{12,4},{1,9},{5,13},{9,1},{13,5},{2,10},{6,14},... | collective-permute-start | bytes 172040 | tf_op jit(solution)/shard_map/ppermute | solution.py:622
  144.2 4.2 %collective-permute-start.21 = (bf16[224,128]{1,0:T(8,128)(2,1)S(1)}, bf16[224,128]{1,0:T(8,128)(2,1)S(1)}, u32[]{:S(2)}, u32[]{:S(2)}) collective-permute-start(bf16[224,128]{1,0:T(8,128)(2,1)S(1)} %maximum_maximum_fusion.2), channel_id=1, source_target_pairs={{0,4},{4,8},{8,12},{12,0},{1,5},{5,9},{9,13},{13,1},{2,6},{6,10},{... | collective-permute-start | bytes 172040 | tf_op jit(solution)/shard_map/ppermute | solution.py:622
  144.9 3.5 %collective-permute-start.22 = (bf16[224,128]{1,0:T(8,128)(2,1)S(1)}, bf16[224,128]{1,0:T(8,128)(2,1)S(1)}, u32[]{:S(2)}, u32[]{:S(2)}) collective-permute-start(bf16[224,128]{1,0:T(8,128)(2,1)S(1)} %maximum_maximum_fusion.2), channel_id=1, source_target_pairs={{0,12},{4,0},{8,4},{12,8},{1,13},{5,1},{9,5},{13,9},{2,14},{6,2},{... | collective-permute-start | bytes 172040 | tf_op jit(solution)/shard_map/ppermute | solution.py:622
  166.1 6.2 %collective-permute-start.23 = (bf16[16,224,128]{2,1,0:T(8,128)(2,1)S(1)}, bf16[16,224,128]{2,1,0:T(8,128)(2,1)S(1)}, u32[]{:S(2)}, u32[]{:S(2)}) collective-permute-start(bf16[16,224,128]{2,1,0:T(8,128)(2,1)S(1)} %all_to_all.10), channel_id=1, source_target_pairs={{0,2},{2,0},{1,3},{3,1},{4,6},{6,4},{5,7},{7,5},{8,10},{10,8},{9,1... | collective-permute-start | bytes 2752520 | tf_op jit(solution)/shard_map/ppermute | solution.py:628
  (24 other events, 167.1 us)

commit v5 on v4

--- a/solution.py
+++ b/solution.py
@@ -107,16 +107,21 @@
     )(*parts)
 
 
+def send_rows(place, top):
+    odd = place % 2
+    return top - top * odd, top * odd
+
+
 def sum_bricks_kernel(
     where_ref,
     a0, a1, a2, a3, b0, b1, b2, b3,
     cot_ref,
     both_ref,
-    low_ref,
-    high_ref,
+    one_ref,
+    two_ref,
     layer_ref,
-    layer_low_ref,
-    layer_high_ref,
+    layer_one_ref,
+    layer_two_ref,
     sums,
     cells,
 ):
@@ -141,8 +146,9 @@
             return carry
 
         lax.fori_loop(0, 4, block, 0)
-    low_ref[...] = both_ref[:, 0:2]
-    high_ref[...] = both_ref[:, 6:8]
+    first_x, second_x = send_rows(where_ref[2], 6)
+    one_ref[...] = both_ref[:, pl.ds(first_x, 2)]
+    two_ref[...] = both_ref[:, pl.ds(second_x, 2)]
     for side, rows in ((0, slice(6, 8)), (1, slice(0, 2))):
 
         @pl.when(where_ref[0] == side)
@@ -150,8 +156,8 @@
             for n in range(2):
                 layer_ref[n] = both_ref[n].astype(F32)[:, :, rows, :].astype(BF16)
 
-    layer_low_ref[...] = layer_ref[:, 0:2]
-    layer_high_ref[...] = layer_ref[:, 6:8]
+    layer_one_ref[...] = layer_ref[:, pl.ds(first_x, 2)]
+    layer_two_ref[...] = layer_ref[:, pl.ds(second_x, 2)]
 
 
 def sum_bricks(where, parts, out_grad):
@@ -173,17 +179,16 @@
     )(where, *parts, out_grad)
 
 
-def ring(axes, shift, place_of):
-    size = 4
-    return [(place_of(i), place_of((i + shift) % size)) for i in range(size)]
-
-
 def along_x(value, shift):
-    return lax.ppermute(value, ("xl", "xh"), ring(0, shift, lambda i: (i % 2) * 2 + i // 2))
-
-
-def along_y(value, shift):
-    return lax.ppermute(value, "y", ring(0, shift, lambda i: i))
+    def place(chip):
+        return chip % 2 * 2 + chip // 2
+
+    pairs = [(place(chip), place((chip + shift) % 4)) for chip in range(4)]
+    return lax.ppermute(value, ("xl", "xh"), pairs)
+
+
+def along(axis, value, shift):
+    return lax.ppermute(value, axis, [(i, (i + shift) % 4) for i in range(4)])
 
 
 def regroup(rows, target_rank, target_slot, out_grad, where, weights):
@@ -196,11 +201,11 @@
     placed_a = place_bricks(codes, rows, 0)
     placed_b = place_bricks(codes, rows, 1)
     came_a = [placed_a[0]] + [along_x(placed_a[n], n) for n in (1, 2, 3)]
-    came_b = [placed_b[0]] + [along_y(placed_b[n], n) for n in (1, 2, 3)]
+    came_b = [placed_b[0]] + [along("y", placed_b[n], n) for n in (1, 2, 3)]
     came_a, weights = lax.optimization_barrier((came_a, weights))
     merged_a = merge_bricks(came_a)
     merged_b = merge_bricks(came_b)
-    came_a = [merged_a[0]] + [along_y(merged_a[n], n) for n in (1, 2, 3)]
+    came_a = [merged_a[0]] + [along("y", merged_a[n], n) for n in (1, 2, 3)]
     came_b = [merged_b[0]] + [along_x(merged_b[n], n) for n in (1, 2, 3)]
     return sum_bricks(where, came_a + came_b, out_grad), weights
 
@@ -250,24 +255,32 @@
 
 
 def fill(volume, which, pieces, where_ref, outside):
-    centre, x_low, x_high, layer, layer_low, layer_high, y_low, y_high = pieces
+    centre, x_one, x_two, layer, layer_one, layer_two, y_one, y_two = pieces
+    first_x, second_x = send_rows(where_ref[2], 10)
+    first_y, second_y = send_rows(where_ref[3], 18)
+    at_one = pl.ds(first_x, 2)
+    at_two = pl.ds(second_x, 2)
     volume[...] = jnp.full(volume.shape, outside, F32)
     volume[2:10, 2:18, 2:10, :] = centre[which].astype(F32)
-    volume[0:2, 2:18, 2:10, :] = x_low[which].astype(F32)
-    volume[10:12, 2:18, 2:10, :] = x_high[which].astype(F32)
-    low = y_low[which].astype(F32)
-    high = y_high[which].astype(F32)
-    volume[:, 0:2, 2:10, :] = low[:, :, 0:8]
-    volume[:, 18:20, 2:10, :] = high[:, :, 0:8]
-    for side, rows in ((0, slice(10, 12)), (1, slice(0, 2))):
+    volume[at_one, 2:18, 2:10, :] = x_one[which].astype(F32)
+    volume[at_two, 2:18, 2:10, :] = x_two[which].astype(F32)
+    sides = ((y_one, pl.ds(first_y, 2)), (y_two, pl.ds(second_y, 2)))
+    spans = ((at_one, slice(0, 2)), (slice(2, 10), slice(2, 10)), (at_two, slice(10, 12)))
+    for came, at_y in sides:
+        values = came[which].astype(F32)
+        for at_x, rows in spans:
+            volume[at_x, at_y, 2:10, :] = values[rows, :, 0:8]
+    for side, at_z in ((0, slice(10, 12)), (1, slice(0, 2))):
 
         @pl.when(where_ref[0] == side)
         def _():
-            volume[2:10, 2:18, rows, :] = layer[which].astype(F32)
-            volume[0:2, 2:18, rows, :] = layer_low[which].astype(F32)
-            volume[10:12, 2:18, rows, :] = layer_high[which].astype(F32)
-            volume[:, 0:2, rows, :] = low[:, :, 8:10]
-            volume[:, 18:20, rows, :] = high[:, :, 8:10]
+            volume[2:10, 2:18, at_z, :] = layer[which].astype(F32)
+            volume[at_one, 2:18, at_z, :] = layer_one[which].astype(F32)
+            volume[at_two, 2:18, at_z, :] = layer_two[which].astype(F32)
+            for came, at_y in sides:
+                values = came[which].astype(F32)
+                for at_x, rows in spans:
+                    volume[at_x, at_y, at_z, :] = values[rows, :, 8:10]
 
     @pl.when(where_ref[2] == 0)
     def _():
@@ -557,27 +570,33 @@
     )(own, other)
 
 
-FORWARD = [(i, i + 1) for i in range(7)]
-BACKWARD = [(i + 1, i) for i in range(7)]
-
-
-def edges(both, send_low, send_high, layer, layer_low, layer_high):
-    far = [(a * 2 + s, b * 2 + 1 - s) for a, b in FORWARD for s in range(2)]
-    near = [(a * 2 + s, b * 2 + 1 - s) for a, b in BACKWARD for s in range(2)]
-    x_low = lax.ppermute(send_high, GX, FORWARD)
-    x_high = lax.ppermute(send_low, GX, BACKWARD)
+FIRST = [(i, i ^ 1) for i in range(8)]
+SECOND = [(i, i - 1 if i % 2 == 0 else i + 1) for i in range(1, 7)]
+
+
+def across(pairs):
+    return [(a * 2 + s, b * 2 + 1 - s) for a, b in pairs for s in range(2)]
+
+
+def edges(both, send_one, send_two, layer, layer_one, layer_two):
+    x_one = lax.ppermute(send_one, GX, FIRST)
+    x_two = lax.ppermute(send_two, GX, SECOND)
     came = lax.ppermute(layer, SA, [(0, 1), (1, 0)])
-    came_low = lax.ppermute(layer_high, PLANE, far)
-    came_high = lax.ppermute(layer_low, PLANE, near)
-
-    def wide(rows):
-        inner = jnp.concatenate([part[:, :, rows] for part in (x_low, both, x_high)], axis=1)
-        outer = jnp.concatenate([part[:, :, rows] for part in (came_low, came, came_high)], axis=1)
+    came_one = lax.ppermute(layer_one, PLANE, across(FIRST))
+    came_two = lax.ppermute(layer_two, PLANE, across(SECOND))
+
+    def wide(start):
+        def rows(part):
+            return lax.dynamic_slice_in_dim(part, start, 2, axis=2)
+
+        inner = jnp.concatenate([rows(part) for part in (x_one, both, x_two)], axis=1)
+        outer = jnp.concatenate([rows(part) for part in (came_one, came, came_two)], axis=1)
         return jnp.concatenate([inner, outer], axis=3)
 
-    y_low = lax.ppermute(wide(slice(14, 16)), GY, FORWARD)
-    y_high = lax.ppermute(wide(slice(0, 2)), GY, BACKWARD)
-    return both, x_low, x_high, came, came_low, came_high, y_low, y_high
+    first_y, second_y = send_rows(lax.axis_index(GY), 14)
+    y_one = lax.ppermute(wide(first_y), GY, FIRST)
+    y_two = lax.ppermute(wide(second_y), GY, SECOND)
+    return both, x_one, x_two, came, came_one, came_two, y_one, y_two
 
 
 def exchange(values, axes):
@@ -618,9 +637,7 @@
 
     total = jnp.sum(shares.astype(F32), axis=0)
     sent = joined(total, jnp.sum(gain_part, axis=0, keepdims=True))
-    parts = [sent] + [
-        lax.ppermute(sent, "z", [(i, (i + shift) % 4) for i in range(4)]) for shift in (1, 2, 3)
-    ]
+    parts = [sent] + [along("z", sent, shift) for shift in (1, 2, 3)]
     parts = [part.astype(F32) for part in parts]
     layers = (parts[0] + parts[2]) + (parts[1] + parts[3])
     sent = joined(layers[:216], layers[216:217] + layers[217:218])

time: 176 us -> 170 us (0.966)
  starting transfers between devices: 57.7 us -> 52.9 us
    ppermute x21, starting transfers between devices: 46.2 us -> 40.3 us  [the longest x9 16 us: along(): return lax.ppermute(value, axis, [(i, (i + shift) % 4) for i in range(4)])]
    ppermute x21, waiting for transfers between devices: 14.9 us -> 11 us  [the longest x6 6.19 us: along_x(): return lax.ppermute(value, ('xl', 'xh'), pairs)]
    ppermute x1, waiting for transfers between devices: 0.01 us -> 3.18 us  [edges(): came = lax.ppermute(layer, SA, [(0, 1), (1, 0)])]
    all_to_all x1, starting transfers between devices: 4.3 us -> 6.66 us  [exchange(): return lax.all_to_all(values, axes, split_axis=0, concat_axis=0, tiled=True)]
  transfers between devices with their start and end apart: 25 -> 25, of which waited for: 10 -> 9; matrix products, arithmetic and copies ran while one was open for 8% -> 8% of each run, Pallas kernels for 10% -> 11%
where the time goes in v5:
time: 170 us
  starting transfers between devices  52.9 us (31%)
  Pallas kernels  47.5 us (28%)
  waiting for transfers between devices  19.5 us (11%)
  local copies, waits for them, and re-layouts  18.5 us (11%)
  blocking collectives  17.4 us (10%)
  other arithmetic  12.6 us (7%)
    pallas_call x1, Pallas kernels, grads_call(): pl.pallas_call(grads_kernel, out_shape=(jax.ShapeDtypeStruct((10, 18, 16,...  22.8 us
    all_to_all x1, blocking collectives, exchange(): return lax.all_to_all(values, axes, split_axis=0, concat_axis=0, tiled=True)  17.4 us
    ppermute x9, starting transfers between devices, along(): return lax.ppermute(value, axis, [(i, (i + shift) % 4) for i in range(4)])  16 us
    unnamed x48, local copies, waits for them, and re-layouts  15 us
    ppermute x1, starting transfers between devices, edges(): y_two = lax.ppermute(wide(second_y), GY, SECOND)  10.1 us
    ppermute x6, starting transfers between devices, along_x(): return lax.ppermute(value, ('xl', 'xh'), pairs)  9.47 us
    pallas_call x1, Pallas kernels, outputs_call(): pl.pallas_call(outputs_kernel, out_shape=(jax.ShapeDtypeStruct((8, 16, 8,...  8.74 us
    concatenate x4, other arithmetic, pair_weights(): return jnp.concatenate([left, right], axis=3).reshape(4608, 256)  6.77 us
  transfers between devices with their start and end apart: 25, of which 9 were waited for; matrix products, arithmetic and copies ran while one was open for 8% of the time, Pallas kernels for 11%

profile of v5, /device:TPU:1, one launch (start us, length us, event | category | flops | bytes accessed | tf_op | source)
XLA Modules:
  0.0 169.5 jit_solution(14405840263377495204)
XLA Ops:
  3.6 3.0 %shard_map.110 = (bf16[4,32,16,128]{3,2,1,0:T(8,128)(2,1)S(1)}, bf16[4,32,16,128]{3,2,1,0:T(8,128)(2,1)}, bf16[4,32,16,128]{3,2,1,0:T(8,128)(2,1)}, bf16[4,32,16,128]{3,2,1,0:T(8,128)(2,1)}) custom-call(s32[2,128]{1,0:T(2,128)S(1)} %fusion.14.code_ref, bf16[128,64,128]{2,1,0:T(8,128)(2,1)S(1)} %bitcast.51), custom_call_target="tpu_custom_call" | custom-call | flops 268435456 | bytes 3145728 | tf_op jit(solution)/shard_map/pallas_call | solution.py:61
  6.6 2.1 %collective-permute-start = (bf16[4,32,16,128]{3,2,1,0:T(8,128)(2,1)}, bf16[4,32,16,128]{3,2,1,0:T(8,128)(2,1)}, u32[]{:S(2)}, u32[]{:S(2)}) collective-permute-start(bf16[4,32,16,128]{3,2,1,0:T(8,128)(2,1)} %get-tuple-element.43), channel_id=1, source_target_pairs={{0,16},{16,1},{1,17},{17,0},{2,18},{18,3},{3,19},{19,2},{4,20},{20... | collective-permute-start | bytes 1572872 | tf_op jit(solution)/shard_map/ppermute | solution.py:187
  8.7 2.4 %collective-permute-start.1 = (bf16[4,32,16,128]{3,2,1,0:T(8,128)(2,1)}, bf16[4,32,16,128]{3,2,1,0:T(8,128)(2,1)}, u32[]{:S(2)}, u32[]{:S(2)}) collective-permute-start(bf16[4,32,16,128]{3,2,1,0:T(8,128)(2,1)} %get-tuple-element.44), channel_id=1, source_target_pairs={{0,1},{16,17},{1,0},{17,16},{2,3},{18,19},{3,2},{19,18},{4,5},{20,... | collective-permute-start | bytes 1572872 | tf_op jit(solution)/shard_map/ppermute | solution.py:187
  12.3 2.9 %shard_map.112 = (bf16[4,32,16,128]{3,2,1,0:T(8,128)(2,1)S(1)}, bf16[4,32,16,128]{3,2,1,0:T(8,128)(2,1)}, bf16[4,32,16,128]{3,2,1,0:T(8,128)(2,1)}, bf16[4,32,16,128]{3,2,1,0:T(8,128)(2,1)S(1)}) custom-call(s32[2,128]{1,0:T(2,128)S(1)} %fusion.14.code_ref, bf16[128,64,128]{2,1,0:T(8,128)(2,1)S(1)} %bitcast.52), custom_call_target="tpu_custom_call" | custom-call | flops 268435456 | bytes 3145728 | tf_op jit(solution)/shard_map/pallas_call | solution.py:61
  17.3 2.6 %collective-permute-start.7 = (bf16[4,32,16,128]{3,2,1,0:T(8,128)(2,1)}, bf16[4,32,16,128]{3,2,1,0:T(8,128)(2,1)}, u32[]{:S(2)}, u32[]{:S(2)}) collective-permute-start(bf16[4,32,16,128]{3,2,1,0:T(8,128)(2,1)} %get-tuple-element.56), channel_id=1, source_target_pairs={{0,64},{32,96},{64,0},{96,32},{1,65},{33,97},{65,1},{97,33},{2,66}... | collective-permute-start | bytes 1572872 | tf_op jit(solution)/shard_map/ppermute | solution.py:191
  21.6 2.2 %rev.6 = bf16[27,128,128]{1,2,0:T(8,128)(2,1)} reverse(bf16[27,128,128]{1,2,0:T(8,128)(2,1)} %copy.12), dimensions={0} | reverse | bytes 1769472 | tf_op jit(solution)/shard_map/rev | solution.py:236
  34.0 3.5 %shard_map.111 = (bf16[32,16,128]{2,1,0:T(8,128)(2,1)S(1)}, bf16[32,16,128]{2,1,0:T(8,128)(2,1)S(1)}, bf16[32,16,128]{2,1,0:T(8,128)(2,1)}, bf16[32,16,128]{2,1,0:T(8,128)(2,1)}) custom-call(bf16[4,32,16,128]{3,2,1,0:T(8,128)(2,1)S(1)} %copy-done.5, bf16[4,32,16,128]{3,2,1,0:T(8,128)(2,1)} %collective-permute-done.p1, ...), custom_call_target="tpu_custom_call" | custom-call | flops 4194304 | bytes 3145728 | tf_op jit(solution)/shard_map/pallas_call | solution.py:99
  38.8 2.6 %collective-permute-start.4 = (bf16[32,16,128]{2,1,0:T(8,128)(2,1)}, bf16[32,16,128]{2,1,0:T(8,128)(2,1)}, u32[]{:S(2)}, u32[]{:S(2)}) collective-permute-start(bf16[32,16,128]{2,1,0:T(8,128)(2,1)} %get-tuple-element.52), channel_id=1, source_target_pairs={{0,64},{32,96},{64,0},{96,32},{1,65},{33,97},{65,1},{97,33},{2,66}... | collective-permute-start | bytes 393224 | tf_op jit(solution)/shard_map/ppermute | solution.py:191
  42.5 3.3 %shard_map.113 = (bf16[32,16,128]{2,1,0:T(8,128)(2,1)S(1)}, bf16[32,16,128]{2,1,0:T(8,128)(2,1)}, bf16[32,16,128]{2,1,0:T(8,128)(2,1)}, bf16[32,16,128]{2,1,0:T(8,128)(2,1)}) custom-call(bf16[4,32,16,128]{3,2,1,0:T(8,128)(2,1)S(1)} %get-tuple-element.54.p0, bf16[4,32,16,128]{3,2,1,0:T(8,128)(2,1)S(1)} %collective-permute-done.6.p1, ...), custom_call_target="tpu_custom_call" | custom-call | flops 4194304 | bytes 3145728 | tf_op jit(solution)/shard_map/pallas_call | solution.py:99
  46.4 2.1 %collective-permute-start.10 = (bf16[32,16,128]{2,1,0:T(8,128)(2,1)}, bf16[32,16,128]{2,1,0:T(8,128)(2,1)S(1)}, u32[]{:S(2)}, u32[]{:S(2)}) collective-permute-start(bf16[32,16,128]{2,1,0:T(8,128)(2,1)} %get-tuple-element.60), channel_id=1, source_target_pairs={{0,1},{16,17},{1,0},{17,16},{2,3},{18,19},{3,2},{19,18},{4,5},{20,... | collective-permute-start | bytes 393224 | tf_op jit(solution)/shard_map/ppermute | solution.py:187
  51.9 3.3 %collective-permute-done.11.b3 = bf16[32,16,128]{2,1,0:T(8,128)(2,1)S(1)} collective-permute-done((bf16[32,16,128]{2,1,0:T(8,128)(2,1)}, bf16[32,16,128]{2,1,0:T(8,128)(2,1)S(1)}, u32[]{:S(2)}, u32[]{:S(2)}) %collective-permute-start.11) | collective-permute-done | bytes 131104 | tf_op jit(solution)/shard_map/ppermute | solution.py:187
  62.4 3.2 %collective-permute-start.15 = (bf16[2,2,16,2,128]{4,3,2,1,0:T(2,128)(2,1)S(1)}, bf16[2,2,16,2,128]{4,3,2,1,0:T(2,128)(2,1)S(1)}, u32[]{:S(2)}, u32[]{:S(2)}) collective-permute-start(bf16[2,2,16,2,128]{4,3,2,1,0:T(2,128)(2,1)S(1)} %get-tuple-element.66), channel_id=1, source_target_pairs={{0,17},{1,16},{16,1},{17,0},{32,49},{33,48},{48,33},{49,32},{64,81... | collective-permute-start | bytes 98312 | tf_op jit(solution)/shard_map/ppermute | solution.py:585
  67.8 3.2 %collective-permute-done.14.p3 = bf16[2,8,16,2,128]{4,3,2,1,0:T(2,128)(2,1)S(1)} collective-permute-done((bf16[2,8,16,2,128]{4,3,2,1,0:T(2,128)(2,1)S(1)}, bf16[2,8,16,2,128]{4,3,2,1,0:T(2,128)(2,1)S(1)}, u32[]{:S(2)}, u32[]{:S(2)}) %collective-permute-start.14) | collective-permute-done | bytes 131104 | tf_op jit(solution)/shard_map/ppermute | solution.py:584
  71.0 10.1 %collective-permute-start.18 = (bf16[2,12,2,10,128]{4,3,2,1,0:T(8,128)(2,1)S(1)}, bf16[2,12,2,10,128]{4,3,2,1,0:T(8,128)(2,1)S(1)}, u32[]{:S(2)}, u32[]{:S(2)}) collective-permute-start(bf16[2,12,2,10,128]{4,3,2,1,0:T(8,128)(2,1)S(1)} %maximum_maximum_fusion.1), channel_id=1, source_target_pairs={{2,4},{4,2},{6,8},{8,6},{10,12},{12,10},{3,5},{5,3},{7,9},{9,7},{1... | collective-permute-start | bytes 368648 | tf_op jit(solution)/shard_map/ppermute | solution.py:598
  81.3 3.2 %collective-permute-done.18.p7 = bf16[2,12,2,10,128]{4,3,2,1,0:T(8,128)(2,1)S(1)} collective-permute-done((bf16[2,12,2,10,128]{4,3,2,1,0:T(8,128)(2,1)S(1)}, bf16[2,12,2,10,128]{4,3,2,1,0:T(8,128)(2,1)S(1)}, u32[]{:S(2)}, u32[]{:S(2)}) %collective-permute-start.18) | collective-permute-done | bytes 122912 | tf_op jit(solution)/shard_map/ppermute | solution.py:598
  86.2 22.8 %shard_map.115 = (bf16[10,18,16,128]{3,2,1,0:T(8,128)(2,1)S(1)}, bf16[10,18,16,128]{3,2,1,0:T(8,128)(2,1)S(1)}, bf16[27,128,128]{2,1,0:T(8,128)(2,1)S(1)}, bf16[27,128,128]{2,1,0:T(8,128)(2,1)S(1)}) custom-call(s32[4]{0:T(128)S(1)} %pad_add_fusion.where_ref, f32[1,128]{1,0:T(1,128)S(1)} %bitcast.57, ...), custom_call_target="tpu_custom_call" | custom-call | flops 10737418240 | bytes 8388608 | tf_op jit(solution)/shard_map/pallas_call | solution.py:425
  109.3 2.3 %collective-permute-done.19.other_ref = bf16[27,128,128]{2,1,0:T(8,128)(2,1)S(1)} collective-permute-done((bf16[27,128,128]{2,1,0:T(8,128)(2,1)S(1)}, bf16[27,128,128]{2,1,0:T(8,128)(2,1)S(1)}, u32[]{:S(2)}, u32[]{:S(2)}) %collective-permute-start.19) | collective-permute-done | bytes 884768 | tf_op jit(solution)/shard_map/ppermute | solution.py:626
  113.2 6.7 %all-to-all-start = ((bf16[16,216,128]{2,1,0:T(8,128)(2,1)}), bf16[16,216,128]{2,1,0:T(8,128)(2,1)}, u32[]{:S(2)}, u32[]{:S(2)}) async-start(bf16[16,216,128]{2,1,0:T(8,128)(2,1)} %bitcast.20), calls=%async_computation | async-start | bytes 1769472 | tf_op jit(solution)/shard_map/all_to_all | solution.py:603
  123.7 8.7 %shard_map.116 = (bf16[8,16,8,128]{3,2,1,0:T(8,128)(2,1)}, bf16[8,16,8,128]{3,2,1,0:T(8,128)(2,1)}, f32[8,128]{1,0:T(8,128)S(1)}) custom-call(f32[1,128]{1,0:T(1,128)S(1)} %bitcast.58, bf16[2,8,16,8,128]{4,3,2,1,0:T(8,128)(2,1)S(1)} %get-tuple-element.62.p0.both_hbm, bf16[10,18,16,128]{3,2,1,0:T(8,128)(2,1)S(1)} %copy-done.15, ...), custom_call_target="tpu_custom_call" | custom-call | flops 8589934592 | bytes 6291456 | tf_op jit(solution)/shard_map/pallas_call | solution.py:531
  134.9 3.3 %collective-permute-start.20 = (bf16[224,128]{1,0:T(8,128)(2,1)S(1)}, bf16[224,128]{1,0:T(8,128)(2,1)S(1)}, u32[]{:S(2)}, u32[]{:S(2)}) collective-permute-start(bf16[224,128]{1,0:T(8,128)(2,1)S(1)} %maximum_maximum_fusion.2), channel_id=1, source_target_pairs={{0,8},{4,12},{8,0},{12,4},{1,9},{5,13},{9,1},{13,5},{2,10},{6,14},... | collective-permute-start | bytes 172040 | tf_op jit(solution)/shard_map/ppermute | solution.py:191
  142.8 17.4 %all_to_all.10 = bf16[16,224,128]{2,1,0:T(8,128)(2,1)S(1)} all-to-all(bf16[16,224,128]{2,1,0:T(8,128)(2,1)S(1)} %broadcast_in_dim.2), channel_id=1, replica_groups=mesh['y'=4,'xl'=2,'z'=4,'c'=2,'xh'=2] {'y','xl','xh'}, dimensions={0} | all-to-all | bytes 1835008 | tf_op jit(solution)/shard_map/all_to_all | solution.py:603
  160.3 4.5 %collective-permute-start.23 = (bf16[16,224,128]{2,1,0:T(8,128)(2,1)S(1)}, bf16[16,224,128]{2,1,0:T(8,128)(2,1)S(1)}, u32[]{:S(2)}, u32[]{:S(2)}) collective-permute-start(bf16[16,224,128]{2,1,0:T(8,128)(2,1)S(1)} %all_to_all.10), channel_id=1, source_target_pairs={{0,2},{2,0},{1,3},{3,1},{4,6},{6,4},{5,7},{7,5},{8,10},{10,8},{9,1... | collective-permute-start | bytes 2752520 | tf_op jit(solution)/shard_map/ppermute | solution.py:645
  164.8 2.1 %collective-permute-done.23 = bf16[16,224,128]{2,1,0:T(8,128)(2,1)S(1)} collective-permute-done((bf16[16,224,128]{2,1,0:T(8,128)(2,1)S(1)}, bf16[16,224,128]{2,1,0:T(8,128)(2,1)S(1)}, u32[]{:S(2)}, u32[]{:S(2)}) %collective-permute-start.23) | collective-permute-done | bytes 917536 | tf_op jit(solution)/shard_map/ppermute | solution.py:645
  167.4 2.1 %convert_multiply_fusion = (f32[16,216,128]{2,1,0:T(8,128)}, f32[16,216,128]{2,1,0:T(8,128)}) fusion(pred[]{:T(512)S(6)} %eq.9, bf16[16,224,128]{2,1,0:T(8,128)(2,1)S(1)} %collective-permute-done.23, bf16[16,224,128]{2,1,0:T(8,128)(2,1)S(1)} %all_to_all.10), kind=kLoop, calls=%fused_computation.14 | loop fusion | flops 2654208 | bytes 5308417 | tf_op jit(solution)/shard_map/mul | solution.py:650
  (116 shorter events, 48.8 us)
Async XLA Ops:
  6.6 23.0 %collective-permute-start = (bf16[4,32,16,128]{3,2,1,0:T(8,128)(2,1)}, bf16[4,32,16,128]{3,2,1,0:T(8,128)(2,1)}, u32[]{:S(2)}, u32[]{:S(2)}) collective-permute-start(bf16[4,32,16,128]{3,2,1,0:T(8,128)(2,1)} %get-tuple-element.43), channel_id=1, source_target_pairs={{0,16},{16,1},{1,17},{17,0},{2,18},{18,3},{3,19},{19,2},{4,20},{20... | collective-permute-start | bytes 1572872 | tf_op jit(solution)/shard_map/ppermute | solution.py:187
  8.7 25.3 %collective-permute-start.1 = (bf16[4,32,16,128]{3,2,1,0:T(8,128)(2,1)}, bf16[4,32,16,128]{3,2,1,0:T(8,128)(2,1)}, u32[]{:S(2)}, u32[]{:S(2)}) collective-permute-start(bf16[4,32,16,128]{3,2,1,0:T(8,128)(2,1)} %get-tuple-element.44), channel_id=1, source_target_pairs={{0,1},{16,17},{1,0},{17,16},{2,3},{18,19},{3,2},{19,18},{4,5},{20,... | collective-permute-start | bytes 1572872 | tf_op jit(solution)/shard_map/ppermute | solution.py:187
  11.1 22.9 %collective-permute-start.2 = (bf16[4,32,16,128]{3,2,1,0:T(8,128)(2,1)}, bf16[4,32,16,128]{3,2,1,0:T(8,128)(2,1)}, u32[]{:S(2)}, u32[]{:S(2)}) collective-permute-start(bf16[4,32,16,128]{3,2,1,0:T(8,128)(2,1)} %get-tuple-element.45), channel_id=1, source_target_pairs={{0,17},{16,0},{1,16},{17,1},{2,19},{18,2},{3,18},{19,3},{4,21},{20... | collective-permute-start | bytes 1572872 | tf_op jit(solution)/shard_map/ppermute | solution.py:187
  16.0 25.4 %collective-permute-start.6 = (bf16[4,32,16,128]{3,2,1,0:T(8,128)(2,1)}, bf16[4,32,16,128]{3,2,1,0:T(8,128)(2,1)S(1)}, u32[]{:S(2)}, u32[]{:S(2)}) collective-permute-start(bf16[4,32,16,128]{3,2,1,0:T(8,128)(2,1)} %get-tuple-element.55), channel_id=1, source_target_pairs={{0,32},{32,64},{64,96},{96,0},{1,33},{33,65},{65,97},{97,1},{2,34}... | collective-permute-start | bytes 1572872 | tf_op jit(solution)/shard_map/ppermute | solution.py:191
  17.3 25.2 %collective-permute-start.7 = (bf16[4,32,16,128]{3,2,1,0:T(8,128)(2,1)}, bf16[4,32,16,128]{3,2,1,0:T(8,128)(2,1)}, u32[]{:S(2)}, u32[]{:S(2)}) collective-permute-start(bf16[4,32,16,128]{3,2,1,0:T(8,128)(2,1)} %get-tuple-element.56), channel_id=1, source_target_pairs={{0,64},{32,96},{64,0},{96,32},{1,65},{33,97},{65,1},{97,33},{2,66}... | collective-permute-start | bytes 1572872 | tf_op jit(solution)/shard_map/ppermute | solution.py:191
  29.6 12.9 %collective-permute-start.8 = (bf16[4,32,16,128]{3,2,1,0:T(8,128)(2,1)S(1)}, bf16[4,32,16,128]{3,2,1,0:T(8,128)(2,1)S(1)}, u32[]{:S(2)}, u32[]{:S(2)}) collective-permute-start(bf16[4,32,16,128]{3,2,1,0:T(8,128)(2,1)S(1)} %copy-done.12), channel_id=1, source_target_pairs={{0,96},{32,0},{64,32},{96,64},{1,97},{33,1},{65,33},{97,65},{2,98}... | collective-permute-start | bytes 1572872 | tf_op jit(solution)/shard_map/ppermute | solution.py:191
  37.5 12.6 %collective-permute-start.3 = (bf16[32,16,128]{2,1,0:T(8,128)(2,1)S(1)}, bf16[32,16,128]{2,1,0:T(8,128)(2,1)S(1)}, u32[]{:S(2)}, u32[]{:S(2)}) collective-permute-start(bf16[32,16,128]{2,1,0:T(8,128)(2,1)S(1)} %get-tuple-element.51), channel_id=1, source_target_pairs={{0,32},{32,64},{64,96},{96,0},{1,33},{33,65},{65,97},{97,1},{2,34}... | collective-permute-start | bytes 393224 | tf_op jit(solution)/shard_map/ppermute | solution.py:191
  38.8 12.1 %collective-permute-start.4 = (bf16[32,16,128]{2,1,0:T(8,128)(2,1)}, bf16[32,16,128]{2,1,0:T(8,128)(2,1)}, u32[]{:S(2)}, u32[]{:S(2)}) collective-permute-start(bf16[32,16,128]{2,1,0:T(8,128)(2,1)} %get-tuple-element.52), channel_id=1, source_target_pairs={{0,64},{32,96},{64,0},{96,32},{1,65},{33,97},{65,1},{97,33},{2,66}... | collective-permute-start | bytes 393224 | tf_op jit(solution)/shard_map/ppermute | solution.py:191
  41.4 9.5 %collective-permute-start.5 = (bf16[32,16,128]{2,1,0:T(8,128)(2,1)}, bf16[32,16,128]{2,1,0:T(8,128)(2,1)}, u32[]{:S(2)}, u32[]{:S(2)}) collective-permute-start(bf16[32,16,128]{2,1,0:T(8,128)(2,1)} %get-tuple-element.53), channel_id=1, source_target_pairs={{0,96},{32,0},{64,32},{96,64},{1,97},{33,1},{65,33},{97,65},{2,98}... | collective-permute-start | bytes 393224 | tf_op jit(solution)/shard_map/ppermute | solution.py:191
  46.4 5.5 %collective-permute-start.10 = (bf16[32,16,128]{2,1,0:T(8,128)(2,1)}, bf16[32,16,128]{2,1,0:T(8,128)(2,1)S(1)}, u32[]{:S(2)}, u32[]{:S(2)}) collective-permute-start(bf16[32,16,128]{2,1,0:T(8,128)(2,1)} %get-tuple-element.60), channel_id=1, source_target_pairs={{0,1},{16,17},{1,0},{17,16},{2,3},{18,19},{3,2},{19,18},{4,5},{20,... | collective-permute-start | bytes 393224 | tf_op jit(solution)/shard_map/ppermute | solution.py:187
  48.5 6.7 %collective-permute-start.11 = (bf16[32,16,128]{2,1,0:T(8,128)(2,1)}, bf16[32,16,128]{2,1,0:T(8,128)(2,1)S(1)}, u32[]{:S(2)}, u32[]{:S(2)}) collective-permute-start(bf16[32,16,128]{2,1,0:T(8,128)(2,1)} %get-tuple-element.61), channel_id=1, source_target_pairs={{0,17},{16,0},{1,16},{17,1},{2,19},{18,2},{3,18},{19,3},{4,21},{20... | collective-permute-start | bytes 393224 | tf_op jit(solution)/shard_map/ppermute | solution.py:187
  50.8 6.3 %collective-permute-start.9 = (bf16[32,16,128]{2,1,0:T(8,128)(2,1)}, bf16[32,16,128]{2,1,0:T(8,128)(2,1)S(1)}, u32[]{:S(2)}, u32[]{:S(2)}) collective-permute-start(bf16[32,16,128]{2,1,0:T(8,128)(2,1)} %get-tuple-element.59), channel_id=1, source_target_pairs={{0,16},{16,1},{1,17},{17,0},{2,18},{18,3},{3,19},{19,2},{4,20},{20... | collective-permute-start | bytes 393224 | tf_op jit(solution)/shard_map/ppermute | solution.py:187
  61.6 6.1 %collective-permute-start.12 = (bf16[2,2,16,8,128]{4,3,2,1,0:T(8,128)(2,1)S(1)}, bf16[2,2,16,8,128]{4,3,2,1,0:T(8,128)(2,1)S(1)}, u32[]{:S(2)}, u32[]{:S(2)}) collective-permute-start(bf16[2,2,16,8,128]{4,3,2,1,0:T(8,128)(2,1)S(1)} %get-tuple-element.63), channel_id=1, source_target_pairs={{0,16},{16,0},{32,48},{48,32},{64,80},{80,64},{96,112},{112,96},{1... | collective-permute-start | bytes 393224 | tf_op jit(solution)/shard_map/ppermute | solution.py:582
  61.7 6.0 %collective-permute-start.13 = (bf16[2,2,16,8,128]{4,3,2,1,0:T(8,128)(2,1)S(1)}, bf16[2,2,16,8,128]{4,3,2,1,0:T(8,128)(2,1)S(1)}, u32[]{:S(2)}, u32[]{:S(2)}) collective-permute-start(bf16[2,2,16,8,128]{4,3,2,1,0:T(8,128)(2,1)S(1)} %get-tuple-element.64), channel_id=1, source_target_pairs={{16,32},{32,16},{48,64},{64,48},{80,96},{96,80},{17,33},{33,17},{4... | collective-permute-start | bytes 393224 | tf_op jit(solution)/shard_map/ppermute | solution.py:583
  62.4 5.3 %collective-permute-start.15 = (bf16[2,2,16,2,128]{4,3,2,1,0:T(2,128)(2,1)S(1)}, bf16[2,2,16,2,128]{4,3,2,1,0:T(2,128)(2,1)S(1)}, u32[]{:S(2)}, u32[]{:S(2)}) collective-permute-start(bf16[2,2,16,2,128]{4,3,2,1,0:T(2,128)(2,1)S(1)} %get-tuple-element.66), channel_id=1, source_target_pairs={{0,17},{1,16},{16,1},{17,0},{32,49},{33,48},{48,33},{49,32},{64,81... | collective-permute-start | bytes 98312 | tf_op jit(solution)/shard_map/ppermute | solution.py:585
  65.6 5.3 %collective-permute-start.14 = (bf16[2,8,16,2,128]{4,3,2,1,0:T(2,128)(2,1)S(1)}, bf16[2,8,16,2,128]{4,3,2,1,0:T(2,128)(2,1)S(1)}, u32[]{:S(2)}, u32[]{:S(2)}) collective-permute-start(bf16[2,8,16,2,128]{4,3,2,1,0:T(2,128)(2,1)S(1)} %get-tuple-element.65), channel_id=1, source_target_pairs={{0,1},{1,0},{2,3},{3,2},{4,5},{5,4},{6,7},{7,6},{8,9},{9,8},{10,11... | collective-permute-start | bytes 393224 | tf_op jit(solution)/shard_map/ppermute | solution.py:584
  71.0 13.5 %collective-permute-start.18 = (bf16[2,12,2,10,128]{4,3,2,1,0:T(8,128)(2,1)S(1)}, bf16[2,12,2,10,128]{4,3,2,1,0:T(8,128)(2,1)S(1)}, u32[]{:S(2)}, u32[]{:S(2)}) collective-permute-start(bf16[2,12,2,10,128]{4,3,2,1,0:T(8,128)(2,1)S(1)} %maximum_maximum_fusion.1), channel_id=1, source_target_pairs={{2,4},{4,2},{6,8},{8,6},{10,12},{12,10},{3,5},{5,3},{7,9},{9,7},{1... | collective-permute-start | bytes 368648 | tf_op jit(solution)/shard_map/ppermute | solution.py:598
  81.2 3.3 %collective-permute-start.17 = (bf16[2,12,2,10,128]{4,3,2,1,0:T(8,128)(2,1)S(1)}, bf16[2,12,2,10,128]{4,3,2,1,0:T(8,128)(2,1)S(1)}, u32[]{:S(2)}, u32[]{:S(2)}) collective-permute-start(bf16[2,12,2,10,128]{4,3,2,1,0:T(8,128)(2,1)S(1)} %maximum_maximum_fusion), channel_id=1, source_target_pairs={{0,2},{2,0},{4,6},{6,4},{8,10},{10,8},{12,14},{14,12},{1,3},{3,1},... | collective-permute-start | bytes 368648 | tf_op jit(solution)/shard_map/ppermute | solution.py:597
  109.1 2.5 %collective-permute-start.19 = (bf16[27,128,128]{2,1,0:T(8,128)(2,1)S(1)}, bf16[27,128,128]{2,1,0:T(8,128)(2,1)S(1)}, u32[]{:S(2)}, u32[]{:S(2)}) collective-permute-start(bf16[27,128,128]{2,1,0:T(8,128)(2,1)S(1)} %get-tuple-element.77), channel_id=1, source_target_pairs={{0,2},{2,0},{1,3},{3,1},{4,6},{6,4},{5,7},{7,5},{8,10},{10,8},{9,1... | collective-permute-start | bytes 2654216 | tf_op jit(solution)/shard_map/ppermute | solution.py:626
  113.2 20.4 %all-to-all-start = ((bf16[16,216,128]{2,1,0:T(8,128)(2,1)}), bf16[16,216,128]{2,1,0:T(8,128)(2,1)}, u32[]{:S(2)}, u32[]{:S(2)}) async-start(bf16[16,216,128]{2,1,0:T(8,128)(2,1)} %bitcast.20), calls=%async_computation | async-start | bytes 1769472 | tf_op jit(solution)/shard_map/all_to_all | solution.py:603
  134.9 6.0 %collective-permute-start.20 = (bf16[224,128]{1,0:T(8,128)(2,1)S(1)}, bf16[224,128]{1,0:T(8,128)(2,1)S(1)}, u32[]{:S(2)}, u32[]{:S(2)}) collective-permute-start(bf16[224,128]{1,0:T(8,128)(2,1)S(1)} %maximum_maximum_fusion.2), channel_id=1, source_target_pairs={{0,8},{4,12},{8,0},{12,4},{1,9},{5,13},{9,1},{13,5},{2,10},{6,14},... | collective-permute-start | bytes 172040 | tf_op jit(solution)/shard_map/ppermute | solution.py:191
  138.2 4.2 %collective-permute-start.21 = (bf16[224,128]{1,0:T(8,128)(2,1)S(1)}, bf16[224,128]{1,0:T(8,128)(2,1)S(1)}, u32[]{:S(2)}, u32[]{:S(2)}) collective-permute-start(bf16[224,128]{1,0:T(8,128)(2,1)S(1)} %maximum_maximum_fusion.2), channel_id=1, source_target_pairs={{0,4},{4,8},{8,12},{12,0},{1,5},{5,9},{9,13},{13,1},{2,6},{6,10},{... | collective-permute-start | bytes 172040 | tf_op jit(solution)/shard_map/ppermute | solution.py:191
  138.9 3.5 %collective-permute-start.22 = (bf16[224,128]{1,0:T(8,128)(2,1)S(1)}, bf16[224,128]{1,0:T(8,128)(2,1)S(1)}, u32[]{:S(2)}, u32[]{:S(2)}) collective-permute-start(bf16[224,128]{1,0:T(8,128)(2,1)S(1)} %maximum_maximum_fusion.2), channel_id=1, source_target_pairs={{0,12},{4,0},{8,4},{12,8},{1,13},{5,1},{9,5},{13,9},{2,14},{6,2},{... | collective-permute-start | bytes 172040 | tf_op jit(solution)/shard_map/ppermute | solution.py:191
  160.3 6.6 %collective-permute-start.23 = (bf16[16,224,128]{2,1,0:T(8,128)(2,1)S(1)}, bf16[16,224,128]{2,1,0:T(8,128)(2,1)S(1)}, u32[]{:S(2)}, u32[]{:S(2)}) collective-permute-start(bf16[16,224,128]{2,1,0:T(8,128)(2,1)S(1)} %all_to_all.10), channel_id=1, source_target_pairs={{0,2},{2,0},{1,3},{3,1},{4,6},{6,4},{5,7},{7,5},{8,10},{10,8},{9,1... | collective-permute-start | bytes 2752520 | tf_op jit(solution)/shard_map/ppermute | solution.py:645
  (24 other events, 150.2 us)

commit v6 on v5

--- a/solution.py
+++ b/solution.py
@@ -89,20 +89,48 @@
     return jnp.where(filled, total, DEAD)
 
 
-def merge_kernel(p0, p1, p2, p3, o0, o1, o2, o3):
-    for shift, out in enumerate((o0, o1, o2, o3)):
-        parts = [part[shift].astype(F32) for part in (p0, p1, p2, p3)]
-        out[...] = added(parts).astype(BF16)
+def merge_kernel(p0, p1, p2, p3, o0, o1, o2, o3, fetched, sums, sems):
+    sources = (p0, p1, p2, p3)
+    copies = [
+        [
+            pltpu.make_async_copy(part.at[shift], fetched.at[shift, n], sems.at[shift, n])
+            for n, part in enumerate(sources)
+        ]
+        for shift in range(4)
+    ]
+    for shift in (1, 2, 3, 0):
+        for copy in copies[shift]:
+            copy.start()
+    stores = []
+    for shift, out in ((1, o1), (2, o2), (3, o3), (0, o0)):
+        for copy in copies[shift]:
+            copy.wait()
+
+        def block(step, carry):
+            at = pl.ds(pl.multiple_of(step * 8, 8), 8)
+            parts = [fetched[shift, n, at].astype(F32) for n in range(4)]
+            sums[shift, at] = added(parts).astype(BF16)
+            return carry
+
+        lax.fori_loop(0, 4, block, 0)
+        stores.append(pltpu.make_async_copy(sums.at[shift], out, sems.at[4, shift]))
+        stores[-1].start()
+    for store in stores:
+        store.wait()
 
 
 def merge_bricks(parts):
     return pl.pallas_call(
         merge_kernel,
         out_shape=(jax.ShapeDtypeStruct((32, 16, 128), BF16),) * 4,
-        grid=(4,),
-        in_specs=[pl.BlockSpec((4, 8, 16, 128), lambda i: (0, i, 0, 0))] * 4,
-        out_specs=(pl.BlockSpec((8, 16, 128), lambda i: (i, 0, 0)),) * 4,
-        compiler_params=pltpu.CompilerParams(vmem_limit_bytes=10 << 20),
+        in_specs=[AN] * 4,
+        out_specs=(AN,) * 4,
+        scratch_shapes=[
+            pltpu.VMEM((4, 4, 32, 16, 128), BF16),
+            pltpu.VMEM((4, 32, 16, 128), BF16),
+            pltpu.SemaphoreType.DMA((5, 4)),
+        ],
+        compiler_params=pltpu.CompilerParams(vmem_limit_bytes=60 << 20),
         cost_estimate=pl.CostEstimate(flops=4 << 20, bytes_accessed=3 << 20, transcendentals=0),
     )(*parts)
 
@@ -174,7 +202,7 @@
         in_specs=[SM] + [VM] * 9,
         out_specs=(VM,) * 6,
         scratch_shapes=[pltpu.VMEM((128, 128), F32), pltpu.VMEM((16, 8, 128), F32)],
-        compiler_params=pltpu.CompilerParams(vmem_limit_bytes=8 << 20),
+        compiler_params=pltpu.CompilerParams(vmem_limit_bytes=60 << 20),
         cost_estimate=pl.CostEstimate(flops=8 << 20, bytes_accessed=2 << 20, transcendentals=0),
     )(where, *parts, out_grad)
 
@@ -307,20 +335,26 @@
     second_hbm,
     act_hbm,
     pre_hbm,
-    own_ref,
-    send_ref,
+    own_hbm,
+    send_hbm,
     cells,
     cots,
     normed3,
     masked3,
     act_t,
     normed_t,
+    row_cells,
+    pair_cells,
+    masked_even,
+    masked_odd,
+    pre_even,
+    pre_odd,
+    found,
     s0, s1, s2, s3, s4, s5, s6, s7,
     first,
     second_t,
     act_ref,
     pre_ref,
-    pre3_ref,
     sems,
 ):
     core = where_ref[1]
@@ -337,8 +371,12 @@
         copy.wait()
     fill(cells, 0, pieces, where_ref, OUT)
     fill(cots, 1, pieces, where_ref, 0.0)
-    z_of = lax.broadcasted_iota(jnp.int32, (256, 128), 0) % 16
-    inside = (z_of >= 2) & (z_of < 10)
+    act_t[:, 0:128] = jnp.zeros((128, 128), BF16)
+    act_t[:, 1408:1536] = jnp.zeros((128, 128), BF16)
+
+    def turned_columns(target, x, values):
+        inner = jnp.where((x >= 2) & (x < 10), values, 0.0).astype(BF16)
+        target[:, pl.ds(pl.multiple_of(x * 128, 128), 128)] = inner.T
 
     def prepare(x, carry):
         values = cells[x].reshape(320, 128)
@@ -347,23 +385,17 @@
         inverse = lax.rsqrt(jnp.mean(held * held, axis=-1, keepdims=True) + epsilon)
         normed = held * inverse * gain[...]
         normed3[x] = neighbours(normed).reshape(20, 16, 384)
+        row_cells[...] = normed.reshape(20, 16, 128)
+        turned_columns(normed_t, x, row_cells[2:18, 2:10, :].reshape(128, 128))
         masked = jnp.where(live, cots[x].reshape(320, 128), 0.0)
         masked3[x] = neighbours(masked).reshape(20, 16, 384)
+        cots[x] = masked.reshape(20, 16, 128)
+        parts = [cots[x, :, 1 + k : 9 + k, :].reshape(160, 128) for k in range(3)]
+        masked_even[x] = jnp.concatenate([part.astype(BF16) for part in parts], axis=1)
+        masked_odd[x] = jnp.concatenate([part[8:152].astype(BF16) for part in parts], axis=1)
         return carry
 
     lax.fori_loop(0, 12, prepare, 0)
-
-    for turned_ref in (normed_t, act_t):
-        turned_ref[:, 0:512] = jnp.zeros((128, 512), BF16)
-        turned_ref[:, 2560:3072] = jnp.zeros((128, 512), BF16)
-
-    def turn(x, carry):
-        normed = normed3[x + 2, 2:18, :, 128:256].reshape(256, 128).astype(F32)
-        columns = pl.ds(pl.multiple_of(x * 256 + 512, 256), 256)
-        normed_t[:, columns] = jnp.where(inside, normed, 0.0).T.astype(BF16)
-        return carry
-
-    lax.fori_loop(0, 8, turn, 0)
     for copy in copies[8:]:
         copy.wait()
 
@@ -375,11 +407,19 @@
         sigmoid = jax.nn.sigmoid(before)
         active = before * sigmoid
         act_ref[pl.ds(x, 2)] = active.astype(BF16).reshape(2, 18, 16, 128)
+        pair_cells[...] = active.reshape(2, 18, 16, 128)
+        for n in range(2):
+            inner = pair_cells[n, 1:17, 2:10, :].reshape(128, 128)
+            turned_columns(act_t, x + 1 + n, inner)
         active_grad = convolve_pair(masked3, x, 18, second_t)
         pre = active_grad * sigmoid * (1.0 + before * (1.0 - sigmoid))
         pre = jnp.where(values > -LIMIT, pre, 0.0)
         pre_ref[pl.ds(x, 2)] = pre.astype(BF16).reshape(2, 18, 16, 128)
-        pre3_ref[pl.ds(x, 2)] = neighbours(pre).reshape(2, 18, 16, 384)
+        pair_cells[...] = pre.reshape(2, 18, 16, 128)
+        for n in range(2):
+            parts = [pair_cells[n, :, 1 + k : 9 + k, :].reshape(144, 128) for k in range(3)]
+            pre_even[x + n] = jnp.concatenate([part.astype(BF16) for part in parts], axis=1)
+            pre_odd[x + n] = jnp.concatenate([part[8:136].astype(BF16) for part in parts], axis=1)
         return carry
 
     lax.fori_loop(0, 5, convolve, 0)
@@ -390,33 +430,27 @@
     for copy in results:
         copy.start()
 
-    def turn_active(x, carry):
-        active = act_ref[x + 1, 1:17].reshape(256, 128).astype(F32)
-        columns = pl.ds(pl.multiple_of(x * 256 + 512, 256), 256)
-        act_t[:, columns] = jnp.where(inside, active, 0.0).T.astype(BF16)
-        return carry
-
-    lax.fori_loop(0, 8, turn_active, 0)
-
-    for which, left, right, start in ((1, act_t, masked3, 1), (0, normed_t, pre3_ref, 0)):
-        for target, here in ((own_ref, which), (send_ref, 1 - which)):
-
-            @pl.when(core == here)
-            def _():
-                def weights(j, carry):
-                    cot = window_rows(right, start, start + 2 - j, 10, 16)
-                    own = [left[:, 256 * (i + 0) : 256 * (i + 10)] for i in range(3)]
-                    own = jnp.concatenate(own, axis=0)
-                    total = jnp.dot(own, cot, preferred_element_type=F32).astype(BF16)
-                    for i in range(3):
-                        for k in range(3):
-                            target[i * 9 + j * 3 + k] = total[
-                                i * 128 : (i + 1) * 128, (2 - k) * 128 : (3 - k) * 128
-                            ]
-                    return carry
-
-                lax.fori_loop(0, 3, weights, 0)
-
+    for which, left, sides in (
+        (1, act_t, ((masked_odd, 16), (masked_even, 16), (masked_odd, 0))),
+        (0, normed_t, ((pre_even, 16), (pre_odd, 0), (pre_even, 0))),
+    ):
+        own = jnp.concatenate([left[:, 128 * i : 128 * (i + 10)] for i in range(3)], axis=0)
+        for j, (cots_at, row) in enumerate(sides):
+            start = which
+            cot = cots_at[start : start + 10, row : row + 128, :].reshape(1280, 384)
+            total = jnp.dot(own, cot, preferred_element_type=F32).astype(BF16)
+            for i in range(3):
+                for k in range(3):
+                    found[which, i * 9 + j * 3 + k] = total[
+                        i * 128 : (i + 1) * 128, (2 - k) * 128 : (3 - k) * 128
+                    ]
+
+    results += [
+        pltpu.make_async_copy(found.at[core], own_hbm, sems.at[2]),
+        pltpu.make_async_copy(found.at[1 - core], send_hbm, sems.at[3]),
+    ]
+    for copy in results[2:]:
+        copy.start()
     for copy in results:
         copy.wait()
 
@@ -431,23 +465,29 @@
             jax.ShapeDtypeStruct((27, 128, 128), BF16),
         ),
         in_specs=[SM, VM] + [AN] * 8 + [HB] * 2,
-        out_specs=(HB, HB, VM, VM),
+        out_specs=(HB, HB, HB, HB),
         scratch_shapes=[
             pltpu.VMEM((12, 20, 16, 128), F32),
             pltpu.VMEM((12, 20, 16, 128), F32),
             pltpu.VMEM((12, 20, 16, 384), BF16),
             pltpu.VMEM((12, 20, 16, 384), BF16),
-            pltpu.VMEM((128, 3072), BF16),
-            pltpu.VMEM((128, 3072), BF16),
+            pltpu.VMEM((128, 1536), BF16),
+            pltpu.VMEM((128, 1536), BF16),
+            pltpu.VMEM((20, 16, 128), F32),
+            pltpu.VMEM((2, 18, 16, 128), F32),
+            pltpu.VMEM((12, 160, 384), BF16),
+            pltpu.VMEM((12, 144, 384), BF16),
+            pltpu.VMEM((10, 144, 384), BF16),
+            pltpu.VMEM((10, 128, 384), BF16),
+            pltpu.VMEM((2, 27, 128, 128), BF16),
             *[pltpu.VMEM(shape, BF16) for shape in PIECES],
             pltpu.VMEM((4608, 256), BF16),
             pltpu.VMEM((4608, 256), BF16),
             pltpu.VMEM((10, 18, 16, 128), BF16),
             pltpu.VMEM((10, 18, 16, 128), BF16),
-            pltpu.VMEM((10, 18, 16, 384), BF16),
             pltpu.SemaphoreType.DMA((10,)),
         ],
-        compiler_params=pltpu.CompilerParams(vmem_limit_bytes=34 << 20),
+        compiler_params=pltpu.CompilerParams(vmem_limit_bytes=60 << 20),
         cost_estimate=pl.CostEstimate(flops=10 << 30, bytes_accessed=8 << 20, transcendentals=1 << 20),
     )(where, gain, *pieces, first, second_t)
 
@@ -548,7 +588,7 @@
             pltpu.VMEM((2, 16, 16, 128), F32),
             pltpu.SemaphoreType.DMA((5,)),
         ],
-        compiler_params=pltpu.CompilerParams(vmem_limit_bytes=20 << 20),
+        compiler_params=pltpu.CompilerParams(vmem_limit_bytes=60 << 20),
         cost_estimate=pl.CostEstimate(flops=8 << 30, bytes_accessed=6 << 20, transcendentals=4096),
     )(gain, both, act, pre, second, first_t)
 
@@ -558,13 +598,11 @@
 
 
 def add_pair(own, other):
-    spec = pl.BlockSpec((9, 128, 128), lambda i: (i, 0, 0))
     return pl.pallas_call(
         add_kernel,
         out_shape=jax.ShapeDtypeStruct((27, 128, 128), BF16),
-        grid=(3,),
-        in_specs=[spec, spec],
-        out_specs=spec,
+        in_specs=[VM, VM],
+        out_specs=VM,
         compiler_params=pltpu.CompilerParams(vmem_limit_bytes=6 << 20),
         cost_estimate=pl.CostEstimate(flops=1 << 19, bytes_accessed=3 << 20, transcendentals=0),
     )(own, other)

time: 170 us -> 166 us (0.976)
  Pallas kernels: 47.5 us -> 42.3 us
  starting transfers between devices: 52.9 us -> 55.4 us
  local copies, waits for them, and re-layouts: 18.5 us -> 16.4 us
    pallas_call x1, Pallas kernels: 22.8 us -> 18.6 us  [grads_call(): pl.pallas_call(grads_kernel, out_shape=(jax.ShapeDtypeStruct((10, 18, 16,...]
    all_to_all x1, starting transfers between devices: 6.66 us -> 10.7 us  [exchange(): return lax.all_to_all(values, axes, split_axis=0, concat_axis=0, tiled=True)]
    unnamed x48 -> x44, local copies, waits for them, and re-layouts: 15 us -> 10.9 us
    ppermute x9, starting transfers between devices: 16 us -> 13.9 us  [along(): return lax.ppermute(value, axis, [(i, (i + shift) % 4) for i in range(4)])]
    pallas_call x2, Pallas kernels: 5.88 us -> 3.91 us  [place_bricks(): pl.pallas_call(functools.partial(place_kernel, half), out_shape=(jax.Shap...]
  transfers between devices with their start and end apart: 25 -> 25, of which waited for: 9 -> 9; matrix products, arithmetic and copies ran while one was open for 8% -> 12% of each run, Pallas kernels for 11% -> 11%
where the time goes in v6:
time: 166 us; the launch traced here: 165 us
  starting transfers between devices  55.4 us (33%)
  Pallas kernels  42.3 us (25%)
  waiting for transfers between devices  19.4 us (12%)
  local copies, waits for them, and re-layouts  16.4 us (10%)
  blocking collectives  16.1 us (10%)
  other arithmetic  14.2 us (9%)
    pallas_call x1, Pallas kernels, grads_call(): pl.pallas_call(grads_kernel, out_shape=(jax.ShapeDtypeStruct((10, 18, 16,...  18.6 us
    all_to_all x1, blocking collectives, exchange(): return lax.all_to_all(values, axes, split_axis=0, concat_axis=0, tiled=True)  16.1 us
    ppermute x9, starting transfers between devices, along(): return lax.ppermute(value, axis, [(i, (i + shift) % 4) for i in range(4)])  13.9 us
    ppermute x1, starting transfers between devices, edges(): y_two = lax.ppermute(wide(second_y), GY, SECOND)  11.3 us
    unnamed x44, local copies, waits for them, and re-layouts  10.9 us
    all_to_all x1, starting transfers between devices, exchange(): return lax.all_to_all(values, axes, split_axis=0, concat_axis=0, tiled=True)  10.7 us
    pallas_call x1, Pallas kernels, outputs_call(): pl.pallas_call(outputs_kernel, out_shape=(jax.ShapeDtypeStruct((8, 16, 8,...  10.4 us
    ppermute x6, starting transfers between devices, along_x(): return lax.ppermute(value, ('xl', 'xh'), pairs)  8.44 us
  transfers between devices with their start and end apart: 25, of which 9 were waited for; matrix products, arithmetic and copies ran while one was open for 12% of the time, Pallas kernels for 11%

profile of v6, /device:TPU:1, one launch (start us, length us, event | category | flops | bytes accessed | tf_op | source)
XLA Modules:
  0.0 164.8 jit_solution(7866136711030998355)
XLA Ops:
  8.4 2.5 %collective-permute-start.1 = (bf16[4,32,16,128]{3,2,1,0:T(8,128)(2,1)S(1)}, bf16[4,32,16,128]{3,2,1,0:T(8,128)(2,1)}, u32[]{:S(2)}, u32[]{:S(2)}) collective-permute-start(bf16[4,32,16,128]{3,2,1,0:T(8,128)(2,1)S(1)} %get-tuple-element.44), channel_id=1, source_target_pairs={{0,1},{16,17},{1,0},{17,16},{2,3},{18,19},{3,2},{19,18},{4,5},{20,... | collective-permute-start | bytes 1572872 | tf_op jit(solution)/shard_map/ppermute | solution.py:215
  16.1 2.6 %collective-permute-start.7 = (bf16[4,32,16,128]{3,2,1,0:T(8,128)(2,1)S(1)}, bf16[4,32,16,128]{3,2,1,0:T(8,128)(2,1)}, u32[]{:S(2)}, u32[]{:S(2)}) collective-permute-start(bf16[4,32,16,128]{3,2,1,0:T(8,128)(2,1)S(1)} %get-tuple-element.56), channel_id=1, source_target_pairs={{0,64},{32,96},{64,0},{96,32},{1,65},{33,97},{65,1},{97,33},{2,66}... | collective-permute-start | bytes 1572872 | tf_op jit(solution)/shard_map/ppermute | solution.py:219
  18.7 2.2 %copy.12 = bf16[27,128,128]{1,2,0:T(8,128)(2,1)} copy(bf16[27,128,128]{2,1,0:T(8,128)(2,1)} %param.10) | data formatting | bytes 1769472 | tf_op args[3]
  20.9 2.2 %rev.6 = bf16[27,128,128]{1,2,0:T(8,128)(2,1)} reverse(bf16[27,128,128]{1,2,0:T(8,128)(2,1)} %copy.12), dimensions={0} | reverse | bytes 1769472 | tf_op jit(solution)/shard_map/rev | solution.py:264
  23.0 2.2 %copy.13 = bf16[27,128,128]{1,2,0:T(8,128)(2,1)} copy(bf16[27,128,128]{2,1,0:T(8,128)(2,1)} %param.11) | data formatting | bytes 1769472 | tf_op args[4]
  25.2 2.2 %rev.7 = bf16[27,128,128]{1,2,0:T(8,128)(2,1)} reverse(bf16[27,128,128]{1,2,0:T(8,128)(2,1)} %copy.13), dimensions={0} | reverse | bytes 1769472 | tf_op jit(solution)/shard_map/rev | solution.py:264
  27.4 3.2 %fusion.10 = bf16[4,3,384,256]{3,2,1,0:T(8,128)(2,1)} fusion(bf16[3,3,384,128]{3,2,1,0:T(8,128)(2,1)} %bitcast.55), kind=kLoop, calls=%fused_computation.12 | loop fusion | flops 9437184 | bytes 3244032 | tf_op jit(solution)/shard_map/concatenate | solution.py:260
  36.8 2.5 %shard_map.111 = (bf16[32,16,128]{2,1,0:T(8,128)(2,1)}, bf16[32,16,128]{2,1,0:T(8,128)(2,1)}, bf16[32,16,128]{2,1,0:T(8,128)(2,1)}, bf16[32,16,128]{2,1,0:T(8,128)(2,1)}) custom-call(bf16[4,32,16,128]{3,2,1,0:T(8,128)(2,1)} %copy-done.3, bf16[4,32,16,128]{3,2,1,0:T(8,128)(2,1)} %collective-permute-done.p1, ...), custom_call_target="tpu_custom_call" | custom-call | flops 4194304 | bytes 3145728 | tf_op jit(solution)/shard_map/pallas_call | solution.py:123
  44.4 2.5 %shard_map.113 = (bf16[32,16,128]{2,1,0:T(8,128)(2,1)}, bf16[32,16,128]{2,1,0:T(8,128)(2,1)}, bf16[32,16,128]{2,1,0:T(8,128)(2,1)}, bf16[32,16,128]{2,1,0:T(8,128)(2,1)}) custom-call(bf16[4,32,16,128]{3,2,1,0:T(8,128)(2,1)} %copy-done.2, bf16[4,32,16,128]{3,2,1,0:T(8,128)(2,1)} %collective-permute-done.6.p1, ...), custom_call_target="tpu_custom_call" | custom-call | flops 4194304 | bytes 3145728 | tf_op jit(solution)/shard_map/pallas_call | solution.py:123
  47.3 2.5 %collective-permute-start.11 = (bf16[32,16,128]{2,1,0:T(8,128)(2,1)}, bf16[32,16,128]{2,1,0:T(8,128)(2,1)S(1)}, u32[]{:S(2)}, u32[]{:S(2)}) collective-permute-start(bf16[32,16,128]{2,1,0:T(8,128)(2,1)} %get-tuple-element.61), channel_id=1, source_target_pairs={{0,17},{16,0},{1,16},{17,1},{2,19},{18,2},{3,18},{19,3},{4,21},{20... | collective-permute-start | bytes 393224 | tf_op jit(solution)/shard_map/ppermute | solution.py:215
  52.6 2.4 %collective-permute-done.9.b1 = bf16[32,16,128]{2,1,0:T(8,128)(2,1)S(1)} collective-permute-done((bf16[32,16,128]{2,1,0:T(8,128)(2,1)}, bf16[32,16,128]{2,1,0:T(8,128)(2,1)S(1)}, u32[]{:S(2)}, u32[]{:S(2)}) %collective-permute-start.9) | collective-permute-done | bytes 131104 | tf_op jit(solution)/shard_map/ppermute | solution.py:215
  55.6 3.1 %shard_map.114 = (bf16[2,8,16,8,128]{4,3,2,1,0:T(8,128)(2,1)}, bf16[2,2,16,8,128]{4,3,2,1,0:T(8,128)(2,1)}, bf16[2,2,16,8,128]{4,3,2,1,0:T(8,128)(2,1)}, bf16[2,...) custom-call(s32[4]{0:T(128)} %pad_add_fusion.where_ref, ...), custom_call_target="tpu_custom_call" | custom-call | flops 8388608 | bytes 2097152 | tf_op jit(solution)/shard_map/pallas_call | solution.py:192
  59.5 2.4 %collective-permute-start.15 = (bf16[2,2,16,2,128]{4,3,2,1,0:T(2,128)(2,1)}, bf16[2,2,16,2,128]{4,3,2,1,0:T(2,128)(2,1)S(1)}, u32[]{:S(2)}, u32[]{:S(2)}) collective-permute-start(bf16[2,2,16,2,128]{4,3,2,1,0:T(2,128)(2,1)} %get-tuple-element.66), channel_id=1, source_target_pairs={{0,17},{1,16},{16,1},{17,0},{32,49},{33,48},{48,33},{49,32},{64,81... | collective-permute-start | bytes 98312 | tf_op jit(solution)/shard_map/ppermute | solution.py:623
  61.9 2.2 %collective-permute-start.14 = (bf16[2,8,16,2,128]{4,3,2,1,0:T(2,128)(2,1)}, bf16[2,8,16,2,128]{4,3,2,1,0:T(2,128)(2,1)S(1)}, u32[]{:S(2)}, u32[]{:S(2)}) collective-permute-start(bf16[2,8,16,2,128]{4,3,2,1,0:T(2,128)(2,1)} %get-tuple-element.65), channel_id=1, source_target_pairs={{0,1},{1,0},{2,3},{3,2},{4,5},{5,4},{6,7},{7,6},{8,9},{9,8},{10,11... | collective-permute-start | bytes 393224 | tf_op jit(solution)/shard_map/ppermute | solution.py:622
  67.5 11.3 %collective-permute-start.18 = (bf16[2,12,2,10,128]{4,3,2,1,0:T(8,128)(2,1)S(1)}, bf16[2,12,2,10,128]{4,3,2,1,0:T(8,128)(2,1)S(1)}, u32[]{:S(2)}, u32[]{:S(2)}) collective-permute-start(bf16[2,12,2,10,128]{4,3,2,1,0:T(8,128)(2,1)S(1)} %maximum_maximum_fusion.1), channel_id=1, source_target_pairs={{2,4},{4,2},{6,8},{8,6},{10,12},{12,10},{3,5},{5,3},{7,9},{9,7},{1... | collective-permute-start | bytes 368648 | tf_op jit(solution)/shard_map/ppermute | solution.py:636
  78.9 3.2 %collective-permute-done.18.p7 = bf16[2,12,2,10,128]{4,3,2,1,0:T(8,128)(2,1)S(1)} collective-permute-done((bf16[2,12,2,10,128]{4,3,2,1,0:T(8,128)(2,1)S(1)}, bf16[2,12,2,10,128]{4,3,2,1,0:T(8,128)(2,1)S(1)}, u32[]{:S(2)}, u32[]{:S(2)}) %collective-permute-start.18) | collective-permute-done | bytes 122912 | tf_op jit(solution)/shard_map/ppermute | solution.py:636
  82.9 18.6 %shard_map.115 = (bf16[10,18,16,128]{3,2,1,0:T(8,128)(2,1)}, bf16[10,18,16,128]{3,2,1,0:T(8,128)(2,1)}, bf16[27,128,128]{2,1,0:T(8,128)(2,1)}, bf16[27,128,128]{2,1,0:T(8,128)(2,1)}) custom-call(s32[4]{0:T(128)} %pad_add_fusion.where_ref, f32[1,128]{1,0:T(1,128)} %bitcast.64, bf16[2,8,16,8,128]{4,3,2,1,0:T(8,128)(2,1)} %get-tuple-element.62.p0.both_hbm, ...), custom_call_target="tpu_custom_call" | custom-call | flops 10737418240 | bytes 8388608 | tf_op jit(solution)/shard_map/pallas_call | solution.py:459
  101.6 2.5 %collective-permute-done.19.other_ref = bf16[27,128,128]{2,1,0:T(8,128)(2,1)S(1)} collective-permute-done((bf16[27,128,128]{2,1,0:T(8,128)(2,1)}, bf16[27,128,128]{2,1,0:T(8,128)(2,1)S(1)}, u32[]{:S(2)}, u32[]{:S(2)}) %collective-permute-start.19) | collective-permute-done | bytes 884768 | tf_op jit(solution)/shard_map/ppermute | solution.py:664
  106.5 10.7 %all-to-all-start = ((bf16[16,216,128]{2,1,0:T(8,128)(2,1)}), bf16[16,216,128]{2,1,0:T(8,128)(2,1)S(1)}, u32[]{:S(2)}, u32[]{:S(2)}) async-start(bf16[16,216,128]{2,1,0:T(8,128)(2,1)} %bitcast.20), calls=%async_computation | async-start | bytes 1769472 | tf_op jit(solution)/shard_map/all_to_all | solution.py:641
  117.2 10.4 %shard_map.116 = (bf16[8,16,8,128]{3,2,1,0:T(8,128)(2,1)}, bf16[8,16,8,128]{3,2,1,0:T(8,128)(2,1)}, f32[8,128]{1,0:T(8,128)}) custom-call(f32[1,128]{1,0:T(1,128)} %bitcast.65, bf16[2,8,16,8,128]{4,3,2,1,0:T(8,128)(2,1)} %get-tuple-element.62.p0.both_hbm, bf16[10,18,16,128]{3,2,1,0:T(8,128)(2,1)} %get-tuple-element.70.act_hbm, ...), custom_call_target="tpu_custom_call" | custom-call | flops 8589934592 | bytes 6291456 | tf_op jit(solution)/shard_map/pallas_call | solution.py:571
  128.4 2.5 %all-to-all-done = bf16[16,216,128]{2,1,0:T(8,128)(2,1)S(1)} async-done(((bf16[16,216,128]{2,1,0:T(8,128)(2,1)}), bf16[16,216,128]{2,1,0:T(8,128)(2,1)S(1)}, u32[]{:S(2)}, u32[]{:S(2)}) %all-to-all-start) | async-done | bytes 884768 | tf_op jit(solution)/shard_map/all_to_all | solution.py:641
  131.1 3.3 %collective-permute-start.20 = (bf16[224,128]{1,0:T(8,128)(2,1)S(1)}, bf16[224,128]{1,0:T(8,128)(2,1)S(1)}, u32[]{:S(2)}, u32[]{:S(2)}) collective-permute-start(bf16[224,128]{1,0:T(8,128)(2,1)S(1)} %maximum_maximum_fusion.2), channel_id=1, source_target_pairs={{0,8},{4,12},{8,0},{12,4},{1,9},{5,13},{9,1},{13,5},{2,10},{6,14},... | collective-permute-start | bytes 172040 | tf_op jit(solution)/shard_map/ppermute | solution.py:219
  139.0 16.1 %all_to_all.10 = bf16[16,224,128]{2,1,0:T(8,128)(2,1)S(1)} all-to-all(bf16[16,224,128]{2,1,0:T(8,128)(2,1)S(1)} %broadcast_in_dim.2), channel_id=1, replica_groups=mesh['y'=4,'xl'=2,'z'=4,'c'=2,'xh'=2] {'y','xl','xh'}, dimensions={0} | all-to-all | bytes 1835008 | tf_op jit(solution)/shard_map/all_to_all | solution.py:641
  155.1 4.9 %collective-permute-start.23 = (bf16[16,224,128]{2,1,0:T(8,128)(2,1)S(1)}, bf16[16,224,128]{2,1,0:T(8,128)(2,1)S(1)}, u32[]{:S(2)}, u32[]{:S(2)}) collective-permute-start(bf16[16,224,128]{2,1,0:T(8,128)(2,1)S(1)} %all_to_all.10), channel_id=1, source_target_pairs={{0,2},{2,0},{1,3},{3,1},{4,6},{6,4},{5,7},{7,5},{8,10},{10,8},{9,1... | collective-permute-start | bytes 2752520 | tf_op jit(solution)/shard_map/ppermute | solution.py:683
  (112 shorter events, 45.5 us)
Async XLA Ops:
  6.3 25.9 %collective-permute-start = (bf16[4,32,16,128]{3,2,1,0:T(8,128)(2,1)S(1)}, bf16[4,32,16,128]{3,2,1,0:T(8,128)(2,1)}, u32[]{:S(2)}, u32[]{:S(2)}) collective-permute-start(bf16[4,32,16,128]{3,2,1,0:T(8,128)(2,1)S(1)} %get-tuple-element.43), channel_id=1, source_target_pairs={{0,16},{16,1},{1,17},{17,0},{2,18},{18,3},{3,19},{19,2},{4,20},{20... | collective-permute-start | bytes 1572872 | tf_op jit(solution)/shard_map/ppermute | solution.py:215
  8.4 28.4 %collective-permute-start.1 = (bf16[4,32,16,128]{3,2,1,0:T(8,128)(2,1)S(1)}, bf16[4,32,16,128]{3,2,1,0:T(8,128)(2,1)}, u32[]{:S(2)}, u32[]{:S(2)}) collective-permute-start(bf16[4,32,16,128]{3,2,1,0:T(8,128)(2,1)S(1)} %get-tuple-element.44), channel_id=1, source_target_pairs={{0,1},{16,17},{1,0},{17,16},{2,3},{18,19},{3,2},{19,18},{4,5},{20,... | collective-permute-start | bytes 1572872 | tf_op jit(solution)/shard_map/ppermute | solution.py:215
  10.8 26.0 %collective-permute-start.2 = (bf16[4,32,16,128]{3,2,1,0:T(8,128)(2,1)S(1)}, bf16[4,32,16,128]{3,2,1,0:T(8,128)(2,1)}, u32[]{:S(2)}, u32[]{:S(2)}) collective-permute-start(bf16[4,32,16,128]{3,2,1,0:T(8,128)(2,1)S(1)} %get-tuple-element.45), channel_id=1, source_target_pairs={{0,17},{16,0},{1,16},{17,1},{2,19},{18,2},{3,18},{19,3},{4,21},{20... | collective-permute-start | bytes 1572872 | tf_op jit(solution)/shard_map/ppermute | solution.py:215
  14.8 25.8 %collective-permute-start.6 = (bf16[4,32,16,128]{3,2,1,0:T(8,128)(2,1)S(1)}, bf16[4,32,16,128]{3,2,1,0:T(8,128)(2,1)}, u32[]{:S(2)}, u32[]{:S(2)}) collective-permute-start(bf16[4,32,16,128]{3,2,1,0:T(8,128)(2,1)S(1)} %get-tuple-element.55), channel_id=1, source_target_pairs={{0,32},{32,64},{64,96},{96,0},{1,33},{33,65},{65,97},{97,1},{2,34}... | collective-permute-start | bytes 1572872 | tf_op jit(solution)/shard_map/ppermute | solution.py:219
  16.1 26.2 %collective-permute-start.7 = (bf16[4,32,16,128]{3,2,1,0:T(8,128)(2,1)S(1)}, bf16[4,32,16,128]{3,2,1,0:T(8,128)(2,1)}, u32[]{:S(2)}, u32[]{:S(2)}) collective-permute-start(bf16[4,32,16,128]{3,2,1,0:T(8,128)(2,1)S(1)} %get-tuple-element.56), channel_id=1, source_target_pairs={{0,64},{32,96},{64,0},{96,32},{1,65},{33,97},{65,1},{97,33},{2,66}... | collective-permute-start | bytes 1572872 | tf_op jit(solution)/shard_map/ppermute | solution.py:219
  32.3 11.3 %collective-permute-start.8 = (bf16[4,32,16,128]{3,2,1,0:T(8,128)(2,1)S(1)}, bf16[4,32,16,128]{3,2,1,0:T(8,128)(2,1)S(1)}, u32[]{:S(2)}, u32[]{:S(2)}) collective-permute-start(bf16[4,32,16,128]{3,2,1,0:T(8,128)(2,1)S(1)} %get-tuple-element.57), channel_id=1, source_target_pairs={{0,96},{32,0},{64,32},{96,64},{1,97},{33,1},{65,33},{97,65},{2,98}... | collective-permute-start | bytes 1572872 | tf_op jit(solution)/shard_map/ppermute | solution.py:219
  39.3 10.4 %collective-permute-start.3 = (bf16[32,16,128]{2,1,0:T(8,128)(2,1)}, bf16[32,16,128]{2,1,0:T(8,128)(2,1)S(1)}, u32[]{:S(2)}, u32[]{:S(2)}) collective-permute-start(bf16[32,16,128]{2,1,0:T(8,128)(2,1)} %get-tuple-element.51), channel_id=1, source_target_pairs={{0,32},{32,64},{64,96},{96,0},{1,33},{33,65},{65,97},{97,1},{2,34}... | collective-permute-start | bytes 393224 | tf_op jit(solution)/shard_map/ppermute | solution.py:219
  39.8 10.6 %collective-permute-start.4 = (bf16[32,16,128]{2,1,0:T(8,128)(2,1)}, bf16[32,16,128]{2,1,0:T(8,128)(2,1)S(1)}, u32[]{:S(2)}, u32[]{:S(2)}) collective-permute-start(bf16[32,16,128]{2,1,0:T(8,128)(2,1)} %get-tuple-element.52), channel_id=1, source_target_pairs={{0,64},{32,96},{64,0},{96,32},{1,65},{33,97},{65,1},{97,33},{2,66}... | collective-permute-start | bytes 393224 | tf_op jit(solution)/shard_map/ppermute | solution.py:219
  40.6 9.8 %collective-permute-start.5 = (bf16[32,16,128]{2,1,0:T(8,128)(2,1)}, bf16[32,16,128]{2,1,0:T(8,128)(2,1)S(1)}, u32[]{:S(2)}, u32[]{:S(2)}) collective-permute-start(bf16[32,16,128]{2,1,0:T(8,128)(2,1)} %get-tuple-element.53), channel_id=1, source_target_pairs={{0,96},{32,0},{64,32},{96,64},{1,97},{33,1},{65,33},{97,65},{2,98}... | collective-permute-start | bytes 393224 | tf_op jit(solution)/shard_map/ppermute | solution.py:219
  47.0 5.6 %collective-permute-start.10 = (bf16[32,16,128]{2,1,0:T(8,128)(2,1)}, bf16[32,16,128]{2,1,0:T(8,128)(2,1)S(1)}, u32[]{:S(2)}, u32[]{:S(2)}) collective-permute-start(bf16[32,16,128]{2,1,0:T(8,128)(2,1)} %get-tuple-element.60), channel_id=1, source_target_pairs={{0,1},{16,17},{1,0},{17,16},{2,3},{18,19},{3,2},{19,18},{4,5},{20,... | collective-permute-start | bytes 393224 | tf_op jit(solution)/shard_map/ppermute | solution.py:215
  47.3 5.3 %collective-permute-start.11 = (bf16[32,16,128]{2,1,0:T(8,128)(2,1)}, bf16[32,16,128]{2,1,0:T(8,128)(2,1)S(1)}, u32[]{:S(2)}, u32[]{:S(2)}) collective-permute-start(bf16[32,16,128]{2,1,0:T(8,128)(2,1)} %get-tuple-element.61), channel_id=1, source_target_pairs={{0,17},{16,0},{1,16},{17,1},{2,19},{18,2},{3,18},{19,3},{4,21},{20... | collective-permute-start | bytes 393224 | tf_op jit(solution)/shard_map/ppermute | solution.py:215
  49.8 5.2 %collective-permute-start.9 = (bf16[32,16,128]{2,1,0:T(8,128)(2,1)}, bf16[32,16,128]{2,1,0:T(8,128)(2,1)S(1)}, u32[]{:S(2)}, u32[]{:S(2)}) collective-permute-start(bf16[32,16,128]{2,1,0:T(8,128)(2,1)} %get-tuple-element.59), channel_id=1, source_target_pairs={{0,16},{16,1},{1,17},{17,0},{2,18},{18,3},{3,19},{19,2},{4,20},{20... | collective-permute-start | bytes 393224 | tf_op jit(solution)/shard_map/ppermute | solution.py:215
  58.8 6.9 %collective-permute-start.12 = (bf16[2,2,16,8,128]{4,3,2,1,0:T(8,128)(2,1)}, bf16[2,2,16,8,128]{4,3,2,1,0:T(8,128)(2,1)S(1)}, u32[]{:S(2)}, u32[]{:S(2)}) collective-permute-start(bf16[2,2,16,8,128]{4,3,2,1,0:T(8,128)(2,1)} %get-tuple-element.63), channel_id=1, source_target_pairs={{0,16},{16,0},{32,48},{48,32},{64,80},{80,64},{96,112},{112,96},{1... | collective-permute-start | bytes 393224 | tf_op jit(solution)/shard_map/ppermute | solution.py:620
  58.8 6.9 %collective-permute-start.13 = (bf16[2,2,16,8,128]{4,3,2,1,0:T(8,128)(2,1)}, bf16[2,2,16,8,128]{4,3,2,1,0:T(8,128)(2,1)S(1)}, u32[]{:S(2)}, u32[]{:S(2)}) collective-permute-start(bf16[2,2,16,8,128]{4,3,2,1,0:T(8,128)(2,1)} %get-tuple-element.64), channel_id=1, source_target_pairs={{16,32},{32,16},{48,64},{64,48},{80,96},{96,80},{17,33},{33,17},{4... | collective-permute-start | bytes 393224 | tf_op jit(solution)/shard_map/ppermute | solution.py:621
  59.5 6.1 %collective-permute-start.15 = (bf16[2,2,16,2,128]{4,3,2,1,0:T(2,128)(2,1)}, bf16[2,2,16,2,128]{4,3,2,1,0:T(2,128)(2,1)S(1)}, u32[]{:S(2)}, u32[]{:S(2)}) collective-permute-start(bf16[2,2,16,2,128]{4,3,2,1,0:T(2,128)(2,1)} %get-tuple-element.66), channel_id=1, source_target_pairs={{0,17},{1,16},{16,1},{17,0},{32,49},{33,48},{48,33},{49,32},{64,81... | collective-permute-start | bytes 98312 | tf_op jit(solution)/shard_map/ppermute | solution.py:623
  61.9 5.5 %collective-permute-start.14 = (bf16[2,8,16,2,128]{4,3,2,1,0:T(2,128)(2,1)}, bf16[2,8,16,2,128]{4,3,2,1,0:T(2,128)(2,1)S(1)}, u32[]{:S(2)}, u32[]{:S(2)}) collective-permute-start(bf16[2,8,16,2,128]{4,3,2,1,0:T(2,128)(2,1)} %get-tuple-element.65), channel_id=1, source_target_pairs={{0,1},{1,0},{2,3},{3,2},{4,5},{5,4},{6,7},{7,6},{8,9},{9,8},{10,11... | collective-permute-start | bytes 393224 | tf_op jit(solution)/shard_map/ppermute | solution.py:622
  67.5 14.6 %collective-permute-start.18 = (bf16[2,12,2,10,128]{4,3,2,1,0:T(8,128)(2,1)S(1)}, bf16[2,12,2,10,128]{4,3,2,1,0:T(8,128)(2,1)S(1)}, u32[]{:S(2)}, u32[]{:S(2)}) collective-permute-start(bf16[2,12,2,10,128]{4,3,2,1,0:T(8,128)(2,1)S(1)} %maximum_maximum_fusion.1), channel_id=1, source_target_pairs={{2,4},{4,2},{6,8},{8,6},{10,12},{12,10},{3,5},{5,3},{7,9},{9,7},{1... | collective-permute-start | bytes 368648 | tf_op jit(solution)/shard_map/ppermute | solution.py:636
  78.8 3.3 %collective-permute-start.17 = (bf16[2,12,2,10,128]{4,3,2,1,0:T(8,128)(2,1)S(1)}, bf16[2,12,2,10,128]{4,3,2,1,0:T(8,128)(2,1)S(1)}, u32[]{:S(2)}, u32[]{:S(2)}) collective-permute-start(bf16[2,12,2,10,128]{4,3,2,1,0:T(8,128)(2,1)S(1)} %maximum_maximum_fusion), channel_id=1, source_target_pairs={{0,2},{2,0},{4,6},{6,4},{8,10},{10,8},{12,14},{14,12},{1,3},{3,1},... | collective-permute-start | bytes 368648 | tf_op jit(solution)/shard_map/ppermute | solution.py:635
  101.5 2.7 %collective-permute-start.19 = (bf16[27,128,128]{2,1,0:T(8,128)(2,1)}, bf16[27,128,128]{2,1,0:T(8,128)(2,1)S(1)}, u32[]{:S(2)}, u32[]{:S(2)}) collective-permute-start(bf16[27,128,128]{2,1,0:T(8,128)(2,1)} %get-tuple-element.77), channel_id=1, source_target_pairs={{0,2},{2,0},{1,3},{3,1},{4,6},{6,4},{5,7},{7,5},{8,10},{10,8},{9,1... | collective-permute-start | bytes 2654216 | tf_op jit(solution)/shard_map/ppermute | solution.py:664
  106.5 24.4 %all-to-all-start = ((bf16[16,216,128]{2,1,0:T(8,128)(2,1)}), bf16[16,216,128]{2,1,0:T(8,128)(2,1)S(1)}, u32[]{:S(2)}, u32[]{:S(2)}) async-start(bf16[16,216,128]{2,1,0:T(8,128)(2,1)} %bitcast.20), calls=%async_computation | async-start | bytes 1769472 | tf_op jit(solution)/shard_map/all_to_all | solution.py:641
  131.1 6.0 %collective-permute-start.20 = (bf16[224,128]{1,0:T(8,128)(2,1)S(1)}, bf16[224,128]{1,0:T(8,128)(2,1)S(1)}, u32[]{:S(2)}, u32[]{:S(2)}) collective-permute-start(bf16[224,128]{1,0:T(8,128)(2,1)S(1)} %maximum_maximum_fusion.2), channel_id=1, source_target_pairs={{0,8},{4,12},{8,0},{12,4},{1,9},{5,13},{9,1},{13,5},{2,10},{6,14},... | collective-permute-start | bytes 172040 | tf_op jit(solution)/shard_map/ppermute | solution.py:219
  134.4 4.2 %collective-permute-start.21 = (bf16[224,128]{1,0:T(8,128)(2,1)S(1)}, bf16[224,128]{1,0:T(8,128)(2,1)S(1)}, u32[]{:S(2)}, u32[]{:S(2)}) collective-permute-start(bf16[224,128]{1,0:T(8,128)(2,1)S(1)} %maximum_maximum_fusion.2), channel_id=1, source_target_pairs={{0,4},{4,8},{8,12},{12,0},{1,5},{5,9},{9,13},{13,1},{2,6},{6,10},{... | collective-permute-start | bytes 172040 | tf_op jit(solution)/shard_map/ppermute | solution.py:219
  135.1 3.5 %collective-permute-start.22 = (bf16[224,128]{1,0:T(8,128)(2,1)S(1)}, bf16[224,128]{1,0:T(8,128)(2,1)S(1)}, u32[]{:S(2)}, u32[]{:S(2)}) collective-permute-start(bf16[224,128]{1,0:T(8,128)(2,1)S(1)} %maximum_maximum_fusion.2), channel_id=1, source_target_pairs={{0,12},{4,0},{8,4},{12,8},{1,13},{5,1},{9,5},{13,9},{2,14},{6,2},{... | collective-permute-start | bytes 172040 | tf_op jit(solution)/shard_map/ppermute | solution.py:219
  155.1 7.0 %collective-permute-start.23 = (bf16[16,224,128]{2,1,0:T(8,128)(2,1)S(1)}, bf16[16,224,128]{2,1,0:T(8,128)(2,1)S(1)}, u32[]{:S(2)}, u32[]{:S(2)}) collective-permute-start(bf16[16,224,128]{2,1,0:T(8,128)(2,1)S(1)} %all_to_all.10), channel_id=1, source_target_pairs={{0,2},{2,0},{1,3},{3,1},{4,6},{6,4},{5,7},{7,5},{8,10},{10,8},{9,1... | collective-permute-start | bytes 2752520 | tf_op jit(solution)/shard_map/ppermute | solution.py:683
  (22 other events, 117.4 us)

commit v7 on v6

--- a/solution.py
+++ b/solution.py
@@ -230,12 +230,12 @@
     placed_b = place_bricks(codes, rows, 1)
     came_a = [placed_a[0]] + [along_x(placed_a[n], n) for n in (1, 2, 3)]
     came_b = [placed_b[0]] + [along("y", placed_b[n], n) for n in (1, 2, 3)]
-    came_a, weights = lax.optimization_barrier((came_a, weights))
+    came_a, weights, where = lax.optimization_barrier((came_a, weights, where))
     merged_a = merge_bricks(came_a)
     merged_b = merge_bricks(came_b)
     came_a = [merged_a[0]] + [along("y", merged_a[n], n) for n in (1, 2, 3)]
     came_b = [merged_b[0]] + [along_x(merged_b[n], n) for n in (1, 2, 3)]
-    return sum_bricks(where, came_a + came_b, out_grad), weights
+    return sum_bricks(where, came_a + came_b, out_grad), weights, where
 
 
 def window_rows(ref, x, y, slabs, rows):
@@ -253,15 +253,34 @@
     return jnp.concatenate([both[:, 0:128], both[:, 128:256]], axis=0)
 
 
+def pair_kernel(weights_ref, plain_ref, turned_ref):
+    a = pl.program_id(0)
+    for j in range(3):
+        for k in range(3):
+            rows = slice(k * 128, (k + 1) * 128)
+            for side in range(2):
+                x = a - side
+                kept = (x >= 0) & (x < 3)
+                at = jnp.clip(x, 0, 2) * 9 + j * 3 + k
+                columns = slice(side * 128, (side + 1) * 128)
+                zero = jnp.zeros((128, 128), BF16)
+                plain_ref[0, j, rows, columns] = jnp.where(kept, weights_ref[at], zero)
+                turned_ref[0, j, rows, columns] = jnp.where(kept, weights_ref[26 - at].T, zero)
+
+
 def pair_weights(weights):
-    blocks = weights.reshape(3, 3, 384, 128)
-    left = jnp.pad(blocks, ((0, 1), (0, 0), (0, 0), (0, 0)))
-    right = jnp.pad(blocks, ((1, 0), (0, 0), (0, 0), (0, 0)))
-    return jnp.concatenate([left, right], axis=3).reshape(4608, 256)
-
-
-def turned(weights):
-    return pair_weights(weights[::-1].transpose(0, 2, 1))
+    out = jax.ShapeDtypeStruct((4, 3, 384, 256), BF16)
+    spec = pl.BlockSpec((1, 3, 384, 256), lambda a: (a, 0, 0, 0))
+    plain, turned = pl.pallas_call(
+        pair_kernel,
+        out_shape=(out, out),
+        grid=(4,),
+        in_specs=[pl.BlockSpec((27, 128, 128), lambda a: (0, 0, 0))],
+        out_specs=(spec, spec),
+        compiler_params=pltpu.CompilerParams(vmem_limit_bytes=60 << 20),
+        cost_estimate=pl.CostEstimate(flops=1 << 20, bytes_accessed=6 << 20, transcendentals=0),
+    )(weights)
+    return plain.reshape(4608, 256), turned.reshape(4608, 256)
 
 
 def neighbours(value):
@@ -646,18 +665,13 @@
     core = lax.axis_index("c")
     where = jnp.stack([lax.axis_index(SA), core, lax.axis_index(GX), lax.axis_index(GY)])
     where = where.astype(jnp.int32)
-    both, (first, second, first_t, second_t) = regroup(
+    both, ((first, first_t), (second, second_t)), where = regroup(
         sweep_bricks.reshape(128, 64, 128),
         target_rank.reshape(1, 128),
         target_slot.reshape(1, 128),
         out_grad,
         where,
-        (
-            pair_weights(conv_first),
-            pair_weights(conv_second),
-            turned(conv_first),
-            turned(conv_second),
-        ),
+        (pair_weights(conv_first), pair_weights(conv_second)),
     )
     pieces = edges(*both)
     act, pre, own, send = grads_call(where, gain, pieces, first, second_t)

time: 166 us -> 159 us (0.958)
  local copies, waits for them, and re-layouts: 16.4 us -> 7.68 us
  Pallas kernels: 42.3 us -> 50.7 us
  other arithmetic: 14.2 us -> 5.96 us
  waiting for transfers between devices: 19.4 us -> 22.3 us
    pallas_call x0 -> x2, Pallas kernels: none -> 8.43 us  [pair_weights(): pl.pallas_call(pair_kernel, out_shape=(out, out), grid=(4,), in_specs=[pl...]
    concatenate x4 -> x0, other arithmetic: 8.26 us -> none  [pair_weights(): return jnp.concatenate([left, right], axis=3).reshape(4608, 256)]
    ppermute x1, starting transfers between devices: 11.3 us -> 6.63 us  [edges(): y_two = lax.ppermute(wide(second_y), GY, SECOND)]
    unnamed x44 -> x38, local copies, waits for them, and re-layouts: 10.9 us -> 6.49 us
    rev x2 -> x0, local copies, waits for them, and re-layouts: 4.35 us -> none  [turned(): return pair_weights(weights[::-1].transpose(0, 2, 1))]
    ppermute x6, waiting for transfers between devices: 4.57 us -> 8.49 us  [along_x(): return lax.ppermute(value, ('xl', 'xh'), pairs)]
    all_to_all x1, starting transfers between devices: 10.7 us -> 6.83 us  [exchange(): return lax.all_to_all(values, axes, split_axis=0, concat_axis=0, tiled=True)]
    ppermute x9, starting transfers between devices: 13.9 us -> 17.7 us  [along(): return lax.ppermute(value, axis, [(i, (i + shift) % 4) for i in range(4)])]
  transfers between devices with their start and end apart: 25 -> 25, of which waited for: 9 -> 10; matrix products, arithmetic and copies ran while one was open for 12% -> 2% of each run, Pallas kernels for 11% -> 16%
where the time goes in v7:
time: 159 us; the launch traced here: 158 us
  starting transfers between devices  54.4 us (34%)
  Pallas kernels  50.7 us (32%)
  waiting for transfers between devices  22.3 us (14%)
  blocking collectives  16.1 us (10%)
  local copies, waits for them, and re-layouts  7.68 us (5%)
  other arithmetic  5.96 us (4%)
    pallas_call x1, Pallas kernels, grads_call(): pl.pallas_call(grads_kernel, out_shape=(jax.ShapeDtypeStruct((10, 18, 16,...  18.6 us
    ppermute x9, starting transfers between devices, along(): return lax.ppermute(value, axis, [(i, (i + shift) % 4) for i in range(4)])  17.7 us
    all_to_all x1, blocking collectives, exchange(): return lax.all_to_all(values, axes, split_axis=0, concat_axis=0, tiled=True)  16.1 us
    pallas_call x1, Pallas kernels, outputs_call(): pl.pallas_call(outputs_kernel, out_shape=(jax.ShapeDtypeStruct((8, 16, 8,...  10.4 us
    ppermute x6, starting transfers between devices, along_x(): return lax.ppermute(value, ('xl', 'xh'), pairs)  9.49 us
    ppermute x6, waiting for transfers between devices, along_x(): return lax.ppermute(value, ('xl', 'xh'), pairs)  8.49 us
    pallas_call x2, Pallas kernels, pair_weights(): pl.pallas_call(pair_kernel, out_shape=(out, out), grid=(4,), in_specs=[pl...  8.43 us
    all_to_all x1, starting transfers between devices, exchange(): return lax.all_to_all(values, axes, split_axis=0, concat_axis=0, tiled=True)  6.83 us
  transfers between devices with their start and end apart: 25, of which 10 were waited for; matrix products, arithmetic and copies ran while one was open for 2% of the time, Pallas kernels for 16%

profile of v7, /device:TPU:1, one launch (start us, length us, event | category | flops | bytes accessed | tf_op | source)
XLA Modules:
  0.0 158.3 jit_solution(10435115175007869997)
XLA Ops:
  8.4 2.5 %collective-permute-start.1 = (bf16[4,32,16,128]{3,2,1,0:T(8,128)(2,1)S(1)}, bf16[4,32,16,128]{3,2,1,0:T(8,128)(2,1)}, u32[]{:S(2)}, u32[]{:S(2)}) collective-permute-start(bf16[4,32,16,128]{3,2,1,0:T(8,128)(2,1)S(1)} %get-tuple-element.49), channel_id=1, source_target_pairs={{0,1},{16,17},{1,0},{17,16},{2,3},{18,19},{3,2},{19,18},{4,5},{20,... | collective-permute-start | bytes 1572872 | tf_op jit(solution)/shard_map/ppermute | solution.py:215
  16.0 2.6 %collective-permute-start.7 = (bf16[4,32,16,128]{3,2,1,0:T(8,128)(2,1)S(1)}, bf16[4,32,16,128]{3,2,1,0:T(8,128)(2,1)}, u32[]{:S(2)}, u32[]{:S(2)}) collective-permute-start(bf16[4,32,16,128]{3,2,1,0:T(8,128)(2,1)S(1)} %get-tuple-element.66), channel_id=1, source_target_pairs={{0,64},{32,96},{64,0},{96,32},{1,65},{33,97},{65,1},{97,33},{2,66}... | collective-permute-start | bytes 1572872 | tf_op jit(solution)/shard_map/ppermute | solution.py:219
  18.7 2.2 %collective-permute-done.p1 = bf16[4,32,16,128]{3,2,1,0:T(8,128)(2,1)S(1)} collective-permute-done((bf16[4,32,16,128]{3,2,1,0:T(8,128)(2,1)S(1)}, bf16[4,32,16,128]{3,2,1,0:T(8,128)(2,1)S(1)}, u32[]{:S(2)}, u32[]{:S(2)}) %collective-permute-start) | collective-permute-done | bytes 524320 | tf_op jit(solution)/shard_map/ppermute | solution.py:215
  21.6 3.1 %collective-permute-start.8 = (bf16[4,32,16,128]{3,2,1,0:T(8,128)(2,1)S(1)}, bf16[4,32,16,128]{3,2,1,0:T(8,128)(2,1)}, u32[]{:S(2)}, u32[]{:S(2)}) collective-permute-start(bf16[4,32,16,128]{3,2,1,0:T(8,128)(2,1)S(1)} %get-tuple-element.67), channel_id=1, source_target_pairs={{0,96},{32,0},{64,32},{96,64},{1,97},{33,1},{65,33},{97,65},{2,98}... | collective-permute-start | bytes 1572872 | tf_op jit(solution)/shard_map/ppermute | solution.py:219
  24.7 4.2 %shard_map.111 = (bf16[4,3,384,256]{3,2,1,0:T(8,128)(2,1)}, bf16[4,3,384,256]{3,2,1,0:T(8,128)(2,1)}) custom-call(bf16[27,128,128]{2,1,0:T(8,128)(2,1)} %weights_ref.2), custom_call_target="tpu_custom_call" | custom-call | flops 1048576 | bytes 6291456 | tf_op jit(solution)/shard_map/pallas_call | solution.py:274
  28.9 4.3 %shard_map.112 = (bf16[4,3,384,256]{3,2,1,0:T(8,128)(2,1)}, bf16[4,3,384,256]{3,2,1,0:T(8,128)(2,1)}) custom-call(bf16[27,128,128]{2,1,0:T(8,128)(2,1)} %weights_ref.3), custom_call_target="tpu_custom_call" | custom-call | flops 1048576 | bytes 6291456 | tf_op jit(solution)/shard_map/pallas_call | solution.py:274
  33.8 2.5 %shard_map.113 = (bf16[32,16,128]{2,1,0:T(8,128)(2,1)}, bf16[32,16,128]{2,1,0:T(8,128)(2,1)}, bf16[32,16,128]{2,1,0:T(8,128)(2,1)}, bf16[32,16,128]{2,1,0:T(8,128)(2,1)}) custom-call(bf16[4,32,16,128]{3,2,1,0:T(8,128)(2,1)} %copy-done.3, bf16[4,32,16,128]{3,2,1,0:T(8,128)(2,1)} %copy-done.5, bf16[4,32,16,128]{3,2,1,0:T(8,128)(2,1)} %collective-permute-done.1.p2, ...), custom_call_target="tpu_custom_call" | custom-call | flops 4194304 | bytes 3145728 | tf_op jit(solution)/shard_map/pallas_call | solution.py:123
  37.4 2.6 %collective-permute-start.4 = (bf16[32,16,128]{2,1,0:T(8,128)(2,1)}, bf16[32,16,128]{2,1,0:T(8,128)(2,1)S(1)}, u32[]{:S(2)}, u32[]{:S(2)}) collective-permute-start(bf16[32,16,128]{2,1,0:T(8,128)(2,1)} %get-tuple-element.62), channel_id=1, source_target_pairs={{0,64},{32,96},{64,0},{96,32},{1,65},{33,97},{65,1},{97,33},{2,66}... | collective-permute-start | bytes 393224 | tf_op jit(solution)/shard_map/ppermute | solution.py:219
  41.1 2.6 %shard_map.115 = (bf16[32,16,128]{2,1,0:T(8,128)(2,1)}, bf16[32,16,128]{2,1,0:T(8,128)(2,1)}, bf16[32,16,128]{2,1,0:T(8,128)(2,1)}, bf16[32,16,128]{2,1,0:T(8,128)(2,1)}) custom-call(bf16[4,32,16,128]{3,2,1,0:T(8,128)(2,1)} %copy-done.2, bf16[4,32,16,128]{3,2,1,0:T(8,128)(2,1)} %copy-done.4, bf16[4,32,16,128]{3,2,1,0:T(8,128)(2,1)} %collective-permute-done.7.p2, ...), custom_call_target="tpu_custom_call" | custom-call | flops 4194304 | bytes 3145728 | tf_op jit(solution)/shard_map/pallas_call | solution.py:123
  43.7 2.2 %collective-permute-start.10 = (bf16[32,16,128]{2,1,0:T(8,128)(2,1)}, bf16[32,16,128]{2,1,0:T(8,128)(2,1)S(1)}, u32[]{:S(2)}, u32[]{:S(2)}) collective-permute-start(bf16[32,16,128]{2,1,0:T(8,128)(2,1)} %get-tuple-element.70), channel_id=1, source_target_pairs={{0,1},{16,17},{1,0},{17,16},{2,3},{18,19},{3,2},{19,18},{4,5},{20,... | collective-permute-start | bytes 393224 | tf_op jit(solution)/shard_map/ppermute | solution.py:215
  49.3 3.3 %collective-permute-done.11.b3 = bf16[32,16,128]{2,1,0:T(8,128)(2,1)S(1)} collective-permute-done((bf16[32,16,128]{2,1,0:T(8,128)(2,1)}, bf16[32,16,128]{2,1,0:T(8,128)(2,1)S(1)}, u32[]{:S(2)}, u32[]{:S(2)}) %collective-permute-start.11) | collective-permute-done | bytes 131104 | tf_op jit(solution)/shard_map/ppermute | solution.py:215
  54.6 3.1 %shard_map.116 = (bf16[2,8,16,8,128]{4,3,2,1,0:T(8,128)(2,1)}, bf16[2,2,16,8,128]{4,3,2,1,0:T(8,128)(2,1)}, bf16[2,2,16,8,128]{4,3,2,1,0:T(8,128)(2,1)}, bf16[2,...) custom-call(s32[4]{0:T(128)} %pad_add_fusion.where_ref, ...), custom_call_target="tpu_custom_call" | custom-call | flops 8388608 | bytes 2097152 | tf_op jit(solution)/shard_map/pallas_call | solution.py:192
  58.4 5.5 %collective-permute-start.15 = (bf16[2,2,16,2,128]{4,3,2,1,0:T(2,128)(2,1)}, bf16[2,2,16,2,128]{4,3,2,1,0:T(2,128)(2,1)S(1)}, u32[]{:S(2)}, u32[]{:S(2)}) collective-permute-start(bf16[2,2,16,2,128]{4,3,2,1,0:T(2,128)(2,1)} %get-tuple-element.76), channel_id=1, source_target_pairs={{0,17},{1,16},{16,1},{17,0},{32,49},{33,48},{48,33},{49,32},{64,81... | collective-permute-start | bytes 98312 | tf_op jit(solution)/shard_map/ppermute | solution.py:642
  69.6 6.6 %collective-permute-start.18 = (bf16[2,12,2,10,128]{4,3,2,1,0:T(8,128)(2,1)S(1)}, bf16[2,12,2,10,128]{4,3,2,1,0:T(8,128)(2,1)S(1)}, u32[]{:S(2)}, u32[]{:S(2)}) collective-permute-start(bf16[2,12,2,10,128]{4,3,2,1,0:T(8,128)(2,1)S(1)} %maximum_maximum_fusion.1), channel_id=1, source_target_pairs={{2,4},{4,2},{6,8},{8,6},{10,12},{12,10},{3,5},{5,3},{7,9},{9,7},{1... | collective-permute-start | bytes 368648 | tf_op jit(solution)/shard_map/ppermute | solution.py:655
  76.4 3.2 %collective-permute-done.18.p7 = bf16[2,12,2,10,128]{4,3,2,1,0:T(8,128)(2,1)S(1)} collective-permute-done((bf16[2,12,2,10,128]{4,3,2,1,0:T(8,128)(2,1)S(1)}, bf16[2,12,2,10,128]{4,3,2,1,0:T(8,128)(2,1)S(1)}, u32[]{:S(2)}, u32[]{:S(2)}) %collective-permute-start.18) | collective-permute-done | bytes 122912 | tf_op jit(solution)/shard_map/ppermute | solution.py:655
  80.3 18.6 %shard_map.117 = (bf16[10,18,16,128]{3,2,1,0:T(8,128)(2,1)}, bf16[10,18,16,128]{3,2,1,0:T(8,128)(2,1)}, bf16[27,128,128]{2,1,0:T(8,128)(2,1)}, bf16[27,128,128]{2,1,0:T(8,128)(2,1)}) custom-call(s32[4]{0:T(128)} %pad_add_fusion.where_ref, f32[1,128]{1,0:T(1,128)} %bitcast.52, bf16[2,8,16,8,128]{4,3,2,1,0:T(8,128)(2,1)} %get-tuple-element.72.p0.both_hbm, ...), custom_call_target="tpu_custom_call" | custom-call | flops 10737418240 | bytes 8388608 | tf_op jit(solution)/shard_map/pallas_call | solution.py:478
  99.1 2.5 %collective-permute-done.19.other_ref = bf16[27,128,128]{2,1,0:T(8,128)(2,1)S(1)} collective-permute-done((bf16[27,128,128]{2,1,0:T(8,128)(2,1)}, bf16[27,128,128]{2,1,0:T(8,128)(2,1)S(1)}, u32[]{:S(2)}, u32[]{:S(2)}) %collective-permute-start.19) | collective-permute-done | bytes 884768 | tf_op jit(solution)/shard_map/ppermute | solution.py:678
  103.9 6.8 %all-to-all-start = ((bf16[16,216,128]{2,1,0:T(8,128)(2,1)}), bf16[16,216,128]{2,1,0:T(8,128)(2,1)S(1)}, u32[]{:S(2)}, u32[]{:S(2)}) async-start(bf16[16,216,128]{2,1,0:T(8,128)(2,1)} %bitcast.12), calls=%async_computation | async-start | bytes 1769472 | tf_op jit(solution)/shard_map/all_to_all | solution.py:660
  110.7 10.4 %shard_map.118 = (bf16[8,16,8,128]{3,2,1,0:T(8,128)(2,1)}, bf16[8,16,8,128]{3,2,1,0:T(8,128)(2,1)}, f32[8,128]{1,0:T(8,128)}) custom-call(f32[1,128]{1,0:T(1,128)} %bitcast.53, bf16[2,8,16,8,128]{4,3,2,1,0:T(8,128)(2,1)} %get-tuple-element.72.p0.both_hbm, bf16[10,18,16,128]{3,2,1,0:T(8,128)(2,1)} %get-tuple-element.80.act_hbm, ...), custom_call_target="tpu_custom_call" | custom-call | flops 8589934592 | bytes 6291456 | tf_op jit(solution)/shard_map/pallas_call | solution.py:590
  121.9 2.5 %all-to-all-done = bf16[16,216,128]{2,1,0:T(8,128)(2,1)S(1)} async-done(((bf16[16,216,128]{2,1,0:T(8,128)(2,1)}), bf16[16,216,128]{2,1,0:T(8,128)(2,1)S(1)}, u32[]{:S(2)}, u32[]{:S(2)}) %all-to-all-start) | async-done | bytes 884768 | tf_op jit(solution)/shard_map/all_to_all | solution.py:660
  124.6 3.3 %collective-permute-start.20 = (bf16[224,128]{1,0:T(8,128)(2,1)S(1)}, bf16[224,128]{1,0:T(8,128)(2,1)S(1)}, u32[]{:S(2)}, u32[]{:S(2)}) collective-permute-start(bf16[224,128]{1,0:T(8,128)(2,1)S(1)} %maximum_maximum_fusion.2), channel_id=1, source_target_pairs={{0,8},{4,12},{8,0},{12,4},{1,9},{5,13},{9,1},{13,5},{2,10},{6,14},... | collective-permute-start | bytes 172040 | tf_op jit(solution)/shard_map/ppermute | solution.py:219
  132.5 16.1 %all_to_all.10 = bf16[16,224,128]{2,1,0:T(8,128)(2,1)S(1)} all-to-all(bf16[16,224,128]{2,1,0:T(8,128)(2,1)S(1)} %broadcast_in_dim.2), channel_id=1, replica_groups=mesh['y'=4,'xl'=2,'z'=4,'c'=2,'xh'=2] {'y','xl','xh'}, dimensions={0} | all-to-all | bytes 1835008 | tf_op jit(solution)/shard_map/all_to_all | solution.py:660
  148.6 4.9 %collective-permute-start.23 = (bf16[16,224,128]{2,1,0:T(8,128)(2,1)S(1)}, bf16[16,224,128]{2,1,0:T(8,128)(2,1)S(1)}, u32[]{:S(2)}, u32[]{:S(2)}) collective-permute-start(bf16[16,224,128]{2,1,0:T(8,128)(2,1)S(1)} %all_to_all.10), channel_id=1, source_target_pairs={{0,2},{2,0},{1,3},{3,1},{4,6},{6,4},{5,7},{7,5},{8,10},{10,8},{9,1... | collective-permute-start | bytes 2752520 | tf_op jit(solution)/shard_map/ppermute | solution.py:697
  156.2 2.1 %convert_multiply_fusion = (f32[16,216,128]{2,1,0:T(8,128)}, f32[16,216,128]{2,1,0:T(8,128)}) fusion(pred[]{:T(512)S(6)} %eq.9, bf16[16,224,128]{2,1,0:T(8,128)(2,1)S(1)} %collective-permute-done.23, bf16[16,224,128]{2,1,0:T(8,128)(2,1)S(1)} %all_to_all.10), kind=kLoop, calls=%fused_computation | loop fusion | flops 2654208 | bytes 5308417 | tf_op jit(solution)/shard_map/mul | solution.py:702
  (102 shorter events, 39.5 us)
Async XLA Ops:
  6.3 14.5 %collective-permute-start = (bf16[4,32,16,128]{3,2,1,0:T(8,128)(2,1)S(1)}, bf16[4,32,16,128]{3,2,1,0:T(8,128)(2,1)S(1)}, u32[]{:S(2)}, u32[]{:S(2)}) collective-permute-start(bf16[4,32,16,128]{3,2,1,0:T(8,128)(2,1)S(1)} %get-tuple-element.48), channel_id=1, source_target_pairs={{0,16},{16,1},{1,17},{17,0},{2,18},{18,3},{3,19},{19,2},{4,20},{20... | collective-permute-start | bytes 1572872 | tf_op jit(solution)/shard_map/ppermute | solution.py:215
  8.4 25.4 %collective-permute-start.1 = (bf16[4,32,16,128]{3,2,1,0:T(8,128)(2,1)S(1)}, bf16[4,32,16,128]{3,2,1,0:T(8,128)(2,1)}, u32[]{:S(2)}, u32[]{:S(2)}) collective-permute-start(bf16[4,32,16,128]{3,2,1,0:T(8,128)(2,1)S(1)} %get-tuple-element.49), channel_id=1, source_target_pairs={{0,1},{16,17},{1,0},{17,16},{2,3},{18,19},{3,2},{19,18},{4,5},{20,... | collective-permute-start | bytes 1572872 | tf_op jit(solution)/shard_map/ppermute | solution.py:215
  10.8 23.0 %collective-permute-start.2 = (bf16[4,32,16,128]{3,2,1,0:T(8,128)(2,1)S(1)}, bf16[4,32,16,128]{3,2,1,0:T(8,128)(2,1)}, u32[]{:S(2)}, u32[]{:S(2)}) collective-permute-start(bf16[4,32,16,128]{3,2,1,0:T(8,128)(2,1)S(1)} %get-tuple-element.50), channel_id=1, source_target_pairs={{0,17},{16,0},{1,16},{17,1},{2,19},{18,2},{3,18},{19,3},{4,21},{20... | collective-permute-start | bytes 1572872 | tf_op jit(solution)/shard_map/ppermute | solution.py:215
  14.8 25.3 %collective-permute-start.6 = (bf16[4,32,16,128]{3,2,1,0:T(8,128)(2,1)S(1)}, bf16[4,32,16,128]{3,2,1,0:T(8,128)(2,1)S(1)}, u32[]{:S(2)}, u32[]{:S(2)}) collective-permute-start(bf16[4,32,16,128]{3,2,1,0:T(8,128)(2,1)S(1)} %get-tuple-element.65), channel_id=1, source_target_pairs={{0,32},{32,64},{64,96},{96,0},{1,33},{33,65},{65,97},{97,1},{2,34}... | collective-permute-start | bytes 1572872 | tf_op jit(solution)/shard_map/ppermute | solution.py:219
  16.0 25.1 %collective-permute-start.7 = (bf16[4,32,16,128]{3,2,1,0:T(8,128)(2,1)S(1)}, bf16[4,32,16,128]{3,2,1,0:T(8,128)(2,1)}, u32[]{:S(2)}, u32[]{:S(2)}) collective-permute-start(bf16[4,32,16,128]{3,2,1,0:T(8,128)(2,1)S(1)} %get-tuple-element.66), channel_id=1, source_target_pairs={{0,64},{32,96},{64,0},{96,32},{1,65},{33,97},{65,1},{97,33},{2,66}... | collective-permute-start | bytes 1572872 | tf_op jit(solution)/shard_map/ppermute | solution.py:219
  21.6 19.5 %collective-permute-start.8 = (bf16[4,32,16,128]{3,2,1,0:T(8,128)(2,1)S(1)}, bf16[4,32,16,128]{3,2,1,0:T(8,128)(2,1)}, u32[]{:S(2)}, u32[]{:S(2)}) collective-permute-start(bf16[4,32,16,128]{3,2,1,0:T(8,128)(2,1)S(1)} %get-tuple-element.67), channel_id=1, source_target_pairs={{0,96},{32,0},{64,32},{96,64},{1,97},{33,1},{65,33},{97,65},{2,98}... | collective-permute-start | bytes 1572872 | tf_op jit(solution)/shard_map/ppermute | solution.py:219
  36.4 11.2 %collective-permute-start.3 = (bf16[32,16,128]{2,1,0:T(8,128)(2,1)}, bf16[32,16,128]{2,1,0:T(8,128)(2,1)S(1)}, u32[]{:S(2)}, u32[]{:S(2)}) collective-permute-start(bf16[32,16,128]{2,1,0:T(8,128)(2,1)} %get-tuple-element.61), channel_id=1, source_target_pairs={{0,32},{32,64},{64,96},{96,0},{1,33},{33,65},{65,97},{97,1},{2,34}... | collective-permute-start | bytes 393224 | tf_op jit(solution)/shard_map/ppermute | solution.py:219
  37.4 10.1 %collective-permute-start.4 = (bf16[32,16,128]{2,1,0:T(8,128)(2,1)}, bf16[32,16,128]{2,1,0:T(8,128)(2,1)S(1)}, u32[]{:S(2)}, u32[]{:S(2)}) collective-permute-start(bf16[32,16,128]{2,1,0:T(8,128)(2,1)} %get-tuple-element.62), channel_id=1, source_target_pairs={{0,64},{32,96},{64,0},{96,32},{1,65},{33,97},{65,1},{97,33},{2,66}... | collective-permute-start | bytes 393224 | tf_op jit(solution)/shard_map/ppermute | solution.py:219
  40.0 7.5 %collective-permute-start.5 = (bf16[32,16,128]{2,1,0:T(8,128)(2,1)}, bf16[32,16,128]{2,1,0:T(8,128)(2,1)S(1)}, u32[]{:S(2)}, u32[]{:S(2)}) collective-permute-start(bf16[32,16,128]{2,1,0:T(8,128)(2,1)} %get-tuple-element.63), channel_id=1, source_target_pairs={{0,96},{32,0},{64,32},{96,64},{1,97},{33,1},{65,33},{97,65},{2,98}... | collective-permute-start | bytes 393224 | tf_op jit(solution)/shard_map/ppermute | solution.py:219
  43.7 5.6 %collective-permute-start.10 = (bf16[32,16,128]{2,1,0:T(8,128)(2,1)}, bf16[32,16,128]{2,1,0:T(8,128)(2,1)S(1)}, u32[]{:S(2)}, u32[]{:S(2)}) collective-permute-start(bf16[32,16,128]{2,1,0:T(8,128)(2,1)} %get-tuple-element.70), channel_id=1, source_target_pairs={{0,1},{16,17},{1,0},{17,16},{2,3},{18,19},{3,2},{19,18},{4,5},{20,... | collective-permute-start | bytes 393224 | tf_op jit(solution)/shard_map/ppermute | solution.py:215
  45.9 6.7 %collective-permute-start.11 = (bf16[32,16,128]{2,1,0:T(8,128)(2,1)}, bf16[32,16,128]{2,1,0:T(8,128)(2,1)S(1)}, u32[]{:S(2)}, u32[]{:S(2)}) collective-permute-start(bf16[32,16,128]{2,1,0:T(8,128)(2,1)} %get-tuple-element.71), channel_id=1, source_target_pairs={{0,17},{16,0},{1,16},{17,1},{2,19},{18,2},{3,18},{19,3},{4,21},{20... | collective-permute-start | bytes 393224 | tf_op jit(solution)/shard_map/ppermute | solution.py:215
  47.5 6.4 %collective-permute-start.9 = (bf16[32,16,128]{2,1,0:T(8,128)(2,1)}, bf16[32,16,128]{2,1,0:T(8,128)(2,1)S(1)}, u32[]{:S(2)}, u32[]{:S(2)}) collective-permute-start(bf16[32,16,128]{2,1,0:T(8,128)(2,1)} %get-tuple-element.69), channel_id=1, source_target_pairs={{0,16},{16,1},{1,17},{17,0},{2,18},{18,3},{3,19},{19,2},{4,20},{20... | collective-permute-start | bytes 393224 | tf_op jit(solution)/shard_map/ppermute | solution.py:215
  57.7 9.7 %collective-permute-start.12 = (bf16[2,2,16,8,128]{4,3,2,1,0:T(8,128)(2,1)}, bf16[2,2,16,8,128]{4,3,2,1,0:T(8,128)(2,1)S(1)}, u32[]{:S(2)}, u32[]{:S(2)}) collective-permute-start(bf16[2,2,16,8,128]{4,3,2,1,0:T(8,128)(2,1)} %get-tuple-element.73), channel_id=1, source_target_pairs={{0,16},{16,0},{32,48},{48,32},{64,80},{80,64},{96,112},{112,96},{1... | collective-permute-start | bytes 393224 | tf_op jit(solution)/shard_map/ppermute | solution.py:639
  57.8 9.7 %collective-permute-start.13 = (bf16[2,2,16,8,128]{4,3,2,1,0:T(8,128)(2,1)}, bf16[2,2,16,8,128]{4,3,2,1,0:T(8,128)(2,1)S(1)}, u32[]{:S(2)}, u32[]{:S(2)}) collective-permute-start(bf16[2,2,16,8,128]{4,3,2,1,0:T(8,128)(2,1)} %get-tuple-element.74), channel_id=1, source_target_pairs={{16,32},{32,16},{48,64},{64,48},{80,96},{96,80},{17,33},{33,17},{4... | collective-permute-start | bytes 393224 | tf_op jit(solution)/shard_map/ppermute | solution.py:640
  58.4 8.9 %collective-permute-start.15 = (bf16[2,2,16,2,128]{4,3,2,1,0:T(2,128)(2,1)}, bf16[2,2,16,2,128]{4,3,2,1,0:T(2,128)(2,1)S(1)}, u32[]{:S(2)}, u32[]{:S(2)}) collective-permute-start(bf16[2,2,16,2,128]{4,3,2,1,0:T(2,128)(2,1)} %get-tuple-element.76), channel_id=1, source_target_pairs={{0,17},{1,16},{16,1},{17,0},{32,49},{33,48},{48,33},{49,32},{64,81... | collective-permute-start | bytes 98312 | tf_op jit(solution)/shard_map/ppermute | solution.py:642
  64.0 5.5 %collective-permute-start.14 = (bf16[2,8,16,2,128]{4,3,2,1,0:T(2,128)(2,1)}, bf16[2,8,16,2,128]{4,3,2,1,0:T(2,128)(2,1)S(1)}, u32[]{:S(2)}, u32[]{:S(2)}) collective-permute-start(bf16[2,8,16,2,128]{4,3,2,1,0:T(2,128)(2,1)} %get-tuple-element.75), channel_id=1, source_target_pairs={{0,1},{1,0},{2,3},{3,2},{4,5},{5,4},{6,7},{7,6},{8,9},{9,8},{10,11... | collective-permute-start | bytes 393224 | tf_op jit(solution)/shard_map/ppermute | solution.py:641
  69.6 10.0 %collective-permute-start.18 = (bf16[2,12,2,10,128]{4,3,2,1,0:T(8,128)(2,1)S(1)}, bf16[2,12,2,10,128]{4,3,2,1,0:T(8,128)(2,1)S(1)}, u32[]{:S(2)}, u32[]{:S(2)}) collective-permute-start(bf16[2,12,2,10,128]{4,3,2,1,0:T(8,128)(2,1)S(1)} %maximum_maximum_fusion.1), channel_id=1, source_target_pairs={{2,4},{4,2},{6,8},{8,6},{10,12},{12,10},{3,5},{5,3},{7,9},{9,7},{1... | collective-permute-start | bytes 368648 | tf_op jit(solution)/shard_map/ppermute | solution.py:655
  76.3 3.3 %collective-permute-start.17 = (bf16[2,12,2,10,128]{4,3,2,1,0:T(8,128)(2,1)S(1)}, bf16[2,12,2,10,128]{4,3,2,1,0:T(8,128)(2,1)S(1)}, u32[]{:S(2)}, u32[]{:S(2)}) collective-permute-start(bf16[2,12,2,10,128]{4,3,2,1,0:T(8,128)(2,1)S(1)} %maximum_maximum_fusion), channel_id=1, source_target_pairs={{0,2},{2,0},{4,6},{6,4},{8,10},{10,8},{12,14},{14,12},{1,3},{3,1},... | collective-permute-start | bytes 368648 | tf_op jit(solution)/shard_map/ppermute | solution.py:654
  98.9 2.7 %collective-permute-start.19 = (bf16[27,128,128]{2,1,0:T(8,128)(2,1)}, bf16[27,128,128]{2,1,0:T(8,128)(2,1)S(1)}, u32[]{:S(2)}, u32[]{:S(2)}) collective-permute-start(bf16[27,128,128]{2,1,0:T(8,128)(2,1)} %get-tuple-element.87), channel_id=1, source_target_pairs={{0,2},{2,0},{1,3},{3,1},{4,6},{6,4},{5,7},{7,5},{8,10},{10,8},{9,1... | collective-permute-start | bytes 2654216 | tf_op jit(solution)/shard_map/ppermute | solution.py:678
  103.9 20.5 %all-to-all-start = ((bf16[16,216,128]{2,1,0:T(8,128)(2,1)}), bf16[16,216,128]{2,1,0:T(8,128)(2,1)S(1)}, u32[]{:S(2)}, u32[]{:S(2)}) async-start(bf16[16,216,128]{2,1,0:T(8,128)(2,1)} %bitcast.12), calls=%async_computation | async-start | bytes 1769472 | tf_op jit(solution)/shard_map/all_to_all | solution.py:660
  124.6 6.0 %collective-permute-start.20 = (bf16[224,128]{1,0:T(8,128)(2,1)S(1)}, bf16[224,128]{1,0:T(8,128)(2,1)S(1)}, u32[]{:S(2)}, u32[]{:S(2)}) collective-permute-start(bf16[224,128]{1,0:T(8,128)(2,1)S(1)} %maximum_maximum_fusion.2), channel_id=1, source_target_pairs={{0,8},{4,12},{8,0},{12,4},{1,9},{5,13},{9,1},{13,5},{2,10},{6,14},... | collective-permute-start | bytes 172040 | tf_op jit(solution)/shard_map/ppermute | solution.py:219
  127.9 4.2 %collective-permute-start.21 = (bf16[224,128]{1,0:T(8,128)(2,1)S(1)}, bf16[224,128]{1,0:T(8,128)(2,1)S(1)}, u32[]{:S(2)}, u32[]{:S(2)}) collective-permute-start(bf16[224,128]{1,0:T(8,128)(2,1)S(1)} %maximum_maximum_fusion.2), channel_id=1, source_target_pairs={{0,4},{4,8},{8,12},{12,0},{1,5},{5,9},{9,13},{13,1},{2,6},{6,10},{... | collective-permute-start | bytes 172040 | tf_op jit(solution)/shard_map/ppermute | solution.py:219
  128.6 3.5 %collective-permute-start.22 = (bf16[224,128]{1,0:T(8,128)(2,1)S(1)}, bf16[224,128]{1,0:T(8,128)(2,1)S(1)}, u32[]{:S(2)}, u32[]{:S(2)}) collective-permute-start(bf16[224,128]{1,0:T(8,128)(2,1)S(1)} %maximum_maximum_fusion.2), channel_id=1, source_target_pairs={{0,12},{4,0},{8,4},{12,8},{1,13},{5,1},{9,5},{13,9},{2,14},{6,2},{... | collective-permute-start | bytes 172040 | tf_op jit(solution)/shard_map/ppermute | solution.py:219
  148.6 7.0 %collective-permute-start.23 = (bf16[16,224,128]{2,1,0:T(8,128)(2,1)S(1)}, bf16[16,224,128]{2,1,0:T(8,128)(2,1)S(1)}, u32[]{:S(2)}, u32[]{:S(2)}) collective-permute-start(bf16[16,224,128]{2,1,0:T(8,128)(2,1)S(1)} %all_to_all.10), channel_id=1, source_target_pairs={{0,2},{2,0},{1,3},{3,1},{4,6},{6,4},{5,7},{7,5},{8,10},{10,8},{9,1... | collective-permute-start | bytes 2752520 | tf_op jit(solution)/shard_map/ppermute | solution.py:697
  (20 other events, 93.8 us)

commit v8 on v7

--- a/solution.py
+++ b/solution.py
@@ -202,7 +202,7 @@
         in_specs=[SM] + [VM] * 9,
         out_specs=(VM,) * 6,
         scratch_shapes=[pltpu.VMEM((128, 128), F32), pltpu.VMEM((16, 8, 128), F32)],
-        compiler_params=pltpu.CompilerParams(vmem_limit_bytes=60 << 20),
+        compiler_params=pltpu.CompilerParams(vmem_limit_bytes=8 << 20),
         cost_estimate=pl.CostEstimate(flops=8 << 20, bytes_accessed=2 << 20, transcendentals=0),
     )(where, *parts, out_grad)
 

time: 159 us -> 157 us (0.987)
  Pallas kernels: 50.7 us -> 49 us
    pallas_call x1, Pallas kernels: 3.15 us -> 1.35 us  [sum_bricks(): pl.pallas_call(sum_bricks_kernel, out_shape=(jax.ShapeDtypeStruct((2, 8,...]
    unnamed x38 -> x34, local copies, waits for them, and re-layouts: 6.49 us -> 6.77 us
  transfers between devices with their start and end apart: 25 -> 25, of which waited for: 10 -> 11; matrix products, arithmetic and copies ran while one was open for 2% -> 1% of each run, Pallas kernels for 16% -> 17%
where the time goes in v8:
time: 157 us
  starting transfers between devices  54.7 us (35%)
  Pallas kernels  49 us (31%)
  waiting for transfers between devices  23.4 us (15%)
  blocking collectives  16.1 us (10%)
  local copies, waits for them, and re-layouts  7.09 us (5%)
  other arithmetic  5.37 us (3%)
    pallas_call x1, Pallas kernels, grads_call(): pl.pallas_call(grads_kernel, out_shape=(jax.ShapeDtypeStruct((10, 18, 16,...  18.6 us
    ppermute x9, starting transfers between devices, along(): return lax.ppermute(value, axis, [(i, (i + shift) % 4) for i in range(4)])  17.9 us
    all_to_all x1, blocking collectives, exchange(): return lax.all_to_all(values, axes, split_axis=0, concat_axis=0, tiled=True)  16.1 us
    pallas_call x1, Pallas kernels, outputs_call(): pl.pallas_call(outputs_kernel, out_shape=(jax.ShapeDtypeStruct((8, 16, 8,...  10.4 us
    ppermute x6, starting transfers between devices, along_x(): return lax.ppermute(value, ('xl', 'xh'), pairs)  9.49 us
    ppermute x6, waiting for transfers between devices, along_x(): return lax.ppermute(value, ('xl', 'xh'), pairs)  8.88 us
    pallas_call x2, Pallas kernels, pair_weights(): pl.pallas_call(pair_kernel, out_shape=(out, out), grid=(4,), in_specs=[pl...  8.44 us
    all_to_all x1, starting transfers between devices, exchange(): return lax.all_to_all(values, axes, split_axis=0, concat_axis=0, tiled=True)  6.83 us
  transfers between devices with their start and end apart: 25, of which 11 were waited for; matrix products, arithmetic and copies ran while one was open for 1% of the time, Pallas kernels for 17%

profile of v8, /device:TPU:1, one launch (start us, length us, event | category | flops | bytes accessed | tf_op | source)
XLA Modules:
  0.0 156.6 jit_solution(3323710626698078905)
XLA Ops:
  8.4 2.5 %collective-permute-start.1 = (bf16[4,32,16,128]{3,2,1,0:T(8,128)(2,1)S(1)}, bf16[4,32,16,128]{3,2,1,0:T(8,128)(2,1)}, u32[]{:S(2)}, u32[]{:S(2)}) collective-permute-start(bf16[4,32,16,128]{3,2,1,0:T(8,128)(2,1)S(1)} %get-tuple-element.49), channel_id=1, source_target_pairs={{0,1},{16,17},{1,0},{17,16},{2,3},{18,19},{3,2},{19,18},{4,5},{20,... | collective-permute-start | bytes 1572872 | tf_op jit(solution)/shard_map/ppermute | solution.py:215
  16.1 2.6 %collective-permute-start.7 = (bf16[4,32,16,128]{3,2,1,0:T(8,128)(2,1)S(1)}, bf16[4,32,16,128]{3,2,1,0:T(8,128)(2,1)}, u32[]{:S(2)}, u32[]{:S(2)}) collective-permute-start(bf16[4,32,16,128]{3,2,1,0:T(8,128)(2,1)S(1)} %get-tuple-element.66), channel_id=1, source_target_pairs={{0,64},{32,96},{64,0},{96,32},{1,65},{33,97},{65,1},{97,33},{2,66}... | collective-permute-start | bytes 1572872 | tf_op jit(solution)/shard_map/ppermute | solution.py:219
  18.7 2.3 %collective-permute-done.p1 = bf16[4,32,16,128]{3,2,1,0:T(8,128)(2,1)S(1)} collective-permute-done((bf16[4,32,16,128]{3,2,1,0:T(8,128)(2,1)S(1)}, bf16[4,32,16,128]{3,2,1,0:T(8,128)(2,1)S(1)}, u32[]{:S(2)}, u32[]{:S(2)}) %collective-permute-start) | collective-permute-done | bytes 524320 | tf_op jit(solution)/shard_map/ppermute | solution.py:215
  21.7 3.0 %collective-permute-start.8 = (bf16[4,32,16,128]{3,2,1,0:T(8,128)(2,1)S(1)}, bf16[4,32,16,128]{3,2,1,0:T(8,128)(2,1)}, u32[]{:S(2)}, u32[]{:S(2)}) collective-permute-start(bf16[4,32,16,128]{3,2,1,0:T(8,128)(2,1)S(1)} %get-tuple-element.67), channel_id=1, source_target_pairs={{0,96},{32,0},{64,32},{96,64},{1,97},{33,1},{65,33},{97,65},{2,98}... | collective-permute-start | bytes 1572872 | tf_op jit(solution)/shard_map/ppermute | solution.py:219
  24.7 4.2 %shard_map.111 = (bf16[4,3,384,256]{3,2,1,0:T(8,128)(2,1)}, bf16[4,3,384,256]{3,2,1,0:T(8,128)(2,1)}) custom-call(bf16[27,128,128]{2,1,0:T(8,128)(2,1)} %weights_ref.2), custom_call_target="tpu_custom_call" | custom-call | flops 1048576 | bytes 6291456 | tf_op jit(solution)/shard_map/pallas_call | solution.py:274
  28.9 4.2 %shard_map.112 = (bf16[4,3,384,256]{3,2,1,0:T(8,128)(2,1)}, bf16[4,3,384,256]{3,2,1,0:T(8,128)(2,1)}) custom-call(bf16[27,128,128]{2,1,0:T(8,128)(2,1)} %weights_ref.3), custom_call_target="tpu_custom_call" | custom-call | flops 1048576 | bytes 6291456 | tf_op jit(solution)/shard_map/pallas_call | solution.py:274
  33.5 2.6 %shard_map.113 = (bf16[32,16,128]{2,1,0:T(8,128)(2,1)}, bf16[32,16,128]{2,1,0:T(8,128)(2,1)}, bf16[32,16,128]{2,1,0:T(8,128)(2,1)}, bf16[32,16,128]{2,1,0:T(8,128)(2,1)}) custom-call(bf16[4,32,16,128]{3,2,1,0:T(8,128)(2,1)} %copy-done.3, bf16[4,32,16,128]{3,2,1,0:T(8,128)(2,1)} %copy-done.9, bf16[4,32,16,128]{3,2,1,0:T(8,128)(2,1)} %collective-permute-done.1.p2, ...), custom_call_target="tpu_custom_call" | custom-call | flops 4194304 | bytes 3145728 | tf_op jit(solution)/shard_map/pallas_call | solution.py:123
  37.5 2.6 %collective-permute-start.4 = (bf16[32,16,128]{2,1,0:T(8,128)(2,1)}, bf16[32,16,128]{2,1,0:T(8,128)(2,1)S(1)}, u32[]{:S(2)}, u32[]{:S(2)}) collective-permute-start(bf16[32,16,128]{2,1,0:T(8,128)(2,1)} %get-tuple-element.62), channel_id=1, source_target_pairs={{0,64},{32,96},{64,0},{96,32},{1,65},{33,97},{65,1},{97,33},{2,66}... | collective-permute-start | bytes 393224 | tf_op jit(solution)/shard_map/ppermute | solution.py:219
  41.2 2.5 %shard_map.115 = (bf16[32,16,128]{2,1,0:T(8,128)(2,1)}, bf16[32,16,128]{2,1,0:T(8,128)(2,1)}, bf16[32,16,128]{2,1,0:T(8,128)(2,1)}, bf16[32,16,128]{2,1,0:T(8,128)(2,1)}) custom-call(bf16[4,32,16,128]{3,2,1,0:T(8,128)(2,1)} %copy-done.2, bf16[4,32,16,128]{3,2,1,0:T(8,128)(2,1)} %collective-permute-done.6.p1, ...), custom_call_target="tpu_custom_call" | custom-call | flops 4194304 | bytes 3145728 | tf_op jit(solution)/shard_map/pallas_call | solution.py:123
  43.7 2.2 %collective-permute-start.10 = (bf16[32,16,128]{2,1,0:T(8,128)(2,1)}, bf16[32,16,128]{2,1,0:T(8,128)(2,1)S(1)}, u32[]{:S(2)}, u32[]{:S(2)}) collective-permute-start(bf16[32,16,128]{2,1,0:T(8,128)(2,1)} %get-tuple-element.70), channel_id=1, source_target_pairs={{0,1},{16,17},{1,0},{17,16},{2,3},{18,19},{3,2},{19,18},{4,5},{20,... | collective-permute-start | bytes 393224 | tf_op jit(solution)/shard_map/ppermute | solution.py:215
  49.3 3.3 %collective-permute-done.11.b3 = bf16[32,16,128]{2,1,0:T(8,128)(2,1)S(1)} collective-permute-done((bf16[32,16,128]{2,1,0:T(8,128)(2,1)}, bf16[32,16,128]{2,1,0:T(8,128)(2,1)S(1)}, u32[]{:S(2)}, u32[]{:S(2)}) %collective-permute-start.11) | collective-permute-done | bytes 131104 | tf_op jit(solution)/shard_map/ppermute | solution.py:215
  57.0 5.5 %collective-permute-start.15 = (bf16[2,2,16,2,128]{4,3,2,1,0:T(2,128)(2,1)S(1)}, bf16[2,2,16,2,128]{4,3,2,1,0:T(2,128)(2,1)S(1)}, u32[]{:S(2)}, u32[]{:S(2)}) collective-permute-start(bf16[2,2,16,2,128]{4,3,2,1,0:T(2,128)(2,1)S(1)} %get-tuple-element.76), channel_id=1, source_target_pairs={{0,17},{1,16},{16,1},{17,0},{32,49},{33,48},{48,33},{49,32},{64,81... | collective-permute-start | bytes 98312 | tf_op jit(solution)/shard_map/ppermute | solution.py:642
  65.1 2.7 %collective-permute-done.14.p3 = bf16[2,8,16,2,128]{4,3,2,1,0:T(2,128)(2,1)S(1)} collective-permute-done((bf16[2,8,16,2,128]{4,3,2,1,0:T(2,128)(2,1)S(1)}, bf16[2,8,16,2,128]{4,3,2,1,0:T(2,128)(2,1)S(1)}, u32[]{:S(2)}, u32[]{:S(2)}) %collective-permute-start.14) | collective-permute-done | bytes 131104 | tf_op jit(solution)/shard_map/ppermute | solution.py:641
  67.9 6.6 %collective-permute-start.18 = (bf16[2,12,2,10,128]{4,3,2,1,0:T(8,128)(2,1)S(1)}, bf16[2,12,2,10,128]{4,3,2,1,0:T(8,128)(2,1)S(1)}, u32[]{:S(2)}, u32[]{:S(2)}) collective-permute-start(bf16[2,12,2,10,128]{4,3,2,1,0:T(8,128)(2,1)S(1)} %maximum_maximum_fusion.1), channel_id=1, source_target_pairs={{2,4},{4,2},{6,8},{8,6},{10,12},{12,10},{3,5},{5,3},{7,9},{9,7},{1... | collective-permute-start | bytes 368648 | tf_op jit(solution)/shard_map/ppermute | solution.py:655
  74.7 3.2 %collective-permute-done.18.p7 = bf16[2,12,2,10,128]{4,3,2,1,0:T(8,128)(2,1)S(1)} collective-permute-done((bf16[2,12,2,10,128]{4,3,2,1,0:T(8,128)(2,1)S(1)}, bf16[2,12,2,10,128]{4,3,2,1,0:T(8,128)(2,1)S(1)}, u32[]{:S(2)}, u32[]{:S(2)}) %collective-permute-start.18) | collective-permute-done | bytes 122912 | tf_op jit(solution)/shard_map/ppermute | solution.py:655
  78.6 18.6 %shard_map.117 = (bf16[10,18,16,128]{3,2,1,0:T(8,128)(2,1)}, bf16[10,18,16,128]{3,2,1,0:T(8,128)(2,1)}, bf16[27,128,128]{2,1,0:T(8,128)(2,1)}, bf16[27,128,128]{2,1,0:T(8,128)(2,1)}) custom-call(s32[4]{0:T(128)} %copy-done.8, f32[1,128]{1,0:T(1,128)} %bitcast.52, bf16[2,8,16,8,128]{4,3,2,1,0:T(8,128)(2,1)} %copy-done.7, ...), custom_call_target="tpu_custom_call" | custom-call | flops 10737418240 | bytes 8388608 | tf_op jit(solution)/shard_map/pallas_call | solution.py:478
  97.4 2.5 %collective-permute-done.19.other_ref = bf16[27,128,128]{2,1,0:T(8,128)(2,1)S(1)} collective-permute-done((bf16[27,128,128]{2,1,0:T(8,128)(2,1)}, bf16[27,128,128]{2,1,0:T(8,128)(2,1)S(1)}, u32[]{:S(2)}, u32[]{:S(2)}) %collective-permute-start.19) | collective-permute-done | bytes 884768 | tf_op jit(solution)/shard_map/ppermute | solution.py:678
  102.2 6.8 %all-to-all-start = ((bf16[16,216,128]{2,1,0:T(8,128)(2,1)}), bf16[16,216,128]{2,1,0:T(8,128)(2,1)S(1)}, u32[]{:S(2)}, u32[]{:S(2)}) async-start(bf16[16,216,128]{2,1,0:T(8,128)(2,1)} %bitcast.12), calls=%async_computation | async-start | bytes 1769472 | tf_op jit(solution)/shard_map/all_to_all | solution.py:660
  109.1 10.4 %shard_map.118 = (bf16[8,16,8,128]{3,2,1,0:T(8,128)(2,1)}, bf16[8,16,8,128]{3,2,1,0:T(8,128)(2,1)}, f32[8,128]{1,0:T(8,128)}) custom-call(f32[1,128]{1,0:T(1,128)} %bitcast.53, bf16[2,8,16,8,128]{4,3,2,1,0:T(8,128)(2,1)} %copy-done.7, bf16[10,18,16,128]{3,2,1,0:T(8,128)(2,1)} %get-tuple-element.80.act_hbm, ...), custom_call_target="tpu_custom_call" | custom-call | flops 8589934592 | bytes 6291456 | tf_op jit(solution)/shard_map/pallas_call | solution.py:590
  120.2 2.5 %all-to-all-done = bf16[16,216,128]{2,1,0:T(8,128)(2,1)S(1)} async-done(((bf16[16,216,128]{2,1,0:T(8,128)(2,1)}), bf16[16,216,128]{2,1,0:T(8,128)(2,1)S(1)}, u32[]{:S(2)}, u32[]{:S(2)}) %all-to-all-start) | async-done | bytes 884768 | tf_op jit(solution)/shard_map/all_to_all | solution.py:660
  122.9 3.3 %collective-permute-start.20 = (bf16[224,128]{1,0:T(8,128)(2,1)S(1)}, bf16[224,128]{1,0:T(8,128)(2,1)S(1)}, u32[]{:S(2)}, u32[]{:S(2)}) collective-permute-start(bf16[224,128]{1,0:T(8,128)(2,1)S(1)} %maximum_maximum_fusion.2), channel_id=1, source_target_pairs={{0,8},{4,12},{8,0},{12,4},{1,9},{5,13},{9,1},{13,5},{2,10},{6,14},... | collective-permute-start | bytes 172040 | tf_op jit(solution)/shard_map/ppermute | solution.py:219
  130.8 16.1 %all_to_all.10 = bf16[16,224,128]{2,1,0:T(8,128)(2,1)S(1)} all-to-all(bf16[16,224,128]{2,1,0:T(8,128)(2,1)S(1)} %broadcast_in_dim.2), channel_id=1, replica_groups=mesh['y'=4,'xl'=2,'z'=4,'c'=2,'xh'=2] {'y','xl','xh'}, dimensions={0} | all-to-all | bytes 1835008 | tf_op jit(solution)/shard_map/all_to_all | solution.py:660
  146.9 4.9 %collective-permute-start.23 = (bf16[16,224,128]{2,1,0:T(8,128)(2,1)S(1)}, bf16[16,224,128]{2,1,0:T(8,128)(2,1)S(1)}, u32[]{:S(2)}, u32[]{:S(2)}) collective-permute-start(bf16[16,224,128]{2,1,0:T(8,128)(2,1)S(1)} %all_to_all.10), channel_id=1, source_target_pairs={{0,2},{2,0},{1,3},{3,1},{4,6},{6,4},{5,7},{7,5},{8,10},{10,8},{9,1... | collective-permute-start | bytes 2752520 | tf_op jit(solution)/shard_map/ppermute | solution.py:697
  154.5 2.1 %convert_multiply_fusion = (f32[16,216,128]{2,1,0:T(8,128)}, f32[16,216,128]{2,1,0:T(8,128)}) fusion(pred[]{:T(512)S(6)} %eq.9, bf16[16,224,128]{2,1,0:T(8,128)(2,1)S(1)} %collective-permute-done.23, bf16[16,224,128]{2,1,0:T(8,128)(2,1)S(1)} %all_to_all.10), kind=kLoop, calls=%fused_computation | loop fusion | flops 2654208 | bytes 5308417 | tf_op jit(solution)/shard_map/mul | solution.py:702
  (98 shorter events, 38.3 us)
Async XLA Ops:
  6.3 14.6 %collective-permute-start = (bf16[4,32,16,128]{3,2,1,0:T(8,128)(2,1)S(1)}, bf16[4,32,16,128]{3,2,1,0:T(8,128)(2,1)S(1)}, u32[]{:S(2)}, u32[]{:S(2)}) collective-permute-start(bf16[4,32,16,128]{3,2,1,0:T(8,128)(2,1)S(1)} %get-tuple-element.48), channel_id=1, source_target_pairs={{0,16},{16,1},{1,17},{17,0},{2,18},{18,3},{3,19},{19,2},{4,20},{20... | collective-permute-start | bytes 1572872 | tf_op jit(solution)/shard_map/ppermute | solution.py:215
  8.4 25.1 %collective-permute-start.1 = (bf16[4,32,16,128]{3,2,1,0:T(8,128)(2,1)S(1)}, bf16[4,32,16,128]{3,2,1,0:T(8,128)(2,1)}, u32[]{:S(2)}, u32[]{:S(2)}) collective-permute-start(bf16[4,32,16,128]{3,2,1,0:T(8,128)(2,1)S(1)} %get-tuple-element.49), channel_id=1, source_target_pairs={{0,1},{16,17},{1,0},{17,16},{2,3},{18,19},{3,2},{19,18},{4,5},{20,... | collective-permute-start | bytes 1572872 | tf_op jit(solution)/shard_map/ppermute | solution.py:215
  10.8 22.7 %collective-permute-start.2 = (bf16[4,32,16,128]{3,2,1,0:T(8,128)(2,1)S(1)}, bf16[4,32,16,128]{3,2,1,0:T(8,128)(2,1)}, u32[]{:S(2)}, u32[]{:S(2)}) collective-permute-start(bf16[4,32,16,128]{3,2,1,0:T(8,128)(2,1)S(1)} %get-tuple-element.50), channel_id=1, source_target_pairs={{0,17},{16,0},{1,16},{17,1},{2,19},{18,2},{3,18},{19,3},{4,21},{20... | collective-permute-start | bytes 1572872 | tf_op jit(solution)/shard_map/ppermute | solution.py:215
  14.8 25.3 %collective-permute-start.6 = (bf16[4,32,16,128]{3,2,1,0:T(8,128)(2,1)S(1)}, bf16[4,32,16,128]{3,2,1,0:T(8,128)(2,1)}, u32[]{:S(2)}, u32[]{:S(2)}) collective-permute-start(bf16[4,32,16,128]{3,2,1,0:T(8,128)(2,1)S(1)} %get-tuple-element.65), channel_id=1, source_target_pairs={{0,32},{32,64},{64,96},{96,0},{1,33},{33,65},{65,97},{97,1},{2,34}... | collective-permute-start | bytes 1572872 | tf_op jit(solution)/shard_map/ppermute | solution.py:219
  16.1 25.1 %collective-permute-start.7 = (bf16[4,32,16,128]{3,2,1,0:T(8,128)(2,1)S(1)}, bf16[4,32,16,128]{3,2,1,0:T(8,128)(2,1)}, u32[]{:S(2)}, u32[]{:S(2)}) collective-permute-start(bf16[4,32,16,128]{3,2,1,0:T(8,128)(2,1)S(1)} %get-tuple-element.66), channel_id=1, source_target_pairs={{0,64},{32,96},{64,0},{96,32},{1,65},{33,97},{65,1},{97,33},{2,66}... | collective-permute-start | bytes 1572872 | tf_op jit(solution)/shard_map/ppermute | solution.py:219
  21.7 19.4 %collective-permute-start.8 = (bf16[4,32,16,128]{3,2,1,0:T(8,128)(2,1)S(1)}, bf16[4,32,16,128]{3,2,1,0:T(8,128)(2,1)}, u32[]{:S(2)}, u32[]{:S(2)}) collective-permute-start(bf16[4,32,16,128]{3,2,1,0:T(8,128)(2,1)S(1)} %get-tuple-element.67), channel_id=1, source_target_pairs={{0,96},{32,0},{64,32},{96,64},{1,97},{33,1},{65,33},{97,65},{2,98}... | collective-permute-start | bytes 1572872 | tf_op jit(solution)/shard_map/ppermute | solution.py:219
  36.1 11.5 %collective-permute-start.3 = (bf16[32,16,128]{2,1,0:T(8,128)(2,1)}, bf16[32,16,128]{2,1,0:T(8,128)(2,1)S(1)}, u32[]{:S(2)}, u32[]{:S(2)}) collective-permute-start(bf16[32,16,128]{2,1,0:T(8,128)(2,1)} %get-tuple-element.61), channel_id=1, source_target_pairs={{0,32},{32,64},{64,96},{96,0},{1,33},{33,65},{65,97},{97,1},{2,34}... | collective-permute-start | bytes 393224 | tf_op jit(solution)/shard_map/ppermute | solution.py:219
  37.5 10.1 %collective-permute-start.4 = (bf16[32,16,128]{2,1,0:T(8,128)(2,1)}, bf16[32,16,128]{2,1,0:T(8,128)(2,1)S(1)}, u32[]{:S(2)}, u32[]{:S(2)}) collective-permute-start(bf16[32,16,128]{2,1,0:T(8,128)(2,1)} %get-tuple-element.62), channel_id=1, source_target_pairs={{0,64},{32,96},{64,0},{96,32},{1,65},{33,97},{65,1},{97,33},{2,66}... | collective-permute-start | bytes 393224 | tf_op jit(solution)/shard_map/ppermute | solution.py:219
  40.1 7.5 %collective-permute-start.5 = (bf16[32,16,128]{2,1,0:T(8,128)(2,1)}, bf16[32,16,128]{2,1,0:T(8,128)(2,1)S(1)}, u32[]{:S(2)}, u32[]{:S(2)}) collective-permute-start(bf16[32,16,128]{2,1,0:T(8,128)(2,1)} %get-tuple-element.63), channel_id=1, source_target_pairs={{0,96},{32,0},{64,32},{96,64},{1,97},{33,1},{65,33},{97,65},{2,98}... | collective-permute-start | bytes 393224 | tf_op jit(solution)/shard_map/ppermute | solution.py:219
  43.7 5.6 %collective-permute-start.10 = (bf16[32,16,128]{2,1,0:T(8,128)(2,1)}, bf16[32,16,128]{2,1,0:T(8,128)(2,1)S(1)}, u32[]{:S(2)}, u32[]{:S(2)}) collective-permute-start(bf16[32,16,128]{2,1,0:T(8,128)(2,1)} %get-tuple-element.70), channel_id=1, source_target_pairs={{0,1},{16,17},{1,0},{17,16},{2,3},{18,19},{3,2},{19,18},{4,5},{20,... | collective-permute-start | bytes 393224 | tf_op jit(solution)/shard_map/ppermute | solution.py:215
  45.9 6.7 %collective-permute-start.11 = (bf16[32,16,128]{2,1,0:T(8,128)(2,1)}, bf16[32,16,128]{2,1,0:T(8,128)(2,1)S(1)}, u32[]{:S(2)}, u32[]{:S(2)}) collective-permute-start(bf16[32,16,128]{2,1,0:T(8,128)(2,1)} %get-tuple-element.71), channel_id=1, source_target_pairs={{0,17},{16,0},{1,16},{17,1},{2,19},{18,2},{3,18},{19,3},{4,21},{20... | collective-permute-start | bytes 393224 | tf_op jit(solution)/shard_map/ppermute | solution.py:215
  47.6 6.4 %collective-permute-start.9 = (bf16[32,16,128]{2,1,0:T(8,128)(2,1)}, bf16[32,16,128]{2,1,0:T(8,128)(2,1)S(1)}, u32[]{:S(2)}, u32[]{:S(2)}) collective-permute-start(bf16[32,16,128]{2,1,0:T(8,128)(2,1)} %get-tuple-element.69), channel_id=1, source_target_pairs={{0,16},{16,1},{1,17},{17,0},{2,18},{18,3},{3,19},{19,2},{4,20},{20... | collective-permute-start | bytes 393224 | tf_op jit(solution)/shard_map/ppermute | solution.py:215
  56.2 8.8 %collective-permute-start.12 = (bf16[2,2,16,8,128]{4,3,2,1,0:T(8,128)(2,1)S(1)}, bf16[2,2,16,8,128]{4,3,2,1,0:T(8,128)(2,1)S(1)}, u32[]{:S(2)}, u32[]{:S(2)}) collective-permute-start(bf16[2,2,16,8,128]{4,3,2,1,0:T(8,128)(2,1)S(1)} %get-tuple-element.73), channel_id=1, source_target_pairs={{0,16},{16,0},{32,48},{48,32},{64,80},{80,64},{96,112},{112,96},{1... | collective-permute-start | bytes 393224 | tf_op jit(solution)/shard_map/ppermute | solution.py:639
  56.3 8.8 %collective-permute-start.13 = (bf16[2,2,16,8,128]{4,3,2,1,0:T(8,128)(2,1)S(1)}, bf16[2,2,16,8,128]{4,3,2,1,0:T(8,128)(2,1)S(1)}, u32[]{:S(2)}, u32[]{:S(2)}) collective-permute-start(bf16[2,2,16,8,128]{4,3,2,1,0:T(8,128)(2,1)S(1)} %get-tuple-element.74), channel_id=1, source_target_pairs={{16,32},{32,16},{48,64},{64,48},{80,96},{96,80},{17,33},{33,17},{4... | collective-permute-start | bytes 393224 | tf_op jit(solution)/shard_map/ppermute | solution.py:640
  57.0 8.0 %collective-permute-start.15 = (bf16[2,2,16,2,128]{4,3,2,1,0:T(2,128)(2,1)S(1)}, bf16[2,2,16,2,128]{4,3,2,1,0:T(2,128)(2,1)S(1)}, u32[]{:S(2)}, u32[]{:S(2)}) collective-permute-start(bf16[2,2,16,2,128]{4,3,2,1,0:T(2,128)(2,1)S(1)} %get-tuple-element.76), channel_id=1, source_target_pairs={{0,17},{1,16},{16,1},{17,0},{32,49},{33,48},{48,33},{49,32},{64,81... | collective-permute-start | bytes 98312 | tf_op jit(solution)/shard_map/ppermute | solution.py:642
  62.5 5.3 %collective-permute-start.14 = (bf16[2,8,16,2,128]{4,3,2,1,0:T(2,128)(2,1)S(1)}, bf16[2,8,16,2,128]{4,3,2,1,0:T(2,128)(2,1)S(1)}, u32[]{:S(2)}, u32[]{:S(2)}) collective-permute-start(bf16[2,8,16,2,128]{4,3,2,1,0:T(2,128)(2,1)S(1)} %get-tuple-element.75), channel_id=1, source_target_pairs={{0,1},{1,0},{2,3},{3,2},{4,5},{5,4},{6,7},{7,6},{8,9},{9,8},{10,11... | collective-permute-start | bytes 393224 | tf_op jit(solution)/shard_map/ppermute | solution.py:641
  67.9 10.0 %collective-permute-start.18 = (bf16[2,12,2,10,128]{4,3,2,1,0:T(8,128)(2,1)S(1)}, bf16[2,12,2,10,128]{4,3,2,1,0:T(8,128)(2,1)S(1)}, u32[]{:S(2)}, u32[]{:S(2)}) collective-permute-start(bf16[2,12,2,10,128]{4,3,2,1,0:T(8,128)(2,1)S(1)} %maximum_maximum_fusion.1), channel_id=1, source_target_pairs={{2,4},{4,2},{6,8},{8,6},{10,12},{12,10},{3,5},{5,3},{7,9},{9,7},{1... | collective-permute-start | bytes 368648 | tf_op jit(solution)/shard_map/ppermute | solution.py:655
  74.6 3.3 %collective-permute-start.17 = (bf16[2,12,2,10,128]{4,3,2,1,0:T(8,128)(2,1)S(1)}, bf16[2,12,2,10,128]{4,3,2,1,0:T(8,128)(2,1)S(1)}, u32[]{:S(2)}, u32[]{:S(2)}) collective-permute-start(bf16[2,12,2,10,128]{4,3,2,1,0:T(8,128)(2,1)S(1)} %maximum_maximum_fusion), channel_id=1, source_target_pairs={{0,2},{2,0},{4,6},{6,4},{8,10},{10,8},{12,14},{14,12},{1,3},{3,1},... | collective-permute-start | bytes 368648 | tf_op jit(solution)/shard_map/ppermute | solution.py:654
  97.2 2.7 %collective-permute-start.19 = (bf16[27,128,128]{2,1,0:T(8,128)(2,1)}, bf16[27,128,128]{2,1,0:T(8,128)(2,1)S(1)}, u32[]{:S(2)}, u32[]{:S(2)}) collective-permute-start(bf16[27,128,128]{2,1,0:T(8,128)(2,1)} %get-tuple-element.87), channel_id=1, source_target_pairs={{0,2},{2,0},{1,3},{3,1},{4,6},{6,4},{5,7},{7,5},{8,10},{10,8},{9,1... | collective-permute-start | bytes 2654216 | tf_op jit(solution)/shard_map/ppermute | solution.py:678
  102.2 20.5 %all-to-all-start = ((bf16[16,216,128]{2,1,0:T(8,128)(2,1)}), bf16[16,216,128]{2,1,0:T(8,128)(2,1)S(1)}, u32[]{:S(2)}, u32[]{:S(2)}) async-start(bf16[16,216,128]{2,1,0:T(8,128)(2,1)} %bitcast.12), calls=%async_computation | async-start | bytes 1769472 | tf_op jit(solution)/shard_map/all_to_all | solution.py:660
  122.9 6.0 %collective-permute-start.20 = (bf16[224,128]{1,0:T(8,128)(2,1)S(1)}, bf16[224,128]{1,0:T(8,128)(2,1)S(1)}, u32[]{:S(2)}, u32[]{:S(2)}) collective-permute-start(bf16[224,128]{1,0:T(8,128)(2,1)S(1)} %maximum_maximum_fusion.2), channel_id=1, source_target_pairs={{0,8},{4,12},{8,0},{12,4},{1,9},{5,13},{9,1},{13,5},{2,10},{6,14},... | collective-permute-start | bytes 172040 | tf_op jit(solution)/shard_map/ppermute | solution.py:219
  126.2 4.2 %collective-permute-start.21 = (bf16[224,128]{1,0:T(8,128)(2,1)S(1)}, bf16[224,128]{1,0:T(8,128)(2,1)S(1)}, u32[]{:S(2)}, u32[]{:S(2)}) collective-permute-start(bf16[224,128]{1,0:T(8,128)(2,1)S(1)} %maximum_maximum_fusion.2), channel_id=1, source_target_pairs={{0,4},{4,8},{8,12},{12,0},{1,5},{5,9},{9,13},{13,1},{2,6},{6,10},{... | collective-permute-start | bytes 172040 | tf_op jit(solution)/shard_map/ppermute | solution.py:219
  127.0 3.5 %collective-permute-start.22 = (bf16[224,128]{1,0:T(8,128)(2,1)S(1)}, bf16[224,128]{1,0:T(8,128)(2,1)S(1)}, u32[]{:S(2)}, u32[]{:S(2)}) collective-permute-start(bf16[224,128]{1,0:T(8,128)(2,1)S(1)} %maximum_maximum_fusion.2), channel_id=1, source_target_pairs={{0,12},{4,0},{8,4},{12,8},{1,13},{5,1},{9,5},{13,9},{2,14},{6,2},{... | collective-permute-start | bytes 172040 | tf_op jit(solution)/shard_map/ppermute | solution.py:219
  146.9 7.0 %collective-permute-start.23 = (bf16[16,224,128]{2,1,0:T(8,128)(2,1)S(1)}, bf16[16,224,128]{2,1,0:T(8,128)(2,1)S(1)}, u32[]{:S(2)}, u32[]{:S(2)}) collective-permute-start(bf16[16,224,128]{2,1,0:T(8,128)(2,1)S(1)} %all_to_all.10), channel_id=1, source_target_pairs={{0,2},{2,0},{1,3},{3,1},{4,6},{6,4},{5,7},{7,5},{8,10},{10,8},{9,1... | collective-permute-start | bytes 2752520 | tf_op jit(solution)/shard_map/ppermute | solution.py:697
  (18 other events, 150.4 us)

commit v9 on v8

--- a/solution.py
+++ b/solution.py
@@ -307,7 +307,8 @@
     first_y, second_y = send_rows(where_ref[3], 18)
     at_one = pl.ds(first_x, 2)
     at_two = pl.ds(second_x, 2)
-    volume[...] = jnp.full(volume.shape, outside, F32)
+    if outside is not None:
+        volume[...] = jnp.full(volume.shape, outside, F32)
     volume[2:10, 2:18, 2:10, :] = centre[which].astype(F32)
     volume[at_one, 2:18, 2:10, :] = x_one[which].astype(F32)
     volume[at_two, 2:18, 2:10, :] = x_two[which].astype(F32)
@@ -328,6 +329,9 @@
                 values = came[which].astype(F32)
                 for at_x, rows in spans:
                     volume[at_x, at_y, at_z, :] = values[rows, :, 8:10]
+
+    if outside is None:
+        return
 
     @pl.when(where_ref[2] == 0)
     def _():
@@ -389,7 +393,7 @@
     for copy in copies[:8]:
         copy.wait()
     fill(cells, 0, pieces, where_ref, OUT)
-    fill(cots, 1, pieces, where_ref, 0.0)
+    fill(cots, 1, pieces, where_ref, None)
     act_t[:, 0:128] = jnp.zeros((128, 128), BF16)
     act_t[:, 1408:1536] = jnp.zeros((128, 128), BF16)
 

time: 157 us -> 157 us (level)
  no operation moved by 1% of the time
where the time goes in v9:
time: 157 us; the launch traced here: 156 us
  starting transfers between devices  54.7 us (35%)
  Pallas kernels  48.8 us (31%)
  waiting for transfers between devices  23.4 us (15%)
  blocking collectives  16.1 us (10%)
  local copies, waits for them, and re-layouts  7.09 us (5%)
  other arithmetic  5.37 us (3%)
    pallas_call x1, Pallas kernels, grads_call(): pl.pallas_call(grads_kernel, out_shape=(jax.ShapeDtypeStruct((10, 18, 16,...  18.4 us
    ppermute x9, starting transfers between devices, along(): return lax.ppermute(value, axis, [(i, (i + shift) % 4) for i in range(4)])  17.9 us
    all_to_all x1, blocking collectives, exchange(): return lax.all_to_all(values, axes, split_axis=0, concat_axis=0, tiled=True)  16.1 us
    pallas_call x1, Pallas kernels, outputs_call(): pl.pallas_call(outputs_kernel, out_shape=(jax.ShapeDtypeStruct((8, 16, 8,...  10.4 us
    ppermute x6, starting transfers between devices, along_x(): return lax.ppermute(value, ('xl', 'xh'), pairs)  9.49 us
    ppermute x6, waiting for transfers between devices, along_x(): return lax.ppermute(value, ('xl', 'xh'), pairs)  8.88 us
    pallas_call x2, Pallas kernels, pair_weights(): pl.pallas_call(pair_kernel, out_shape=(out, out), grid=(4,), in_specs=[pl...  8.44 us
    all_to_all x1, starting transfers between devices, exchange(): return lax.all_to_all(values, axes, split_axis=0, concat_axis=0, tiled=True)  6.85 us
  transfers between devices with their start and end apart: 25, of which 11 were waited for; matrix products, arithmetic and copies ran while one was open for 1% of the time, Pallas kernels for 17%

profile of v9, /device:TPU:1, one launch (start us, length us, event | category | flops | bytes accessed | tf_op | source)
XLA Modules:
  0.0 156.4 jit_solution(16899133802253639496)
XLA Ops:
  8.4 2.5 %collective-permute-start.1 = (bf16[4,32,16,128]{3,2,1,0:T(8,128)(2,1)S(1)}, bf16[4,32,16,128]{3,2,1,0:T(8,128)(2,1)}, u32[]{:S(2)}, u32[]{:S(2)}) collective-permute-start(bf16[4,32,16,128]{3,2,1,0:T(8,128)(2,1)S(1)} %get-tuple-element.49), channel_id=1, source_target_pairs={{0,1},{16,17},{1,0},{17,16},{2,3},{18,19},{3,2},{19,18},{4,5},{20,... | collective-permute-start | bytes 1572872 | tf_op jit(solution)/shard_map/ppermute | solution.py:215
  16.1 2.6 %collective-permute-start.7 = (bf16[4,32,16,128]{3,2,1,0:T(8,128)(2,1)S(1)}, bf16[4,32,16,128]{3,2,1,0:T(8,128)(2,1)}, u32[]{:S(2)}, u32[]{:S(2)}) collective-permute-start(bf16[4,32,16,128]{3,2,1,0:T(8,128)(2,1)S(1)} %get-tuple-element.66), channel_id=1, source_target_pairs={{0,64},{32,96},{64,0},{96,32},{1,65},{33,97},{65,1},{97,33},{2,66}... | collective-permute-start | bytes 1572872 | tf_op jit(solution)/shard_map/ppermute | solution.py:219
  18.7 2.3 %collective-permute-done.p1 = bf16[4,32,16,128]{3,2,1,0:T(8,128)(2,1)S(1)} collective-permute-done((bf16[4,32,16,128]{3,2,1,0:T(8,128)(2,1)S(1)}, bf16[4,32,16,128]{3,2,1,0:T(8,128)(2,1)S(1)}, u32[]{:S(2)}, u32[]{:S(2)}) %collective-permute-start) | collective-permute-done | bytes 524320 | tf_op jit(solution)/shard_map/ppermute | solution.py:215
  21.7 3.0 %collective-permute-start.8 = (bf16[4,32,16,128]{3,2,1,0:T(8,128)(2,1)S(1)}, bf16[4,32,16,128]{3,2,1,0:T(8,128)(2,1)}, u32[]{:S(2)}, u32[]{:S(2)}) collective-permute-start(bf16[4,32,16,128]{3,2,1,0:T(8,128)(2,1)S(1)} %get-tuple-element.67), channel_id=1, source_target_pairs={{0,96},{32,0},{64,32},{96,64},{1,97},{33,1},{65,33},{97,65},{2,98}... | collective-permute-start | bytes 1572872 | tf_op jit(solution)/shard_map/ppermute | solution.py:219
  24.7 4.2 %shard_map.111 = (bf16[4,3,384,256]{3,2,1,0:T(8,128)(2,1)}, bf16[4,3,384,256]{3,2,1,0:T(8,128)(2,1)}) custom-call(bf16[27,128,128]{2,1,0:T(8,128)(2,1)} %weights_ref.2), custom_call_target="tpu_custom_call" | custom-call | flops 1048576 | bytes 6291456 | tf_op jit(solution)/shard_map/pallas_call | solution.py:274
  28.9 4.2 %shard_map.112 = (bf16[4,3,384,256]{3,2,1,0:T(8,128)(2,1)}, bf16[4,3,384,256]{3,2,1,0:T(8,128)(2,1)}) custom-call(bf16[27,128,128]{2,1,0:T(8,128)(2,1)} %weights_ref.3), custom_call_target="tpu_custom_call" | custom-call | flops 1048576 | bytes 6291456 | tf_op jit(solution)/shard_map/pallas_call | solution.py:274
  33.5 2.6 %shard_map.113 = (bf16[32,16,128]{2,1,0:T(8,128)(2,1)}, bf16[32,16,128]{2,1,0:T(8,128)(2,1)}, bf16[32,16,128]{2,1,0:T(8,128)(2,1)}, bf16[32,16,128]{2,1,0:T(8,128)(2,1)}) custom-call(bf16[4,32,16,128]{3,2,1,0:T(8,128)(2,1)} %copy-done.3, bf16[4,32,16,128]{3,2,1,0:T(8,128)(2,1)} %copy-done.9, bf16[4,32,16,128]{3,2,1,0:T(8,128)(2,1)} %collective-permute-done.1.p2, ...), custom_call_target="tpu_custom_call" | custom-call | flops 4194304 | bytes 3145728 | tf_op jit(solution)/shard_map/pallas_call | solution.py:123
  37.5 2.6 %collective-permute-start.4 = (bf16[32,16,128]{2,1,0:T(8,128)(2,1)}, bf16[32,16,128]{2,1,0:T(8,128)(2,1)S(1)}, u32[]{:S(2)}, u32[]{:S(2)}) collective-permute-start(bf16[32,16,128]{2,1,0:T(8,128)(2,1)} %get-tuple-element.62), channel_id=1, source_target_pairs={{0,64},{32,96},{64,0},{96,32},{1,65},{33,97},{65,1},{97,33},{2,66}... | collective-permute-start | bytes 393224 | tf_op jit(solution)/shard_map/ppermute | solution.py:219
  41.2 2.5 %shard_map.115 = (bf16[32,16,128]{2,1,0:T(8,128)(2,1)}, bf16[32,16,128]{2,1,0:T(8,128)(2,1)}, bf16[32,16,128]{2,1,0:T(8,128)(2,1)}, bf16[32,16,128]{2,1,0:T(8,128)(2,1)}) custom-call(bf16[4,32,16,128]{3,2,1,0:T(8,128)(2,1)} %copy-done.2, bf16[4,32,16,128]{3,2,1,0:T(8,128)(2,1)} %collective-permute-done.6.p1, ...), custom_call_target="tpu_custom_call" | custom-call | flops 4194304 | bytes 3145728 | tf_op jit(solution)/shard_map/pallas_call | solution.py:123
  43.7 2.2 %collective-permute-start.10 = (bf16[32,16,128]{2,1,0:T(8,128)(2,1)}, bf16[32,16,128]{2,1,0:T(8,128)(2,1)S(1)}, u32[]{:S(2)}, u32[]{:S(2)}) collective-permute-start(bf16[32,16,128]{2,1,0:T(8,128)(2,1)} %get-tuple-element.70), channel_id=1, source_target_pairs={{0,1},{16,17},{1,0},{17,16},{2,3},{18,19},{3,2},{19,18},{4,5},{20,... | collective-permute-start | bytes 393224 | tf_op jit(solution)/shard_map/ppermute | solution.py:215
  49.3 3.3 %collective-permute-done.11.b3 = bf16[32,16,128]{2,1,0:T(8,128)(2,1)S(1)} collective-permute-done((bf16[32,16,128]{2,1,0:T(8,128)(2,1)}, bf16[32,16,128]{2,1,0:T(8,128)(2,1)S(1)}, u32[]{:S(2)}, u32[]{:S(2)}) %collective-permute-start.11) | collective-permute-done | bytes 131104 | tf_op jit(solution)/shard_map/ppermute | solution.py:215
  57.0 5.5 %collective-permute-start.15 = (bf16[2,2,16,2,128]{4,3,2,1,0:T(2,128)(2,1)S(1)}, bf16[2,2,16,2,128]{4,3,2,1,0:T(2,128)(2,1)S(1)}, u32[]{:S(2)}, u32[]{:S(2)}) collective-permute-start(bf16[2,2,16,2,128]{4,3,2,1,0:T(2,128)(2,1)S(1)} %get-tuple-element.76), channel_id=1, source_target_pairs={{0,17},{1,16},{16,1},{17,0},{32,49},{33,48},{48,33},{49,32},{64,81... | collective-permute-start | bytes 98312 | tf_op jit(solution)/shard_map/ppermute | solution.py:646
  65.1 2.7 %collective-permute-done.14.p3 = bf16[2,8,16,2,128]{4,3,2,1,0:T(2,128)(2,1)S(1)} collective-permute-done((bf16[2,8,16,2,128]{4,3,2,1,0:T(2,128)(2,1)S(1)}, bf16[2,8,16,2,128]{4,3,2,1,0:T(2,128)(2,1)S(1)}, u32[]{:S(2)}, u32[]{:S(2)}) %collective-permute-start.14) | collective-permute-done | bytes 131104 | tf_op jit(solution)/shard_map/ppermute | solution.py:645
  67.9 6.6 %collective-permute-start.18 = (bf16[2,12,2,10,128]{4,3,2,1,0:T(8,128)(2,1)S(1)}, bf16[2,12,2,10,128]{4,3,2,1,0:T(8,128)(2,1)S(1)}, u32[]{:S(2)}, u32[]{:S(2)}) collective-permute-start(bf16[2,12,2,10,128]{4,3,2,1,0:T(8,128)(2,1)S(1)} %maximum_maximum_fusion.1), channel_id=1, source_target_pairs={{2,4},{4,2},{6,8},{8,6},{10,12},{12,10},{3,5},{5,3},{7,9},{9,7},{1... | collective-permute-start | bytes 368648 | tf_op jit(solution)/shard_map/ppermute | solution.py:659
  74.7 3.2 %collective-permute-done.18.p7 = bf16[2,12,2,10,128]{4,3,2,1,0:T(8,128)(2,1)S(1)} collective-permute-done((bf16[2,12,2,10,128]{4,3,2,1,0:T(8,128)(2,1)S(1)}, bf16[2,12,2,10,128]{4,3,2,1,0:T(8,128)(2,1)S(1)}, u32[]{:S(2)}, u32[]{:S(2)}) %collective-permute-start.18) | collective-permute-done | bytes 122912 | tf_op jit(solution)/shard_map/ppermute | solution.py:659
  78.6 18.4 %shard_map.117 = (bf16[10,18,16,128]{3,2,1,0:T(8,128)(2,1)}, bf16[10,18,16,128]{3,2,1,0:T(8,128)(2,1)}, bf16[27,128,128]{2,1,0:T(8,128)(2,1)}, bf16[27,128,128]{2,1,0:T(8,128)(2,1)}) custom-call(s32[4]{0:T(128)} %copy-done.8, f32[1,128]{1,0:T(1,128)} %bitcast.52, bf16[2,8,16,8,128]{4,3,2,1,0:T(8,128)(2,1)} %copy-done.7, ...), custom_call_target="tpu_custom_call" | custom-call | flops 10737418240 | bytes 8388608 | tf_op jit(solution)/shard_map/pallas_call | solution.py:482
  97.2 2.5 %collective-permute-done.19.other_ref = bf16[27,128,128]{2,1,0:T(8,128)(2,1)S(1)} collective-permute-done((bf16[27,128,128]{2,1,0:T(8,128)(2,1)}, bf16[27,128,128]{2,1,0:T(8,128)(2,1)S(1)}, u32[]{:S(2)}, u32[]{:S(2)}) %collective-permute-start.19) | collective-permute-done | bytes 884768 | tf_op jit(solution)/shard_map/ppermute | solution.py:682
  102.0 6.8 %all-to-all-start = ((bf16[16,216,128]{2,1,0:T(8,128)(2,1)}), bf16[16,216,128]{2,1,0:T(8,128)(2,1)S(1)}, u32[]{:S(2)}, u32[]{:S(2)}) async-start(bf16[16,216,128]{2,1,0:T(8,128)(2,1)} %bitcast.12), calls=%async_computation | async-start | bytes 1769472 | tf_op jit(solution)/shard_map/all_to_all | solution.py:664
  108.9 10.4 %shard_map.118 = (bf16[8,16,8,128]{3,2,1,0:T(8,128)(2,1)}, bf16[8,16,8,128]{3,2,1,0:T(8,128)(2,1)}, f32[8,128]{1,0:T(8,128)}) custom-call(f32[1,128]{1,0:T(1,128)} %bitcast.53, bf16[2,8,16,8,128]{4,3,2,1,0:T(8,128)(2,1)} %copy-done.7, bf16[10,18,16,128]{3,2,1,0:T(8,128)(2,1)} %get-tuple-element.80.act_hbm, ...), custom_call_target="tpu_custom_call" | custom-call | flops 8589934592 | bytes 6291456 | tf_op jit(solution)/shard_map/pallas_call | solution.py:594
  120.1 2.5 %all-to-all-done = bf16[16,216,128]{2,1,0:T(8,128)(2,1)S(1)} async-done(((bf16[16,216,128]{2,1,0:T(8,128)(2,1)}), bf16[16,216,128]{2,1,0:T(8,128)(2,1)S(1)}, u32[]{:S(2)}, u32[]{:S(2)}) %all-to-all-start) | async-done | bytes 884768 | tf_op jit(solution)/shard_map/all_to_all | solution.py:664
  122.8 3.3 %collective-permute-start.20 = (bf16[224,128]{1,0:T(8,128)(2,1)S(1)}, bf16[224,128]{1,0:T(8,128)(2,1)S(1)}, u32[]{:S(2)}, u32[]{:S(2)}) collective-permute-start(bf16[224,128]{1,0:T(8,128)(2,1)S(1)} %maximum_maximum_fusion.2), channel_id=1, source_target_pairs={{0,8},{4,12},{8,0},{12,4},{1,9},{5,13},{9,1},{13,5},{2,10},{6,14},... | collective-permute-start | bytes 172040 | tf_op jit(solution)/shard_map/ppermute | solution.py:219
  130.7 16.1 %all_to_all.10 = bf16[16,224,128]{2,1,0:T(8,128)(2,1)S(1)} all-to-all(bf16[16,224,128]{2,1,0:T(8,128)(2,1)S(1)} %broadcast_in_dim.2), channel_id=1, replica_groups=mesh['y'=4,'xl'=2,'z'=4,'c'=2,'xh'=2] {'y','xl','xh'}, dimensions={0} | all-to-all | bytes 1835008 | tf_op jit(solution)/shard_map/all_to_all | solution.py:664
  146.7 4.9 %collective-permute-start.23 = (bf16[16,224,128]{2,1,0:T(8,128)(2,1)S(1)}, bf16[16,224,128]{2,1,0:T(8,128)(2,1)S(1)}, u32[]{:S(2)}, u32[]{:S(2)}) collective-permute-start(bf16[16,224,128]{2,1,0:T(8,128)(2,1)S(1)} %all_to_all.10), channel_id=1, source_target_pairs={{0,2},{2,0},{1,3},{3,1},{4,6},{6,4},{5,7},{7,5},{8,10},{10,8},{9,1... | collective-permute-start | bytes 2752520 | tf_op jit(solution)/shard_map/ppermute | solution.py:701
  154.3 2.1 %convert_multiply_fusion = (f32[16,216,128]{2,1,0:T(8,128)}, f32[16,216,128]{2,1,0:T(8,128)}) fusion(pred[]{:T(512)S(6)} %eq.9, bf16[16,224,128]{2,1,0:T(8,128)(2,1)S(1)} %collective-permute-done.23, bf16[16,224,128]{2,1,0:T(8,128)(2,1)S(1)} %all_to_all.10), kind=kLoop, calls=%fused_computation | loop fusion | flops 2654208 | bytes 5308417 | tf_op jit(solution)/shard_map/mul | solution.py:706
  (98 shorter events, 38.3 us)
Async XLA Ops:
  6.3 14.6 %collective-permute-start = (bf16[4,32,16,128]{3,2,1,0:T(8,128)(2,1)S(1)}, bf16[4,32,16,128]{3,2,1,0:T(8,128)(2,1)S(1)}, u32[]{:S(2)}, u32[]{:S(2)}) collective-permute-start(bf16[4,32,16,128]{3,2,1,0:T(8,128)(2,1)S(1)} %get-tuple-element.48), channel_id=1, source_target_pairs={{0,16},{16,1},{1,17},{17,0},{2,18},{18,3},{3,19},{19,2},{4,20},{20... | collective-permute-start | bytes 1572872 | tf_op jit(solution)/shard_map/ppermute | solution.py:215
  8.4 25.1 %collective-permute-start.1 = (bf16[4,32,16,128]{3,2,1,0:T(8,128)(2,1)S(1)}, bf16[4,32,16,128]{3,2,1,0:T(8,128)(2,1)}, u32[]{:S(2)}, u32[]{:S(2)}) collective-permute-start(bf16[4,32,16,128]{3,2,1,0:T(8,128)(2,1)S(1)} %get-tuple-element.49), channel_id=1, source_target_pairs={{0,1},{16,17},{1,0},{17,16},{2,3},{18,19},{3,2},{19,18},{4,5},{20,... | collective-permute-start | bytes 1572872 | tf_op jit(solution)/shard_map/ppermute | solution.py:215
  10.8 22.7 %collective-permute-start.2 = (bf16[4,32,16,128]{3,2,1,0:T(8,128)(2,1)S(1)}, bf16[4,32,16,128]{3,2,1,0:T(8,128)(2,1)}, u32[]{:S(2)}, u32[]{:S(2)}) collective-permute-start(bf16[4,32,16,128]{3,2,1,0:T(8,128)(2,1)S(1)} %get-tuple-element.50), channel_id=1, source_target_pairs={{0,17},{16,0},{1,16},{17,1},{2,19},{18,2},{3,18},{19,3},{4,21},{20... | collective-permute-start | bytes 1572872 | tf_op jit(solution)/shard_map/ppermute | solution.py:215
  14.8 25.3 %collective-permute-start.6 = (bf16[4,32,16,128]{3,2,1,0:T(8,128)(2,1)S(1)}, bf16[4,32,16,128]{3,2,1,0:T(8,128)(2,1)}, u32[]{:S(2)}, u32[]{:S(2)}) collective-permute-start(bf16[4,32,16,128]{3,2,1,0:T(8,128)(2,1)S(1)} %get-tuple-element.65), channel_id=1, source_target_pairs={{0,32},{32,64},{64,96},{96,0},{1,33},{33,65},{65,97},{97,1},{2,34}... | collective-permute-start | bytes 1572872 | tf_op jit(solution)/shard_map/ppermute | solution.py:219
  16.1 25.1 %collective-permute-start.7 = (bf16[4,32,16,128]{3,2,1,0:T(8,128)(2,1)S(1)}, bf16[4,32,16,128]{3,2,1,0:T(8,128)(2,1)}, u32[]{:S(2)}, u32[]{:S(2)}) collective-permute-start(bf16[4,32,16,128]{3,2,1,0:T(8,128)(2,1)S(1)} %get-tuple-element.66), channel_id=1, source_target_pairs={{0,64},{32,96},{64,0},{96,32},{1,65},{33,97},{65,1},{97,33},{2,66}... | collective-permute-start | bytes 1572872 | tf_op jit(solution)/shard_map/ppermute | solution.py:219
  21.7 19.4 %collective-permute-start.8 = (bf16[4,32,16,128]{3,2,1,0:T(8,128)(2,1)S(1)}, bf16[4,32,16,128]{3,2,1,0:T(8,128)(2,1)}, u32[]{:S(2)}, u32[]{:S(2)}) collective-permute-start(bf16[4,32,16,128]{3,2,1,0:T(8,128)(2,1)S(1)} %get-tuple-element.67), channel_id=1, source_target_pairs={{0,96},{32,0},{64,32},{96,64},{1,97},{33,1},{65,33},{97,65},{2,98}... | collective-permute-start | bytes 1572872 | tf_op jit(solution)/shard_map/ppermute | solution.py:219
  36.1 11.5 %collective-permute-start.3 = (bf16[32,16,128]{2,1,0:T(8,128)(2,1)}, bf16[32,16,128]{2,1,0:T(8,128)(2,1)S(1)}, u32[]{:S(2)}, u32[]{:S(2)}) collective-permute-start(bf16[32,16,128]{2,1,0:T(8,128)(2,1)} %get-tuple-element.61), channel_id=1, source_target_pairs={{0,32},{32,64},{64,96},{96,0},{1,33},{33,65},{65,97},{97,1},{2,34}... | collective-permute-start | bytes 393224 | tf_op jit(solution)/shard_map/ppermute | solution.py:219
  37.5 10.1 %collective-permute-start.4 = (bf16[32,16,128]{2,1,0:T(8,128)(2,1)}, bf16[32,16,128]{2,1,0:T(8,128)(2,1)S(1)}, u32[]{:S(2)}, u32[]{:S(2)}) collective-permute-start(bf16[32,16,128]{2,1,0:T(8,128)(2,1)} %get-tuple-element.62), channel_id=1, source_target_pairs={{0,64},{32,96},{64,0},{96,32},{1,65},{33,97},{65,1},{97,33},{2,66}... | collective-permute-start | bytes 393224 | tf_op jit(solution)/shard_map/ppermute | solution.py:219
  40.1 7.5 %collective-permute-start.5 = (bf16[32,16,128]{2,1,0:T(8,128)(2,1)}, bf16[32,16,128]{2,1,0:T(8,128)(2,1)S(1)}, u32[]{:S(2)}, u32[]{:S(2)}) collective-permute-start(bf16[32,16,128]{2,1,0:T(8,128)(2,1)} %get-tuple-element.63), channel_id=1, source_target_pairs={{0,96},{32,0},{64,32},{96,64},{1,97},{33,1},{65,33},{97,65},{2,98}... | collective-permute-start | bytes 393224 | tf_op jit(solution)/shard_map/ppermute | solution.py:219
  43.7 5.6 %collective-permute-start.10 = (bf16[32,16,128]{2,1,0:T(8,128)(2,1)}, bf16[32,16,128]{2,1,0:T(8,128)(2,1)S(1)}, u32[]{:S(2)}, u32[]{:S(2)}) collective-permute-start(bf16[32,16,128]{2,1,0:T(8,128)(2,1)} %get-tuple-element.70), channel_id=1, source_target_pairs={{0,1},{16,17},{1,0},{17,16},{2,3},{18,19},{3,2},{19,18},{4,5},{20,... | collective-permute-start | bytes 393224 | tf_op jit(solution)/shard_map/ppermute | solution.py:215
  45.9 6.7 %collective-permute-start.11 = (bf16[32,16,128]{2,1,0:T(8,128)(2,1)}, bf16[32,16,128]{2,1,0:T(8,128)(2,1)S(1)}, u32[]{:S(2)}, u32[]{:S(2)}) collective-permute-start(bf16[32,16,128]{2,1,0:T(8,128)(2,1)} %get-tuple-element.71), channel_id=1, source_target_pairs={{0,17},{16,0},{1,16},{17,1},{2,19},{18,2},{3,18},{19,3},{4,21},{20... | collective-permute-start | bytes 393224 | tf_op jit(solution)/shard_map/ppermute | solution.py:215
  47.6 6.4 %collective-permute-start.9 = (bf16[32,16,128]{2,1,0:T(8,128)(2,1)}, bf16[32,16,128]{2,1,0:T(8,128)(2,1)S(1)}, u32[]{:S(2)}, u32[]{:S(2)}) collective-permute-start(bf16[32,16,128]{2,1,0:T(8,128)(2,1)} %get-tuple-element.69), channel_id=1, source_target_pairs={{0,16},{16,1},{1,17},{17,0},{2,18},{18,3},{3,19},{19,2},{4,20},{20... | collective-permute-start | bytes 393224 | tf_op jit(solution)/shard_map/ppermute | solution.py:215
  56.2 8.8 %collective-permute-start.12 = (bf16[2,2,16,8,128]{4,3,2,1,0:T(8,128)(2,1)S(1)}, bf16[2,2,16,8,128]{4,3,2,1,0:T(8,128)(2,1)S(1)}, u32[]{:S(2)}, u32[]{:S(2)}) collective-permute-start(bf16[2,2,16,8,128]{4,3,2,1,0:T(8,128)(2,1)S(1)} %get-tuple-element.73), channel_id=1, source_target_pairs={{0,16},{16,0},{32,48},{48,32},{64,80},{80,64},{96,112},{112,96},{1... | collective-permute-start | bytes 393224 | tf_op jit(solution)/shard_map/ppermute | solution.py:643
  56.3 8.8 %collective-permute-start.13 = (bf16[2,2,16,8,128]{4,3,2,1,0:T(8,128)(2,1)S(1)}, bf16[2,2,16,8,128]{4,3,2,1,0:T(8,128)(2,1)S(1)}, u32[]{:S(2)}, u32[]{:S(2)}) collective-permute-start(bf16[2,2,16,8,128]{4,3,2,1,0:T(8,128)(2,1)S(1)} %get-tuple-element.74), channel_id=1, source_target_pairs={{16,32},{32,16},{48,64},{64,48},{80,96},{96,80},{17,33},{33,17},{4... | collective-permute-start | bytes 393224 | tf_op jit(solution)/shard_map/ppermute | solution.py:644
  57.0 8.0 %collective-permute-start.15 = (bf16[2,2,16,2,128]{4,3,2,1,0:T(2,128)(2,1)S(1)}, bf16[2,2,16,2,128]{4,3,2,1,0:T(2,128)(2,1)S(1)}, u32[]{:S(2)}, u32[]{:S(2)}) collective-permute-start(bf16[2,2,16,2,128]{4,3,2,1,0:T(2,128)(2,1)S(1)} %get-tuple-element.76), channel_id=1, source_target_pairs={{0,17},{1,16},{16,1},{17,0},{32,49},{33,48},{48,33},{49,32},{64,81... | collective-permute-start | bytes 98312 | tf_op jit(solution)/shard_map/ppermute | solution.py:646
  62.5 5.3 %collective-permute-start.14 = (bf16[2,8,16,2,128]{4,3,2,1,0:T(2,128)(2,1)S(1)}, bf16[2,8,16,2,128]{4,3,2,1,0:T(2,128)(2,1)S(1)}, u32[]{:S(2)}, u32[]{:S(2)}) collective-permute-start(bf16[2,8,16,2,128]{4,3,2,1,0:T(2,128)(2,1)S(1)} %get-tuple-element.75), channel_id=1, source_target_pairs={{0,1},{1,0},{2,3},{3,2},{4,5},{5,4},{6,7},{7,6},{8,9},{9,8},{10,11... | collective-permute-start | bytes 393224 | tf_op jit(solution)/shard_map/ppermute | solution.py:645
  67.9 10.0 %collective-permute-start.18 = (bf16[2,12,2,10,128]{4,3,2,1,0:T(8,128)(2,1)S(1)}, bf16[2,12,2,10,128]{4,3,2,1,0:T(8,128)(2,1)S(1)}, u32[]{:S(2)}, u32[]{:S(2)}) collective-permute-start(bf16[2,12,2,10,128]{4,3,2,1,0:T(8,128)(2,1)S(1)} %maximum_maximum_fusion.1), channel_id=1, source_target_pairs={{2,4},{4,2},{6,8},{8,6},{10,12},{12,10},{3,5},{5,3},{7,9},{9,7},{1... | collective-permute-start | bytes 368648 | tf_op jit(solution)/shard_map/ppermute | solution.py:659
  74.6 3.3 %collective-permute-start.17 = (bf16[2,12,2,10,128]{4,3,2,1,0:T(8,128)(2,1)S(1)}, bf16[2,12,2,10,128]{4,3,2,1,0:T(8,128)(2,1)S(1)}, u32[]{:S(2)}, u32[]{:S(2)}) collective-permute-start(bf16[2,12,2,10,128]{4,3,2,1,0:T(8,128)(2,1)S(1)} %maximum_maximum_fusion), channel_id=1, source_target_pairs={{0,2},{2,0},{4,6},{6,4},{8,10},{10,8},{12,14},{14,12},{1,3},{3,1},... | collective-permute-start | bytes 368648 | tf_op jit(solution)/shard_map/ppermute | solution.py:658
  97.0 2.7 %collective-permute-start.19 = (bf16[27,128,128]{2,1,0:T(8,128)(2,1)}, bf16[27,128,128]{2,1,0:T(8,128)(2,1)S(1)}, u32[]{:S(2)}, u32[]{:S(2)}) collective-permute-start(bf16[27,128,128]{2,1,0:T(8,128)(2,1)} %get-tuple-element.87), channel_id=1, source_target_pairs={{0,2},{2,0},{1,3},{3,1},{4,6},{6,4},{5,7},{7,5},{8,10},{10,8},{9,1... | collective-permute-start | bytes 2654216 | tf_op jit(solution)/shard_map/ppermute | solution.py:682
  102.0 20.5 %all-to-all-start = ((bf16[16,216,128]{2,1,0:T(8,128)(2,1)}), bf16[16,216,128]{2,1,0:T(8,128)(2,1)S(1)}, u32[]{:S(2)}, u32[]{:S(2)}) async-start(bf16[16,216,128]{2,1,0:T(8,128)(2,1)} %bitcast.12), calls=%async_computation | async-start | bytes 1769472 | tf_op jit(solution)/shard_map/all_to_all | solution.py:664
  122.8 6.0 %collective-permute-start.20 = (bf16[224,128]{1,0:T(8,128)(2,1)S(1)}, bf16[224,128]{1,0:T(8,128)(2,1)S(1)}, u32[]{:S(2)}, u32[]{:S(2)}) collective-permute-start(bf16[224,128]{1,0:T(8,128)(2,1)S(1)} %maximum_maximum_fusion.2), channel_id=1, source_target_pairs={{0,8},{4,12},{8,0},{12,4},{1,9},{5,13},{9,1},{13,5},{2,10},{6,14},... | collective-permute-start | bytes 172040 | tf_op jit(solution)/shard_map/ppermute | solution.py:219
  126.1 4.2 %collective-permute-start.21 = (bf16[224,128]{1,0:T(8,128)(2,1)S(1)}, bf16[224,128]{1,0:T(8,128)(2,1)S(1)}, u32[]{:S(2)}, u32[]{:S(2)}) collective-permute-start(bf16[224,128]{1,0:T(8,128)(2,1)S(1)} %maximum_maximum_fusion.2), channel_id=1, source_target_pairs={{0,4},{4,8},{8,12},{12,0},{1,5},{5,9},{9,13},{13,1},{2,6},{6,10},{... | collective-permute-start | bytes 172040 | tf_op jit(solution)/shard_map/ppermute | solution.py:219
  126.8 3.5 %collective-permute-start.22 = (bf16[224,128]{1,0:T(8,128)(2,1)S(1)}, bf16[224,128]{1,0:T(8,128)(2,1)S(1)}, u32[]{:S(2)}, u32[]{:S(2)}) collective-permute-start(bf16[224,128]{1,0:T(8,128)(2,1)S(1)} %maximum_maximum_fusion.2), channel_id=1, source_target_pairs={{0,12},{4,0},{8,4},{12,8},{1,13},{5,1},{9,5},{13,9},{2,14},{6,2},{... | collective-permute-start | bytes 172040 | tf_op jit(solution)/shard_map/ppermute | solution.py:219
  146.7 7.0 %collective-permute-start.23 = (bf16[16,224,128]{2,1,0:T(8,128)(2,1)S(1)}, bf16[16,224,128]{2,1,0:T(8,128)(2,1)S(1)}, u32[]{:S(2)}, u32[]{:S(2)}) collective-permute-start(bf16[16,224,128]{2,1,0:T(8,128)(2,1)S(1)} %all_to_all.10), channel_id=1, source_target_pairs={{0,2},{2,0},{1,3},{3,1},{4,6},{6,4},{5,7},{7,5},{8,10},{10,8},{9,1... | collective-permute-start | bytes 2752520 | tf_op jit(solution)/shard_map/ppermute | solution.py:701
  (18 other events, 150.4 us)
